TPU v7x, 256 devices: a whole 4x4x8 slice. The times are simulated.
256 devices in a mesh: strip: 64 (over x, z, core), chan: 4 (over y).
Axes of the slice: x: 4, y: 4, z: 8, core: 2. Of those that a mesh axis runs over, the one named last changes fastest.
Arguments:
- section_input: bfloat16 [48, 8192, 256], P(None, 'strip'), may hold values from -6 to 6
- conv_weight: bfloat16 [3, 3, 256, 256], replicated, may hold values from -0.125 to 0.125
- conv_bias: float32 [256], replicated, may hold values from -3 to 3
- deep_weight: bfloat16 [3, 3, 256, 512], P(None, None, None, 'chan'), may hold values from -0.125 to 0.125
- deep_bias: float32 [512], P('chan'), may hold values from -3 to 3
- labels: int32 [24, 4096], P(None, 'strip'), may hold values from 0 to 32, as said below
- slot_ids: int32 [2048], P('strip'), may hold values from 0 to 4095, as said below
- embed_grad: float32 [4096, 512], P('strip', 'chan'), may hold values from -0.8 to 0.8
Outputs:
- embeddings: float32 [4096, 512], P('strip', 'chan')
- weight_grad: float32 [3, 3, 256, 512], P(None, None, None, 'chan')
- bias_grad: float32 [512], P('chan')
Inputs may be any that keep to these rules, and one draw needn't show every extreme that they name: `labels`: the value 32 marks background; any other value v names entry v of the list of the strip that holds the pixel. `slot_ids`: A value s names slot s % 64 of owner s // 64 (an index of strip). The slots within one strip's list differ; a slot stands in the lists of at most two strips, which are neighbours (a crack across a strip border). Every owner holds at most 64 components and some owner holds exactly 64.
All inputs are finite; a program needn't handle non-finite values.
Results may differ from a plain program's by a relative error of at most 0.0035.
Values may be sent and summed in bfloat16 or wider, within the bound.
A program may use at most 64 MiB of HBM per device.

v0:
```python
import jax
import jax.numpy as jnp
from jax import lax
from jax.sharding import PartitionSpec as P


def with_halo(cells, sides, width):
    for axis, dim in sides:
        count = lax.axis_size(axis)
        ends = count - 1
        head = lax.slice_in_dim(cells, 0, width, axis=dim)
        tail = lax.slice_in_dim(cells, cells.shape[dim] - width, cells.shape[dim], axis=dim)
        cells = jnp.concatenate(
            [
                lax.ppermute(tail, axis, [(i, (i + 1) % count) for i in range(ends)]),
                cells,
                lax.ppermute(head, axis, [((i + 1) % count, i) for i in range(ends)]),
            ],
            axis=dim,
        )
    return cells


def swish(value):
    return value * jax.nn.sigmoid(value)


def swish_slope(value):
    sigma = jax.nn.sigmoid(value)
    return sigma * (1.0 + value * (1.0 - sigma))


def convolve(padded, weight, row_count, col_count):
    channels = padded.shape[-1]
    running = None
    for shift_row in range(3):
        for shift_col in range(3):
            window = padded[
                shift_row : shift_row + row_count, shift_col : shift_col + col_count
            ].reshape(row_count * col_count, channels)
            partial_term = jnp.dot(
                window, weight[shift_row, shift_col], preferred_element_type=jnp.float32
            )
            running = partial_term if running is None else running + partial_term
    return running.reshape(row_count, col_count, weight.shape[-1])


def pool_pairs(hidden):
    row_count, col_count, channels = hidden.shape
    return (
        hidden.reshape(row_count // 2, 2, col_count // 2, 2, channels)
        .mean(axis=(1, 3))
        .astype(jnp.bfloat16)
    )


def body(
    section_input, conv_weight, conv_bias, deep_weight, deep_bias, labels, slot_ids, embed_grad
):
    chan_count = lax.axis_size("chan")
    chan_pos = lax.axis_index("chan")
    strip_count = lax.axis_size("strip")
    strip_pos = lax.axis_index("strip")
    row_total, col_local, channels = section_input.shape
    row_part = row_total // chan_count
    half_cols = col_local // 2
    padded_rows = jnp.pad(section_input, ((1, 1), (0, 0), (0, 0)))
    own_rows = lax.dynamic_slice_in_dim(padded_rows, chan_pos * row_part, row_part + 2, 0)
    extended = with_halo(own_rows, (("strip", 1),), 3)
    hidden = swish(convolve(extended, conv_weight, row_part, col_local + 4) + conv_bias)
    pooled = pool_pairs(hidden)
    column = jnp.arange(half_cols + 2)
    outside = (column == 0) & (strip_pos == 0) | (column == half_cols + 1) & (
        strip_pos == strip_count - 1
    )
    pooled = jnp.where(outside[None, :, None], jnp.zeros_like(pooled), pooled)
    gathered = lax.all_gather(pooled, "chan", axis=0, tiled=True)
    padded_deep = jnp.pad(gathered, ((1, 1), (0, 0), (0, 0)))
    half_rows = gathered.shape[0]
    deep_pre = convolve(padded_deep, deep_weight, half_rows, half_cols) + deep_bias
    width_deep = deep_weight.shape[-1]
    features = swish(deep_pre).astype(jnp.bfloat16).reshape(-1, width_deep)
    flat_labels = labels.reshape(-1)
    list_len = slot_ids.shape[0]
    member = flat_labels[None, :] == jnp.arange(list_len, dtype=jnp.int32)[:, None]
    part_sums = jnp.dot(member.astype(jnp.bfloat16), features, preferred_element_type=jnp.float32)
    part_counts = jnp.sum(member.astype(jnp.float32), axis=1)
    owned = embed_grad.shape[0]
    dense_sums = (
        jnp.zeros((owned * strip_count, width_deep), jnp.float32).at[slot_ids].set(part_sums)
    )
    dense_counts = jnp.zeros((owned * strip_count,), jnp.float32).at[slot_ids].set(part_counts)
    slot_sums, slot_counts = (
        lax.psum_scatter(dense_sums, "strip", scatter_dimension=0, tiled=True),
        lax.psum_scatter(dense_counts, "strip", scatter_dimension=0, tiled=True),
    )
    divisor = jnp.maximum(slot_counts, 1.0)[:, None]
    embeddings = slot_sums / divisor
    every_grad = lax.all_gather(embed_grad / divisor, "strip", axis=0, tiled=True)
    entry_grad = every_grad[slot_ids]
    pixel_grad = lax.dot_general(
        member.astype(jnp.float32),
        entry_grad,
        (((0,), (0,)), ((), ())),
        precision=lax.Precision.HIGHEST,
        preferred_element_type=jnp.float32,
    )
    deep_grad = (pixel_grad * swish_slope(deep_pre.reshape(-1, width_deep))).astype(jnp.bfloat16)
    pieces = []
    for shift_row in range(3):
        for shift_col in range(3):
            window = padded_deep[
                shift_row : shift_row + half_rows, shift_col : shift_col + half_cols
            ].reshape(-1, channels)
            pieces.append(
                lax.dot_general(
                    window, deep_grad, (((0,), (0,)), ((), ())), preferred_element_type=jnp.float32
                )
            )
    local_weight = jnp.stack(pieces).reshape(3, 3, channels, width_deep)
    local_bias = jnp.sum(deep_grad.astype(jnp.float32), axis=0)
    weight_grad, bias_grad = lax.psum((local_weight, local_bias), "strip")
    return (embeddings, weight_grad, bias_grad)


def solution(mesh):
    placed = (
        P(None, "strip", None),
        P(),
        P(),
        P(None, None, None, "chan"),
        P("chan"),
        P(None, "strip"),
        P("strip"),
        P("strip", "chan"),
    )
    return jax.shard_map(
        body,
        mesh=mesh,
        in_specs=placed,
        out_specs=(P("strip", "chan"), P(None, None, None, "chan"), P("chan")),
        check_vma=False,
    )
```

profile of v0, /device:TPU:1, one launch (start us, length us, event | category | flops | bytes accessed | tf_op | source)
XLA Modules:
  0.0 597.2 jit_solution(9862695185246819074)
XLA Ops:
  8.3 5.1 collective-permute-start.1
  13.4 1.9 collective-permute-start
  16.5 1.6 pad_maximum_fusion
  18.1 2.6 fusion.59
  20.7 2.1 reshape.94
  22.7 2.0 reshape.93
  24.8 2.1 reshape.95
  26.8 2.1 reshape.96
  28.9 2.1 reshape.97
  32.0 1.0 reshape.99
  33.2 1.1 reshape.101
  34.3 1.4 fusion.23
  44.5 2.7 fusion.2
  47.3 12.5 %all_gather.6 = bf16[24,66,256]{2,1,0:T(8,128)(2,1)S(1)} all-gather(bf16[6,66,256]{2,1,0:T(8,128)(2,1)S(1)} %fusion.15), channel_id=1, replica_groups=mesh['strip'=64,'chan'=4] {'chan'}, dimensions={0}, use_global_device_ids=true | all-gather | bytes 1013760 | tf_op jit(solution)/shard_map/all_gather | solution.py:77
  59.7 1.4 pad_slice_fusion
  66.7 2.1 scatter_custom_fusion
  71.0 247.4 %all-reduce.2 = f32[4096]{0:T(1024)S(1)} all-reduce(f32[4096]{0:T(1024)S(1)} %scatter_custom_fusion.1), channel_id=3, replica_groups=mesh['strip'=64,'chan'=4] {'strip'}, use_global_device_ids=true, to_apply=%region_5.6.clone | all-reduce | flops 4096 | bytes 32768
  318.5 1.5 broadcast_divide_fusion
  320.0 76.1 %all-gather.2.cloned.1.call-done = f32[4096,128]{1,0:T(8,128)} async-done(((f32[64,128]{1,0:T(8,128)}), f32[4096,128]{1,0:T(8,128)}) %all-gather.2.cloned.1.call-update) | async-done | bytes 2097168 | tf_op jit(solution)/shard_map/all_gather | solution.py:99
  396.1 2.2 gather_fusion
  398.3 2.1 convert_reduce_fusion
  405.9 124.2 %psum.15 = f32[128]{0:T(128)} all-reduce(f32[128]{0:T(128)S(1)} %get-tuple-element.25), channel_id=1, replica_groups=mesh['strip'=64,'chan'=4] {'strip'}, use_global_device_ids=true, to_apply=%region_8.9 | all-reduce | flops 128 | bytes 1024 | tf_op jit(solution)/shard_map/psum | solution.py:122
  530.1 58.2 %all-reduce.5.cloned.1.call-done = f32[3,3,256,128]{3,2,1,0:T(8,128)} async-done(((f32[3,3,256,128]{3,2,1,0:T(8,128)}), f32[3,3,256,128]{3,2,1,0:T(8,128)}) %all-reduce.5.cloned.1.call-update) | async-done | bytes 1179664 | tf_op jit(solution)/shard_map/psum | solution.py:122
  588.3 2.4 copy.20
  (108 shorter events, 24.6 us)
Async XLA Ops:
  7.2 8.2 %copy-start = (bf16[48,128,256]{2,1,0:T(8,128)(2,1)S(1)}, bf16[48,128,256]{2,1,0:T(8,128)(2,1)}, u32[]{:S(2)}) copy-start(bf16[48,128,256]{2,1,0:T(8,128)(2,1)} %param.8) | copy-start | bytes 9437188
  7.2 311.3 %reduce-scatter.2.cloned.1.call-start = ((), (), s32[]{:S(2)}) async-start(), calls=%async_computation.1 | async-start | bytes 2129920 | tf_op jit(solution)/shard_map/reduce_scatter | solution.py:94
  8.3 8.2 %collective-permute-start.1 = (bf16[14,3,256]{2,1,0:T(4,128)(2,1)S(1)}, bf16[14,3,256]{2,1,0:T(4,128)(2,1)S(1)}, u32[]{:S(2)}, u32[]{:S(2)}) collective-permute-start(bf16[14,3,256]{2,1,0:T(4,128)(2,1)S(1)} %get-tuple-element.4), channel_id=1, source_target_pairs={{4,0},{8,4},{12,8},{16,12},{20,16},{24,20},{28,24},{32,28},{36,32}... | collective-permute-start | bytes 64520 | tf_op jit(solution)/shard_map/ppermute | solution.py:17
  13.4 3.0 copy-start.27
  13.4 3.0 copy-start.24
  13.4 3.1 collective-permute-start
  33.0 1.2 copy-start.11
  34.3 1.4 copy-start.18
  34.3 1.6 copy-start.20
  35.8 1.1 copy-start.17
  37.0 1.1 copy-start.16
  41.9 1.1 copy-start.12
  59.7 1.5 copy-start.22
  61.2 1.4 copy-start.5
  61.2 1.7 copy-start.3
  61.2 2.1 copy-start.1
  66.7 3.0 copy-start.28
  66.7 251.8 %copy-start.23 = (f32[64,128]{1,0:T(8,128)S(1)}, f32[64,128]{1,0:T(8,128)}, u32[]{:S(2)}) copy-start(f32[64,128]{1,0:T(8,128)} %param.15) | copy-start | bytes 98308
  68.8 327.3 %all-gather.2.cloned.1.call-start = ((), (), s32[]{:S(2)}) async-start(), calls=%async_computation.2 | async-start | bytes 2129920 | tf_op jit(solution)/shard_map/all_gather | solution.py:99
  320.0 268.3 %all-reduce.5.cloned.1.call-start = ((), (), s32[]{:S(2)}) async-start(), calls=%async_computation.3 | async-start | bytes 2359296 | tf_op jit(solution)/shard_map/psum | solution.py:122
  398.3 2.1 copy-start.10
  398.3 2.5 copy-start.8
  400.9 1.2 copy-start.4
  401.6 1.2 copy-start.2
  (10 other events, 10.1 us)
Sparse Core Ops, SparseCore 0:
  68.9 141.4 reduce-scatter.1
  320.1 76.0 all-gather.1
  406.0 182.2 all-reduce.4
where the time goes:
time: 599 us; the launch traced here: 597 us
  blocking collectives  384 us (64%)
  waiting for transfers between devices  134 us (22%)
  local copies, waits for them, and re-layouts  36.6 us (6%)
  between operations  14.9 us (2%)
  matrix products  13.8 us (2%)
  starting transfers between devices  7.19 us (1%)
  other arithmetic  6.09 us (1%)
    unnamed x1, blocking collectives  247 us
    psum x1, blocking collectives, body(): weight_grad, bias_grad = lax.psum((local_weight, local_bias), 'strip')  124 us
    all_gather x1, waiting for transfers between devices, body(): lax.all_gather(embed_grad / divisor, 'strip', axis=0, tiled=True)  76.1 us
    psum x1, waiting for transfers between devices, body(): weight_grad, bias_grad = lax.psum((local_weight, local_bias), 'strip')  58.2 us
    reshape x9, local copies, waits for them, and re-layouts, convolve(): window = padded[shift_row:shift_row + row_count, shift_col:shift_col + co...  13.6 us
    all_gather x1, blocking collectives, body(): gathered = lax.all_gather(pooled, 'chan', axis=0, tiled=True)  12.5 us
  transfers between devices with their start and end apart: 5, of which 2 were waited for; matrix products, arithmetic and copies ran while one was open for 0% of the time, Pallas kernels for 0%

commit v1 on v0

--- a/solution.py
+++ b/solution.py
@@ -64,6 +64,22 @@
     row_total, col_local, channels = section_input.shape
     row_part = row_total // chan_count
     half_cols = col_local // 2
+    list_len = slot_ids.shape[0]
+    owned, width_deep = embed_grad.shape
+    lanes = embed_grad.shape[1]
+
+    flat_labels = labels.reshape(-1)
+    member = flat_labels[None, :] == jnp.arange(list_len, dtype=jnp.int32)[:, None]
+    part_counts = jnp.sum(member.astype(jnp.float32), axis=1)
+    meta = jnp.zeros((8, lanes), jnp.float32)
+    meta = meta.at[0, :list_len].set(part_counts)
+    meta = meta.at[0, list_len : 2 * list_len].set(slot_ids.astype(jnp.float32))
+    packed = jnp.concatenate([embed_grad, meta], axis=0)
+    every = lax.all_gather(packed, "strip", axis=0, tiled=False)
+    every_grad = every[:, :owned].reshape(strip_count * owned, lanes)
+    every_counts = every[:, owned, :list_len].reshape(-1)
+    every_slots = jnp.round(every[:, owned, list_len : 2 * list_len]).astype(jnp.int32).reshape(-1)
+
     padded_rows = jnp.pad(section_input, ((1, 1), (0, 0), (0, 0)))
     own_rows = lax.dynamic_slice_in_dim(padded_rows, chan_pos * row_part, row_part + 2, 0)
     extended = with_halo(own_rows, (("strip", 1),), 3)
@@ -78,26 +94,12 @@
     padded_deep = jnp.pad(gathered, ((1, 1), (0, 0), (0, 0)))
     half_rows = gathered.shape[0]
     deep_pre = convolve(padded_deep, deep_weight, half_rows, half_cols) + deep_bias
-    width_deep = deep_weight.shape[-1]
     features = swish(deep_pre).astype(jnp.bfloat16).reshape(-1, width_deep)
-    flat_labels = labels.reshape(-1)
-    list_len = slot_ids.shape[0]
-    member = flat_labels[None, :] == jnp.arange(list_len, dtype=jnp.int32)[:, None]
     part_sums = jnp.dot(member.astype(jnp.bfloat16), features, preferred_element_type=jnp.float32)
-    part_counts = jnp.sum(member.astype(jnp.float32), axis=1)
-    owned = embed_grad.shape[0]
-    dense_sums = (
-        jnp.zeros((owned * strip_count, width_deep), jnp.float32).at[slot_ids].set(part_sums)
-    )
-    dense_counts = jnp.zeros((owned * strip_count,), jnp.float32).at[slot_ids].set(part_counts)
-    slot_sums, slot_counts = (
-        lax.psum_scatter(dense_sums, "strip", scatter_dimension=0, tiled=True),
-        lax.psum_scatter(dense_counts, "strip", scatter_dimension=0, tiled=True),
-    )
-    divisor = jnp.maximum(slot_counts, 1.0)[:, None]
-    embeddings = slot_sums / divisor
-    every_grad = lax.all_gather(embed_grad / divisor, "strip", axis=0, tiled=True)
-    entry_grad = every_grad[slot_ids]
+
+    same_slot = (slot_ids[:, None] == every_slots[None, :]).astype(jnp.float32)
+    entry_counts = jnp.dot(same_slot, every_counts, precision=lax.Precision.HIGHEST)
+    entry_grad = every_grad[slot_ids] / jnp.maximum(entry_counts, 1.0)[:, None]
     pixel_grad = lax.dot_general(
         member.astype(jnp.float32),
         entry_grad,
@@ -117,9 +119,20 @@
                     window, deep_grad, (((0,), (0,)), ((), ())), preferred_element_type=jnp.float32
                 )
             )
-    local_weight = jnp.stack(pieces).reshape(3, 3, channels, width_deep)
     local_bias = jnp.sum(deep_grad.astype(jnp.float32), axis=0)
-    weight_grad, bias_grad = lax.psum((local_weight, local_bias), "strip")
+    bias_rows = jnp.zeros((8, width_deep), jnp.float32).at[0].set(local_bias)
+    local_grads = jnp.concatenate(pieces + [bias_rows], axis=0)
+
+    every_sums = lax.all_gather(part_sums, "strip", axis=0, tiled=True)
+    mine = strip_pos * owned + jnp.arange(owned, dtype=jnp.int32)
+    pick = (mine[:, None] == every_slots[None, :]).astype(jnp.float32)
+    slot_sums = jnp.dot(pick, every_sums, precision=lax.Precision.HIGHEST)
+    slot_counts = jnp.dot(pick, every_counts, precision=lax.Precision.HIGHEST)
+    embeddings = slot_sums / jnp.maximum(slot_counts, 1.0)[:, None]
+
+    total_grads = lax.psum(local_grads, "strip")
+    weight_grad = total_grads[: 9 * channels].reshape(3, 3, channels, width_deep)
+    bias_grad = total_grads[9 * channels]
     return (embeddings, weight_grad, bias_grad)
 
 

time: 599 us -> 371 us (0.62)
  blocking collectives: 384 us -> 13 us
  waiting for transfers between devices: 134 us -> 264 us
  matrix products: 13.8 us -> 23.4 us
    unnamed x1 -> x0, blocking collectives: 247 us -> none
    psum x1, waiting for transfers between devices: 58.2 us -> 183 us  [body(): total_grads = lax.psum(local_grads, 'strip')]
    psum x1 -> x0, blocking collectives: 124 us -> none  [body(): weight_grad, bias_grad = lax.psum((local_weight, local_bias), 'strip')]
    slice x0 -> x3, local copies, waits for them, and re-layouts: none -> 6.7 us  [the longest x1 3.19 us: body(): every_grad = every[:, :owned].reshape(strip_count * owned, lanes)]
    all_gather x1 -> x2, waiting for transfers between devices: 76.1 us -> 78.6 us  [the longest x1 57.6 us: body(): every_sums = lax.all_gather(part_sums, 'strip', axis=0, tiled=True)]
  transfers between devices with their start and end apart: 5 -> 5, of which waited for: 2 -> 4; matrix products, arithmetic and copies ran while one was open for 0% -> 15% of each run, Pallas kernels for 0% -> 0%
where the time goes in v1:
time: 371 us; the launch traced here: 370 us
  waiting for transfers between devices  264 us (71%)
  local copies, waits for them, and re-layouts  39.1 us (11%)
  matrix products  23.4 us (6%)
  between operations  14.1 us (4%)
  blocking collectives  13 us (4%)
  other arithmetic  9.91 us (3%)
  starting transfers between devices  6.98 us (2%)
    psum x1, waiting for transfers between devices, body(): total_grads = lax.psum(local_grads, 'strip')  183 us
    all_gather x1, waiting for transfers between devices, body(): every_sums = lax.all_gather(part_sums, 'strip', axis=0, tiled=True)  57.6 us
    all_gather x1, waiting for transfers between devices, body(): every = lax.all_gather(packed, 'strip', axis=0, tiled=False)  21 us
    all_gather x1, blocking collectives, body(): gathered = lax.all_gather(pooled, 'chan', axis=0, tiled=True)  13 us
    reshape x9, local copies, waits for them, and re-layouts, convolve(): window = padded[shift_row:shift_row + row_count, shift_col:shift_col + co...  11.8 us
    dot_general x9, matrix products, body(): lax.dot_general(window, deep_grad, (((0,), (0,)), ((), ())), preferred_el...  9.57 us
    dot_general x18, matrix products, convolve(): jnp.dot(window, weight[shift_row, shift_col], preferred_element_type=jnp....  7.67 us
  transfers between devices with their start and end apart: 5, of which 4 were waited for; matrix products, arithmetic and copies ran while one was open for 15% of the time, Pallas kernels for 0%

profile of v1, /device:TPU:1, one launch (start us, length us, event | category | flops | bytes accessed | tf_op | source)
XLA Modules:
  0.0 370.2 jit_solution(11321671961429360854)
XLA Ops:
  10.0 2.7 broadcast_select_fusion
  12.7 1.6 scatter.11
  14.3 1.4 pad_maximum_fusion.1
  16.8 4.9 %collective-permute-start = (bf16[14,3,256]{2,1,0:T(4,128)(2,1)S(1)}, bf16[14,3,256]{2,1,0:T(4,128)(2,1)S(1)}, u32[]{:S(2)}, u32[]{:S(2)}) collective-permute-start(bf16[14,3,256]{2,1,0:T(4,128)(2,1)S(1)} %get-tuple-element.39), channel_id=1, source_target_pairs={{0,4},{4,8},{8,12},{12,16},{16,20},{20,24},{24,28},{28,32},{32,36}... | collective-permute-start | bytes 64520 | tf_op jit(solution)/shard_map/ppermute | solution.py:15
  21.7 1.9 collective-permute-start.1
  24.7 2.2 collective-permute-done.1
  26.9 1.6 pad_maximum_fusion
  28.5 2.8 fusion.60
  31.3 2.1 reshape.210
  33.4 2.0 reshape.209
  35.4 2.1 reshape.208
  37.5 2.1 reshape.207
  39.6 2.0 reshape.206
  53.1 2.7 fusion.2
  55.9 13.0 %all_gather.14 = bf16[24,66,256]{2,1,0:T(8,128)(2,1)S(1)} all-gather(bf16[6,66,256]{2,1,0:T(8,128)(2,1)S(1)} %fusion.13), channel_id=1, replica_groups=mesh['strip'=64,'chan'=4] {'chan'}, dimensions={0}, use_global_device_ids=true | all-gather | bytes 1013760 | tf_op jit(solution)/shard_map/all_gather | solution.py:93
  68.9 1.4 pad_slice_fusion
  76.5 21.0 %all-gather.6.cloned.1.call-done = f32[4608,128]{1,0:T(8,128)} async-done(((f32[72,128]{1,0:T(8,128)}), f32[4608,128]{1,0:T(8,128)}) %all-gather.6.cloned.1.call-update) | async-done | bytes 2359312 | tf_op jit(solution)/shard_map/all_gather | solution.py:78
  98.8 3.2 slice.254
  102.1 2.2 gather_fusion
  104.5 2.2 convert_reduce_fusion
  117.3 57.6 %all-gather.4.cloned.1.call-done = f32[2048,128]{1,0:T(8,128)} async-done(((f32[32,128]{1,0:T(8,128)}), f32[2048,128]{1,0:T(8,128)}) %all-gather.4.cloned.1.call-update) | async-done | bytes 1048592 | tf_op jit(solution)/shard_map/all_gather | solution.py:126
  174.9 2.4 convolution_divide_fusion
  177.3 182.9 %all-reduce.6.cloned.1.call-done = f32[2312,128]{1,0:T(8,128)} async-done(((f32[2312,128]{1,0:T(8,128)}), f32[2312,128]{1,0:T(8,128)}) %all-reduce.6.cloned.1.call-update) | async-done | bytes 1183760 | tf_op jit(solution)/shard_map/psum | solution.py:133
  361.4 2.4 slice.255
  (107 shorter events, 35.9 us)
Async XLA Ops:
  7.2 90.4 %all-gather.6.cloned.1.call-start = ((), (), s32[]{:S(2)}) async-start(), calls=%async_computation.2 | async-start | bytes 2396160 | tf_op jit(solution)/shard_map/all_gather | solution.py:78
  15.7 8.0 %copy-start.21 = (s32[32]{0:T(128)S(1)}, s32[32]{0:T(128)}, u32[]{:S(2)}) copy-start(s32[32]{0:T(128)} %param.20) | copy-start | bytes 388
  15.7 8.0 %copy-start = (bf16[48,128,256]{2,1,0:T(8,128)(2,1)S(1)}, bf16[48,128,256]{2,1,0:T(8,128)(2,1)}, u32[]{:S(2)}) copy-start(bf16[48,128,256]{2,1,0:T(8,128)(2,1)} %param.14) | copy-start | bytes 9437188
  15.7 159.2 %all-gather.4.cloned.1.call-start = ((), (), s32[]{:S(2)}) async-start(), calls=%async_computation | async-start | bytes 1064960 | tf_op jit(solution)/shard_map/all_gather | solution.py:126
  16.8 7.9 %collective-permute-start = (bf16[14,3,256]{2,1,0:T(4,128)(2,1)S(1)}, bf16[14,3,256]{2,1,0:T(4,128)(2,1)S(1)}, u32[]{:S(2)}, u32[]{:S(2)}) collective-permute-start(bf16[14,3,256]{2,1,0:T(4,128)(2,1)S(1)} %get-tuple-element.39), channel_id=1, source_target_pairs={{0,4},{4,8},{8,12},{12,16},{16,20},{20,24},{24,28},{28,32},{32,36}... | collective-permute-start | bytes 64520 | tf_op jit(solution)/shard_map/ppermute | solution.py:15
  21.7 5.2 %collective-permute-start.1 = (bf16[14,3,256]{2,1,0:T(4,128)(2,1)S(1)}, bf16[14,3,256]{2,1,0:T(4,128)(2,1)S(1)}, u32[]{:S(2)}, u32[]{:S(2)}) collective-permute-start(bf16[14,3,256]{2,1,0:T(4,128)(2,1)S(1)} %get-tuple-element.40), channel_id=1, source_target_pairs={{4,0},{8,4},{12,8},{16,12},{20,16},{24,20},{28,24},{32,28},{36,32}... | collective-permute-start | bytes 64520 | tf_op jit(solution)/shard_map/ppermute | solution.py:17
  43.1 1.4 copy-start.17
  44.9 1.1 copy-start.16
  46.0 1.1 copy-start.15
  47.2 1.1 copy-start.14
  48.3 1.1 copy-start.13
  49.4 1.1 copy-start.12
  50.6 1.1 copy-start.11
  68.9 1.5 copy-start.19
  70.3 1.1 copy-start.9
  70.3 1.4 copy-start.5
  70.3 1.7 copy-start.3
  70.3 2.1 copy-start.1
  76.5 283.7 %all-reduce.6.cloned.1.call-start = ((), (), s32[]{:S(2)}) async-start(), calls=%async_computation.1 | async-start | bytes 2367488 | tf_op jit(solution)/shard_map/psum | solution.py:133
  104.5 2.2 copy-start.10
  104.5 3.3 copy-start.8
  106.7 2.2 copy-start.6
  107.8 2.1 copy-start.4
  108.8 2.1 copy-start.2
  (4 other events, 3.5 us)
Sparse Core Ops, SparseCore 0:
  15.8 81.7 all-gather.5
  100.9 73.9 all-gather.3
  178.4 181.7 all-reduce.5

commit v2 on v1

--- a/solution.py
+++ b/solution.py
@@ -1,4 +1,5 @@
 import jax
+import numpy as np
 import jax.numpy as jnp
 from jax import lax
 from jax.sharding import PartitionSpec as P
@@ -19,6 +20,41 @@
             axis=dim,
         )
     return cells
+
+
+def tree_gather(block, axis, order):
+    count = lax.axis_size(axis)
+    me = lax.axis_index(axis)
+    held = block
+    for dist in order:
+        other = lax.ppermute(held, axis, [(i, i ^ dist) for i in range(count)])
+        high = (me // dist) % 2
+        size = held.shape[0]
+        both = jnp.zeros((2 * size,) + held.shape[1:], held.dtype)
+        both = lax.dynamic_update_slice_in_dim(both, held, high * size, 0)
+        held = lax.dynamic_update_slice_in_dim(both, other, (1 - high) * size, 0)
+    return held
+
+
+def gather_position(order, count):
+    return np.array(
+        [sum(((j // dist) % 2) << k for k, dist in enumerate(order)) for j in range(count)],
+        np.int32,
+    )
+
+
+def tree_sum(block, axis):
+    count = lax.axis_size(axis)
+    me = lax.axis_index(axis)
+    order = [1 << k for k in range(count.bit_length() - 1)]
+    held = block
+    for dist in order:
+        half = held.shape[0] // 2
+        high = (me // dist) % 2
+        keep = lax.dynamic_slice_in_dim(held, high * half, half, 0)
+        send = lax.dynamic_slice_in_dim(held, (1 - high) * half, half, 0)
+        held = keep + lax.ppermute(send, axis, [(i, i ^ dist) for i in range(count)])
+    return tree_gather(held, axis, order[::-1])
 
 
 def swish(value):
@@ -75,8 +111,10 @@
     meta = meta.at[0, :list_len].set(part_counts)
     meta = meta.at[0, list_len : 2 * list_len].set(slot_ids.astype(jnp.float32))
     packed = jnp.concatenate([embed_grad, meta], axis=0)
-    every = lax.all_gather(packed, "strip", axis=0, tiled=False)
+    order = [strip_count >> (k + 1) for k in range(strip_count.bit_length() - 1)]
+    every = tree_gather(packed, "strip", order).reshape(strip_count, owned + 8, lanes)
     every_grad = every[:, :owned].reshape(strip_count * owned, lanes)
+    position = jnp.asarray(gather_position(order, strip_count))
     every_counts = every[:, owned, :list_len].reshape(-1)
     every_slots = jnp.round(every[:, owned, list_len : 2 * list_len]).astype(jnp.int32).reshape(-1)
 
@@ -99,7 +137,8 @@
 
     same_slot = (slot_ids[:, None] == every_slots[None, :]).astype(jnp.float32)
     entry_counts = jnp.dot(same_slot, every_counts, precision=lax.Precision.HIGHEST)
-    entry_grad = every_grad[slot_ids] / jnp.maximum(entry_counts, 1.0)[:, None]
+    grad_row = position[slot_ids // owned] * owned + slot_ids % owned
+    entry_grad = every_grad[grad_row] / jnp.maximum(entry_counts, 1.0)[:, None]
     pixel_grad = lax.dot_general(
         member.astype(jnp.float32),
         entry_grad,
@@ -120,17 +159,17 @@
                 )
             )
     local_bias = jnp.sum(deep_grad.astype(jnp.float32), axis=0)
-    bias_rows = jnp.zeros((8, width_deep), jnp.float32).at[0].set(local_bias)
+    bias_rows = jnp.zeros((strip_count, width_deep), jnp.float32).at[0].set(local_bias)
     local_grads = jnp.concatenate(pieces + [bias_rows], axis=0)
 
-    every_sums = lax.all_gather(part_sums, "strip", axis=0, tiled=True)
+    every_sums = tree_gather(part_sums, "strip", order)
     mine = strip_pos * owned + jnp.arange(owned, dtype=jnp.int32)
     pick = (mine[:, None] == every_slots[None, :]).astype(jnp.float32)
     slot_sums = jnp.dot(pick, every_sums, precision=lax.Precision.HIGHEST)
     slot_counts = jnp.dot(pick, every_counts, precision=lax.Precision.HIGHEST)
     embeddings = slot_sums / jnp.maximum(slot_counts, 1.0)[:, None]
 
-    total_grads = lax.psum(local_grads, "strip")
+    total_grads = tree_sum(local_grads, "strip")
     weight_grad = total_grads[: 9 * channels].reshape(3, 3, channels, width_deep)
     bias_grad = total_grads[9 * channels]
     return (embeddings, weight_grad, bias_grad)

time: 371 us -> 214 us (0.58)
  waiting for transfers between devices: 264 us -> 52.1 us
  starting transfers between devices: 6.98 us -> 79.4 us
  between operations: 14.1 us -> 1.81 us
  matrix products: 23.4 us -> 16.5 us
    psum x1 -> x0, waiting for transfers between devices: 183 us -> none  [body(): total_grads = lax.psum(local_grads, 'strip')]
    all_gather x2 -> x0, waiting for transfers between devices: 78.6 us -> none  [the longest x1 57.6 us: body(): every_sums = lax.all_gather(part_sums, 'strip', axis=0, tiled=True)]
    ppermute x0 -> x24, starting transfers between devices: none -> 73.1 us  [the longest x18 58.6 us: tree_gather(): other = lax.ppermute(held, axis, [(i, i ^ dist) for i in range(count)])]
    ppermute x0 -> x24, waiting for transfers between devices: none -> 50.5 us  [the longest x18 37.8 us: tree_gather(): other = lax.ppermute(held, axis, [(i, i ^ dist) for i in range(count)])]
    dot_general x9, matrix products: 9.57 us -> 3.68 us  [body(): lax.dot_general(window, deep_grad, (((0,), (0,)), ((), ())), preferred_el...]
    unnamed x46 -> x52, local copies, waits for them, and re-layouts: 6.42 us -> 7.53 us
  transfers between devices with their start and end apart: 5 -> 26, of which waited for: 4 -> 16; matrix products, arithmetic and copies ran while one was open for 15% -> 17% of each run, Pallas kernels for 0% -> 0%
where the time goes in v2:
time: 214 us; the launch traced here: 211 us
  starting transfers between devices  79.4 us (37%)
  waiting for transfers between devices  52.1 us (24%)
  local copies, waits for them, and re-layouts  39.2 us (18%)
  matrix products  16.5 us (8%)
  blocking collectives  12.9 us (6%)
  other arithmetic  9.53 us (4%)
    ppermute x18, starting transfers between devices, tree_gather(): other = lax.ppermute(held, axis, [(i, i ^ dist) for i in range(count)])  58.6 us
    ppermute x18, waiting for transfers between devices, tree_gather(): other = lax.ppermute(held, axis, [(i, i ^ dist) for i in range(count)])  37.8 us
    ppermute x6, starting transfers between devices, tree_sum(): lax.ppermute(send, axis, [(i, i ^ dist) for i in range(count)])  14.5 us
    all_gather x1, blocking collectives, body(): gathered = lax.all_gather(pooled, 'chan', axis=0, tiled=True)  12.9 us
    reshape x9, local copies, waits for them, and re-layouts, convolve(): window = padded[shift_row:shift_row + row_count, shift_col:shift_col + co...  12.7 us
    ppermute x6, waiting for transfers between devices, tree_sum(): lax.ppermute(send, axis, [(i, i ^ dist) for i in range(count)])  12.6 us
    dot_general x18, matrix products, convolve(): jnp.dot(window, weight[shift_row, shift_col], preferred_element_type=jnp....  8.56 us
    unnamed x52, local copies, waits for them, and re-layouts  7.53 us
  transfers between devices with their start and end apart: 26, of which 16 were waited for; matrix products, arithmetic and copies ran while one was open for 17% of the time, Pallas kernels for 0%

profile of v2, /device:TPU:1, one launch (start us, length us, event | category | flops | bytes accessed | tf_op | source)
XLA Modules:
  0.0 211.4 jit_solution(12739471482053040687)
XLA Ops:
  8.5 3.6 %collective-permute-start = (f32[72,128]{1,0:T(8,128)S(1)}, f32[72,128]{1,0:T(8,128)S(1)}, u32[]{:S(2)}, u32[]{:S(2)}) collective-permute-start(f32[72,128]{1,0:T(8,128)S(1)} %get-tuple-element.59), channel_id=1, source_target_pairs={{0,128},{4,132},{8,136},{12,140},{16,144},{20,148},{24,152},{28,15... | collective-permute-start | bytes 110600 | tf_op jit(solution)/shard_map/ppermute | solution.py:30
  13.1 4.4 %collective-permute-start.6 = (bf16[14,3,256]{2,1,0:T(4,128)(2,1)S(1)}, bf16[14,3,256]{2,1,0:T(4,128)(2,1)S(1)}, u32[]{:S(2)}, u32[]{:S(2)}) collective-permute-start(bf16[14,3,256]{2,1,0:T(4,128)(2,1)S(1)} %get-tuple-element.39), channel_id=1, source_target_pairs={{0,4},{4,8},{8,12},{12,16},{16,20},{20,24},{24,28},{28,32},{32,36}... | collective-permute-start | bytes 64520 | tf_op jit(solution)/shard_map/ppermute | solution.py:16
  50.9 12.9 %all_gather.3 = bf16[24,66,256]{2,1,0:T(8,128)(2,1)S(1)} all-gather(bf16[6,66,256]{2,1,0:T(8,128)(2,1)S(1)} %fusion.13), channel_id=1, replica_groups=mesh['strip'=64,'chan'=4] {'chan'}, dimensions={0}, use_global_device_ids=true | all-gather | bytes 1013760 | tf_op jit(solution)/shard_map/all_gather | solution.py:131
  66.5 3.1 %collective-permute-done.1 = f32[144,128]{1,0:T(8,128)S(1)} collective-permute-done((f32[144,128]{1,0:T(8,128)S(1)}, f32[144,128]{1,0:T(8,128)S(1)}, u32[]{:S(2)}, u32[]{:S(2)}) %collective-permute-start.1) | collective-permute-done | bytes 73760 | tf_op jit(solution)/shard_map/ppermute | solution.py:30
  69.6 6.1 %collective-permute-start.2 = (f32[288,128]{1,0:T(8,128)S(1)}, f32[288,128]{1,0:T(8,128)S(1)}, u32[]{:S(2)}, u32[]{:S(2)}) collective-permute-start(f32[288,128]{1,0:T(8,128)S(1)} %constant_dynamic-update-slice_fusion.26), channel_id=1, source_target_pairs={{0,32},{4,36},{8,40},{12,44},{16,48},{20,52},{24,56},{28,60},{32,0... | collective-permute-start | bytes 442376 | tf_op jit(solution)/shard_map/ppermute | solution.py:30
  78.4 4.4 %collective-permute-start.3 = (f32[576,128]{1,0:T(8,128)S(1)}, f32[576,128]{1,0:T(8,128)S(1)}, u32[]{:S(2)}, u32[]{:S(2)}) collective-permute-start(f32[576,128]{1,0:T(8,128)S(1)} %constant_dynamic-update-slice_fusion.24), channel_id=1, source_target_pairs={{0,16},{4,20},{8,24},{12,28},{16,0},{20,4},{24,8},{28,12},{32,48},... | collective-permute-start | bytes 884744 | tf_op jit(solution)/shard_map/ppermute | solution.py:30
  83.2 4.6 %collective-permute-done.3 = f32[576,128]{1,0:T(8,128)S(1)} collective-permute-done((f32[576,128]{1,0:T(8,128)S(1)}, f32[576,128]{1,0:T(8,128)S(1)}, u32[]{:S(2)}, u32[]{:S(2)}) %collective-permute-start.3) | collective-permute-done | bytes 294944 | tf_op jit(solution)/shard_map/ppermute | solution.py:30
  87.9 8.3 %collective-permute-start.4 = (f32[1152,128]{1,0:T(8,128)S(1)}, f32[1152,128]{1,0:T(8,128)S(1)}, u32[]{:S(2)}, u32[]{:S(2)}) collective-permute-start(f32[1152,128]{1,0:T(8,128)S(1)} %constant_dynamic-update-slice_fusion.22), channel_id=1, source_target_pairs={{0,8},{4,12},{8,0},{12,4},{16,24},{20,28},{24,16},{28,20},{32,40},... | collective-permute-start | bytes 1769480 | tf_op jit(solution)/shard_map/ppermute | solution.py:30
  97.0 10.2 %collective-permute-done.4 = f32[1152,128]{1,0:T(8,128)S(1)} collective-permute-done((f32[1152,128]{1,0:T(8,128)S(1)}, f32[1152,128]{1,0:T(8,128)S(1)}, u32[]{:S(2)}, u32[]{:S(2)}) %collective-permute-start.4) | collective-permute-done | bytes 589856 | tf_op jit(solution)/shard_map/ppermute | solution.py:30
  107.2 3.4 %collective-permute-start.5 = (f32[2304,128]{1,0:T(8,128)S(1)}, f32[2304,128]{1,0:T(8,128)S(1)}, u32[]{:S(2)}, u32[]{:S(2)}) collective-permute-start(f32[2304,128]{1,0:T(8,128)S(1)} %constant_dynamic-update-slice_fusion.20), channel_id=1, source_target_pairs={{0,4},{4,0},{8,12},{12,8},{16,20},{20,16},{24,28},{28,24},{32,36},... | collective-permute-start | bytes 3538952 | tf_op jit(solution)/shard_map/ppermute | solution.py:30
  131.1 3.1 %collective-permute-start.8 = (f32[32,128]{1,0:T(8,128)S(1)}, f32[32,128]{1,0:T(8,128)S(1)}, u32[]{:S(2)}, u32[]{:S(2)}) collective-permute-start(f32[32,128]{1,0:T(8,128)S(1)} %get-tuple-element.64), channel_id=1, source_target_pairs={{0,128},{4,132},{8,136},{12,140},{16,144},{20,148},{24,152},{28,15... | collective-permute-start | bytes 49160 | tf_op jit(solution)/shard_map/ppermute | solution.py:30
  135.4 3.4 %collective-permute-start.9 = (f32[64,128]{1,0:T(8,128)S(1)}, f32[64,128]{1,0:T(8,128)S(1)}, u32[]{:S(2)}, u32[]{:S(2)}) collective-permute-start(f32[64,128]{1,0:T(8,128)S(1)} %constant_dynamic-update-slice_fusion.16), channel_id=1, source_target_pairs={{0,64},{4,68},{8,72},{12,76},{16,80},{20,84},{24,88},{28,92},{32,9... | collective-permute-start | bytes 98312 | tf_op jit(solution)/shard_map/ppermute | solution.py:30
  138.8 3.2 %collective-permute-start.16 = (f32[296,128]{1,0:T(8,128)S(1)}, f32[296,128]{1,0:T(8,128)S(1)}, u32[]{:S(2)}, u32[]{:S(2)}) collective-permute-start(f32[296,128]{1,0:T(8,128)S(1)} %constant_dynamic-slice_fusion.3), channel_id=1, source_target_pairs={{0,16},{4,20},{8,24},{12,28},{16,0},{20,4},{24,8},{28,12},{32,48},... | collective-permute-start | bytes 454664 | tf_op jit(solution)/shard_map/ppermute | solution.py:56
  142.0 3.0 %collective-permute-start.10 = (f32[128,128]{1,0:T(8,128)S(1)}, f32[128,128]{1,0:T(8,128)S(1)}, u32[]{:S(2)}, u32[]{:S(2)}) collective-permute-start(f32[128,128]{1,0:T(8,128)S(1)} %constant_dynamic-update-slice_fusion.14), channel_id=1, source_target_pairs={{0,32},{4,36},{8,40},{12,44},{16,48},{20,52},{24,56},{28,60},{32,0... | collective-permute-start | bytes 196616 | tf_op jit(solution)/shard_map/ppermute | solution.py:30
  145.1 5.7 %collective-permute-done.16 = f32[296,128]{1,0:T(8,128)S(1)} collective-permute-done((f32[296,128]{1,0:T(8,128)S(1)}, f32[296,128]{1,0:T(8,128)S(1)}, u32[]{:S(2)}, u32[]{:S(2)}) %collective-permute-start.16) | collective-permute-done | bytes 151584 | tf_op jit(solution)/shard_map/ppermute | solution.py:56
  150.8 4.6 %collective-permute-start.17 = (f32[148,128]{1,0:T(8,128)S(1)}, f32[148,128]{1,0:T(8,128)S(1)}, u32[]{:S(2)}, u32[]{:S(2)}) collective-permute-start(f32[148,128]{1,0:T(8,128)S(1)} %constant_dynamic-slice_fusion.2), channel_id=1, source_target_pairs={{0,32},{4,36},{8,40},{12,44},{16,48},{20,52},{24,56},{28,60},{32,0... | collective-permute-start | bytes 227336 | tf_op jit(solution)/shard_map/ppermute | solution.py:56
  155.5 3.3 %collective-permute-done.17 = f32[148,128]{1,0:T(8,128)S(1)} collective-permute-done((f32[148,128]{1,0:T(8,128)S(1)}, f32[148,128]{1,0:T(8,128)S(1)}, u32[]{:S(2)}, u32[]{:S(2)}) %collective-permute-start.17) | collective-permute-done | bytes 75808 | tf_op jit(solution)/shard_map/ppermute | solution.py:56
  158.9 3.0 %collective-permute-start.18 = (f32[74,128]{1,0:T(8,128)S(1)}, f32[74,128]{1,0:T(8,128)S(1)}, u32[]{:S(2)}, u32[]{:S(2)}) collective-permute-start(f32[74,128]{1,0:T(8,128)S(1)} %constant_dynamic-slice_fusion.1), channel_id=1, source_target_pairs={{0,64},{4,68},{8,72},{12,76},{16,80},{20,84},{24,88},{28,92},{32,9... | collective-permute-start | bytes 113672 | tf_op jit(solution)/shard_map/ppermute | solution.py:56
  167.6 3.1 %collective-permute-start.20 = (f32[37,128]{1,0:T(8,128)S(1)}, f32[37,128]{1,0:T(8,128)S(1)}, u32[]{:S(2)}, u32[]{:S(2)}) collective-permute-start(f32[37,128]{1,0:T(8,128)S(1)} %dynamic-slice_add_fusion.5), channel_id=1, source_target_pairs={{0,128},{4,132},{8,136},{12,140},{16,144},{20,148},{24,152},{28,15... | collective-permute-start | bytes 56840 | tf_op jit(solution)/shard_map/ppermute | solution.py:30
  176.7 4.4 %collective-permute-start.22 = (f32[148,128]{1,0:T(8,128)S(1)}, f32[148,128]{1,0:T(8,128)S(1)}, u32[]{:S(2)}, u32[]{:S(2)}) collective-permute-start(f32[148,128]{1,0:T(8,128)S(1)} %dynamic_update_slice.135), channel_id=1, source_target_pairs={{0,32},{4,36},{8,40},{12,44},{16,48},{20,52},{24,56},{28,60},{32,0... | collective-permute-start | bytes 227336 | tf_op jit(solution)/shard_map/ppermute | solution.py:30
  181.1 6.9 %collective-permute-start.13 = (f32[1024,128]{1,0:T(8,128)S(1)}, f32[1024,128]{1,0:T(8,128)S(1)}, u32[]{:S(2)}, u32[]{:S(2)}) collective-permute-start(f32[1024,128]{1,0:T(8,128)S(1)} %constant_dynamic-update-slice_fusion.8), channel_id=1, source_target_pairs={{0,4},{4,0},{8,12},{12,8},{16,20},{20,16},{24,28},{28,24},{32,36},... | collective-permute-start | bytes 1572872 | tf_op jit(solution)/shard_map/ppermute | solution.py:30
  189.3 5.4 %collective-permute-done.23 = f32[296,128]{1,0:T(8,128)S(1)} collective-permute-done((f32[296,128]{1,0:T(8,128)S(1)}, f32[296,128]{1,0:T(8,128)S(1)}, u32[]{:S(2)}, u32[]{:S(2)}) %collective-permute-start.23) | collective-permute-done | bytes 151584 | tf_op jit(solution)/shard_map/ppermute | solution.py:30
  195.1 7.0 %collective-permute-done.24 = f32[592,128]{1,0:T(8,128)S(1)} collective-permute-done((f32[592,128]{1,0:T(8,128)S(1)}, f32[592,128]{1,0:T(8,128)S(1)}, u32[]{:S(2)}, u32[]{:S(2)}) %collective-permute-start.24) | collective-permute-done | bytes 303136 | tf_op jit(solution)/shard_map/ppermute | solution.py:30
  202.1 6.0 %collective-permute-start.25 = (f32[1184,128]{1,0:T(8,128)S(1)}, f32[1184,128]{1,0:T(8,128)S(1)}, u32[]{:S(2)}, u32[]{:S(2)}) collective-permute-start(f32[1184,128]{1,0:T(8,128)S(1)} %constant_dynamic-update-slice_fusion.2), channel_id=1, source_target_pairs={{0,4},{4,0},{8,12},{12,8},{16,20},{20,16},{24,28},{28,24},{32,36},... | collective-permute-start | bytes 1818632 | tf_op jit(solution)/shard_map/ppermute | solution.py:30
  (219 shorter events, 86.7 us)
Async XLA Ops:
  8.5 57.8 %collective-permute-start = (f32[72,128]{1,0:T(8,128)S(1)}, f32[72,128]{1,0:T(8,128)S(1)}, u32[]{:S(2)}, u32[]{:S(2)}) collective-permute-start(f32[72,128]{1,0:T(8,128)S(1)} %get-tuple-element.59), channel_id=1, source_target_pairs={{0,128},{4,132},{8,136},{12,140},{16,144},{20,148},{24,152},{28,15... | collective-permute-start | bytes 110600 | tf_op jit(solution)/shard_map/ppermute | solution.py:30
  13.1 7.9 %collective-permute-start.6 = (bf16[14,3,256]{2,1,0:T(4,128)(2,1)S(1)}, bf16[14,3,256]{2,1,0:T(4,128)(2,1)S(1)}, u32[]{:S(2)}, u32[]{:S(2)}) collective-permute-start(bf16[14,3,256]{2,1,0:T(4,128)(2,1)S(1)} %get-tuple-element.39), channel_id=1, source_target_pairs={{0,4},{4,8},{8,12},{12,16},{16,20},{20,24},{24,28},{28,32},{32,36}... | collective-permute-start | bytes 64520 | tf_op jit(solution)/shard_map/ppermute | solution.py:16
  17.5 5.2 %collective-permute-start.7 = (bf16[14,3,256]{2,1,0:T(4,128)(2,1)S(1)}, bf16[14,3,256]{2,1,0:T(4,128)(2,1)S(1)}, u32[]{:S(2)}, u32[]{:S(2)}) collective-permute-start(bf16[14,3,256]{2,1,0:T(4,128)(2,1)S(1)} %get-tuple-element.40), channel_id=1, source_target_pairs={{4,0},{8,4},{12,8},{16,12},{20,16},{24,20},{28,24},{32,28},{36,32}... | collective-permute-start | bytes 64520 | tf_op jit(solution)/shard_map/ppermute | solution.py:18
  69.6 8.7 %collective-permute-start.2 = (f32[288,128]{1,0:T(8,128)S(1)}, f32[288,128]{1,0:T(8,128)S(1)}, u32[]{:S(2)}, u32[]{:S(2)}) collective-permute-start(f32[288,128]{1,0:T(8,128)S(1)} %constant_dynamic-update-slice_fusion.26), channel_id=1, source_target_pairs={{0,32},{4,36},{8,40},{12,44},{16,48},{20,52},{24,56},{28,60},{32,0... | collective-permute-start | bytes 442376 | tf_op jit(solution)/shard_map/ppermute | solution.py:30
  78.4 9.4 %collective-permute-start.3 = (f32[576,128]{1,0:T(8,128)S(1)}, f32[576,128]{1,0:T(8,128)S(1)}, u32[]{:S(2)}, u32[]{:S(2)}) collective-permute-start(f32[576,128]{1,0:T(8,128)S(1)} %constant_dynamic-update-slice_fusion.24), channel_id=1, source_target_pairs={{0,16},{4,20},{8,24},{12,28},{16,0},{20,4},{24,8},{28,12},{32,48},... | collective-permute-start | bytes 884744 | tf_op jit(solution)/shard_map/ppermute | solution.py:30
  87.9 19.3 %collective-permute-start.4 = (f32[1152,128]{1,0:T(8,128)S(1)}, f32[1152,128]{1,0:T(8,128)S(1)}, u32[]{:S(2)}, u32[]{:S(2)}) collective-permute-start(f32[1152,128]{1,0:T(8,128)S(1)} %constant_dynamic-update-slice_fusion.22), channel_id=1, source_target_pairs={{0,8},{4,12},{8,0},{12,4},{16,24},{20,28},{24,16},{28,20},{32,40},... | collective-permute-start | bytes 1769480 | tf_op jit(solution)/shard_map/ppermute | solution.py:30
  107.2 5.9 %collective-permute-start.5 = (f32[2304,128]{1,0:T(8,128)S(1)}, f32[2304,128]{1,0:T(8,128)S(1)}, u32[]{:S(2)}, u32[]{:S(2)}) collective-permute-start(f32[2304,128]{1,0:T(8,128)S(1)} %constant_dynamic-update-slice_fusion.20), channel_id=1, source_target_pairs={{0,4},{4,0},{8,12},{12,8},{16,20},{20,16},{24,28},{28,24},{32,36},... | collective-permute-start | bytes 3538952 | tf_op jit(solution)/shard_map/ppermute | solution.py:30
  129.0 9.7 %collective-permute-start.15 = (f32[592,128]{1,0:T(8,128)S(1)}, f32[592,128]{1,0:T(8,128)S(1)}, u32[]{:S(2)}, u32[]{:S(2)}) collective-permute-start(f32[592,128]{1,0:T(8,128)S(1)} %constant_dynamic-slice_fusion.4), channel_id=1, source_target_pairs={{0,8},{4,12},{8,0},{12,4},{16,24},{20,28},{24,16},{28,20},{32,40},... | collective-permute-start | bytes 909320 | tf_op jit(solution)/shard_map/ppermute | solution.py:56
  131.1 4.2 %collective-permute-start.8 = (f32[32,128]{1,0:T(8,128)S(1)}, f32[32,128]{1,0:T(8,128)S(1)}, u32[]{:S(2)}, u32[]{:S(2)}) collective-permute-start(f32[32,128]{1,0:T(8,128)S(1)} %get-tuple-element.64), channel_id=1, source_target_pairs={{0,128},{4,132},{8,136},{12,140},{16,144},{20,148},{24,152},{28,15... | collective-permute-start | bytes 49160 | tf_op jit(solution)/shard_map/ppermute | solution.py:30
  135.4 6.6 %collective-permute-start.9 = (f32[64,128]{1,0:T(8,128)S(1)}, f32[64,128]{1,0:T(8,128)S(1)}, u32[]{:S(2)}, u32[]{:S(2)}) collective-permute-start(f32[64,128]{1,0:T(8,128)S(1)} %constant_dynamic-update-slice_fusion.16), channel_id=1, source_target_pairs={{0,64},{4,68},{8,72},{12,76},{16,80},{20,84},{24,88},{28,92},{32,9... | collective-permute-start | bytes 98312 | tf_op jit(solution)/shard_map/ppermute | solution.py:30
  138.8 11.9 %collective-permute-start.16 = (f32[296,128]{1,0:T(8,128)S(1)}, f32[296,128]{1,0:T(8,128)S(1)}, u32[]{:S(2)}, u32[]{:S(2)}) collective-permute-start(f32[296,128]{1,0:T(8,128)S(1)} %constant_dynamic-slice_fusion.3), channel_id=1, source_target_pairs={{0,16},{4,20},{8,24},{12,28},{16,0},{20,4},{24,8},{28,12},{32,48},... | collective-permute-start | bytes 454664 | tf_op jit(solution)/shard_map/ppermute | solution.py:56
  142.0 13.4 %collective-permute-start.10 = (f32[128,128]{1,0:T(8,128)S(1)}, f32[128,128]{1,0:T(8,128)S(1)}, u32[]{:S(2)}, u32[]{:S(2)}) collective-permute-start(f32[128,128]{1,0:T(8,128)S(1)} %constant_dynamic-update-slice_fusion.14), channel_id=1, source_target_pairs={{0,32},{4,36},{8,40},{12,44},{16,48},{20,52},{24,56},{28,60},{32,0... | collective-permute-start | bytes 196616 | tf_op jit(solution)/shard_map/ppermute | solution.py:30
  150.8 8.1 %collective-permute-start.17 = (f32[148,128]{1,0:T(8,128)S(1)}, f32[148,128]{1,0:T(8,128)S(1)}, u32[]{:S(2)}, u32[]{:S(2)}) collective-permute-start(f32[148,128]{1,0:T(8,128)S(1)} %constant_dynamic-slice_fusion.2), channel_id=1, source_target_pairs={{0,32},{4,36},{8,40},{12,44},{16,48},{20,52},{24,56},{28,60},{32,0... | collective-permute-start | bytes 227336 | tf_op jit(solution)/shard_map/ppermute | solution.py:56
  155.4 11.5 %collective-permute-start.11 = (f32[256,128]{1,0:T(8,128)S(1)}, f32[256,128]{1,0:T(8,128)S(1)}, u32[]{:S(2)}, u32[]{:S(2)}) collective-permute-start(f32[256,128]{1,0:T(8,128)S(1)} %constant_dynamic-update-slice_fusion.12), channel_id=1, source_target_pairs={{0,16},{4,20},{8,24},{12,28},{16,0},{20,4},{24,8},{28,12},{32,48},... | collective-permute-start | bytes 393224 | tf_op jit(solution)/shard_map/ppermute | solution.py:30
  158.9 4.4 %collective-permute-start.18 = (f32[74,128]{1,0:T(8,128)S(1)}, f32[74,128]{1,0:T(8,128)S(1)}, u32[]{:S(2)}, u32[]{:S(2)}) collective-permute-start(f32[74,128]{1,0:T(8,128)S(1)} %constant_dynamic-slice_fusion.1), channel_id=1, source_target_pairs={{0,64},{4,68},{8,72},{12,76},{16,80},{20,84},{24,88},{28,92},{32,9... | collective-permute-start | bytes 113672 | tf_op jit(solution)/shard_map/ppermute | solution.py:56
  163.4 4.2 %collective-permute-start.19 = (f32[37,128]{1,0:T(8,128)S(1)}, f32[37,128]{1,0:T(8,128)S(1)}, u32[]{:S(2)}, u32[]{:S(2)}) collective-permute-start(f32[37,128]{1,0:T(8,128)S(1)} %constant_dynamic-slice_fusion), channel_id=1, source_target_pairs={{0,128},{4,132},{8,136},{12,140},{16,144},{20,148},{24,152},{28,15... | collective-permute-start | bytes 56840 | tf_op jit(solution)/shard_map/ppermute | solution.py:56
  166.9 14.1 %collective-permute-start.12 = (f32[512,128]{1,0:T(8,128)S(1)}, f32[512,128]{1,0:T(8,128)S(1)}, u32[]{:S(2)}, u32[]{:S(2)}) collective-permute-start(f32[512,128]{1,0:T(8,128)S(1)} %constant_dynamic-update-slice_fusion.10), channel_id=1, source_target_pairs={{0,8},{4,12},{8,0},{12,4},{16,24},{20,28},{24,16},{28,20},{32,40},... | collective-permute-start | bytes 786440 | tf_op jit(solution)/shard_map/ppermute | solution.py:30
  167.6 4.2 %collective-permute-start.20 = (f32[37,128]{1,0:T(8,128)S(1)}, f32[37,128]{1,0:T(8,128)S(1)}, u32[]{:S(2)}, u32[]{:S(2)}) collective-permute-start(f32[37,128]{1,0:T(8,128)S(1)} %dynamic-slice_add_fusion.5), channel_id=1, source_target_pairs={{0,128},{4,132},{8,136},{12,140},{16,144},{20,148},{24,152},{28,15... | collective-permute-start | bytes 56840 | tf_op jit(solution)/shard_map/ppermute | solution.py:30
  172.0 4.4 %collective-permute-start.21 = (f32[74,128]{1,0:T(8,128)S(1)}, f32[74,128]{1,0:T(8,128)S(1)}, u32[]{:S(2)}, u32[]{:S(2)}) collective-permute-start(f32[74,128]{1,0:T(8,128)S(1)} %dynamic_update_slice.133), channel_id=1, source_target_pairs={{0,64},{4,68},{8,72},{12,76},{16,80},{20,84},{24,88},{28,92},{32,9... | collective-permute-start | bytes 113672 | tf_op jit(solution)/shard_map/ppermute | solution.py:30
  176.7 11.9 %collective-permute-start.22 = (f32[148,128]{1,0:T(8,128)S(1)}, f32[148,128]{1,0:T(8,128)S(1)}, u32[]{:S(2)}, u32[]{:S(2)}) collective-permute-start(f32[148,128]{1,0:T(8,128)S(1)} %dynamic_update_slice.135), channel_id=1, source_target_pairs={{0,32},{4,36},{8,40},{12,44},{16,48},{20,52},{24,56},{28,60},{32,0... | collective-permute-start | bytes 227336 | tf_op jit(solution)/shard_map/ppermute | solution.py:30
  181.1 13.8 %collective-permute-start.13 = (f32[1024,128]{1,0:T(8,128)S(1)}, f32[1024,128]{1,0:T(8,128)S(1)}, u32[]{:S(2)}, u32[]{:S(2)}) collective-permute-start(f32[1024,128]{1,0:T(8,128)S(1)} %constant_dynamic-update-slice_fusion.8), channel_id=1, source_target_pairs={{0,4},{4,0},{8,12},{12,8},{16,20},{20,16},{24,28},{28,24},{32,36},... | collective-permute-start | bytes 1572872 | tf_op jit(solution)/shard_map/ppermute | solution.py:30
  189.1 5.6 %collective-permute-start.23 = (f32[296,128]{1,0:T(8,128)S(1)}, f32[296,128]{1,0:T(8,128)S(1)}, u32[]{:S(2)}, u32[]{:S(2)}) collective-permute-start(f32[296,128]{1,0:T(8,128)S(1)} %dynamic_update_slice.137), channel_id=1, source_target_pairs={{0,16},{4,20},{8,24},{12,28},{16,0},{20,4},{24,8},{28,12},{32,48},... | collective-permute-start | bytes 454664 | tf_op jit(solution)/shard_map/ppermute | solution.py:30
  194.7 7.4 %collective-permute-start.24 = (f32[592,128]{1,0:T(8,128)S(1)}, f32[592,128]{1,0:T(8,128)S(1)}, u32[]{:S(2)}, u32[]{:S(2)}) collective-permute-start(f32[592,128]{1,0:T(8,128)S(1)} %constant_dynamic-update-slice_fusion.4), channel_id=1, source_target_pairs={{0,8},{4,12},{8,0},{12,4},{16,24},{20,28},{24,16},{28,20},{32,40},... | collective-permute-start | bytes 909320 | tf_op jit(solution)/shard_map/ppermute | solution.py:30
  202.1 7.7 %collective-permute-start.25 = (f32[1184,128]{1,0:T(8,128)S(1)}, f32[1184,128]{1,0:T(8,128)S(1)}, u32[]{:S(2)}, u32[]{:S(2)}) collective-permute-start(f32[1184,128]{1,0:T(8,128)S(1)} %constant_dynamic-update-slice_fusion.2), channel_id=1, source_target_pairs={{0,4},{4,0},{8,12},{12,8},{16,20},{20,16},{24,28},{28,24},{32,36},... | collective-permute-start | bytes 1818632 | tf_op jit(solution)/shard_map/ppermute | solution.py:30
  (28 other events, 107.9 us)

commit v3 on v2

--- a/solution.py
+++ b/solution.py
@@ -43,7 +43,7 @@
     )
 
 
-def tree_sum(block, axis):
+def tree_sum(block, axis, rider):
     count = lax.axis_size(axis)
     me = lax.axis_index(axis)
     order = [1 << k for k in range(count.bit_length() - 1)]
@@ -54,7 +54,10 @@
         keep = lax.dynamic_slice_in_dim(held, high * half, half, 0)
         send = lax.dynamic_slice_in_dim(held, (1 - high) * half, half, 0)
         held = keep + lax.ppermute(send, axis, [(i, i ^ dist) for i in range(count)])
-    return tree_gather(held, axis, order[::-1])
+    chunk = held.shape[0]
+    both = tree_gather(jnp.concatenate([held, rider], axis=0), axis, order[::-1])
+    both = both.reshape(count, chunk + rider.shape[0], *held.shape[1:])
+    return both[:, :chunk].reshape(count * chunk, *held.shape[1:]), both[:, chunk:]
 
 
 def swish(value):
@@ -112,15 +115,14 @@
     meta = meta.at[0, list_len : 2 * list_len].set(slot_ids.astype(jnp.float32))
     packed = jnp.concatenate([embed_grad, meta], axis=0)
     order = [strip_count >> (k + 1) for k in range(strip_count.bit_length() - 1)]
-    every = tree_gather(packed, "strip", order).reshape(strip_count, owned + 8, lanes)
-    every_grad = every[:, :owned].reshape(strip_count * owned, lanes)
     position = jnp.asarray(gather_position(order, strip_count))
-    every_counts = every[:, owned, :list_len].reshape(-1)
-    every_slots = jnp.round(every[:, owned, list_len : 2 * list_len]).astype(jnp.int32).reshape(-1)
+    early = tree_gather(packed, "strip", order[:2])
 
     padded_rows = jnp.pad(section_input, ((1, 1), (0, 0), (0, 0)))
     own_rows = lax.dynamic_slice_in_dim(padded_rows, chan_pos * row_part, row_part + 2, 0)
     extended = with_halo(own_rows, (("strip", 1),), 3)
+    extended, early = lax.optimization_barrier((extended, early))
+    early = tree_gather(early, "strip", order[2:4])
     hidden = swish(convolve(extended, conv_weight, row_part, col_local + 4) + conv_bias)
     pooled = pool_pairs(hidden)
     column = jnp.arange(half_cols + 2)
@@ -128,6 +130,11 @@
         strip_pos == strip_count - 1
     )
     pooled = jnp.where(outside[None, :, None], jnp.zeros_like(pooled), pooled)
+    pooled, early = lax.optimization_barrier((pooled, early))
+    every = tree_gather(early, "strip", order[4:]).reshape(strip_count, owned + 8, lanes)
+    every_grad = every[:, :owned].reshape(strip_count * owned, lanes)
+    every_counts = every[:, owned, :list_len].reshape(-1)
+    every_slots = jnp.round(every[:, owned, list_len : 2 * list_len]).astype(jnp.int32).reshape(-1)
     gathered = lax.all_gather(pooled, "chan", axis=0, tiled=True)
     padded_deep = jnp.pad(gathered, ((1, 1), (0, 0), (0, 0)))
     half_rows = gathered.shape[0]
@@ -162,14 +169,14 @@
     bias_rows = jnp.zeros((strip_count, width_deep), jnp.float32).at[0].set(local_bias)
     local_grads = jnp.concatenate(pieces + [bias_rows], axis=0)
 
-    every_sums = tree_gather(part_sums, "strip", order)
+    total_grads, every_sums = tree_sum(local_grads, "strip", part_sums)
+    every_sums = every_sums.reshape(-1, width_deep)
     mine = strip_pos * owned + jnp.arange(owned, dtype=jnp.int32)
     pick = (mine[:, None] == every_slots[None, :]).astype(jnp.float32)
     slot_sums = jnp.dot(pick, every_sums, precision=lax.Precision.HIGHEST)
     slot_counts = jnp.dot(pick, every_counts, precision=lax.Precision.HIGHEST)
     embeddings = slot_sums / jnp.maximum(slot_counts, 1.0)[:, None]
 
-    total_grads = tree_sum(local_grads, "strip")
     weight_grad = total_grads[: 9 * channels].reshape(3, 3, channels, width_deep)
     bias_grad = total_grads[9 * channels]
     return (embeddings, weight_grad, bias_grad)

time: 214 us -> 213 us (level)
  starting transfers between devices: 79.4 us -> 36.2 us
  waiting for transfers between devices: 52.1 us -> 82.6 us
  local copies, waits for them, and re-layouts: 39.2 us -> 53 us
    ppermute x18 -> x12, starting transfers between devices: 58.6 us -> 23.5 us  [tree_gather(): other = lax.ppermute(held, axis, [(i, i ^ dist) for i in range(count)])]
    ppermute x6, waiting for transfers between devices: 12.6 us -> 28.2 us  [tree_sum(): lax.ppermute(send, axis, [(i, i ^ dist) for i in range(count)])]
    ppermute x18 -> x12, waiting for transfers between devices: 37.8 us -> 52.3 us  [tree_gather(): other = lax.ppermute(held, axis, [(i, i ^ dist) for i in range(count)])]
    ppermute x6, starting transfers between devices: 14.5 us -> 6.37 us  [tree_sum(): lax.ppermute(send, axis, [(i, i ^ dist) for i in range(count)])]
    reshape x0 -> x2, local copies, waits for them, and re-layouts: none -> 4.07 us  [the longest x1 2.38 us: tree_sum(): both[:, :chunk].reshape(count * chunk, *held.shape[1:])]
    dynamic_update_slice x18 -> x12, local copies, waits for them, and re-layouts: 1.21 us -> 3.46 us  [tree_gather(): held = lax.dynamic_update_slice_in_dim(both, other, (1 - high) * size, 0)]
    unnamed x52 -> x54, local copies, waits for them, and re-layouts: 7.53 us -> 7.77 us
  transfers between devices with their start and end apart: 26 -> 20, of which waited for: 16 -> 14; matrix products, arithmetic and copies ran while one was open for 17% -> 18% of each run, Pallas kernels for 0% -> 0%
where the time goes in v3:
time: 213 us; the launch traced here: 212 us
  waiting for transfers between devices  82.6 us (39%)
  local copies, waits for them, and re-layouts  53 us (25%)
  starting transfers between devices  36.2 us (17%)
  matrix products  16.5 us (8%)
  blocking collectives  12.9 us (6%)
  other arithmetic  9.54 us (4%)
    ppermute x12, waiting for transfers between devices, tree_gather(): other = lax.ppermute(held, axis, [(i, i ^ dist) for i in range(count)])  52.3 us
    ppermute x6, waiting for transfers between devices, tree_sum(): lax.ppermute(send, axis, [(i, i ^ dist) for i in range(count)])  28.2 us
    ppermute x12, starting transfers between devices, tree_gather(): other = lax.ppermute(held, axis, [(i, i ^ dist) for i in range(count)])  23.5 us
    reshape x9, local copies, waits for them, and re-layouts, convolve(): window = padded[shift_row:shift_row + row_count, shift_col:shift_col + co...  13.5 us
    all_gather x1, blocking collectives, body(): gathered = lax.all_gather(pooled, 'chan', axis=0, tiled=True)  12.9 us
    dot_general x18, matrix products, convolve(): jnp.dot(window, weight[shift_row, shift_col], preferred_element_type=jnp....  8.6 us
    unnamed x54, local copies, waits for them, and re-layouts  7.77 us
    ppermute x6, starting transfers between devices, tree_sum(): lax.ppermute(send, axis, [(i, i ^ dist) for i in range(count)])  6.37 us
  transfers between devices with their start and end apart: 20, of which 14 were waited for; matrix products, arithmetic and copies ran while one was open for 18% of the time, Pallas kernels for 0%

profile of v3, /device:TPU:1, one launch (start us, length us, event | category | flops | bytes accessed | tf_op | source)
XLA Modules:
  0.0 212.5 jit_solution(15142694964070461759)
XLA Ops:
  3.5 2.7 %broadcast_select_fusion = f32[1,32]{1,0:T(1,128)S(1)} fusion(pred[]{:T(512)} %and_reduce_fusion, s32[]{:T(128)} %bitcast.2, s32[]{:T(128)} %bitcast.3, f32[1,32]{1,0:T(1,128)S(1)} %bitcast.147, s32[32]{0:T(128)} %param.21), kind=kLoop, calls=%fused_computation.155 | loop fusion | flops 64 | bytes 393 | tf_op jit(solution)/shard_map/select.4
  8.5 3.6 %collective-permute-start.2 = (f32[72,128]{1,0:T(8,128)S(1)}, f32[72,128]{1,0:T(8,128)S(1)}, u32[]{:S(2)}, u32[]{:S(2)}) collective-permute-start(f32[72,128]{1,0:T(8,128)S(1)} %get-tuple-element.67), channel_id=1, source_target_pairs={{0,128},{4,132},{8,136},{12,140},{16,144},{20,148},{24,152},{28,15... | collective-permute-start | bytes 110600 | tf_op jit(solution)/shard_map/ppermute | solution.py:30
  13.1 4.4 %collective-permute-start = (bf16[14,3,256]{2,1,0:T(4,128)(2,1)S(1)}, bf16[14,3,256]{2,1,0:T(4,128)(2,1)S(1)}, u32[]{:S(2)}, u32[]{:S(2)}) collective-permute-start(bf16[14,3,256]{2,1,0:T(4,128)(2,1)S(1)} %get-tuple-element.47), channel_id=1, source_target_pairs={{0,4},{4,8},{8,12},{12,16},{16,20},{20,24},{24,28},{28,32},{32,36}... | collective-permute-start | bytes 64520 | tf_op jit(solution)/shard_map/ppermute | solution.py:16
  23.9 2.6 %collective-permute-done.3 = f32[144,128]{1,0:T(8,128)S(1)} collective-permute-done((f32[144,128]{1,0:T(8,128)S(1)}, f32[144,128]{1,0:T(8,128)S(1)}, u32[]{:S(2)}, u32[]{:S(2)}) %collective-permute-start.3) | collective-permute-done | bytes 73760 | tf_op jit(solution)/shard_map/ppermute | solution.py:30
  26.5 6.3 %collective-permute-start.4 = (f32[288,128]{1,0:T(8,128)S(1)}, f32[288,128]{1,0:T(8,128)}, u32[]{:S(2)}, u32[]{:S(2)}) collective-permute-start(f32[288,128]{1,0:T(8,128)S(1)} %constant_dynamic-update-slice_fusion.14), channel_id=1, source_target_pairs={{0,32},{4,36},{8,40},{12,44},{16,48},{20,52},{24,56},{28,60},{32,0... | collective-permute-start | bytes 442376 | tf_op jit(solution)/shard_map/ppermute | solution.py:30
  32.8 2.5 %fusion.62 = (bf16[12,132,256]{2,1,0:T(8,128)(2,1)S(1)}, bf16[12,132,256]{2,1,0:T(8,128)(2,1)S(1)}, bf16[12,132,256]{2,1,0:T(8,128)(2,1)S(1)}, bf16[12,132,256]{...) fusion(bf16[14,134,256]{2,1,0:T(8,128)(2,1)S(1)} %pad_maximum_f, ...), kind=kLoop, calls=%fused_computation.161 | loop fusion | bytes 14598144 | tf_op jit(solution)/shard_map/slice | solution.py:77
  59.0 2.7 %fusion.2 = f32[6,66,256]{2,1,0:T(8,128)S(1)} fusion(f32[6,2,66,2,256]{4,3,2,1,0:T(2,128)S(1)} %reshape.224, f32[256]{0:T(256)S(1)} %copy-done.24), kind=kLoop, calls=%fused_computation.25 | loop fusion | flops 2331648 | bytes 2028544 | tf_op jit(solution)/shard_map/reduce_sum | solution.py:91
  64.9 12.7 %collective-permute-done.5 = f32[576,128]{1,0:T(8,128)S(1)} collective-permute-done((f32[576,128]{1,0:T(8,128)S(1)}, f32[576,128]{1,0:T(8,128)S(1)}, u32[]{:S(2)}, u32[]{:S(2)}) %collective-permute-start.5) | collective-permute-done | bytes 294944 | tf_op jit(solution)/shard_map/ppermute | solution.py:30
  78.0 12.9 %all_gather.3 = bf16[24,66,256]{2,1,0:T(8,128)(2,1)S(1)} all-gather(bf16[6,66,256]{2,1,0:T(8,128)(2,1)S(1)} %fusion.13), channel_id=1, replica_groups=mesh['strip'=64,'chan'=4] {'chan'}, dimensions={0}, use_global_device_ids=true | all-gather | bytes 1013760 | tf_op jit(solution)/shard_map/all_gather | solution.py:138
  95.4 3.7 %collective-permute-start.7 = (f32[2304,128]{1,0:T(8,128)S(1)}, f32[2304,128]{1,0:T(8,128)S(1)}, u32[]{:S(2)}, u32[]{:S(2)}) collective-permute-start(f32[2304,128]{1,0:T(8,128)S(1)} %constant_dynamic-update-slice_fusion.8), channel_id=1, source_target_pairs={{0,4},{4,0},{8,12},{12,8},{16,20},{20,16},{24,28},{28,24},{32,36},... | collective-permute-start | bytes 3538952 | tf_op jit(solution)/shard_map/ppermute | solution.py:30
  104.0 2.2 %gather_fusion.1 = f32[32,128]{1,0:T(8,128)S(1)} fusion(f32[4096,128]{1,0:T(8,128)} %bitcast.144, s32[1024]{0:T(1024)S(1)} %pad_clamp_fusion), kind=kCustom, calls=%fused_computation.1 | custom fusion | bytes 32896 | tf_op jit(solution)/shard_map/gather | solution.py:148
  119.3 7.3 %collective-permute-done.9 = f32[592,128]{1,0:T(8,128)S(1)} collective-permute-done((f32[592,128]{1,0:T(8,128)S(1)}, f32[592,128]{1,0:T(8,128)S(1)}, u32[]{:S(2)}, u32[]{:S(2)}) %collective-permute-start.9) | collective-permute-done | bytes 303136 | tf_op jit(solution)/shard_map/ppermute | solution.py:56
  128.8 6.9 %collective-permute-done.10 = f32[296,128]{1,0:T(8,128)S(1)} collective-permute-done((f32[296,128]{1,0:T(8,128)S(1)}, f32[296,128]{1,0:T(8,128)S(1)}, u32[]{:S(2)}, u32[]{:S(2)}) %collective-permute-start.10) | collective-permute-done | bytes 151584 | tf_op jit(solution)/shard_map/ppermute | solution.py:56
  136.2 6.8 %collective-permute-done.11 = f32[148,128]{1,0:T(8,128)S(1)} collective-permute-done((f32[148,128]{1,0:T(8,128)S(1)}, f32[148,128]{1,0:T(8,128)S(1)}, u32[]{:S(2)}, u32[]{:S(2)}) %collective-permute-start.11) | collective-permute-done | bytes 75808 | tf_op jit(solution)/shard_map/ppermute | solution.py:56
  143.4 2.5 %collective-permute-done.12 = f32[74,128]{1,0:T(8,128)S(1)} collective-permute-done((f32[74,128]{1,0:T(8,128)S(1)}, f32[74,128]{1,0:T(8,128)S(1)}, u32[]{:S(2)}, u32[]{:S(2)}) %collective-permute-start.12) | collective-permute-done | bytes 37920 | tf_op jit(solution)/shard_map/ppermute | solution.py:56
  147.5 3.0 %collective-permute-done.13 = f32[37,128]{1,0:T(8,128)S(1)} collective-permute-done((f32[37,128]{1,0:T(8,128)S(1)}, f32[37,128]{1,0:T(8,128)S(1)}, u32[]{:S(2)}, u32[]{:S(2)}) %collective-permute-start.13) | collective-permute-done | bytes 18976 | tf_op jit(solution)/shard_map/ppermute | solution.py:56
  151.8 3.6 %collective-permute-done.14 = f32[69,128]{1,0:T(8,128)S(1)} collective-permute-done((f32[69,128]{1,0:T(8,128)S(1)}, f32[69,128]{1,0:T(8,128)S(1)}, u32[]{:S(2)}, u32[]{:S(2)}) %collective-permute-start.14) | collective-permute-done | bytes 35360 | tf_op jit(solution)/shard_map/ppermute | solution.py:30
  156.4 2.9 %collective-permute-done.15 = f32[138,128]{1,0:T(8,128)S(1)} collective-permute-done((f32[138,128]{1,0:T(8,128)S(1)}, f32[138,128]{1,0:T(8,128)S(1)}, u32[]{:S(2)}, u32[]{:S(2)}) %collective-permute-start.15) | collective-permute-done | bytes 70688 | tf_op jit(solution)/shard_map/ppermute | solution.py:30
  160.9 6.7 %collective-permute-done.16 = f32[276,128]{1,0:T(8,128)S(1)} collective-permute-done((f32[276,128]{1,0:T(8,128)S(1)}, f32[276,128]{1,0:T(8,128)S(1)}, u32[]{:S(2)}, u32[]{:S(2)}) %collective-permute-start.16) | collective-permute-done | bytes 141344 | tf_op jit(solution)/shard_map/ppermute | solution.py:30
  168.5 11.4 %collective-permute-done.17 = f32[552,128]{1,0:T(8,128)S(1)} collective-permute-done((f32[552,128]{1,0:T(8,128)S(1)}, f32[552,128]{1,0:T(8,128)S(1)}, u32[]{:S(2)}, u32[]{:S(2)}) %collective-permute-start.17) | collective-permute-done | bytes 282656 | tf_op jit(solution)/shard_map/ppermute | solution.py:30
  180.1 12.5 %collective-permute-done.18 = f32[1104,128]{1,0:T(8,128)S(1)} collective-permute-done((f32[1104,128]{1,0:T(8,128)S(1)}, f32[1104,128]{1,0:T(8,128)S(1)}, u32[]{:S(2)}, u32[]{:S(2)}) %collective-permute-start.18) | collective-permute-done | bytes 565280 | tf_op jit(solution)/shard_map/ppermute | solution.py:30
  192.7 5.6 %collective-permute-start.19 = (f32[2208,128]{1,0:T(8,128)S(1)}, f32[2208,128]{1,0:T(8,128)S(1)}, u32[]{:S(2)}, u32[]{:S(2)}) collective-permute-start(f32[2208,128]{1,0:T(8,128)S(1)} %constant_dynamic-update-slice_fusion.2), channel_id=1, source_target_pairs={{0,4},{4,0},{8,12},{12,8},{16,20},{20,16},{24,28},{28,24},{32,36},... | collective-permute-start | bytes 3391496 | tf_op jit(solution)/shard_map/ppermute | solution.py:30
  205.2 2.4 %reshape.239 = f32[2368,128]{1,0:T(8,128)} reshape(f32[64,37,128]{2,1,0:T(8,128)} %slice.257) | data formatting | bytes 2424832 | tf_op jit(solution)/shard_map/reshape | solution.py:60
  207.6 2.4 %slice.258 = f32[2304,128]{1,0:T(8,128)} slice(f32[2368,128]{1,0:T(8,128)} %reshape.239), slice={[0:2304], [0:128]} | slice | bytes 2359296 | tf_op jit(solution)/shard_map/slice | solution.py:180
  (197 shorter events, 80.8 us)
Async XLA Ops:
  8.5 14.6 %collective-permute-start.2 = (f32[72,128]{1,0:T(8,128)S(1)}, f32[72,128]{1,0:T(8,128)S(1)}, u32[]{:S(2)}, u32[]{:S(2)}) collective-permute-start(f32[72,128]{1,0:T(8,128)S(1)} %get-tuple-element.67), channel_id=1, source_target_pairs={{0,128},{4,132},{8,136},{12,140},{16,144},{20,148},{24,152},{28,15... | collective-permute-start | bytes 110600 | tf_op jit(solution)/shard_map/ppermute | solution.py:30
  12.1 7.4 %copy-start.1 = (bf16[48,128,256]{2,1,0:T(8,128)(2,1)S(1)}, bf16[48,128,256]{2,1,0:T(8,128)(2,1)}, u32[]{:S(2)}) copy-start(bf16[48,128,256]{2,1,0:T(8,128)(2,1)} %param.15) | copy-start | bytes 9437188
  13.1 7.4 %collective-permute-start = (bf16[14,3,256]{2,1,0:T(4,128)(2,1)S(1)}, bf16[14,3,256]{2,1,0:T(4,128)(2,1)S(1)}, u32[]{:S(2)}, u32[]{:S(2)}) collective-permute-start(bf16[14,3,256]{2,1,0:T(4,128)(2,1)S(1)} %get-tuple-element.47), channel_id=1, source_target_pairs={{0,4},{4,8},{8,12},{12,16},{16,20},{20,24},{24,28},{28,32},{32,36}... | collective-permute-start | bytes 64520 | tf_op jit(solution)/shard_map/ppermute | solution.py:16
  17.5 2.1 copy-start
  17.5 5.2 %collective-permute-start.1 = (bf16[14,3,256]{2,1,0:T(4,128)(2,1)S(1)}, bf16[14,3,256]{2,1,0:T(4,128)(2,1)S(1)}, u32[]{:S(2)}, u32[]{:S(2)}) collective-permute-start(bf16[14,3,256]{2,1,0:T(4,128)(2,1)S(1)} %get-tuple-element.48), channel_id=1, source_target_pairs={{4,0},{8,4},{12,8},{16,12},{20,16},{24,20},{28,24},{32,28},{36,32}... | collective-permute-start | bytes 64520 | tf_op jit(solution)/shard_map/ppermute | solution.py:18
  23.2 3.3 %collective-permute-start.3 = (f32[144,128]{1,0:T(8,128)S(1)}, f32[144,128]{1,0:T(8,128)S(1)}, u32[]{:S(2)}, u32[]{:S(2)}) collective-permute-start(f32[144,128]{1,0:T(8,128)S(1)} %constant_dynamic-update-slice_fusion.16), channel_id=1, source_target_pairs={{0,64},{4,68},{8,72},{12,76},{16,80},{20,84},{24,88},{28,92},{32,9... | collective-permute-start | bytes 221192 | tf_op jit(solution)/shard_map/ppermute | solution.py:30
  26.5 35.3 %collective-permute-start.4 = (f32[288,128]{1,0:T(8,128)S(1)}, f32[288,128]{1,0:T(8,128)}, u32[]{:S(2)}, u32[]{:S(2)}) collective-permute-start(f32[288,128]{1,0:T(8,128)S(1)} %constant_dynamic-update-slice_fusion.14), channel_id=1, source_target_pairs={{0,32},{4,36},{8,40},{12,44},{16,48},{20,52},{24,56},{28,60},{32,0... | collective-permute-start | bytes 442376 | tf_op jit(solution)/shard_map/ppermute | solution.py:30
  62.7 14.9 %collective-permute-start.5 = (f32[576,128]{1,0:T(8,128)S(1)}, f32[576,128]{1,0:T(8,128)S(1)}, u32[]{:S(2)}, u32[]{:S(2)}) collective-permute-start(f32[576,128]{1,0:T(8,128)S(1)} %constant_dynamic-update-slice_fusion.12), channel_id=1, source_target_pairs={{0,16},{4,20},{8,24},{12,28},{16,0},{20,4},{24,8},{28,12},{32,48},... | collective-permute-start | bytes 884744 | tf_op jit(solution)/shard_map/ppermute | solution.py:30
  77.7 17.6 %collective-permute-start.6 = (f32[1152,128]{1,0:T(8,128)S(1)}, f32[1152,128]{1,0:T(8,128)S(1)}, u32[]{:S(2)}, u32[]{:S(2)}) collective-permute-start(f32[1152,128]{1,0:T(8,128)S(1)} %constant_dynamic-update-slice_fusion.10), channel_id=1, source_target_pairs={{0,8},{4,12},{8,0},{12,4},{16,24},{20,28},{24,16},{28,20},{32,40},... | collective-permute-start | bytes 1769480 | tf_op jit(solution)/shard_map/ppermute | solution.py:30
  92.3 2.3 %copy-start.2 = (bf16[24,64,256]{2,1,0:T(8,128)(2,1)}, bf16[24,64,256]{2,1,0:T(8,128)(2,1)S(1)}, u32[]{:S(2)}) copy-start(bf16[24,64,256]{2,1,0:T(8,128)(2,1)S(1)} %get-tuple-element.64) | copy-start | bytes 2359300
  95.4 6.2 %collective-permute-start.7 = (f32[2304,128]{1,0:T(8,128)S(1)}, f32[2304,128]{1,0:T(8,128)S(1)}, u32[]{:S(2)}, u32[]{:S(2)}) collective-permute-start(f32[2304,128]{1,0:T(8,128)S(1)} %constant_dynamic-update-slice_fusion.8), channel_id=1, source_target_pairs={{0,4},{4,0},{8,12},{12,8},{16,20},{20,16},{24,28},{28,24},{32,36},... | collective-permute-start | bytes 3538952 | tf_op jit(solution)/shard_map/ppermute | solution.py:30
  114.2 2.1 collective-permute-start.8
  117.5 29.7 %copy-start.22 = (f32[1536,128]{1,0:T(8,128)S(1)}, f32[1536,128]{1,0:T(8,128)}, u32[]{:S(2)}) copy-start(f32[1536,128]{1,0:T(8,128)} %fusion) | copy-start | bytes 2359300
  117.5 9.0 %collective-permute-start.9 = (f32[592,128]{1,0:T(8,128)S(1)}, f32[592,128]{1,0:T(8,128)S(1)}, u32[]{:S(2)}, u32[]{:S(2)}) collective-permute-start(f32[592,128]{1,0:T(8,128)S(1)} %constant_dynamic-slice_fusion.4), channel_id=1, source_target_pairs={{0,8},{4,12},{8,0},{12,4},{16,24},{20,28},{24,16},{28,20},{32,40},... | collective-permute-start | bytes 909320 | tf_op jit(solution)/shard_map/ppermute | solution.py:56
  126.6 9.1 %collective-permute-start.10 = (f32[296,128]{1,0:T(8,128)S(1)}, f32[296,128]{1,0:T(8,128)S(1)}, u32[]{:S(2)}, u32[]{:S(2)}) collective-permute-start(f32[296,128]{1,0:T(8,128)S(1)} %constant_dynamic-slice_fusion.3), channel_id=1, source_target_pairs={{0,16},{4,20},{8,24},{12,28},{16,0},{20,4},{24,8},{28,12},{32,48},... | collective-permute-start | bytes 454664 | tf_op jit(solution)/shard_map/ppermute | solution.py:56
  135.8 7.2 %collective-permute-start.11 = (f32[148,128]{1,0:T(8,128)S(1)}, f32[148,128]{1,0:T(8,128)S(1)}, u32[]{:S(2)}, u32[]{:S(2)}) collective-permute-start(f32[148,128]{1,0:T(8,128)S(1)} %constant_dynamic-slice_fusion.2), channel_id=1, source_target_pairs={{0,32},{4,36},{8,40},{12,44},{16,48},{20,52},{24,56},{28,60},{32,0... | collective-permute-start | bytes 227336 | tf_op jit(solution)/shard_map/ppermute | solution.py:56
  143.0 2.9 %collective-permute-start.12 = (f32[74,128]{1,0:T(8,128)S(1)}, f32[74,128]{1,0:T(8,128)S(1)}, u32[]{:S(2)}, u32[]{:S(2)}) collective-permute-start(f32[74,128]{1,0:T(8,128)S(1)} %constant_dynamic-slice_fusion.1), channel_id=1, source_target_pairs={{0,64},{4,68},{8,72},{12,76},{16,80},{20,84},{24,88},{28,92},{32,9... | collective-permute-start | bytes 113672 | tf_op jit(solution)/shard_map/ppermute | solution.py:56
  146.0 4.5 %collective-permute-start.13 = (f32[37,128]{1,0:T(8,128)S(1)}, f32[37,128]{1,0:T(8,128)S(1)}, u32[]{:S(2)}, u32[]{:S(2)}) collective-permute-start(f32[37,128]{1,0:T(8,128)S(1)} %constant_dynamic-slice_fusion), channel_id=1, source_target_pairs={{0,128},{4,132},{8,136},{12,140},{16,144},{20,148},{24,152},{28,15... | collective-permute-start | bytes 56840 | tf_op jit(solution)/shard_map/ppermute | solution.py:56
  150.5 4.9 %collective-permute-start.14 = (f32[69,128]{1,0:T(8,128)S(1)}, f32[69,128]{1,0:T(8,128)S(1)}, u32[]{:S(2)}, u32[]{:S(2)}) collective-permute-start(f32[69,128]{1,0:T(8,128)S(1)} %pad_maximum_fusion.2), channel_id=1, source_target_pairs={{0,128},{4,132},{8,136},{12,140},{16,144},{20,148},{24,152},{28,15... | collective-permute-start | bytes 105992 | tf_op jit(solution)/shard_map/ppermute | solution.py:30
  155.6 3.7 %collective-permute-start.15 = (f32[138,128]{1,0:T(8,128)S(1)}, f32[138,128]{1,0:T(8,128)S(1)}, u32[]{:S(2)}, u32[]{:S(2)}) collective-permute-start(f32[138,128]{1,0:T(8,128)S(1)} %dynamic_update_slice.85), channel_id=1, source_target_pairs={{0,64},{4,68},{8,72},{12,76},{16,80},{20,84},{24,88},{28,92},{32,9... | collective-permute-start | bytes 211976 | tf_op jit(solution)/shard_map/ppermute | solution.py:30
  159.7 7.9 %collective-permute-start.16 = (f32[276,128]{1,0:T(8,128)S(1)}, f32[276,128]{1,0:T(8,128)S(1)}, u32[]{:S(2)}, u32[]{:S(2)}) collective-permute-start(f32[276,128]{1,0:T(8,128)S(1)} %dynamic_update_slice.87), channel_id=1, source_target_pairs={{0,32},{4,36},{8,40},{12,44},{16,48},{20,52},{24,56},{28,60},{32,0... | collective-permute-start | bytes 423944 | tf_op jit(solution)/shard_map/ppermute | solution.py:30
  168.3 11.6 %collective-permute-start.17 = (f32[552,128]{1,0:T(8,128)S(1)}, f32[552,128]{1,0:T(8,128)S(1)}, u32[]{:S(2)}, u32[]{:S(2)}) collective-permute-start(f32[552,128]{1,0:T(8,128)S(1)} %dynamic_update_slice.89), channel_id=1, source_target_pairs={{0,16},{4,20},{8,24},{12,28},{16,0},{20,4},{24,8},{28,12},{32,48},... | collective-permute-start | bytes 847880 | tf_op jit(solution)/shard_map/ppermute | solution.py:30
  179.9 12.8 %collective-permute-start.18 = (f32[1104,128]{1,0:T(8,128)S(1)}, f32[1104,128]{1,0:T(8,128)S(1)}, u32[]{:S(2)}, u32[]{:S(2)}) collective-permute-start(f32[1104,128]{1,0:T(8,128)S(1)} %constant_dynamic-update-slice_fusion.4), channel_id=1, source_target_pairs={{0,8},{4,12},{8,0},{12,4},{16,24},{20,28},{24,16},{28,20},{32,40},... | collective-permute-start | bytes 1695752 | tf_op jit(solution)/shard_map/ppermute | solution.py:30
  192.7 8.6 %collective-permute-start.19 = (f32[2208,128]{1,0:T(8,128)S(1)}, f32[2208,128]{1,0:T(8,128)S(1)}, u32[]{:S(2)}, u32[]{:S(2)}) collective-permute-start(f32[2208,128]{1,0:T(8,128)S(1)} %constant_dynamic-update-slice_fusion.2), channel_id=1, source_target_pairs={{0,4},{4,0},{8,12},{12,8},{16,20},{20,16},{24,28},{28,24},{32,36},... | collective-permute-start | bytes 3391496 | tf_op jit(solution)/shard_map/ppermute | solution.py:30
  (23 other events, 29.6 us)

commit v4 on v3

--- a/solution.py
+++ b/solution.py
@@ -1,7 +1,11 @@
+import functools
+
 import jax
 import numpy as np
 import jax.numpy as jnp
 from jax import lax
+from jax.experimental import pallas as pl
+from jax.experimental.pallas import tpu as pltpu
 from jax.sharding import PartitionSpec as P
 
 
@@ -43,21 +47,113 @@
     )
 
 
-def tree_sum(block, axis, rider):
+def tree_kernel(count, chunk, width, grads_ref, sums_ref, out_ref, every_ref, landing, sems, free):
+    me = lax.axis_index("strip")
+    chan = lax.axis_index("chan")
+    dists = [1 << k for k in range(count.bit_length() - 1)]
+    mesh_id = pl.DeviceIdType.MESH
+
+    def partner(dist):
+        return me + dist - 2 * dist * ((me // dist) % 2)
+
+    barrier = pltpu.get_barrier_semaphore()
+    for dist in dists:
+        pl.semaphore_signal(barrier, inc=1, device_id=(partner(dist), chan), device_id_type=mesh_id)
+    pl.semaphore_wait(barrier, len(dists))
+
+    out_ref[...] = grads_ref[...]
+    place = 0
+    for k, dist in enumerate(dists):
+        place = place + ((me // dist) % 2) * (count // (2 * dist))
+    every_ref[pl.ds(pl.multiple_of(place * width, 8), width)] = sums_ref[...]
+
+    low = 0
+    size = count * chunk
+    offset = 0
+    for k, dist in enumerate(dists):
+        half = size // 2
+        high = (me // dist) % 2
+        keep = low + high * half
+        give = low + (1 - high) * half
+        copy = pltpu.make_async_remote_copy(
+            src_ref=out_ref.at[pl.ds(pl.multiple_of(give, 8), half)],
+            dst_ref=landing.at[pl.ds(offset, half)],
+            send_sem=sems.at[0, k],
+            recv_sem=sems.at[1, k],
+            device_id=(partner(dist), chan),
+            device_id_type=mesh_id,
+        )
+        copy.start()
+        copy.wait()
+        pl.semaphore_signal(
+            free.at[k], inc=1, device_id=(partner(dist), chan), device_id_type=mesh_id
+        )
+
+        def accumulate(step, carry, keep=keep, offset=offset):
+            mine = pl.ds(pl.multiple_of(keep + step * chunk, 8), chunk)
+            got = pl.ds(pl.multiple_of(offset + step * chunk, 8), chunk)
+            out_ref[mine] = out_ref[mine] + landing[got]
+            return carry
+
+        lax.fori_loop(0, half // chunk, accumulate, 0)
+        low = keep
+        size = half
+        offset += half
+
+    blocks = 1
+    for k in reversed(range(len(dists))):
+        dist = dists[k]
+        pl.semaphore_wait(free.at[k], 1)
+        rows = pl.ds(pl.multiple_of(low, 8), size)
+        spot = pl.ds(pl.multiple_of(place * width, 8), blocks * width)
+        grads_copy = pltpu.make_async_remote_copy(
+            src_ref=out_ref.at[rows],
+            dst_ref=out_ref.at[rows],
+            send_sem=sems.at[2, k],
+            recv_sem=sems.at[3, k],
+            device_id=(partner(dist), chan),
+            device_id_type=mesh_id,
+        )
+        sums_copy = pltpu.make_async_remote_copy(
+            src_ref=every_ref.at[spot],
+            dst_ref=every_ref.at[spot],
+            send_sem=sems.at[4, k],
+            recv_sem=sems.at[5, k],
+            device_id=(partner(dist), chan),
+            device_id_type=mesh_id,
+        )
+        grads_copy.start()
+        sums_copy.start()
+        grads_copy.wait()
+        sums_copy.wait()
+        high = (me // dist) % 2
+        low = low - high * size
+        place = place - high * blocks
+        size = size * 2
+        blocks = blocks * 2
+
+
+def tree_sum(grads, sums, axis):
     count = lax.axis_size(axis)
-    me = lax.axis_index(axis)
-    order = [1 << k for k in range(count.bit_length() - 1)]
-    held = block
-    for dist in order:
-        half = held.shape[0] // 2
-        high = (me // dist) % 2
-        keep = lax.dynamic_slice_in_dim(held, high * half, half, 0)
-        send = lax.dynamic_slice_in_dim(held, (1 - high) * half, half, 0)
-        held = keep + lax.ppermute(send, axis, [(i, i ^ dist) for i in range(count)])
-    chunk = held.shape[0]
-    both = tree_gather(jnp.concatenate([held, rider], axis=0), axis, order[::-1])
-    both = both.reshape(count, chunk + rider.shape[0], *held.shape[1:])
-    return both[:, :chunk].reshape(count * chunk, *held.shape[1:]), both[:, chunk:]
+    rows, lanes = grads.shape
+    chunk = rows // count
+    width = sums.shape[0]
+    steps = count.bit_length() - 1
+    return pl.pallas_call(
+        functools.partial(tree_kernel, count, chunk, width),
+        out_shape=(
+            jax.ShapeDtypeStruct((rows, lanes), jnp.float32),
+            jax.ShapeDtypeStruct((count * width, lanes), jnp.float32),
+        ),
+        in_specs=[pl.BlockSpec(memory_space=pltpu.VMEM)] * 2,
+        out_specs=(pl.BlockSpec(memory_space=pltpu.VMEM),) * 2,
+        scratch_shapes=[
+            pltpu.VMEM((rows, lanes), jnp.float32),
+            pltpu.SemaphoreType.DMA((6, steps)),
+            pltpu.SemaphoreType.REGULAR((steps,)),
+        ],
+        compiler_params=pltpu.CompilerParams(collective_id=0, has_side_effects=True),
+    )(grads, sums)
 
 
 def swish(value):
@@ -166,11 +262,11 @@
                 )
             )
     local_bias = jnp.sum(deep_grad.astype(jnp.float32), axis=0)
-    bias_rows = jnp.zeros((strip_count, width_deep), jnp.float32).at[0].set(local_bias)
+    bias_rows = jnp.zeros((strip_count * 8 - 9 * channels % (strip_count * 8), width_deep), jnp.float32)
+    bias_rows = bias_rows.at[0].set(local_bias)
     local_grads = jnp.concatenate(pieces + [bias_rows], axis=0)
 
-    total_grads, every_sums = tree_sum(local_grads, "strip", part_sums)
-    every_sums = every_sums.reshape(-1, width_deep)
+    total_grads, every_sums = tree_sum(local_grads, part_sums, "strip")
     mine = strip_pos * owned + jnp.arange(owned, dtype=jnp.int32)
     pick = (mine[:, None] == every_slots[None, :]).astype(jnp.float32)
     slot_sums = jnp.dot(pick, every_sums, precision=lax.Precision.HIGHEST)

time: 213 us -> 206 us (0.967)
  Pallas kernels: 0 us -> 79.8 us
  waiting for transfers between devices: 82.6 us -> 16.6 us
  starting transfers between devices: 36.2 us -> 22.2 us
  local copies, waits for them, and re-layouts: 53 us -> 40.2 us
  matrix products: 16.5 us -> 22.1 us
    pallas_call x0 -> x1, Pallas kernels: none -> 79.8 us  [tree_sum(): pl.pallas_call(functools.partial(tree_kernel, count, chunk, width), out_s...]
    ppermute x12 -> x6, waiting for transfers between devices: 52.3 us -> 15.3 us  [tree_gather(): other = lax.ppermute(held, axis, [(i, i ^ dist) for i in range(count)])]
    ppermute x6 -> x0, waiting for transfers between devices: 28.2 us -> none  [tree_sum(): lax.ppermute(send, axis, [(i, i ^ dist) for i in range(count)])]
    ppermute x12 -> x6, starting transfers between devices: 23.5 us -> 15.9 us  [tree_gather(): other = lax.ppermute(held, axis, [(i, i ^ dist) for i in range(count)])]
    ppermute x6 -> x0, starting transfers between devices: 6.37 us -> none  [tree_sum(): lax.ppermute(send, axis, [(i, i ^ dist) for i in range(count)])]
    dot_general x9, matrix products: 3.68 us -> 9.59 us  [body(): lax.dot_general(window, deep_grad, (((0,), (0,)), ((), ())), preferred_el...]
    reshape x2 -> x0, local copies, waits for them, and re-layouts: 4.07 us -> none  [the longest x1 2.38 us: tree_sum(): both[:, :chunk].reshape(count * chunk, *held.shape[1:])]
    dynamic_update_slice x11 -> x5, local copies, waits for them, and re-layouts: 3.43 us -> 0.19 us  [tree_gather(): both = lax.dynamic_update_slice_in_dim(both, held, high * size, 0)]
  transfers between devices with their start and end apart: 20 -> 8, of which waited for: 14 -> 3; matrix products, arithmetic and copies ran while one was open for 18% -> 17% of each run, Pallas kernels for 0% -> 0%
where the time goes in v4:
time: 206 us; the launch traced here: 205 us
  Pallas kernels  79.8 us (39%)
  local copies, waits for them, and re-layouts  40.2 us (20%)
  starting transfers between devices  22.2 us (11%)
  matrix products  22.1 us (11%)
  waiting for transfers between devices  16.6 us (8%)
  blocking collectives  13.2 us (6%)
  other arithmetic  9.48 us (5%)
    pallas_call x1, Pallas kernels, tree_sum(): pl.pallas_call(functools.partial(tree_kernel, count, chunk, width), out_s...  79.8 us
    ppermute x6, starting transfers between devices, tree_gather(): other = lax.ppermute(held, axis, [(i, i ^ dist) for i in range(count)])  15.9 us
    ppermute x6, waiting for transfers between devices, tree_gather(): other = lax.ppermute(held, axis, [(i, i ^ dist) for i in range(count)])  15.3 us
    reshape x9, local copies, waits for them, and re-layouts, convolve(): window = padded[shift_row:shift_row + row_count, shift_col:shift_col + co...  13.6 us
    all_gather x1, blocking collectives, body(): gathered = lax.all_gather(pooled, 'chan', axis=0, tiled=True)  13.2 us
    dot_general x9, matrix products, body(): lax.dot_general(window, deep_grad, (((0,), (0,)), ((), ())), preferred_el...  9.59 us
    dot_general x18, matrix products, convolve(): jnp.dot(window, weight[shift_row, shift_col], preferred_element_type=jnp....  7.67 us
    unnamed x54, local copies, waits for them, and re-layouts  6.3 us
  transfers between devices with their start and end apart: 8, of which 3 were waited for; matrix products, arithmetic and copies ran while one was open for 17% of the time, Pallas kernels for 0%

profile of v4, /device:TPU:1, one launch (start us, length us, event | category | flops | bytes accessed | tf_op | source)
XLA Modules:
  0.0 205.0 jit_solution(1122570981484541285)
XLA Ops:
  3.5 2.7 %broadcast_select_fusion = f32[1,32]{1,0:T(1,128)S(1)} fusion(pred[]{:T(512)} %and_reduce_fusion, s32[]{:T(128)} %bitcast.2, s32[]{:T(128)} %bitcast.3, f32[1,32]{1,0:T(1,128)S(1)} %bitcast.145, s32[32]{0:T(128)} %param.21), kind=kLoop, calls=%fused_computation.136 | loop fusion | flops 64 | bytes 393 | tf_op jit(solution)/shard_map/select.4
  6.2 1.6 scatter.11
  8.5 3.6 %collective-permute-start.2 = (f32[72,128]{1,0:T(8,128)S(1)}, f32[72,128]{1,0:T(8,128)S(1)}, u32[]{:S(2)}, u32[]{:S(2)}) collective-permute-start(f32[72,128]{1,0:T(8,128)S(1)} %get-tuple-element.71), channel_id=1, source_target_pairs={{0,128},{4,132},{8,136},{12,140},{16,144},{20,148},{24,152},{28,15... | collective-permute-start | bytes 110600 | tf_op jit(solution)/shard_map/ppermute | solution.py:34
  13.0 4.4 %collective-permute-start = (bf16[14,3,256]{2,1,0:T(4,128)(2,1)S(1)}, bf16[14,3,256]{2,1,0:T(4,128)(2,1)S(1)}, u32[]{:S(2)}, u32[]{:S(2)}) collective-permute-start(bf16[14,3,256]{2,1,0:T(4,128)(2,1)S(1)} %get-tuple-element.51), channel_id=1, source_target_pairs={{0,4},{4,8},{8,12},{12,16},{16,20},{20,24},{24,28},{28,32},{32,36}... | collective-permute-start | bytes 64520 | tf_op jit(solution)/shard_map/ppermute | solution.py:20
  17.4 1.9 collective-permute-start.1
  22.6 1.6 pad_maximum_fusion
  24.9 2.6 %collective-permute-done.3 = f32[144,128]{1,0:T(8,128)S(1)} collective-permute-done((f32[144,128]{1,0:T(8,128)S(1)}, f32[144,128]{1,0:T(8,128)S(1)}, u32[]{:S(2)}, u32[]{:S(2)}) %collective-permute-start.3) | collective-permute-done | bytes 73760 | tf_op jit(solution)/shard_map/ppermute | solution.py:34
  27.5 6.3 %collective-permute-start.4 = (f32[288,128]{1,0:T(8,128)S(1)}, f32[288,128]{1,0:T(8,128)}, u32[]{:S(2)}, u32[]{:S(2)}) collective-permute-start(f32[288,128]{1,0:T(8,128)S(1)} %constant_dynamic-update-slice_fusion.8), channel_id=1, source_target_pairs={{0,32},{4,36},{8,40},{12,44},{16,48},{20,52},{24,56},{28,60},{32,0... | collective-permute-start | bytes 442376 | tf_op jit(solution)/shard_map/ppermute | solution.py:34
  33.8 2.5 %fusion.62 = (bf16[12,132,256]{2,1,0:T(8,128)(2,1)S(1)}, bf16[12,132,256]{2,1,0:T(8,128)(2,1)S(1)}, bf16[12,132,256]{2,1,0:T(8,128)(2,1)S(1)}, bf16[12,132,256]{...) fusion(bf16[14,134,256]{2,1,0:T(8,128)(2,1)S(1)} %pad_maximum_f, ...), kind=kLoop, calls=%fused_computation.142 | loop fusion | bytes 14598144 | tf_op jit(solution)/shard_map/slice | solution.py:173
  36.3 2.0 reshape.206
  38.4 2.1 %reshape.207 = bf16[1584,256]{1,0:T(8,128)(2,1)} reshape(bf16[12,132,256]{2,1,0:T(8,128)(2,1)} %get-tuple-element.60) | data formatting | bytes 1622016 | tf_op jit(solution)/shard_map/reshape | solution.py:175
  40.4 2.1 %reshape.208 = bf16[1584,256]{1,0:T(8,128)(2,1)} reshape(bf16[12,132,256]{2,1,0:T(8,128)(2,1)} %get-tuple-element.59) | data formatting | bytes 1622016 | tf_op jit(solution)/shard_map/reshape | solution.py:175
  42.5 2.1 %reshape.209 = bf16[1584,256]{1,0:T(8,128)(2,1)} reshape(bf16[12,132,256]{2,1,0:T(8,128)(2,1)} %get-tuple-element.58) | data formatting | bytes 1622016 | tf_op jit(solution)/shard_map/reshape | solution.py:175
  44.6 2.1 %reshape.210 = bf16[1584,256]{1,0:T(8,128)(2,1)} reshape(bf16[12,132,256]{2,1,0:T(8,128)(2,1)} %get-tuple-element.57) | data formatting | bytes 1622016 | tf_op jit(solution)/shard_map/reshape | solution.py:175
  60.1 2.7 %fusion.2 = f32[6,66,256]{2,1,0:T(8,128)S(1)} fusion(f32[6,2,66,2,256]{4,3,2,1,0:T(2,128)S(1)} %reshape.215, f32[256]{0:T(256)S(1)} %copy-done.24), kind=kLoop, calls=%fused_computation.25 | loop fusion | flops 2331648 | bytes 2028544 | tf_op jit(solution)/shard_map/reduce_sum | solution.py:187
  63.8 2.0 collective-permute-start.5
  66.0 12.7 %collective-permute-done.5 = f32[576,128]{1,0:T(8,128)S(1)} collective-permute-done((f32[576,128]{1,0:T(8,128)S(1)}, f32[576,128]{1,0:T(8,128)S(1)}, u32[]{:S(2)}, u32[]{:S(2)}) %collective-permute-start.5) | collective-permute-done | bytes 294944 | tf_op jit(solution)/shard_map/ppermute | solution.py:34
  80.1 13.2 %all_gather.3 = bf16[24,66,256]{2,1,0:T(8,128)(2,1)S(1)} all-gather(bf16[6,66,256]{2,1,0:T(8,128)(2,1)S(1)} %fusion.13), channel_id=1, replica_groups=mesh['strip'=64,'chan'=4] {'chan'}, dimensions={0}, use_global_device_ids=true | all-gather | bytes 1013760 | tf_op jit(solution)/shard_map/all_gather | solution.py:234
  98.2 2.0 collective-permute-start.7
  103.3 1.6 slice.243
  105.4 2.2 %gather_fusion.1 = f32[32,128]{1,0:T(8,128)S(1)} fusion(f32[4096,128]{1,0:T(8,128)} %bitcast.142, s32[1024]{0:T(1024)S(1)} %pad_clamp_fusion), kind=kCustom, calls=%fused_computation.1 | custom fusion | bytes 32896 | tf_op jit(solution)/shard_map/gather | solution.py:244
  107.6 2.1 %convert_reduce_fusion = (f32[128]{0:T(128)S(1)}, bf16[1536,128]{1,0:T(8,128)(2,1)S(1)}) fusion(f32[1536,128]{1,0:T(8,128)} %copy-done.22, f32[32,128]{1,0:T(8,128)S(1)} %gather_fusion.1, f32[32]{0:T(128)S(1)} %fusion.4, s32[1536]{0:T(1024)S(1)} %eq.83), kind=kOutput, calls=%fused_computation.42 | convolution fusion | flops 77713280 | bytes 1202816 | tf_op jit(solution)/shard_map/dot_general | solution.py:245
  120.0 79.8 %shard_map.112 = (f32[2560,128]{1,0:T(8,128)}, f32[2048,128]{1,0:T(8,128)}) custom-call(f32[2560,128]{1,0:T(8,128)} %pad_dynamic-update-slice_fusion.grads_ref, f32[32,128]{1,0:T(8,128)} %fusion.7.sums_ref), custom_call_target="tpu_custom_call" | custom-call | tf_op jit(solution)/shard_map/pallas_call | solution.py:142
  199.8 2.4 %slice.236 = f32[2304,128]{1,0:T(8,128)} slice(f32[2560,128]{1,0:T(8,128)} %get-tuple-element.50), slice={[0:2304], [0:128]} | slice | bytes 2359296 | tf_op jit(solution)/shard_map/slice | solution.py:276
  (139 shorter events, 45.4 us)
Async XLA Ops:
  8.5 10.8 %copy-start.1 = (bf16[48,128,256]{2,1,0:T(8,128)(2,1)S(1)}, bf16[48,128,256]{2,1,0:T(8,128)(2,1)}, u32[]{:S(2)}) copy-start(bf16[48,128,256]{2,1,0:T(8,128)(2,1)} %param.15) | copy-start | bytes 9437188
  8.5 15.7 %collective-permute-start.2 = (f32[72,128]{1,0:T(8,128)S(1)}, f32[72,128]{1,0:T(8,128)S(1)}, u32[]{:S(2)}, u32[]{:S(2)}) collective-permute-start(f32[72,128]{1,0:T(8,128)S(1)} %get-tuple-element.71), channel_id=1, source_target_pairs={{0,128},{4,132},{8,136},{12,140},{16,144},{20,148},{24,152},{28,15... | collective-permute-start | bytes 110600 | tf_op jit(solution)/shard_map/ppermute | solution.py:34
  13.0 8.3 %collective-permute-start = (bf16[14,3,256]{2,1,0:T(4,128)(2,1)S(1)}, bf16[14,3,256]{2,1,0:T(4,128)(2,1)S(1)}, u32[]{:S(2)}, u32[]{:S(2)}) collective-permute-start(bf16[14,3,256]{2,1,0:T(4,128)(2,1)S(1)} %get-tuple-element.51), channel_id=1, source_target_pairs={{0,4},{4,8},{8,12},{12,16},{16,20},{20,24},{24,28},{28,32},{32,36}... | collective-permute-start | bytes 64520 | tf_op jit(solution)/shard_map/ppermute | solution.py:20
  17.4 3.0 %copy-start.25 = (s32[32]{0:T(128)S(1)}, s32[32]{0:T(128)}, u32[]{:S(2)}) copy-start(s32[32]{0:T(128)} %param.21) | copy-start | bytes 388
  17.4 3.0 %copy-start = (s32[64]{0:T(128)S(1)}, s32[64]{0:T(128)}, u32[]{:S(2)}) copy-start(s32[64]{0:T(128)} %constant.254.clone) | copy-start | bytes 772
  17.4 5.2 %collective-permute-start.1 = (bf16[14,3,256]{2,1,0:T(4,128)(2,1)S(1)}, bf16[14,3,256]{2,1,0:T(4,128)(2,1)S(1)}, u32[]{:S(2)}, u32[]{:S(2)}) collective-permute-start(bf16[14,3,256]{2,1,0:T(4,128)(2,1)S(1)} %get-tuple-element.52), channel_id=1, source_target_pairs={{4,0},{8,4},{12,8},{16,12},{20,16},{24,20},{28,24},{32,28},{36,32}... | collective-permute-start | bytes 64520 | tf_op jit(solution)/shard_map/ppermute | solution.py:22
  24.2 3.3 %collective-permute-start.3 = (f32[144,128]{1,0:T(8,128)S(1)}, f32[144,128]{1,0:T(8,128)S(1)}, u32[]{:S(2)}, u32[]{:S(2)}) collective-permute-start(f32[144,128]{1,0:T(8,128)S(1)} %constant_dynamic-update-slice_fusion.10), channel_id=1, source_target_pairs={{0,64},{4,68},{8,72},{12,76},{16,80},{20,84},{24,88},{28,92},{32,9... | collective-permute-start | bytes 221192 | tf_op jit(solution)/shard_map/ppermute | solution.py:34
  27.5 35.3 %collective-permute-start.4 = (f32[288,128]{1,0:T(8,128)S(1)}, f32[288,128]{1,0:T(8,128)}, u32[]{:S(2)}, u32[]{:S(2)}) collective-permute-start(f32[288,128]{1,0:T(8,128)S(1)} %constant_dynamic-update-slice_fusion.8), channel_id=1, source_target_pairs={{0,32},{4,36},{8,40},{12,44},{16,48},{20,52},{24,56},{28,60},{32,0... | collective-permute-start | bytes 442376 | tf_op jit(solution)/shard_map/ppermute | solution.py:34
  49.9 1.4 copy-start.19
  49.9 1.6 copy-start.20
  63.8 14.9 %collective-permute-start.5 = (f32[576,128]{1,0:T(8,128)S(1)}, f32[576,128]{1,0:T(8,128)S(1)}, u32[]{:S(2)}, u32[]{:S(2)}) collective-permute-start(f32[576,128]{1,0:T(8,128)S(1)} %constant_dynamic-update-slice_fusion.6), channel_id=1, source_target_pairs={{0,16},{4,20},{8,24},{12,28},{16,0},{20,4},{24,8},{28,12},{32,48},... | collective-permute-start | bytes 884744 | tf_op jit(solution)/shard_map/ppermute | solution.py:34
  78.7 19.3 %collective-permute-start.6 = (f32[1152,128]{1,0:T(8,128)S(1)}, f32[1152,128]{1,0:T(8,128)S(1)}, u32[]{:S(2)}, u32[]{:S(2)}) collective-permute-start(f32[1152,128]{1,0:T(8,128)S(1)} %constant_dynamic-update-slice_fusion.4), channel_id=1, source_target_pairs={{0,8},{4,12},{8,0},{12,4},{16,24},{20,28},{24,16},{28,20},{32,40},... | collective-permute-start | bytes 1769480 | tf_op jit(solution)/shard_map/ppermute | solution.py:34
  93.3 1.5 copy-start.23
  94.7 1.4 copy-start.6
  94.7 1.8 copy-start.4
  94.7 2.1 %copy-start.2 = (bf16[24,64,256]{2,1,0:T(8,128)(2,1)}, bf16[24,64,256]{2,1,0:T(8,128)(2,1)S(1)}, u32[]{:S(2)}) copy-start(bf16[24,64,256]{2,1,0:T(8,128)(2,1)S(1)} %get-tuple-element.68) | copy-start | bytes 2359300
  98.1 2.4 %copy-start.26 = (f32[128]{0:T(128)S(1)}, f32[128]{0:T(128)}, u32[]{:S(2)}) copy-start(f32[128]{0:T(128)} %param.19) | copy-start | bytes 1540
  98.2 4.8 %collective-permute-start.7 = (f32[2304,128]{1,0:T(8,128)S(1)}, f32[2304,128]{1,0:T(8,128)S(1)}, u32[]{:S(2)}, u32[]{:S(2)}) collective-permute-start(f32[2304,128]{1,0:T(8,128)S(1)} %constant_dynamic-update-slice_fusion.2), channel_id=1, source_target_pairs={{0,4},{4,0},{8,12},{12,8},{16,20},{20,16},{24,28},{28,24},{32,36},... | collective-permute-start | bytes 3538952 | tf_op jit(solution)/shard_map/ppermute | solution.py:34
  107.6 2.1 %copy-start.11 = (bf16[24,64,256]{2,1,0:T(8,128)(2,1)S(1)}, bf16[24,64,256]{2,1,0:T(8,128)(2,1)}, u32[]{:S(2)}) copy-start(bf16[24,64,256]{2,1,0:T(8,128)(2,1)} %copy-done.10) | copy-start | bytes 2359300
  107.6 3.2 %copy-start.9 = (bf16[24,64,256]{2,1,0:T(8,128)(2,1)S(1)}, bf16[24,64,256]{2,1,0:T(8,128)(2,1)}, u32[]{:S(2)}) copy-start(bf16[24,64,256]{2,1,0:T(8,128)(2,1)} %copy-done.8) | copy-start | bytes 2359300
  109.7 2.1 %copy-start.7 = (bf16[24,64,256]{2,1,0:T(8,128)(2,1)S(1)}, bf16[24,64,256]{2,1,0:T(8,128)(2,1)}, u32[]{:S(2)}) copy-start(bf16[24,64,256]{2,1,0:T(8,128)(2,1)} %copy-done.6) | copy-start | bytes 2359300
  110.8 2.1 %copy-start.5 = (bf16[24,64,256]{2,1,0:T(8,128)(2,1)S(1)}, bf16[24,64,256]{2,1,0:T(8,128)(2,1)}, u32[]{:S(2)}) copy-start(bf16[24,64,256]{2,1,0:T(8,128)(2,1)} %copy-done.4) | copy-start | bytes 2359300
  111.9 2.1 %copy-start.3 = (bf16[24,64,256]{2,1,0:T(8,128)(2,1)S(1)}, bf16[24,64,256]{2,1,0:T(8,128)(2,1)}, u32[]{:S(2)}) copy-start(bf16[24,64,256]{2,1,0:T(8,128)(2,1)} %copy-done.2) | copy-start | bytes 2359300
  199.8 4.0 %copy-start.21 = (f32[2048,128]{1,0:T(8,128)S(1)}, f32[2048,128]{1,0:T(8,128)}, u32[]{:S(2)}) copy-start(f32[2048,128]{1,0:T(8,128)} %get-tuple-element.49) | copy-start | bytes 3145732
  (11 other events, 12.0 us)

commit v5 on v3

--- a/solution.py
+++ b/solution.py
@@ -1,7 +1,11 @@
+import functools
+
 import jax
 import numpy as np
 import jax.numpy as jnp
 from jax import lax
+from jax.experimental import pallas as pl
+from jax.experimental.pallas import tpu as pltpu
 from jax.sharding import PartitionSpec as P
 
 
@@ -43,21 +47,136 @@
     )
 
 
-def tree_sum(block, axis, rider):
+def tree_kernel(count, orders, width, grads_ref, sums_ref, out_ref, every_ref, landing, sems, free):
+    me = lax.axis_index("strip")
+    chan = lax.axis_index("chan")
+    mesh_id = pl.DeviceIdType.MESH
+    steps = len(orders[0])
+    rows = grads_ref.shape[0]
+    sizes = [rows // 3, rows - rows // 3]
+    bases = [0, rows // 3]
+    chunks = [size // count for size in sizes]
+
+    def partner(dist):
+        return me + dist - 2 * dist * ((me // dist) % 2)
+
+    def bit(dist):
+        return (me // dist) % 2
+
+    barrier = pltpu.get_barrier_semaphore()
+    for dist in orders[0]:
+        pl.semaphore_signal(barrier, inc=1, device_id=(partner(dist), chan), device_id_type=mesh_id)
+    pl.semaphore_wait(barrier, steps)
+
+    out_ref[...] = grads_ref[...]
+    place = 0
+    for k, dist in enumerate(orders[0]):
+        place = place + bit(dist) * (count >> (k + 1))
+    every_ref[pl.ds(pl.multiple_of(place * width, 8), width)] = sums_ref[...]
+
+    lows = [0, 0]
+    offsets = [0, 0]
+    for k in range(steps):
+        copies = []
+        keeps = []
+        for t in range(2):
+            dist = orders[t][k]
+            half = sizes[t] // 2
+            keep = lows[t] + bit(dist) * half
+            give = lows[t] + (1 - bit(dist)) * half
+            copies.append(
+                pltpu.make_async_remote_copy(
+                    src_ref=out_ref.at[pl.ds(pl.multiple_of(bases[t] + give, 8), half)],
+                    dst_ref=landing.at[pl.ds(bases[t] + offsets[t], half)],
+                    send_sem=sems.at[0, t, k],
+                    recv_sem=sems.at[1, t, k],
+                    device_id=(partner(dist), chan),
+                    device_id_type=mesh_id,
+                )
+            )
+            keeps.append(keep)
+        for copy in copies:
+            copy.start()
+        for t in range(2):
+            copies[t].wait()
+            pl.semaphore_signal(
+                free.at[t, k], inc=1, device_id=(partner(orders[t][k]), chan),
+                device_id_type=mesh_id,
+            )
+        for t in range(2):
+            half = sizes[t] // 2
+            chunk = chunks[t]
+
+            def accumulate(step, carry, t=t, keep=keeps[t], offset=offsets[t], chunk=chunk):
+                mine = pl.ds(pl.multiple_of(bases[t] + keep + step * chunk, 8), chunk)
+                got = pl.ds(pl.multiple_of(bases[t] + offset + step * chunk, 8), chunk)
+                out_ref[mine] = out_ref[mine] + landing[got]
+                return carry
+
+            lax.fori_loop(0, half // chunk, accumulate, 0)
+            lows[t] = keeps[t]
+            offsets[t] += half
+            sizes[t] = half
+
+    blocks = 1
+    for k in reversed(range(steps)):
+        copies = []
+        for t in range(2):
+            dist = orders[t][k]
+            pl.semaphore_wait(free.at[t, k], 1)
+            span = pl.ds(pl.multiple_of(bases[t] + lows[t], 8), sizes[t])
+            copies.append(
+                pltpu.make_async_remote_copy(
+                    src_ref=out_ref.at[span],
+                    dst_ref=out_ref.at[span],
+                    send_sem=sems.at[2, t, k],
+                    recv_sem=sems.at[3, t, k],
+                    device_id=(partner(dist), chan),
+                    device_id_type=mesh_id,
+                )
+            )
+        spot = pl.ds(pl.multiple_of(place * width, 8), blocks * width)
+        copies.append(
+            pltpu.make_async_remote_copy(
+                src_ref=every_ref.at[spot],
+                dst_ref=every_ref.at[spot],
+                send_sem=sems.at[4, 0, k],
+                recv_sem=sems.at[5, 0, k],
+                device_id=(partner(orders[0][k]), chan),
+                device_id_type=mesh_id,
+            )
+        )
+        for copy in copies:
+            copy.start()
+        for copy in copies:
+            copy.wait()
+        for t in range(2):
+            lows[t] = lows[t] - bit(orders[t][k]) * sizes[t]
+            sizes[t] = sizes[t] * 2
+        place = place - bit(orders[0][k]) * blocks
+        blocks = blocks * 2
+
+
+def tree_sum(grads, sums, axis, orders):
     count = lax.axis_size(axis)
-    me = lax.axis_index(axis)
-    order = [1 << k for k in range(count.bit_length() - 1)]
-    held = block
-    for dist in order:
-        half = held.shape[0] // 2
-        high = (me // dist) % 2
-        keep = lax.dynamic_slice_in_dim(held, high * half, half, 0)
-        send = lax.dynamic_slice_in_dim(held, (1 - high) * half, half, 0)
-        held = keep + lax.ppermute(send, axis, [(i, i ^ dist) for i in range(count)])
-    chunk = held.shape[0]
-    both = tree_gather(jnp.concatenate([held, rider], axis=0), axis, order[::-1])
-    both = both.reshape(count, chunk + rider.shape[0], *held.shape[1:])
-    return both[:, :chunk].reshape(count * chunk, *held.shape[1:]), both[:, chunk:]
+    rows, lanes = grads.shape
+    width = sums.shape[0]
+    steps = len(orders[0])
+    return pl.pallas_call(
+        functools.partial(tree_kernel, count, orders, width),
+        out_shape=(
+            jax.ShapeDtypeStruct((rows, lanes), jnp.float32),
+            jax.ShapeDtypeStruct((count * width, lanes), jnp.float32),
+        ),
+        in_specs=[pl.BlockSpec(memory_space=pltpu.VMEM)] * 2,
+        out_specs=(pl.BlockSpec(memory_space=pltpu.VMEM),) * 2,
+        scratch_shapes=[
+            pltpu.VMEM((rows, lanes), jnp.float32),
+            pltpu.SemaphoreType.DMA((6, 2, steps)),
+            pltpu.SemaphoreType.REGULAR((2, steps)),
+        ],
+        compiler_params=pltpu.CompilerParams(collective_id=0, has_side_effects=True),
+    )(grads, sums)
 
 
 def swish(value):
@@ -114,7 +233,11 @@
     meta = meta.at[0, :list_len].set(part_counts)
     meta = meta.at[0, list_len : 2 * list_len].set(slot_ids.astype(jnp.float32))
     packed = jnp.concatenate([embed_grad, meta], axis=0)
-    order = [strip_count >> (k + 1) for k in range(strip_count.bit_length() - 1)]
+    steps = strip_count.bit_length() - 1
+    halving = [[1 << k for k in range(steps)], [1 << k for k in range(steps)]]
+    if steps == 6:
+        halving = [[1, 2, 16, 4, 32, 8], [2, 1, 4, 16, 8, 32]]
+    order = halving[0][::-1]
     position = jnp.asarray(gather_position(order, strip_count))
     early = tree_gather(packed, "strip", order[:2])
 
@@ -166,11 +289,11 @@
                 )
             )
     local_bias = jnp.sum(deep_grad.astype(jnp.float32), axis=0)
-    bias_rows = jnp.zeros((strip_count, width_deep), jnp.float32).at[0].set(local_bias)
+    bias_rows = jnp.zeros((strip_count * 48 - 9 * channels % (strip_count * 48), width_deep), jnp.float32)
+    bias_rows = bias_rows.at[0].set(local_bias)
     local_grads = jnp.concatenate(pieces + [bias_rows], axis=0)
 
-    total_grads, every_sums = tree_sum(local_grads, "strip", part_sums)
-    every_sums = every_sums.reshape(-1, width_deep)
+    total_grads, every_sums = tree_sum(local_grads, part_sums, "strip", halving)
     mine = strip_pos * owned + jnp.arange(owned, dtype=jnp.int32)
     pick = (mine[:, None] == every_slots[None, :]).astype(jnp.float32)
     slot_sums = jnp.dot(pick, every_sums, precision=lax.Precision.HIGHEST)

time: 213 us -> 208 us (0.977); the launches traced: 212 us -> 203 us
  Pallas kernels: 0 us -> 83.8 us
  waiting for transfers between devices: 82.6 us -> 9.29 us
  local copies, waits for them, and re-layouts: 53 us -> 40.3 us
  starting transfers between devices: 36.2 us -> 25.1 us
  matrix products: 16.5 us -> 22.1 us
    pallas_call x0 -> x1, Pallas kernels: none -> 83.8 us  [tree_sum(): pl.pallas_call(functools.partial(tree_kernel, count, orders, width), out_...]
    ppermute x12 -> x6, waiting for transfers between devices: 52.3 us -> 8.02 us  [tree_gather(): other = lax.ppermute(held, axis, [(i, i ^ dist) for i in range(count)])]
    ppermute x6 -> x0, waiting for transfers between devices: 28.2 us -> none  [tree_sum(): lax.ppermute(send, axis, [(i, i ^ dist) for i in range(count)])]
    ppermute x6 -> x0, starting transfers between devices: 6.37 us -> none  [tree_sum(): lax.ppermute(send, axis, [(i, i ^ dist) for i in range(count)])]
    dot_general x9, matrix products: 3.68 us -> 9.59 us  [body(): lax.dot_general(window, deep_grad, (((0,), (0,)), ((), ())), preferred_el...]
    reshape x2 -> x0, local copies, waits for them, and re-layouts: 4.07 us -> none  [the longest x1 2.38 us: tree_sum(): both[:, :chunk].reshape(count * chunk, *held.shape[1:])]
    ppermute x12 -> x6, starting transfers between devices: 23.5 us -> 19.7 us  [tree_gather(): other = lax.ppermute(held, axis, [(i, i ^ dist) for i in range(count)])]
    dynamic_update_slice x11 -> x5, local copies, waits for them, and re-layouts: 3.43 us -> 0.19 us  [tree_gather(): both = lax.dynamic_update_slice_in_dim(both, held, high * size, 0)]
  transfers between devices with their start and end apart: 20 -> 8, of which waited for: 14 -> 3; matrix products, arithmetic and copies ran while one was open for 18% -> 17% of each run, Pallas kernels for 0% -> 0%
where the time goes in v5:
time: 208 us; the launch traced here: 203 us
  Pallas kernels  83.8 us (40%)
  local copies, waits for them, and re-layouts  40.3 us (19%)
  starting transfers between devices  25.1 us (12%)
  matrix products  22.1 us (11%)
  blocking collectives  11.9 us (6%)
  other arithmetic  9.48 us (5%)
  waiting for transfers between devices  9.29 us (4%)
    pallas_call x1, Pallas kernels, tree_sum(): pl.pallas_call(functools.partial(tree_kernel, count, orders, width), out_...  83.8 us
    ppermute x6, starting transfers between devices, tree_gather(): other = lax.ppermute(held, axis, [(i, i ^ dist) for i in range(count)])  19.7 us
    reshape x9, local copies, waits for them, and re-layouts, convolve(): window = padded[shift_row:shift_row + row_count, shift_col:shift_col + co...  13.6 us
    all_gather x1, blocking collectives, body(): gathered = lax.all_gather(pooled, 'chan', axis=0, tiled=True)  11.9 us
    dot_general x9, matrix products, body(): lax.dot_general(window, deep_grad, (((0,), (0,)), ((), ())), preferred_el...  9.59 us
    ppermute x6, waiting for transfers between devices, tree_gather(): other = lax.ppermute(held, axis, [(i, i ^ dist) for i in range(count)])  8.02 us
    dot_general x18, matrix products, convolve(): jnp.dot(window, weight[shift_row, shift_col], preferred_element_type=jnp....  7.66 us
    unnamed x54, local copies, waits for them, and re-layouts  6.29 us
  transfers between devices with their start and end apart: 8, of which 3 were waited for; matrix products, arithmetic and copies ran while one was open for 17% of the time, Pallas kernels for 0%

profile of v5, /device:TPU:1, one launch (start us, length us, event | category | flops | bytes accessed | tf_op | source)
XLA Modules:
  0.0 203.4 jit_solution(9525287798297731267)
XLA Ops:
  3.5 2.7 %broadcast_select_fusion = f32[1,32]{1,0:T(1,128)S(1)} fusion(pred[]{:T(512)} %and_reduce_fusion, s32[]{:T(128)} %bitcast.2, s32[]{:T(128)} %bitcast.3, f32[1,32]{1,0:T(1,128)S(1)} %bitcast.145, s32[32]{0:T(128)} %param.21), kind=kLoop, calls=%fused_computation.136 | loop fusion | flops 64 | bytes 393 | tf_op jit(solution)/shard_map/select.4
  6.2 1.6 scatter.11
  8.5 7.7 %collective-permute-start.2 = (f32[72,128]{1,0:T(8,128)S(1)}, f32[72,128]{1,0:T(8,128)S(1)}, u32[]{:S(2)}, u32[]{:S(2)}) collective-permute-start(f32[72,128]{1,0:T(8,128)S(1)} %get-tuple-element.71), channel_id=1, source_target_pairs={{0,32},{4,36},{8,40},{12,44},{16,48},{20,52},{24,56},{28,60},{32,0... | collective-permute-start | bytes 110600 | tf_op jit(solution)/shard_map/ppermute | solution.py:34
  17.1 3.5 %collective-permute-start = (bf16[14,3,256]{2,1,0:T(4,128)(2,1)S(1)}, bf16[14,3,256]{2,1,0:T(4,128)(2,1)S(1)}, u32[]{:S(2)}, u32[]{:S(2)}) collective-permute-start(bf16[14,3,256]{2,1,0:T(4,128)(2,1)S(1)} %get-tuple-element.51), channel_id=1, source_target_pairs={{0,4},{4,8},{8,12},{12,16},{16,20},{20,24},{24,28},{28,32},{32,36}... | collective-permute-start | bytes 64520 | tf_op jit(solution)/shard_map/ppermute | solution.py:20
  20.6 1.9 collective-permute-start.1
  25.8 1.6 pad_maximum_fusion
  27.5 2.8 %collective-permute-start.3 = (f32[144,128]{1,0:T(8,128)S(1)}, f32[144,128]{1,0:T(8,128)S(1)}, u32[]{:S(2)}, u32[]{:S(2)}) collective-permute-start(f32[144,128]{1,0:T(8,128)S(1)} %constant_dynamic-update-slice_fusion.10), channel_id=1, source_target_pairs={{0,128},{4,132},{8,136},{12,140},{16,144},{20,148},{24,152},{28,15... | collective-permute-start | bytes 221192 | tf_op jit(solution)/shard_map/ppermute | solution.py:34
  30.3 1.9 collective-permute-done.3
  32.3 2.2 %collective-permute-start.4 = (f32[288,128]{1,0:T(8,128)S(1)}, f32[288,128]{1,0:T(8,128)}, u32[]{:S(2)}, u32[]{:S(2)}) collective-permute-start(f32[288,128]{1,0:T(8,128)S(1)} %constant_dynamic-update-slice_fusion.8), channel_id=1, source_target_pairs={{0,16},{4,20},{8,24},{12,28},{16,0},{20,4},{24,8},{28,12},{32,48},... | collective-permute-start | bytes 442376 | tf_op jit(solution)/shard_map/ppermute | solution.py:34
  34.5 2.5 %fusion.62 = (bf16[12,132,256]{2,1,0:T(8,128)(2,1)S(1)}, bf16[12,132,256]{2,1,0:T(8,128)(2,1)S(1)}, bf16[12,132,256]{2,1,0:T(8,128)(2,1)S(1)}, bf16[12,132,256]{...) fusion(bf16[14,134,256]{2,1,0:T(8,128)(2,1)S(1)} %pad_maximum_f, ...), kind=kLoop, calls=%fused_computation.142 | loop fusion | bytes 14598144 | tf_op jit(solution)/shard_map/slice | solution.py:196
  37.0 2.0 %reshape.206 = bf16[1584,256]{1,0:T(8,128)(2,1)} reshape(bf16[12,132,256]{2,1,0:T(8,128)(2,1)} %get-tuple-element.61) | data formatting | bytes 1622016 | tf_op jit(solution)/shard_map/reshape | solution.py:198
  39.1 2.1 %reshape.207 = bf16[1584,256]{1,0:T(8,128)(2,1)} reshape(bf16[12,132,256]{2,1,0:T(8,128)(2,1)} %get-tuple-element.60) | data formatting | bytes 1622016 | tf_op jit(solution)/shard_map/reshape | solution.py:198
  41.1 2.1 %reshape.208 = bf16[1584,256]{1,0:T(8,128)(2,1)} reshape(bf16[12,132,256]{2,1,0:T(8,128)(2,1)} %get-tuple-element.59) | data formatting | bytes 1622016 | tf_op jit(solution)/shard_map/reshape | solution.py:198
  43.2 2.1 %reshape.209 = bf16[1584,256]{1,0:T(8,128)(2,1)} reshape(bf16[12,132,256]{2,1,0:T(8,128)(2,1)} %get-tuple-element.58) | data formatting | bytes 1622016 | tf_op jit(solution)/shard_map/reshape | solution.py:198
  45.3 2.1 %reshape.210 = bf16[1584,256]{1,0:T(8,128)(2,1)} reshape(bf16[12,132,256]{2,1,0:T(8,128)(2,1)} %get-tuple-element.57) | data formatting | bytes 1622016 | tf_op jit(solution)/shard_map/reshape | solution.py:198
  60.8 2.7 %fusion.2 = f32[6,66,256]{2,1,0:T(8,128)S(1)} fusion(f32[6,2,66,2,256]{4,3,2,1,0:T(2,128)S(1)} %reshape.215, f32[256]{0:T(256)S(1)} %copy-done.24), kind=kLoop, calls=%fused_computation.25 | loop fusion | flops 2331648 | bytes 2028544 | tf_op jit(solution)/shard_map/reduce_sum | solution.py:210
  66.0 6.1 %collective-permute-done.5 = f32[576,128]{1,0:T(8,128)S(1)} collective-permute-done((f32[576,128]{1,0:T(8,128)S(1)}, f32[576,128]{1,0:T(8,128)S(1)}, u32[]{:S(2)}, u32[]{:S(2)}) %collective-permute-start.5) | collective-permute-done | bytes 294944 | tf_op jit(solution)/shard_map/ppermute | solution.py:34
  72.2 11.9 %all_gather.3 = bf16[24,66,256]{2,1,0:T(8,128)(2,1)S(1)} all-gather(bf16[6,66,256]{2,1,0:T(8,128)(2,1)S(1)} %fusion.13), channel_id=1, replica_groups=mesh['strip'=64,'chan'=4] {'chan'}, dimensions={0}, use_global_device_ids=true | all-gather | bytes 1013760 | tf_op jit(solution)/shard_map/all_gather | solution.py:261
  88.9 5.5 %collective-permute-start.7 = (f32[2304,128]{1,0:T(8,128)S(1)}, f32[2304,128]{1,0:T(8,128)S(1)}, u32[]{:S(2)}, u32[]{:S(2)}) collective-permute-start(f32[2304,128]{1,0:T(8,128)S(1)} %constant_dynamic-update-slice_fusion.2), channel_id=1, source_target_pairs={{0,4},{4,0},{8,12},{12,8},{16,20},{20,16},{24,28},{28,24},{32,36},... | collective-permute-start | bytes 3538952 | tf_op jit(solution)/shard_map/ppermute | solution.py:34
  97.6 1.6 slice.243
  99.7 2.2 %gather_fusion.1 = f32[32,128]{1,0:T(8,128)S(1)} fusion(f32[4096,128]{1,0:T(8,128)} %bitcast.142, s32[1024]{0:T(1024)S(1)} %pad_clamp_fusion), kind=kCustom, calls=%fused_computation.1 | custom fusion | bytes 32896 | tf_op jit(solution)/shard_map/gather | solution.py:271
  101.9 2.1 %convert_reduce_fusion = (f32[128]{0:T(128)S(1)}, bf16[1536,128]{1,0:T(8,128)(2,1)S(1)}) fusion(f32[1536,128]{1,0:T(8,128)} %copy-done.22, f32[32,128]{1,0:T(8,128)S(1)} %gather_fusion.1, f32[32]{0:T(128)S(1)} %fusion.4, s32[1536]{0:T(1024)S(1)} %eq.83), kind=kOutput, calls=%fused_computation.42 | convolution fusion | flops 77713280 | bytes 1202816 | tf_op jit(solution)/shard_map/dot_general | solution.py:272
  114.4 83.8 %shard_map.112 = (f32[3072,128]{1,0:T(8,128)}, f32[2048,128]{1,0:T(8,128)}) custom-call(f32[3072,128]{1,0:T(8,128)} %pad_dynamic-update-slice_fusion.grads_ref, f32[32,128]{1,0:T(8,128)} %fusion.7.sums_ref), custom_call_target="tpu_custom_call" | custom-call | tf_op jit(solution)/shard_map/pallas_call | solution.py:165
  198.2 2.4 %slice.236 = f32[2304,128]{1,0:T(8,128)} slice(f32[3072,128]{1,0:T(8,128)} %get-tuple-element.50), slice={[0:2304], [0:128]} | slice | bytes 2359296 | tf_op jit(solution)/shard_map/slice | solution.py:303
  (139 shorter events, 44.8 us)
Async XLA Ops:
  8.5 14.1 %copy-start.1 = (bf16[48,128,256]{2,1,0:T(8,128)(2,1)S(1)}, bf16[48,128,256]{2,1,0:T(8,128)(2,1)}, u32[]{:S(2)}) copy-start(bf16[48,128,256]{2,1,0:T(8,128)(2,1)} %param.15) | copy-start | bytes 9437188
  8.5 18.9 %collective-permute-start.2 = (f32[72,128]{1,0:T(8,128)S(1)}, f32[72,128]{1,0:T(8,128)S(1)}, u32[]{:S(2)}, u32[]{:S(2)}) collective-permute-start(f32[72,128]{1,0:T(8,128)S(1)} %get-tuple-element.71), channel_id=1, source_target_pairs={{0,32},{4,36},{8,40},{12,44},{16,48},{20,52},{24,56},{28,60},{32,0... | collective-permute-start | bytes 110600 | tf_op jit(solution)/shard_map/ppermute | solution.py:34
  17.1 7.4 %collective-permute-start = (bf16[14,3,256]{2,1,0:T(4,128)(2,1)S(1)}, bf16[14,3,256]{2,1,0:T(4,128)(2,1)S(1)}, u32[]{:S(2)}, u32[]{:S(2)}) collective-permute-start(bf16[14,3,256]{2,1,0:T(4,128)(2,1)S(1)} %get-tuple-element.51), channel_id=1, source_target_pairs={{0,4},{4,8},{8,12},{12,16},{16,20},{20,24},{24,28},{28,32},{32,36}... | collective-permute-start | bytes 64520 | tf_op jit(solution)/shard_map/ppermute | solution.py:20
  20.6 3.0 %copy-start.25 = (s32[32]{0:T(128)S(1)}, s32[32]{0:T(128)}, u32[]{:S(2)}) copy-start(s32[32]{0:T(128)} %param.21) | copy-start | bytes 388
  20.6 3.0 %copy-start = (s32[64]{0:T(128)S(1)}, s32[64]{0:T(128)}, u32[]{:S(2)}) copy-start(s32[64]{0:T(128)} %constant.254.clone) | copy-start | bytes 772
  20.6 5.2 %collective-permute-start.1 = (bf16[14,3,256]{2,1,0:T(4,128)(2,1)S(1)}, bf16[14,3,256]{2,1,0:T(4,128)(2,1)S(1)}, u32[]{:S(2)}, u32[]{:S(2)}) collective-permute-start(bf16[14,3,256]{2,1,0:T(4,128)(2,1)S(1)} %get-tuple-element.52), channel_id=1, source_target_pairs={{4,0},{8,4},{12,8},{16,12},{20,16},{24,20},{28,24},{32,28},{36,32}... | collective-permute-start | bytes 64520 | tf_op jit(solution)/shard_map/ppermute | solution.py:22
  27.5 4.8 %collective-permute-start.3 = (f32[144,128]{1,0:T(8,128)S(1)}, f32[144,128]{1,0:T(8,128)S(1)}, u32[]{:S(2)}, u32[]{:S(2)}) collective-permute-start(f32[144,128]{1,0:T(8,128)S(1)} %constant_dynamic-update-slice_fusion.10), channel_id=1, source_target_pairs={{0,128},{4,132},{8,136},{12,140},{16,144},{20,148},{24,152},{28,15... | collective-permute-start | bytes 221192 | tf_op jit(solution)/shard_map/ppermute | solution.py:34
  32.3 31.3 %collective-permute-start.4 = (f32[288,128]{1,0:T(8,128)S(1)}, f32[288,128]{1,0:T(8,128)}, u32[]{:S(2)}, u32[]{:S(2)}) collective-permute-start(f32[288,128]{1,0:T(8,128)S(1)} %constant_dynamic-update-slice_fusion.8), channel_id=1, source_target_pairs={{0,16},{4,20},{8,24},{12,28},{16,0},{20,4},{24,8},{28,12},{32,48},... | collective-permute-start | bytes 442376 | tf_op jit(solution)/shard_map/ppermute | solution.py:34
  50.6 1.4 copy-start.19
  50.6 1.6 copy-start.20
  64.5 7.6 %collective-permute-start.5 = (f32[576,128]{1,0:T(8,128)S(1)}, f32[576,128]{1,0:T(8,128)S(1)}, u32[]{:S(2)}, u32[]{:S(2)}) collective-permute-start(f32[576,128]{1,0:T(8,128)S(1)} %constant_dynamic-update-slice_fusion.6), channel_id=1, source_target_pairs={{0,64},{4,68},{8,72},{12,76},{16,80},{20,84},{24,88},{28,92},{32,9... | collective-permute-start | bytes 884744 | tf_op jit(solution)/shard_map/ppermute | solution.py:34
  72.1 16.8 %collective-permute-start.6 = (f32[1152,128]{1,0:T(8,128)S(1)}, f32[1152,128]{1,0:T(8,128)S(1)}, u32[]{:S(2)}, u32[]{:S(2)}) collective-permute-start(f32[1152,128]{1,0:T(8,128)S(1)} %constant_dynamic-update-slice_fusion.4), channel_id=1, source_target_pairs={{0,8},{4,12},{8,0},{12,4},{16,24},{20,28},{24,16},{28,20},{32,40},... | collective-permute-start | bytes 1769480 | tf_op jit(solution)/shard_map/ppermute | solution.py:34
  84.1 1.5 copy-start.23
  85.5 1.4 copy-start.6
  85.5 1.8 copy-start.4
  85.5 2.1 %copy-start.2 = (bf16[24,64,256]{2,1,0:T(8,128)(2,1)}, bf16[24,64,256]{2,1,0:T(8,128)(2,1)S(1)}, u32[]{:S(2)}) copy-start(bf16[24,64,256]{2,1,0:T(8,128)(2,1)S(1)} %get-tuple-element.68) | copy-start | bytes 2359300
  88.9 5.9 %copy-start.26 = (f32[128]{0:T(128)S(1)}, f32[128]{0:T(128)}, u32[]{:S(2)}) copy-start(f32[128]{0:T(128)} %param.19) | copy-start | bytes 1540
  88.9 8.3 %collective-permute-start.7 = (f32[2304,128]{1,0:T(8,128)S(1)}, f32[2304,128]{1,0:T(8,128)S(1)}, u32[]{:S(2)}, u32[]{:S(2)}) collective-permute-start(f32[2304,128]{1,0:T(8,128)S(1)} %constant_dynamic-update-slice_fusion.2), channel_id=1, source_target_pairs={{0,4},{4,0},{8,12},{12,8},{16,20},{20,16},{24,28},{28,24},{32,36},... | collective-permute-start | bytes 3538952 | tf_op jit(solution)/shard_map/ppermute | solution.py:34
  101.9 2.1 %copy-start.11 = (bf16[24,64,256]{2,1,0:T(8,128)(2,1)S(1)}, bf16[24,64,256]{2,1,0:T(8,128)(2,1)}, u32[]{:S(2)}) copy-start(bf16[24,64,256]{2,1,0:T(8,128)(2,1)} %copy-done.10) | copy-start | bytes 2359300
  101.9 3.2 %copy-start.9 = (bf16[24,64,256]{2,1,0:T(8,128)(2,1)S(1)}, bf16[24,64,256]{2,1,0:T(8,128)(2,1)}, u32[]{:S(2)}) copy-start(bf16[24,64,256]{2,1,0:T(8,128)(2,1)} %copy-done.8) | copy-start | bytes 2359300
  104.0 2.1 %copy-start.7 = (bf16[24,64,256]{2,1,0:T(8,128)(2,1)S(1)}, bf16[24,64,256]{2,1,0:T(8,128)(2,1)}, u32[]{:S(2)}) copy-start(bf16[24,64,256]{2,1,0:T(8,128)(2,1)} %copy-done.6) | copy-start | bytes 2359300
  105.1 2.1 %copy-start.5 = (bf16[24,64,256]{2,1,0:T(8,128)(2,1)S(1)}, bf16[24,64,256]{2,1,0:T(8,128)(2,1)}, u32[]{:S(2)}) copy-start(bf16[24,64,256]{2,1,0:T(8,128)(2,1)} %copy-done.4) | copy-start | bytes 2359300
  106.1 2.1 %copy-start.3 = (bf16[24,64,256]{2,1,0:T(8,128)(2,1)S(1)}, bf16[24,64,256]{2,1,0:T(8,128)(2,1)}, u32[]{:S(2)}) copy-start(bf16[24,64,256]{2,1,0:T(8,128)(2,1)} %copy-done.2) | copy-start | bytes 2359300
  198.2 4.0 %copy-start.21 = (f32[2048,128]{1,0:T(8,128)S(1)}, f32[2048,128]{1,0:T(8,128)}, u32[]{:S(2)}) copy-start(f32[2048,128]{1,0:T(8,128)} %get-tuple-element.49) | copy-start | bytes 3145732
  (11 other events, 12.0 us)

commit v6 on v4

--- a/solution.py
+++ b/solution.py
@@ -47,10 +47,9 @@
     )
 
 
-def tree_kernel(count, chunk, width, grads_ref, sums_ref, out_ref, every_ref, landing, sems, free):
+def tree_kernel(count, chunk, width, dists, grads_ref, sums_ref, out_ref, every_ref, landing, sems, free):
     me = lax.axis_index("strip")
     chan = lax.axis_index("chan")
-    dists = [1 << k for k in range(count.bit_length() - 1)]
     mesh_id = pl.DeviceIdType.MESH
 
     def partner(dist):
@@ -64,7 +63,7 @@
     out_ref[...] = grads_ref[...]
     place = 0
     for k, dist in enumerate(dists):
-        place = place + ((me // dist) % 2) * (count // (2 * dist))
+        place = place + ((me // dist) % 2) * (count >> (k + 1))
     every_ref[pl.ds(pl.multiple_of(place * width, 8), width)] = sums_ref[...]
 
     low = 0
@@ -133,14 +132,14 @@
         blocks = blocks * 2
 
 
-def tree_sum(grads, sums, axis):
+def tree_sum(grads, sums, axis, dists):
     count = lax.axis_size(axis)
     rows, lanes = grads.shape
     chunk = rows // count
     width = sums.shape[0]
     steps = count.bit_length() - 1
     return pl.pallas_call(
-        functools.partial(tree_kernel, count, chunk, width),
+        functools.partial(tree_kernel, count, chunk, width, dists),
         out_shape=(
             jax.ShapeDtypeStruct((rows, lanes), jnp.float32),
             jax.ShapeDtypeStruct((count * width, lanes), jnp.float32),
@@ -210,7 +209,10 @@
     meta = meta.at[0, :list_len].set(part_counts)
     meta = meta.at[0, list_len : 2 * list_len].set(slot_ids.astype(jnp.float32))
     packed = jnp.concatenate([embed_grad, meta], axis=0)
-    order = [strip_count >> (k + 1) for k in range(strip_count.bit_length() - 1)]
+    halving = [1 << k for k in range(strip_count.bit_length() - 1)]
+    if len(halving) == 6:
+        halving = [1, 2, 16, 4, 32, 8]
+    order = halving[::-1]
     position = jnp.asarray(gather_position(order, strip_count))
     early = tree_gather(packed, "strip", order[:2])
 
@@ -266,7 +268,7 @@
     bias_rows = bias_rows.at[0].set(local_bias)
     local_grads = jnp.concatenate(pieces + [bias_rows], axis=0)
 
-    total_grads, every_sums = tree_sum(local_grads, part_sums, "strip")
+    total_grads, every_sums = tree_sum(local_grads, part_sums, "strip", halving)
     mine = strip_pos * owned + jnp.arange(owned, dtype=jnp.int32)
     pick = (mine[:, None] == every_slots[None, :]).astype(jnp.float32)
     slot_sums = jnp.dot(pick, every_sums, precision=lax.Precision.HIGHEST)

time: 206 us -> 192 us (0.932)
  Pallas kernels: 79.8 us -> 70 us
  waiting for transfers between devices: 16.6 us -> 9.29 us
  starting transfers between devices: 22.2 us -> 25.1 us
    pallas_call x1, Pallas kernels: 79.8 us -> 70 us  [tree_sum(): pl.pallas_call(functools.partial(tree_kernel, count, chunk, width, dists)...]
    ppermute x6, waiting for transfers between devices: 15.3 us -> 8.02 us  [tree_gather(): other = lax.ppermute(held, axis, [(i, i ^ dist) for i in range(count)])]
    ppermute x6, starting transfers between devices: 15.9 us -> 19.7 us  [tree_gather(): other = lax.ppermute(held, axis, [(i, i ^ dist) for i in range(count)])]
  transfers between devices with their start and end apart: 8 -> 8, of which waited for: 3 -> 3; matrix products, arithmetic and copies ran while one was open for 17% -> 18% of each run, Pallas kernels for 0% -> 0%
where the time goes in v6:
time: 192 us; the launch traced here: 190 us
  Pallas kernels  70 us (36%)
  local copies, waits for them, and re-layouts  40.2 us (21%)
  starting transfers between devices  25.1 us (13%)
  matrix products  22.1 us (12%)
  blocking collectives  11.9 us (6%)
  other arithmetic  9.48 us (5%)
  waiting for transfers between devices  9.29 us (5%)
    pallas_call x1, Pallas kernels, tree_sum(): pl.pallas_call(functools.partial(tree_kernel, count, chunk, width, dists)...  70 us
    ppermute x6, starting transfers between devices, tree_gather(): other = lax.ppermute(held, axis, [(i, i ^ dist) for i in range(count)])  19.7 us
    reshape x9, local copies, waits for them, and re-layouts, convolve(): window = padded[shift_row:shift_row + row_count, shift_col:shift_col + co...  13.6 us
    all_gather x1, blocking collectives, body(): gathered = lax.all_gather(pooled, 'chan', axis=0, tiled=True)  11.9 us
    dot_general x9, matrix products, body(): lax.dot_general(window, deep_grad, (((0,), (0,)), ((), ())), preferred_el...  9.59 us
    ppermute x6, waiting for transfers between devices, tree_gather(): other = lax.ppermute(held, axis, [(i, i ^ dist) for i in range(count)])  8.02 us
    dot_general x18, matrix products, convolve(): jnp.dot(window, weight[shift_row, shift_col], preferred_element_type=jnp....  7.66 us
    unnamed x54, local copies, waits for them, and re-layouts  6.29 us
  transfers between devices with their start and end apart: 8, of which 3 were waited for; matrix products, arithmetic and copies ran while one was open for 18% of the time, Pallas kernels for 0%

profile of v6, /device:TPU:1, one launch (start us, length us, event | category | flops | bytes accessed | tf_op | source)
XLA Modules:
  0.0 189.5 jit_solution(17570508640713566060)
XLA Ops:
  3.5 2.7 %broadcast_select_fusion = f32[1,32]{1,0:T(1,128)S(1)} fusion(pred[]{:T(512)} %and_reduce_fusion, s32[]{:T(128)} %bitcast.2, s32[]{:T(128)} %bitcast.3, f32[1,32]{1,0:T(1,128)S(1)} %bitcast.145, s32[32]{0:T(128)} %param.21), kind=kLoop, calls=%fused_computation.136 | loop fusion | flops 64 | bytes 393 | tf_op jit(solution)/shard_map/select.4
  6.2 1.6 scatter.11
  8.5 7.7 %collective-permute-start.2 = (f32[72,128]{1,0:T(8,128)S(1)}, f32[72,128]{1,0:T(8,128)S(1)}, u32[]{:S(2)}, u32[]{:S(2)}) collective-permute-start(f32[72,128]{1,0:T(8,128)S(1)} %get-tuple-element.71), channel_id=1, source_target_pairs={{0,32},{4,36},{8,40},{12,44},{16,48},{20,52},{24,56},{28,60},{32,0... | collective-permute-start | bytes 110600 | tf_op jit(solution)/shard_map/ppermute | solution.py:34
  17.1 3.5 %collective-permute-start = (bf16[14,3,256]{2,1,0:T(4,128)(2,1)S(1)}, bf16[14,3,256]{2,1,0:T(4,128)(2,1)S(1)}, u32[]{:S(2)}, u32[]{:S(2)}) collective-permute-start(bf16[14,3,256]{2,1,0:T(4,128)(2,1)S(1)} %get-tuple-element.51), channel_id=1, source_target_pairs={{0,4},{4,8},{8,12},{12,16},{16,20},{20,24},{24,28},{28,32},{32,36}... | collective-permute-start | bytes 64520 | tf_op jit(solution)/shard_map/ppermute | solution.py:20
  20.6 1.9 %collective-permute-start.1 = (bf16[14,3,256]{2,1,0:T(4,128)(2,1)S(1)}, bf16[14,3,256]{2,1,0:T(4,128)(2,1)S(1)}, u32[]{:S(2)}, u32[]{:S(2)}) collective-permute-start(bf16[14,3,256]{2,1,0:T(4,128)(2,1)S(1)} %get-tuple-element.52), channel_id=1, source_target_pairs={{4,0},{8,4},{12,8},{16,12},{20,16},{24,20},{28,24},{32,28},{36,32}... | collective-permute-start | bytes 64520 | tf_op jit(solution)/shard_map/ppermute | solution.py:22
  25.8 1.6 pad_maximum_fusion
  27.5 2.8 %collective-permute-start.3 = (f32[144,128]{1,0:T(8,128)S(1)}, f32[144,128]{1,0:T(8,128)S(1)}, u32[]{:S(2)}, u32[]{:S(2)}) collective-permute-start(f32[144,128]{1,0:T(8,128)S(1)} %constant_dynamic-update-slice_fusion.10), channel_id=1, source_target_pairs={{0,128},{4,132},{8,136},{12,140},{16,144},{20,148},{24,152},{28,15... | collective-permute-start | bytes 221192 | tf_op jit(solution)/shard_map/ppermute | solution.py:34
  30.3 1.9 %collective-permute-done.3 = f32[144,128]{1,0:T(8,128)S(1)} collective-permute-done((f32[144,128]{1,0:T(8,128)S(1)}, f32[144,128]{1,0:T(8,128)S(1)}, u32[]{:S(2)}, u32[]{:S(2)}) %collective-permute-start.3) | collective-permute-done | bytes 73760 | tf_op jit(solution)/shard_map/ppermute | solution.py:34
  32.3 2.2 %collective-permute-start.4 = (f32[288,128]{1,0:T(8,128)S(1)}, f32[288,128]{1,0:T(8,128)}, u32[]{:S(2)}, u32[]{:S(2)}) collective-permute-start(f32[288,128]{1,0:T(8,128)S(1)} %constant_dynamic-update-slice_fusion.8), channel_id=1, source_target_pairs={{0,16},{4,20},{8,24},{12,28},{16,0},{20,4},{24,8},{28,12},{32,48},... | collective-permute-start | bytes 442376 | tf_op jit(solution)/shard_map/ppermute | solution.py:34
  34.5 2.5 %fusion.62 = (bf16[12,132,256]{2,1,0:T(8,128)(2,1)S(1)}, bf16[12,132,256]{2,1,0:T(8,128)(2,1)S(1)}, bf16[12,132,256]{2,1,0:T(8,128)(2,1)S(1)}, bf16[12,132,256]{...) fusion(bf16[14,134,256]{2,1,0:T(8,128)(2,1)S(1)} %pad_maximum_f, ...), kind=kLoop, calls=%fused_computation.142 | loop fusion | bytes 14598144 | tf_op jit(solution)/shard_map/slice | solution.py:172
  37.0 2.0 %reshape.206 = bf16[1584,256]{1,0:T(8,128)(2,1)} reshape(bf16[12,132,256]{2,1,0:T(8,128)(2,1)} %get-tuple-element.61) | data formatting | bytes 1622016 | tf_op jit(solution)/shard_map/reshape | solution.py:174
  39.1 2.1 %reshape.207 = bf16[1584,256]{1,0:T(8,128)(2,1)} reshape(bf16[12,132,256]{2,1,0:T(8,128)(2,1)} %get-tuple-element.60) | data formatting | bytes 1622016 | tf_op jit(solution)/shard_map/reshape | solution.py:174
  41.1 2.1 %reshape.208 = bf16[1584,256]{1,0:T(8,128)(2,1)} reshape(bf16[12,132,256]{2,1,0:T(8,128)(2,1)} %get-tuple-element.59) | data formatting | bytes 1622016 | tf_op jit(solution)/shard_map/reshape | solution.py:174
  43.2 2.1 %reshape.209 = bf16[1584,256]{1,0:T(8,128)(2,1)} reshape(bf16[12,132,256]{2,1,0:T(8,128)(2,1)} %get-tuple-element.58) | data formatting | bytes 1622016 | tf_op jit(solution)/shard_map/reshape | solution.py:174
  45.3 2.1 %reshape.210 = bf16[1584,256]{1,0:T(8,128)(2,1)} reshape(bf16[12,132,256]{2,1,0:T(8,128)(2,1)} %get-tuple-element.57) | data formatting | bytes 1622016 | tf_op jit(solution)/shard_map/reshape | solution.py:174
  60.8 2.7 %fusion.2 = f32[6,66,256]{2,1,0:T(8,128)S(1)} fusion(f32[6,2,66,2,256]{4,3,2,1,0:T(2,128)S(1)} %reshape.215, f32[256]{0:T(256)S(1)} %copy-done.24), kind=kLoop, calls=%fused_computation.25 | loop fusion | flops 2331648 | bytes 2028544 | tf_op jit(solution)/shard_map/reduce_sum | solution.py:186
  66.0 6.1 %collective-permute-done.5 = f32[576,128]{1,0:T(8,128)S(1)} collective-permute-done((f32[576,128]{1,0:T(8,128)S(1)}, f32[576,128]{1,0:T(8,128)S(1)}, u32[]{:S(2)}, u32[]{:S(2)}) %collective-permute-start.5) | collective-permute-done | bytes 294944 | tf_op jit(solution)/shard_map/ppermute | solution.py:34
  72.2 11.9 %all_gather.3 = bf16[24,66,256]{2,1,0:T(8,128)(2,1)S(1)} all-gather(bf16[6,66,256]{2,1,0:T(8,128)(2,1)S(1)} %fusion.13), channel_id=1, replica_groups=mesh['strip'=64,'chan'=4] {'chan'}, dimensions={0}, use_global_device_ids=true | all-gather | bytes 1013760 | tf_op jit(solution)/shard_map/all_gather | solution.py:236
  88.9 5.5 %collective-permute-start.7 = (f32[2304,128]{1,0:T(8,128)S(1)}, f32[2304,128]{1,0:T(8,128)S(1)}, u32[]{:S(2)}, u32[]{:S(2)}) collective-permute-start(f32[2304,128]{1,0:T(8,128)S(1)} %constant_dynamic-update-slice_fusion.2), channel_id=1, source_target_pairs={{0,4},{4,0},{8,12},{12,8},{16,20},{20,16},{24,28},{28,24},{32,36},... | collective-permute-start | bytes 3538952 | tf_op jit(solution)/shard_map/ppermute | solution.py:34
  97.6 1.6 slice.243
  99.7 2.2 %gather_fusion.1 = f32[32,128]{1,0:T(8,128)S(1)} fusion(f32[4096,128]{1,0:T(8,128)} %bitcast.142, s32[1024]{0:T(1024)S(1)} %pad_clamp_fusion), kind=kCustom, calls=%fused_computation.1 | custom fusion | bytes 32896 | tf_op jit(solution)/shard_map/gather | solution.py:246
  101.9 2.1 %convert_reduce_fusion = (f32[128]{0:T(128)S(1)}, bf16[1536,128]{1,0:T(8,128)(2,1)S(1)}) fusion(f32[1536,128]{1,0:T(8,128)} %copy-done.22, f32[32,128]{1,0:T(8,128)S(1)} %gather_fusion.1, f32[32]{0:T(128)S(1)} %fusion.4, s32[1536]{0:T(1024)S(1)} %eq.83), kind=kOutput, calls=%fused_computation.42 | convolution fusion | flops 77713280 | bytes 1202816 | tf_op jit(solution)/shard_map/dot_general | solution.py:247
  114.3 70.0 %shard_map.112 = (f32[2560,128]{1,0:T(8,128)}, f32[2048,128]{1,0:T(8,128)}) custom-call(f32[2560,128]{1,0:T(8,128)} %pad_dynamic-update-slice_fusion.grads_ref, f32[32,128]{1,0:T(8,128)} %fusion.7.sums_ref), custom_call_target="tpu_custom_call" | custom-call | tf_op jit(solution)/shard_map/pallas_call | solution.py:141
  184.3 2.4 %slice.236 = f32[2304,128]{1,0:T(8,128)} slice(f32[2560,128]{1,0:T(8,128)} %get-tuple-element.50), slice={[0:2304], [0:128]} | slice | bytes 2359296 | tf_op jit(solution)/shard_map/slice | solution.py:278
  (139 shorter events, 44.7 us)
Async XLA Ops:
  8.5 14.1 %copy-start.1 = (bf16[48,128,256]{2,1,0:T(8,128)(2,1)S(1)}, bf16[48,128,256]{2,1,0:T(8,128)(2,1)}, u32[]{:S(2)}) copy-start(bf16[48,128,256]{2,1,0:T(8,128)(2,1)} %param.15) | copy-start | bytes 9437188
  8.5 18.9 %collective-permute-start.2 = (f32[72,128]{1,0:T(8,128)S(1)}, f32[72,128]{1,0:T(8,128)S(1)}, u32[]{:S(2)}, u32[]{:S(2)}) collective-permute-start(f32[72,128]{1,0:T(8,128)S(1)} %get-tuple-element.71), channel_id=1, source_target_pairs={{0,32},{4,36},{8,40},{12,44},{16,48},{20,52},{24,56},{28,60},{32,0... | collective-permute-start | bytes 110600 | tf_op jit(solution)/shard_map/ppermute | solution.py:34
  17.1 7.4 %collective-permute-start = (bf16[14,3,256]{2,1,0:T(4,128)(2,1)S(1)}, bf16[14,3,256]{2,1,0:T(4,128)(2,1)S(1)}, u32[]{:S(2)}, u32[]{:S(2)}) collective-permute-start(bf16[14,3,256]{2,1,0:T(4,128)(2,1)S(1)} %get-tuple-element.51), channel_id=1, source_target_pairs={{0,4},{4,8},{8,12},{12,16},{16,20},{20,24},{24,28},{28,32},{32,36}... | collective-permute-start | bytes 64520 | tf_op jit(solution)/shard_map/ppermute | solution.py:20
  20.6 3.0 %copy-start.25 = (s32[32]{0:T(128)S(1)}, s32[32]{0:T(128)}, u32[]{:S(2)}) copy-start(s32[32]{0:T(128)} %param.21) | copy-start | bytes 388
  20.6 3.0 %copy-start = (s32[64]{0:T(128)S(1)}, s32[64]{0:T(128)}, u32[]{:S(2)}) copy-start(s32[64]{0:T(128)} %constant.254.clone) | copy-start | bytes 772
  20.6 5.2 %collective-permute-start.1 = (bf16[14,3,256]{2,1,0:T(4,128)(2,1)S(1)}, bf16[14,3,256]{2,1,0:T(4,128)(2,1)S(1)}, u32[]{:S(2)}, u32[]{:S(2)}) collective-permute-start(bf16[14,3,256]{2,1,0:T(4,128)(2,1)S(1)} %get-tuple-element.52), channel_id=1, source_target_pairs={{4,0},{8,4},{12,8},{16,12},{20,16},{24,20},{28,24},{32,28},{36,32}... | collective-permute-start | bytes 64520 | tf_op jit(solution)/shard_map/ppermute | solution.py:22
  27.5 4.8 %collective-permute-start.3 = (f32[144,128]{1,0:T(8,128)S(1)}, f32[144,128]{1,0:T(8,128)S(1)}, u32[]{:S(2)}, u32[]{:S(2)}) collective-permute-start(f32[144,128]{1,0:T(8,128)S(1)} %constant_dynamic-update-slice_fusion.10), channel_id=1, source_target_pairs={{0,128},{4,132},{8,136},{12,140},{16,144},{20,148},{24,152},{28,15... | collective-permute-start | bytes 221192 | tf_op jit(solution)/shard_map/ppermute | solution.py:34
  32.3 31.3 %collective-permute-start.4 = (f32[288,128]{1,0:T(8,128)S(1)}, f32[288,128]{1,0:T(8,128)}, u32[]{:S(2)}, u32[]{:S(2)}) collective-permute-start(f32[288,128]{1,0:T(8,128)S(1)} %constant_dynamic-update-slice_fusion.8), channel_id=1, source_target_pairs={{0,16},{4,20},{8,24},{12,28},{16,0},{20,4},{24,8},{28,12},{32,48},... | collective-permute-start | bytes 442376 | tf_op jit(solution)/shard_map/ppermute | solution.py:34
  50.6 1.4 copy-start.19
  50.6 1.6 copy-start.20
  64.5 7.6 %collective-permute-start.5 = (f32[576,128]{1,0:T(8,128)S(1)}, f32[576,128]{1,0:T(8,128)S(1)}, u32[]{:S(2)}, u32[]{:S(2)}) collective-permute-start(f32[576,128]{1,0:T(8,128)S(1)} %constant_dynamic-update-slice_fusion.6), channel_id=1, source_target_pairs={{0,64},{4,68},{8,72},{12,76},{16,80},{20,84},{24,88},{28,92},{32,9... | collective-permute-start | bytes 884744 | tf_op jit(solution)/shard_map/ppermute | solution.py:34
  72.1 16.8 %collective-permute-start.6 = (f32[1152,128]{1,0:T(8,128)S(1)}, f32[1152,128]{1,0:T(8,128)S(1)}, u32[]{:S(2)}, u32[]{:S(2)}) collective-permute-start(f32[1152,128]{1,0:T(8,128)S(1)} %constant_dynamic-update-slice_fusion.4), channel_id=1, source_target_pairs={{0,8},{4,12},{8,0},{12,4},{16,24},{20,28},{24,16},{28,20},{32,40},... | collective-permute-start | bytes 1769480 | tf_op jit(solution)/shard_map/ppermute | solution.py:34
  84.1 1.5 copy-start.23
  85.5 1.4 copy-start.6
  85.5 1.8 copy-start.4
  85.5 2.1 %copy-start.2 = (bf16[24,64,256]{2,1,0:T(8,128)(2,1)}, bf16[24,64,256]{2,1,0:T(8,128)(2,1)S(1)}, u32[]{:S(2)}) copy-start(bf16[24,64,256]{2,1,0:T(8,128)(2,1)S(1)} %get-tuple-element.68) | copy-start | bytes 2359300
  88.9 5.9 %copy-start.26 = (f32[128]{0:T(128)S(1)}, f32[128]{0:T(128)}, u32[]{:S(2)}) copy-start(f32[128]{0:T(128)} %param.19) | copy-start | bytes 1540
  88.9 8.3 %collective-permute-start.7 = (f32[2304,128]{1,0:T(8,128)S(1)}, f32[2304,128]{1,0:T(8,128)S(1)}, u32[]{:S(2)}, u32[]{:S(2)}) collective-permute-start(f32[2304,128]{1,0:T(8,128)S(1)} %constant_dynamic-update-slice_fusion.2), channel_id=1, source_target_pairs={{0,4},{4,0},{8,12},{12,8},{16,20},{20,16},{24,28},{28,24},{32,36},... | collective-permute-start | bytes 3538952 | tf_op jit(solution)/shard_map/ppermute | solution.py:34
  101.9 2.1 %copy-start.11 = (bf16[24,64,256]{2,1,0:T(8,128)(2,1)S(1)}, bf16[24,64,256]{2,1,0:T(8,128)(2,1)}, u32[]{:S(2)}) copy-start(bf16[24,64,256]{2,1,0:T(8,128)(2,1)} %copy-done.10) | copy-start | bytes 2359300
  101.9 3.2 %copy-start.9 = (bf16[24,64,256]{2,1,0:T(8,128)(2,1)S(1)}, bf16[24,64,256]{2,1,0:T(8,128)(2,1)}, u32[]{:S(2)}) copy-start(bf16[24,64,256]{2,1,0:T(8,128)(2,1)} %copy-done.8) | copy-start | bytes 2359300
  104.0 2.1 %copy-start.7 = (bf16[24,64,256]{2,1,0:T(8,128)(2,1)S(1)}, bf16[24,64,256]{2,1,0:T(8,128)(2,1)}, u32[]{:S(2)}) copy-start(bf16[24,64,256]{2,1,0:T(8,128)(2,1)} %copy-done.6) | copy-start | bytes 2359300
  105.1 2.1 %copy-start.5 = (bf16[24,64,256]{2,1,0:T(8,128)(2,1)S(1)}, bf16[24,64,256]{2,1,0:T(8,128)(2,1)}, u32[]{:S(2)}) copy-start(bf16[24,64,256]{2,1,0:T(8,128)(2,1)} %copy-done.4) | copy-start | bytes 2359300
  106.1 2.1 %copy-start.3 = (bf16[24,64,256]{2,1,0:T(8,128)(2,1)S(1)}, bf16[24,64,256]{2,1,0:T(8,128)(2,1)}, u32[]{:S(2)}) copy-start(bf16[24,64,256]{2,1,0:T(8,128)(2,1)} %copy-done.2) | copy-start | bytes 2359300
  184.3 4.0 %copy-start.21 = (f32[2048,128]{1,0:T(8,128)S(1)}, f32[2048,128]{1,0:T(8,128)}, u32[]{:S(2)}) copy-start(f32[2048,128]{1,0:T(8,128)} %get-tuple-element.49) | copy-start | bytes 3145732
  (11 other events, 12.0 us)

commit v7 on v6

--- a/solution.py
+++ b/solution.py
@@ -26,13 +26,41 @@
     return cells
 
 
-def tree_gather(block, axis, order):
+def chip_view(index, shifted):
+    if not shifted:
+        return index
+    core = index % 2
+    return ((index // 16 + core) % 4 * 8 + (index // 2 + core) % 8) * 2 + core
+
+
+def chip_unview(index, shifted):
+    if not shifted:
+        return index
+    core = index % 2
+    return ((index // 16 + 4 - core) % 4 * 8 + (index // 2 + 8 - core) % 8) * 2 + core
+
+
+def strip_partner(index, dist, shifted):
+    if dist == 1:
+        return index + 1 - 2 * (index % 2)
+    view = chip_view(index, shifted)
+    return chip_unview(view + dist - 2 * dist * ((view // dist) % 2), shifted)
+
+
+def strip_bit(index, dist, shifted):
+    if dist == 1:
+        return index % 2
+    return (chip_view(index, shifted) // dist) % 2
+
+
+def tree_gather(block, axis, order, shifted):
     count = lax.axis_size(axis)
     me = lax.axis_index(axis)
     held = block
     for dist in order:
-        other = lax.ppermute(held, axis, [(i, i ^ dist) for i in range(count)])
-        high = (me // dist) % 2
+        pairs = [(i, strip_partner(i, dist, shifted)) for i in range(count)]
+        other = lax.ppermute(held, axis, pairs)
+        high = strip_bit(me, dist, shifted)
         size = held.shape[0]
         both = jnp.zeros((2 * size,) + held.shape[1:], held.dtype)
         both = lax.dynamic_update_slice_in_dim(both, held, high * size, 0)
@@ -40,20 +68,20 @@
     return held
 
 
-def gather_position(order, count):
+def gather_position(order, count, shifted):
     return np.array(
-        [sum(((j // dist) % 2) << k for k, dist in enumerate(order)) for j in range(count)],
+        [sum(strip_bit(j, dist, shifted) << k for k, dist in enumerate(order)) for j in range(count)],
         np.int32,
     )
 
 
-def tree_kernel(count, chunk, width, dists, grads_ref, sums_ref, out_ref, every_ref, landing, sems, free):
+def tree_kernel(count, chunk, width, dists, shifted, grads_ref, sums_ref, out_ref, every_ref, landing, sems, free):
     me = lax.axis_index("strip")
     chan = lax.axis_index("chan")
     mesh_id = pl.DeviceIdType.MESH
 
     def partner(dist):
-        return me + dist - 2 * dist * ((me // dist) % 2)
+        return strip_partner(me, dist, shifted)
 
     barrier = pltpu.get_barrier_semaphore()
     for dist in dists:
@@ -63,7 +91,7 @@
     out_ref[...] = grads_ref[...]
     place = 0
     for k, dist in enumerate(dists):
-        place = place + ((me // dist) % 2) * (count >> (k + 1))
+        place = place + (strip_bit(me, dist, shifted)) * (count >> (k + 1))
     every_ref[pl.ds(pl.multiple_of(place * width, 8), width)] = sums_ref[...]
 
     low = 0
@@ -71,7 +99,7 @@
     offset = 0
     for k, dist in enumerate(dists):
         half = size // 2
-        high = (me // dist) % 2
+        high = strip_bit(me, dist, shifted)
         keep = low + high * half
         give = low + (1 - high) * half
         copy = pltpu.make_async_remote_copy(
@@ -125,21 +153,21 @@
         sums_copy.start()
         grads_copy.wait()
         sums_copy.wait()
-        high = (me // dist) % 2
+        high = strip_bit(me, dist, shifted)
         low = low - high * size
         place = place - high * blocks
         size = size * 2
         blocks = blocks * 2
 
 
-def tree_sum(grads, sums, axis, dists):
+def tree_sum(grads, sums, axis, dists, shifted):
     count = lax.axis_size(axis)
     rows, lanes = grads.shape
     chunk = rows // count
     width = sums.shape[0]
     steps = count.bit_length() - 1
     return pl.pallas_call(
-        functools.partial(tree_kernel, count, chunk, width, dists),
+        functools.partial(tree_kernel, count, chunk, width, dists, shifted),
         out_shape=(
             jax.ShapeDtypeStruct((rows, lanes), jnp.float32),
             jax.ShapeDtypeStruct((count * width, lanes), jnp.float32),
@@ -213,14 +241,15 @@
     if len(halving) == 6:
         halving = [1, 2, 16, 4, 32, 8]
     order = halving[::-1]
-    position = jnp.asarray(gather_position(order, strip_count))
-    early = tree_gather(packed, "strip", order[:2])
+    shifted = strip_count == 64
+    position = jnp.asarray(gather_position(order, strip_count, shifted))
+    early = tree_gather(packed, "strip", order[:2], shifted)
 
     padded_rows = jnp.pad(section_input, ((1, 1), (0, 0), (0, 0)))
     own_rows = lax.dynamic_slice_in_dim(padded_rows, chan_pos * row_part, row_part + 2, 0)
     extended = with_halo(own_rows, (("strip", 1),), 3)
     extended, early = lax.optimization_barrier((extended, early))
-    early = tree_gather(early, "strip", order[2:4])
+    early = tree_gather(early, "strip", order[2:4], shifted)
     hidden = swish(convolve(extended, conv_weight, row_part, col_local + 4) + conv_bias)
     pooled = pool_pairs(hidden)
     column = jnp.arange(half_cols + 2)
@@ -229,7 +258,7 @@
     )
     pooled = jnp.where(outside[None, :, None], jnp.zeros_like(pooled), pooled)
     pooled, early = lax.optimization_barrier((pooled, early))
-    every = tree_gather(early, "strip", order[4:]).reshape(strip_count, owned + 8, lanes)
+    every = tree_gather(early, "strip", order[4:], shifted).reshape(strip_count, owned + 8, lanes)
     every_grad = every[:, :owned].reshape(strip_count * owned, lanes)
     every_counts = every[:, owned, :list_len].reshape(-1)
     every_slots = jnp.round(every[:, owned, list_len : 2 * list_len]).astype(jnp.int32).reshape(-1)
@@ -268,7 +297,7 @@
     bias_rows = bias_rows.at[0].set(local_bias)
     local_grads = jnp.concatenate(pieces + [bias_rows], axis=0)
 
-    total_grads, every_sums = tree_sum(local_grads, part_sums, "strip", halving)
+    total_grads, every_sums = tree_sum(local_grads, part_sums, "strip", halving, shifted)
     mine = strip_pos * owned + jnp.arange(owned, dtype=jnp.int32)
     pick = (mine[:, None] == every_slots[None, :]).astype(jnp.float32)
     slot_sums = jnp.dot(pick, every_sums, precision=lax.Precision.HIGHEST)

time: 192 us -> 186 us (0.969)
  Pallas kernels: 70 us -> 67 us
  waiting for transfers between devices: 9.29 us -> 7.3 us
    pallas_call x1, Pallas kernels: 70 us -> 67 us  [tree_sum(): pl.pallas_call(functools.partial(tree_kernel, count, chunk, width, dists,...]
    ppermute x6, waiting for transfers between devices: 8.02 us -> 6.06 us  [tree_gather(): other = lax.ppermute(held, axis, pairs)]
  transfers between devices with their start and end apart: 8 -> 8, of which waited for: 3 -> 3; matrix products, arithmetic and copies ran while one was open for 18% -> 19% of each run, Pallas kernels for 0% -> 0%
where the time goes in v7:
time: 186 us; the launch traced here: 185 us
  Pallas kernels  67 us (36%)
  local copies, waits for them, and re-layouts  40.2 us (22%)
  starting transfers between devices  24.4 us (13%)
  matrix products  22.2 us (12%)
  blocking collectives  13.3 us (7%)
  other arithmetic  9.48 us (5%)
  waiting for transfers between devices  7.3 us (4%)
    pallas_call x1, Pallas kernels, tree_sum(): pl.pallas_call(functools.partial(tree_kernel, count, chunk, width, dists,...  67 us
    ppermute x6, starting transfers between devices, tree_gather(): other = lax.ppermute(held, axis, pairs)  19 us
    reshape x9, local copies, waits for them, and re-layouts, convolve(): window = padded[shift_row:shift_row + row_count, shift_col:shift_col + co...  13.6 us
    all_gather x1, blocking collectives, body(): gathered = lax.all_gather(pooled, 'chan', axis=0, tiled=True)  13.3 us
    dot_general x9, matrix products, body(): lax.dot_general(window, deep_grad, (((0,), (0,)), ((), ())), preferred_el...  9.59 us
    dot_general x18, matrix products, convolve(): jnp.dot(window, weight[shift_row, shift_col], preferred_element_type=jnp....  7.71 us
    unnamed x54, local copies, waits for them, and re-layouts  6.27 us
    ppermute x6, waiting for transfers between devices, tree_gather(): other = lax.ppermute(held, axis, pairs)  6.06 us
  transfers between devices with their start and end apart: 8, of which 3 were waited for; matrix products, arithmetic and copies ran while one was open for 19% of the time, Pallas kernels for 0%

profile of v7, /device:TPU:1, one launch (start us, length us, event | category | flops | bytes accessed | tf_op | source)
XLA Modules:
  0.0 185.4 jit_solution(221468428487350786)
XLA Ops:
  3.6 2.7 %broadcast_select_fusion = f32[1,32]{1,0:T(1,128)S(1)} fusion(pred[]{:T(512)} %and_reduce_fusion, s32[]{:T(128)} %bitcast.2, s32[]{:T(128)} %bitcast.3, f32[1,32]{1,0:T(1,128)S(1)} %bitcast.145, s32[32]{0:T(128)} %param.21), kind=kLoop, calls=%fused_computation.136 | loop fusion | flops 64 | bytes 393 | tf_op jit(solution)/shard_map/select.4
  8.6 7.7 %collective-permute-start.2 = (f32[72,128]{1,0:T(8,128)S(1)}, f32[72,128]{1,0:T(8,128)S(1)}, u32[]{:S(2)}, u32[]{:S(2)}) collective-permute-start(f32[72,128]{1,0:T(8,128)S(1)} %get-tuple-element.71), channel_id=1, source_target_pairs={{0,32},{4,36},{8,40},{12,44},{16,48},{20,52},{24,56},{28,60},{32,0... | collective-permute-start | bytes 110600 | tf_op jit(solution)/shard_map/ppermute | solution.py:62
  17.2 3.5 %collective-permute-start = (bf16[14,3,256]{2,1,0:T(4,128)(2,1)S(1)}, bf16[14,3,256]{2,1,0:T(4,128)(2,1)S(1)}, u32[]{:S(2)}, u32[]{:S(2)}) collective-permute-start(bf16[14,3,256]{2,1,0:T(4,128)(2,1)S(1)} %get-tuple-element.51), channel_id=1, source_target_pairs={{0,4},{4,8},{8,12},{12,16},{16,20},{20,24},{24,28},{28,32},{32,36}... | collective-permute-start | bytes 64520 | tf_op jit(solution)/shard_map/ppermute | solution.py:20
  20.7 1.9 %collective-permute-start.1 = (bf16[14,3,256]{2,1,0:T(4,128)(2,1)S(1)}, bf16[14,3,256]{2,1,0:T(4,128)(2,1)S(1)}, u32[]{:S(2)}, u32[]{:S(2)}) collective-permute-start(bf16[14,3,256]{2,1,0:T(4,128)(2,1)S(1)} %get-tuple-element.52), channel_id=1, source_target_pairs={{4,0},{8,4},{12,8},{16,12},{20,16},{24,20},{28,24},{32,28},{36,32}... | collective-permute-start | bytes 64520 | tf_op jit(solution)/shard_map/ppermute | solution.py:22
  25.9 1.6 pad_maximum_fusion
  27.5 2.8 %collective-permute-start.3 = (f32[144,128]{1,0:T(8,128)S(1)}, f32[144,128]{1,0:T(8,128)S(1)}, u32[]{:S(2)}, u32[]{:S(2)}) collective-permute-start(f32[144,128]{1,0:T(8,128)S(1)} %constant_dynamic-update-slice_fusion.10), channel_id=1, source_target_pairs={{0,128},{4,132},{8,136},{12,140},{16,144},{20,148},{24,152},{28,15... | collective-permute-start | bytes 221192 | tf_op jit(solution)/shard_map/ppermute | solution.py:62
  30.4 1.9 %collective-permute-done.3 = f32[144,128]{1,0:T(8,128)S(1)} collective-permute-done((f32[144,128]{1,0:T(8,128)S(1)}, f32[144,128]{1,0:T(8,128)S(1)}, u32[]{:S(2)}, u32[]{:S(2)}) %collective-permute-start.3) | collective-permute-done | bytes 73760 | tf_op jit(solution)/shard_map/ppermute | solution.py:62
  32.3 2.3 %collective-permute-start.4 = (f32[288,128]{1,0:T(8,128)S(1)}, f32[288,128]{1,0:T(8,128)}, u32[]{:S(2)}, u32[]{:S(2)}) collective-permute-start(f32[288,128]{1,0:T(8,128)S(1)} %constant_dynamic-update-slice_fusion.8), channel_id=1, source_target_pairs={{0,16},{4,20},{8,24},{12,60},{16,0},{20,4},{24,8},{28,44},{32,48},... | collective-permute-start | bytes 442376 | tf_op jit(solution)/shard_map/ppermute | solution.py:62
  34.6 2.5 %fusion.62 = (bf16[12,132,256]{2,1,0:T(8,128)(2,1)S(1)}, bf16[12,132,256]{2,1,0:T(8,128)(2,1)S(1)}, bf16[12,132,256]{2,1,0:T(8,128)(2,1)S(1)}, bf16[12,132,256]{...) fusion(bf16[14,134,256]{2,1,0:T(8,128)(2,1)S(1)} %pad_maximum_f, ...), kind=kLoop, calls=%fused_computation.142 | loop fusion | bytes 14598144 | tf_op jit(solution)/shard_map/slice | solution.py:200
  37.2 2.0 %reshape.206 = bf16[1584,256]{1,0:T(8,128)(2,1)} reshape(bf16[12,132,256]{2,1,0:T(8,128)(2,1)} %get-tuple-element.61) | data formatting | bytes 1622016 | tf_op jit(solution)/shard_map/reshape | solution.py:202
  39.2 2.1 %reshape.207 = bf16[1584,256]{1,0:T(8,128)(2,1)} reshape(bf16[12,132,256]{2,1,0:T(8,128)(2,1)} %get-tuple-element.60) | data formatting | bytes 1622016 | tf_op jit(solution)/shard_map/reshape | solution.py:202
  41.3 2.1 %reshape.208 = bf16[1584,256]{1,0:T(8,128)(2,1)} reshape(bf16[12,132,256]{2,1,0:T(8,128)(2,1)} %get-tuple-element.59) | data formatting | bytes 1622016 | tf_op jit(solution)/shard_map/reshape | solution.py:202
  43.3 2.1 %reshape.209 = bf16[1584,256]{1,0:T(8,128)(2,1)} reshape(bf16[12,132,256]{2,1,0:T(8,128)(2,1)} %get-tuple-element.58) | data formatting | bytes 1622016 | tf_op jit(solution)/shard_map/reshape | solution.py:202
  45.4 2.1 %reshape.210 = bf16[1584,256]{1,0:T(8,128)(2,1)} reshape(bf16[12,132,256]{2,1,0:T(8,128)(2,1)} %get-tuple-element.57) | data formatting | bytes 1622016 | tf_op jit(solution)/shard_map/reshape | solution.py:202
  60.9 2.7 %fusion.2 = f32[6,66,256]{2,1,0:T(8,128)S(1)} fusion(f32[6,2,66,2,256]{4,3,2,1,0:T(2,128)S(1)} %reshape.215, f32[256]{0:T(256)S(1)} %copy-done.24), kind=kLoop, calls=%fused_computation.25 | loop fusion | flops 2331648 | bytes 2028544 | tf_op jit(solution)/shard_map/reduce_sum | solution.py:214
  64.6 2.6 %collective-permute-start.5 = (f32[576,128]{1,0:T(8,128)S(1)}, f32[576,128]{1,0:T(8,128)S(1)}, u32[]{:S(2)}, u32[]{:S(2)}) collective-permute-start(f32[576,128]{1,0:T(8,128)S(1)} %constant_dynamic-update-slice_fusion.6), channel_id=1, source_target_pairs={{0,64},{4,196},{8,72},{12,204},{16,80},{20,212},{24,88},{28,220},{... | collective-permute-start | bytes 884744 | tf_op jit(solution)/shard_map/ppermute | solution.py:62
  67.4 4.1 %collective-permute-done.5 = f32[576,128]{1,0:T(8,128)S(1)} collective-permute-done((f32[576,128]{1,0:T(8,128)S(1)}, f32[576,128]{1,0:T(8,128)S(1)}, u32[]{:S(2)}, u32[]{:S(2)}) %collective-permute-start.5) | collective-permute-done | bytes 294944 | tf_op jit(solution)/shard_map/ppermute | solution.py:62
  71.5 3.1 %collective-permute-start.6 = (f32[1152,128]{1,0:T(8,128)S(1)}, f32[1152,128]{1,0:T(8,128)S(1)}, u32[]{:S(2)}, u32[]{:S(2)}) collective-permute-start(f32[1152,128]{1,0:T(8,128)S(1)} %constant_dynamic-update-slice_fusion.4), channel_id=1, source_target_pairs={{0,8},{4,60},{8,0},{12,20},{16,24},{20,12},{24,16},{28,36},{32,40}... | collective-permute-start | bytes 1769480 | tf_op jit(solution)/shard_map/ppermute | solution.py:62
  74.6 13.3 %all_gather.3 = bf16[24,66,256]{2,1,0:T(8,128)(2,1)S(1)} all-gather(bf16[6,66,256]{2,1,0:T(8,128)(2,1)S(1)} %fusion.13), channel_id=1, replica_groups=mesh['strip'=64,'chan'=4] {'chan'}, dimensions={0}, use_global_device_ids=true | all-gather | bytes 1013760 | tf_op jit(solution)/shard_map/all_gather | solution.py:265
  96.5 1.6 slice.243
  98.6 2.2 %gather_fusion.1 = f32[32,128]{1,0:T(8,128)S(1)} fusion(f32[4096,128]{1,0:T(8,128)} %bitcast.142, s32[1024]{0:T(1024)S(1)} %pad_clamp_fusion), kind=kCustom, calls=%fused_computation.1 | custom fusion | bytes 32896 | tf_op jit(solution)/shard_map/gather | solution.py:275
  100.8 2.1 %convert_reduce_fusion = (f32[128]{0:T(128)S(1)}, bf16[1536,128]{1,0:T(8,128)(2,1)S(1)}) fusion(f32[1536,128]{1,0:T(8,128)} %copy-done.22, f32[32,128]{1,0:T(8,128)S(1)} %gather_fusion.1, f32[32]{0:T(128)S(1)} %fusion.4, s32[1536]{0:T(1024)S(1)} %eq.98), kind=kOutput, calls=%fused_computation.42 | convolution fusion | flops 77713280 | bytes 1202816 | tf_op jit(solution)/shard_map/dot_general | solution.py:276
  113.2 67.0 %shard_map.112 = (f32[2560,128]{1,0:T(8,128)}, f32[2048,128]{1,0:T(8,128)}) custom-call(f32[2560,128]{1,0:T(8,128)} %pad_dynamic-update-slice_fusion.grads_ref, f32[32,128]{1,0:T(8,128)} %fusion.7.sums_ref), custom_call_target="tpu_custom_call" | custom-call | tf_op jit(solution)/shard_map/pallas_call | solution.py:169
  180.2 2.4 %slice.236 = f32[2304,128]{1,0:T(8,128)} slice(f32[2560,128]{1,0:T(8,128)} %get-tuple-element.50), slice={[0:2304], [0:128]} | slice | bytes 2359296 | tf_op jit(solution)/shard_map/slice | solution.py:307
  (139 shorter events, 45.4 us)
Async XLA Ops:
  8.6 14.1 %copy-start.1 = (bf16[48,128,256]{2,1,0:T(8,128)(2,1)S(1)}, bf16[48,128,256]{2,1,0:T(8,128)(2,1)}, u32[]{:S(2)}) copy-start(bf16[48,128,256]{2,1,0:T(8,128)(2,1)} %param.15) | copy-start | bytes 9437188
  8.6 18.9 %collective-permute-start.2 = (f32[72,128]{1,0:T(8,128)S(1)}, f32[72,128]{1,0:T(8,128)S(1)}, u32[]{:S(2)}, u32[]{:S(2)}) collective-permute-start(f32[72,128]{1,0:T(8,128)S(1)} %get-tuple-element.71), channel_id=1, source_target_pairs={{0,32},{4,36},{8,40},{12,44},{16,48},{20,52},{24,56},{28,60},{32,0... | collective-permute-start | bytes 110600 | tf_op jit(solution)/shard_map/ppermute | solution.py:62
  17.2 7.5 %collective-permute-start = (bf16[14,3,256]{2,1,0:T(4,128)(2,1)S(1)}, bf16[14,3,256]{2,1,0:T(4,128)(2,1)S(1)}, u32[]{:S(2)}, u32[]{:S(2)}) collective-permute-start(bf16[14,3,256]{2,1,0:T(4,128)(2,1)S(1)} %get-tuple-element.51), channel_id=1, source_target_pairs={{0,4},{4,8},{8,12},{12,16},{16,20},{20,24},{24,28},{28,32},{32,36}... | collective-permute-start | bytes 64520 | tf_op jit(solution)/shard_map/ppermute | solution.py:20
  20.7 3.0 %copy-start.25 = (s32[32]{0:T(128)S(1)}, s32[32]{0:T(128)}, u32[]{:S(2)}) copy-start(s32[32]{0:T(128)} %param.21) | copy-start | bytes 388
  20.7 3.0 %copy-start = (s32[64]{0:T(128)S(1)}, s32[64]{0:T(128)}, u32[]{:S(2)}) copy-start(s32[64]{0:T(128)} %constant.317.clone) | copy-start | bytes 772
  20.7 5.2 %collective-permute-start.1 = (bf16[14,3,256]{2,1,0:T(4,128)(2,1)S(1)}, bf16[14,3,256]{2,1,0:T(4,128)(2,1)S(1)}, u32[]{:S(2)}, u32[]{:S(2)}) collective-permute-start(bf16[14,3,256]{2,1,0:T(4,128)(2,1)S(1)} %get-tuple-element.52), channel_id=1, source_target_pairs={{4,0},{8,4},{12,8},{16,12},{20,16},{24,20},{28,24},{32,28},{36,32}... | collective-permute-start | bytes 64520 | tf_op jit(solution)/shard_map/ppermute | solution.py:22
  27.5 4.8 %collective-permute-start.3 = (f32[144,128]{1,0:T(8,128)S(1)}, f32[144,128]{1,0:T(8,128)S(1)}, u32[]{:S(2)}, u32[]{:S(2)}) collective-permute-start(f32[144,128]{1,0:T(8,128)S(1)} %constant_dynamic-update-slice_fusion.10), channel_id=1, source_target_pairs={{0,128},{4,132},{8,136},{12,140},{16,144},{20,148},{24,152},{28,15... | collective-permute-start | bytes 221192 | tf_op jit(solution)/shard_map/ppermute | solution.py:62
  32.3 31.3 %collective-permute-start.4 = (f32[288,128]{1,0:T(8,128)S(1)}, f32[288,128]{1,0:T(8,128)}, u32[]{:S(2)}, u32[]{:S(2)}) collective-permute-start(f32[288,128]{1,0:T(8,128)S(1)} %constant_dynamic-update-slice_fusion.8), channel_id=1, source_target_pairs={{0,16},{4,20},{8,24},{12,60},{16,0},{20,4},{24,8},{28,44},{32,48},... | collective-permute-start | bytes 442376 | tf_op jit(solution)/shard_map/ppermute | solution.py:62
  49.5 1.2 copy-start.12
  50.8 1.4 copy-start.19
  50.8 1.6 copy-start.20
  64.6 6.9 %collective-permute-start.5 = (f32[576,128]{1,0:T(8,128)S(1)}, f32[576,128]{1,0:T(8,128)S(1)}, u32[]{:S(2)}, u32[]{:S(2)}) collective-permute-start(f32[576,128]{1,0:T(8,128)S(1)} %constant_dynamic-update-slice_fusion.6), channel_id=1, source_target_pairs={{0,64},{4,196},{8,72},{12,204},{16,80},{20,212},{24,88},{28,220},{... | collective-permute-start | bytes 884744 | tf_op jit(solution)/shard_map/ppermute | solution.py:62
  71.5 21.2 %collective-permute-start.6 = (f32[1152,128]{1,0:T(8,128)S(1)}, f32[1152,128]{1,0:T(8,128)S(1)}, u32[]{:S(2)}, u32[]{:S(2)}) collective-permute-start(f32[1152,128]{1,0:T(8,128)S(1)} %constant_dynamic-update-slice_fusion.4), channel_id=1, source_target_pairs={{0,8},{4,60},{8,0},{12,20},{16,24},{20,12},{24,16},{28,36},{32,40}... | collective-permute-start | bytes 1769480 | tf_op jit(solution)/shard_map/ppermute | solution.py:62
  88.0 1.5 copy-start.23
  89.4 1.4 copy-start.6
  89.4 1.8 copy-start.4
  89.4 2.1 %copy-start.2 = (bf16[24,64,256]{2,1,0:T(8,128)(2,1)}, bf16[24,64,256]{2,1,0:T(8,128)(2,1)S(1)}, u32[]{:S(2)}) copy-start(bf16[24,64,256]{2,1,0:T(8,128)(2,1)S(1)} %get-tuple-element.68) | copy-start | bytes 2359300
  92.8 3.3 %collective-permute-start.7 = (f32[2304,128]{1,0:T(8,128)S(1)}, f32[2304,128]{1,0:T(8,128)S(1)}, u32[]{:S(2)}, u32[]{:S(2)}) collective-permute-start(f32[2304,128]{1,0:T(8,128)S(1)} %constant_dynamic-update-slice_fusion.2), channel_id=1, source_target_pairs={{0,4},{4,0},{8,12},{12,8},{16,20},{20,16},{24,28},{28,24},{32,36},... | collective-permute-start | bytes 3538952 | tf_op jit(solution)/shard_map/ppermute | solution.py:62
  100.8 2.1 %copy-start.11 = (bf16[24,64,256]{2,1,0:T(8,128)(2,1)S(1)}, bf16[24,64,256]{2,1,0:T(8,128)(2,1)}, u32[]{:S(2)}) copy-start(bf16[24,64,256]{2,1,0:T(8,128)(2,1)} %copy-done.10) | copy-start | bytes 2359300
  100.8 3.2 %copy-start.9 = (bf16[24,64,256]{2,1,0:T(8,128)(2,1)S(1)}, bf16[24,64,256]{2,1,0:T(8,128)(2,1)}, u32[]{:S(2)}) copy-start(bf16[24,64,256]{2,1,0:T(8,128)(2,1)} %copy-done.8) | copy-start | bytes 2359300
  102.9 2.1 %copy-start.7 = (bf16[24,64,256]{2,1,0:T(8,128)(2,1)S(1)}, bf16[24,64,256]{2,1,0:T(8,128)(2,1)}, u32[]{:S(2)}) copy-start(bf16[24,64,256]{2,1,0:T(8,128)(2,1)} %copy-done.6) | copy-start | bytes 2359300
  104.0 2.1 %copy-start.5 = (bf16[24,64,256]{2,1,0:T(8,128)(2,1)S(1)}, bf16[24,64,256]{2,1,0:T(8,128)(2,1)}, u32[]{:S(2)}) copy-start(bf16[24,64,256]{2,1,0:T(8,128)(2,1)} %copy-done.4) | copy-start | bytes 2359300
  105.0 2.1 %copy-start.3 = (bf16[24,64,256]{2,1,0:T(8,128)(2,1)S(1)}, bf16[24,64,256]{2,1,0:T(8,128)(2,1)}, u32[]{:S(2)}) copy-start(bf16[24,64,256]{2,1,0:T(8,128)(2,1)} %copy-done.2) | copy-start | bytes 2359300
  180.2 4.0 %copy-start.21 = (f32[2048,128]{1,0:T(8,128)S(1)}, f32[2048,128]{1,0:T(8,128)}, u32[]{:S(2)}) copy-start(f32[2048,128]{1,0:T(8,128)} %get-tuple-element.49) | copy-start | bytes 3145732
  (11 other events, 11.7 us)

commit v8 on v7

--- a/solution.py
+++ b/solution.py
@@ -262,7 +262,16 @@
     every_grad = every[:, :owned].reshape(strip_count * owned, lanes)
     every_counts = every[:, owned, :list_len].reshape(-1)
     every_slots = jnp.round(every[:, owned, list_len : 2 * list_len]).astype(jnp.int32).reshape(-1)
-    gathered = lax.all_gather(pooled, "chan", axis=0, tiled=True)
+    part_rows = pooled.shape[0]
+    gathered = jnp.zeros((chan_count * part_rows,) + pooled.shape[1:], pooled.dtype)
+    for shift in range(chan_count):
+        block = pooled
+        if shift:
+            block = lax.ppermute(
+                pooled, "chan", [(i, (i + shift) % chan_count) for i in range(chan_count)]
+            )
+        source = (chan_pos + chan_count - shift) % chan_count
+        gathered = lax.dynamic_update_slice_in_dim(gathered, block, source * part_rows, 0)
     padded_deep = jnp.pad(gathered, ((1, 1), (0, 0), (0, 0)))
     half_rows = gathered.shape[0]
     deep_pre = convolve(padded_deep, deep_weight, half_rows, half_cols) + deep_bias

time: 186 us -> 183 us (0.984)
  blocking collectives: 13.3 us -> 0 us
  starting transfers between devices: 24.4 us -> 30.8 us
  waiting for transfers between devices: 7.3 us -> 12.6 us
    all_gather x1 -> x0, blocking collectives: 13.3 us -> none  [body(): gathered = lax.all_gather(pooled, 'chan', axis=0, tiled=True)]
    ppermute x0 -> x3, starting transfers between devices: none -> 5.09 us  [body(): lax.ppermute(pooled, 'chan', [(i, (i + shift) % chan_count) for i in rang...]
    ppermute x0 -> x3, waiting for transfers between devices: none -> 4.85 us  [body(): lax.ppermute(pooled, 'chan', [(i, (i + shift) % chan_count) for i in rang...]
  transfers between devices with their start and end apart: 8 -> 11, of which waited for: 3 -> 5; matrix products, arithmetic and copies ran while one was open for 19% -> 19% of each run, Pallas kernels for 0% -> 0%
where the time goes in v8:
time: 183 us; the launch traced here: 182 us
  Pallas kernels  65.5 us (36%)
  local copies, waits for them, and re-layouts  39.4 us (22%)
  starting transfers between devices  30.8 us (17%)
  matrix products  22.1 us (12%)
  waiting for transfers between devices  12.6 us (7%)
  other arithmetic  9.48 us (5%)
    pallas_call x1, Pallas kernels, tree_sum(): pl.pallas_call(functools.partial(tree_kernel, count, chunk, width, dists,...  65.5 us
    ppermute x6, starting transfers between devices, tree_gather(): other = lax.ppermute(held, axis, pairs)  20.3 us
    reshape x9, local copies, waits for them, and re-layouts, convolve(): window = padded[shift_row:shift_row + row_count, shift_col:shift_col + co...  13.6 us
    dot_general x9, matrix products, body(): lax.dot_general(window, deep_grad, (((0,), (0,)), ((), ())), preferred_el...  9.5 us
    dot_general x18, matrix products, convolve(): jnp.dot(window, weight[shift_row, shift_col], preferred_element_type=jnp....  7.71 us
    ppermute x6, waiting for transfers between devices, tree_gather(): other = lax.ppermute(held, axis, pairs)  6.58 us
    unnamed x54, local copies, waits for them, and re-layouts  5.17 us
    ppermute x3, starting transfers between devices, body(): lax.ppermute(pooled, 'chan', [(i, (i + shift) % chan_count) for i in rang...  5.09 us
  transfers between devices with their start and end apart: 11, of which 5 were waited for; matrix products, arithmetic and copies ran while one was open for 19% of the time, Pallas kernels for 0%

profile of v8, /device:TPU:1, one launch (start us, length us, event | category | flops | bytes accessed | tf_op | source)
XLA Modules:
  0.0 181.5 jit_solution(4596634883095408428)
XLA Ops:
  3.6 2.7 %broadcast_select_fusion = f32[1,32]{1,0:T(1,128)S(1)} fusion(pred[]{:T(512)} %and_reduce_fusion, s32[]{:T(128)} %bitcast.2, s32[]{:T(128)} %bitcast.3, f32[1,32]{1,0:T(1,128)S(1)} %bitcast.145, s32[32]{0:T(128)} %param.21), kind=kLoop, calls=%fused_computation.143 | loop fusion | flops 64 | bytes 393 | tf_op jit(solution)/shard_map/select.4
  8.6 7.7 %collective-permute-start.2 = (f32[72,128]{1,0:T(8,128)S(1)}, f32[72,128]{1,0:T(8,128)S(1)}, u32[]{:S(2)}, u32[]{:S(2)}) collective-permute-start(f32[72,128]{1,0:T(8,128)S(1)} %get-tuple-element.71), channel_id=1, source_target_pairs={{0,32},{4,36},{8,40},{12,44},{16,48},{20,52},{24,56},{28,60},{32,0... | collective-permute-start | bytes 110600 | tf_op jit(solution)/shard_map/ppermute | solution.py:62
  17.2 3.5 %collective-permute-start = (bf16[14,3,256]{2,1,0:T(4,128)(2,1)S(1)}, bf16[14,3,256]{2,1,0:T(4,128)(2,1)S(1)}, u32[]{:S(2)}, u32[]{:S(2)}) collective-permute-start(bf16[14,3,256]{2,1,0:T(4,128)(2,1)S(1)} %get-tuple-element.51), channel_id=1, source_target_pairs={{0,4},{4,8},{8,12},{12,16},{16,20},{20,24},{24,28},{28,32},{32,36}... | collective-permute-start | bytes 64520 | tf_op jit(solution)/shard_map/ppermute | solution.py:20
  20.7 1.9 %collective-permute-start.1 = (bf16[14,3,256]{2,1,0:T(4,128)(2,1)S(1)}, bf16[14,3,256]{2,1,0:T(4,128)(2,1)S(1)}, u32[]{:S(2)}, u32[]{:S(2)}) collective-permute-start(bf16[14,3,256]{2,1,0:T(4,128)(2,1)S(1)} %get-tuple-element.52), channel_id=1, source_target_pairs={{4,0},{8,4},{12,8},{16,12},{20,16},{24,20},{28,24},{32,28},{36,32}... | collective-permute-start | bytes 64520 | tf_op jit(solution)/shard_map/ppermute | solution.py:22
  27.5 2.8 %collective-permute-start.3 = (f32[144,128]{1,0:T(8,128)S(1)}, f32[144,128]{1,0:T(8,128)S(1)}, u32[]{:S(2)}, u32[]{:S(2)}) collective-permute-start(f32[144,128]{1,0:T(8,128)S(1)} %constant_dynamic-update-slice_fusion.14), channel_id=1, source_target_pairs={{0,128},{4,132},{8,136},{12,140},{16,144},{20,148},{24,152},{28,15... | collective-permute-start | bytes 221192 | tf_op jit(solution)/shard_map/ppermute | solution.py:62
  30.4 1.9 %collective-permute-done.3 = f32[144,128]{1,0:T(8,128)S(1)} collective-permute-done((f32[144,128]{1,0:T(8,128)S(1)}, f32[144,128]{1,0:T(8,128)S(1)}, u32[]{:S(2)}, u32[]{:S(2)}) %collective-permute-start.3) | collective-permute-done | bytes 73760 | tf_op jit(solution)/shard_map/ppermute | solution.py:62
  32.3 2.2 %collective-permute-start.4 = (f32[288,128]{1,0:T(8,128)S(1)}, f32[288,128]{1,0:T(8,128)}, u32[]{:S(2)}, u32[]{:S(2)}) collective-permute-start(f32[288,128]{1,0:T(8,128)S(1)} %constant_dynamic-update-slice_fusion.12), channel_id=1, source_target_pairs={{0,16},{4,20},{8,24},{12,60},{16,0},{20,4},{24,8},{28,44},{32,48},... | collective-permute-start | bytes 442376 | tf_op jit(solution)/shard_map/ppermute | solution.py:62
  34.6 2.5 %fusion.68 = (bf16[12,132,256]{2,1,0:T(8,128)(2,1)S(1)}, bf16[12,132,256]{2,1,0:T(8,128)(2,1)S(1)}, bf16[12,132,256]{2,1,0:T(8,128)(2,1)S(1)}, bf16[12,132,256]{...) fusion(bf16[14,134,256]{2,1,0:T(8,128)(2,1)S(1)} %pad_maximum_f, ...), kind=kLoop, calls=%fused_computation.149 | loop fusion | bytes 14598144 | tf_op jit(solution)/shard_map/slice | solution.py:200
  37.1 2.0 %reshape.206 = bf16[1584,256]{1,0:T(8,128)(2,1)} reshape(bf16[12,132,256]{2,1,0:T(8,128)(2,1)} %get-tuple-element.61) | data formatting | bytes 1622016 | tf_op jit(solution)/shard_map/reshape | solution.py:202
  39.1 2.0 %reshape.207 = bf16[1584,256]{1,0:T(8,128)(2,1)} reshape(bf16[12,132,256]{2,1,0:T(8,128)(2,1)} %get-tuple-element.60) | data formatting | bytes 1622016 | tf_op jit(solution)/shard_map/reshape | solution.py:202
  41.2 2.1 %reshape.208 = bf16[1584,256]{1,0:T(8,128)(2,1)} reshape(bf16[12,132,256]{2,1,0:T(8,128)(2,1)} %get-tuple-element.59) | data formatting | bytes 1622016 | tf_op jit(solution)/shard_map/reshape | solution.py:202
  43.2 2.1 %reshape.209 = bf16[1584,256]{1,0:T(8,128)(2,1)} reshape(bf16[12,132,256]{2,1,0:T(8,128)(2,1)} %get-tuple-element.58) | data formatting | bytes 1622016 | tf_op jit(solution)/shard_map/reshape | solution.py:202
  45.3 2.1 %reshape.210 = bf16[1584,256]{1,0:T(8,128)(2,1)} reshape(bf16[12,132,256]{2,1,0:T(8,128)(2,1)} %get-tuple-element.57) | data formatting | bytes 1622016 | tf_op jit(solution)/shard_map/reshape | solution.py:202
  60.8 2.7 %fusion.5 = f32[6,66,256]{2,1,0:T(8,128)S(1)} fusion(f32[6,2,66,2,256]{4,3,2,1,0:T(2,128)S(1)} %reshape.215, f32[256]{0:T(256)S(1)} %copy-done.24), kind=kLoop, calls=%fused_computation.25 | loop fusion | flops 2331648 | bytes 2028544 | tf_op jit(solution)/shard_map/reduce_sum | solution.py:214
  64.5 2.6 %collective-permute-start.5 = (f32[576,128]{1,0:T(8,128)S(1)}, f32[576,128]{1,0:T(8,128)S(1)}, u32[]{:S(2)}, u32[]{:S(2)}) collective-permute-start(f32[576,128]{1,0:T(8,128)S(1)} %constant_dynamic-update-slice_fusion.10), channel_id=1, source_target_pairs={{0,64},{4,196},{8,72},{12,204},{16,80},{20,212},{24,88},{28,220},{... | collective-permute-start | bytes 884744 | tf_op jit(solution)/shard_map/ppermute | solution.py:62
  67.3 4.1 %collective-permute-done.5 = f32[576,128]{1,0:T(8,128)S(1)} collective-permute-done((f32[576,128]{1,0:T(8,128)S(1)}, f32[576,128]{1,0:T(8,128)S(1)}, u32[]{:S(2)}, u32[]{:S(2)}) %collective-permute-start.5) | collective-permute-done | bytes 294944 | tf_op jit(solution)/shard_map/ppermute | solution.py:62
  72.8 2.6 %collective-permute-start.9 = (bf16[6,66,256]{2,1,0:T(8,128)(2,1)S(1)}, bf16[6,66,256]{2,1,0:T(8,128)(2,1)S(1)}, u32[]{:S(2)}, u32[]{:S(2)}) collective-permute-start(bf16[6,66,256]{2,1,0:T(8,128)(2,1)S(1)} %fusion.16), channel_id=1, source_target_pairs={{0,2},{1,3},{2,0},{3,1},{4,6},{5,7},{6,4},{7,5},{8,10},{9,11},{10,... | collective-permute-start | bytes 608264 | tf_op jit(solution)/shard_map/ppermute | solution.py:270
  76.5 3.1 %collective-permute-start.6 = (f32[1152,128]{1,0:T(8,128)S(1)}, f32[1152,128]{1,0:T(8,128)S(1)}, u32[]{:S(2)}, u32[]{:S(2)}) collective-permute-start(f32[1152,128]{1,0:T(8,128)S(1)} %constant_dynamic-update-slice_fusion.8), channel_id=1, source_target_pairs={{0,8},{4,60},{8,0},{12,20},{16,24},{20,12},{24,16},{28,36},{32,40}... | collective-permute-start | bytes 1769480 | tf_op jit(solution)/shard_map/ppermute | solution.py:62
  79.9 4.8 %collective-permute-done.9 = bf16[6,66,256]{2,1,0:T(8,128)(2,1)S(1)} collective-permute-done((bf16[6,66,256]{2,1,0:T(8,128)(2,1)S(1)}, bf16[6,66,256]{2,1,0:T(8,128)(2,1)S(1)}, u32[]{:S(2)}, u32[]{:S(2)}) %collective-permute-start.9) | collective-permute-done | bytes 202784 | tf_op jit(solution)/shard_map/ppermute | solution.py:270
  89.6 1.9 %collective-permute-start.7 = (f32[2304,128]{1,0:T(8,128)S(1)}, f32[2304,128]{1,0:T(8,128)S(1)}, u32[]{:S(2)}, u32[]{:S(2)}) collective-permute-start(f32[2304,128]{1,0:T(8,128)S(1)} %constant_dynamic-update-slice_fusion.6), channel_id=1, source_target_pairs={{0,4},{4,0},{8,12},{12,8},{16,20},{20,16},{24,28},{28,24},{32,36},... | collective-permute-start | bytes 3538952 | tf_op jit(solution)/shard_map/ppermute | solution.py:62
  96.3 2.2 %gather_fusion.1 = f32[32,128]{1,0:T(8,128)S(1)} fusion(f32[4096,128]{1,0:T(8,128)} %bitcast.142, s32[1024]{0:T(1024)S(1)} %pad_clamp_fusion), kind=kCustom, calls=%fused_computation.1 | custom fusion | bytes 32896 | tf_op jit(solution)/shard_map/gather | solution.py:284
  98.6 2.1 %convert_reduce_fusion = (f32[128]{0:T(128)S(1)}, bf16[1536,128]{1,0:T(8,128)(2,1)S(1)}) fusion(f32[1536,128]{1,0:T(8,128)} %copy-done.22, f32[32,128]{1,0:T(8,128)S(1)} %gather_fusion.1, f32[32]{0:T(128)S(1)} %fusion.7, s32[1536]{0:T(1024)S(1)} %eq.102), kind=kOutput, calls=%fused_computation.42 | convolution fusion | flops 77713280 | bytes 1202816 | tf_op jit(solution)/shard_map/dot_general | solution.py:285
  110.9 65.5 %shard_map.112 = (f32[2560,128]{1,0:T(8,128)}, f32[2048,128]{1,0:T(8,128)}) custom-call(f32[2560,128]{1,0:T(8,128)} %pad_dynamic-update-slice_fusion.grads_ref, f32[32,128]{1,0:T(8,128)} %fusion.10.sums_ref), custom_call_target="tpu_custom_call" | custom-call | tf_op jit(solution)/shard_map/pallas_call | solution.py:169
  176.4 2.4 %slice.236 = f32[2304,128]{1,0:T(8,128)} slice(f32[2560,128]{1,0:T(8,128)} %get-tuple-element.50), slice={[0:2304], [0:128]} | slice | bytes 2359296 | tf_op jit(solution)/shard_map/slice | solution.py:316
  (149 shorter events, 50.2 us)
Async XLA Ops:
  8.6 14.1 %copy-start.1 = (bf16[48,128,256]{2,1,0:T(8,128)(2,1)S(1)}, bf16[48,128,256]{2,1,0:T(8,128)(2,1)}, u32[]{:S(2)}) copy-start(bf16[48,128,256]{2,1,0:T(8,128)(2,1)} %param.15) | copy-start | bytes 9437188
  8.6 18.9 %collective-permute-start.2 = (f32[72,128]{1,0:T(8,128)S(1)}, f32[72,128]{1,0:T(8,128)S(1)}, u32[]{:S(2)}, u32[]{:S(2)}) collective-permute-start(f32[72,128]{1,0:T(8,128)S(1)} %get-tuple-element.71), channel_id=1, source_target_pairs={{0,32},{4,36},{8,40},{12,44},{16,48},{20,52},{24,56},{28,60},{32,0... | collective-permute-start | bytes 110600 | tf_op jit(solution)/shard_map/ppermute | solution.py:62
  17.2 7.5 %collective-permute-start = (bf16[14,3,256]{2,1,0:T(4,128)(2,1)S(1)}, bf16[14,3,256]{2,1,0:T(4,128)(2,1)S(1)}, u32[]{:S(2)}, u32[]{:S(2)}) collective-permute-start(bf16[14,3,256]{2,1,0:T(4,128)(2,1)S(1)} %get-tuple-element.51), channel_id=1, source_target_pairs={{0,4},{4,8},{8,12},{12,16},{16,20},{20,24},{24,28},{28,32},{32,36}... | collective-permute-start | bytes 64520 | tf_op jit(solution)/shard_map/ppermute | solution.py:20
  20.7 3.0 %copy-start.25 = (s32[32]{0:T(128)S(1)}, s32[32]{0:T(128)}, u32[]{:S(2)}) copy-start(s32[32]{0:T(128)} %param.21) | copy-start | bytes 388
  20.7 3.0 %copy-start = (s32[64]{0:T(128)S(1)}, s32[64]{0:T(128)}, u32[]{:S(2)}) copy-start(s32[64]{0:T(128)} %constant.344.clone) | copy-start | bytes 772
  20.7 5.2 %collective-permute-start.1 = (bf16[14,3,256]{2,1,0:T(4,128)(2,1)S(1)}, bf16[14,3,256]{2,1,0:T(4,128)(2,1)S(1)}, u32[]{:S(2)}, u32[]{:S(2)}) collective-permute-start(bf16[14,3,256]{2,1,0:T(4,128)(2,1)S(1)} %get-tuple-element.52), channel_id=1, source_target_pairs={{4,0},{8,4},{12,8},{16,12},{20,16},{24,20},{28,24},{32,28},{36,32}... | collective-permute-start | bytes 64520 | tf_op jit(solution)/shard_map/ppermute | solution.py:22
  27.5 4.8 %collective-permute-start.3 = (f32[144,128]{1,0:T(8,128)S(1)}, f32[144,128]{1,0:T(8,128)S(1)}, u32[]{:S(2)}, u32[]{:S(2)}) collective-permute-start(f32[144,128]{1,0:T(8,128)S(1)} %constant_dynamic-update-slice_fusion.14), channel_id=1, source_target_pairs={{0,128},{4,132},{8,136},{12,140},{16,144},{20,148},{24,152},{28,15... | collective-permute-start | bytes 221192 | tf_op jit(solution)/shard_map/ppermute | solution.py:62
  32.3 31.2 %collective-permute-start.4 = (f32[288,128]{1,0:T(8,128)S(1)}, f32[288,128]{1,0:T(8,128)}, u32[]{:S(2)}, u32[]{:S(2)}) collective-permute-start(f32[288,128]{1,0:T(8,128)S(1)} %constant_dynamic-update-slice_fusion.12), channel_id=1, source_target_pairs={{0,16},{4,20},{8,24},{12,60},{16,0},{20,4},{24,8},{28,44},{32,48},... | collective-permute-start | bytes 442376 | tf_op jit(solution)/shard_map/ppermute | solution.py:62
  64.5 6.9 %collective-permute-start.5 = (f32[576,128]{1,0:T(8,128)S(1)}, f32[576,128]{1,0:T(8,128)S(1)}, u32[]{:S(2)}, u32[]{:S(2)}) collective-permute-start(f32[576,128]{1,0:T(8,128)S(1)} %constant_dynamic-update-slice_fusion.10), channel_id=1, source_target_pairs={{0,64},{4,196},{8,72},{12,204},{16,80},{20,212},{24,88},{28,220},{... | collective-permute-start | bytes 884744 | tf_op jit(solution)/shard_map/ppermute | solution.py:62
  71.4 8.4 %collective-permute-start.8 = (bf16[6,66,256]{2,1,0:T(8,128)(2,1)S(1)}, bf16[6,66,256]{2,1,0:T(8,128)(2,1)S(1)}, u32[]{:S(2)}, u32[]{:S(2)}) collective-permute-start(bf16[6,66,256]{2,1,0:T(8,128)(2,1)S(1)} %fusion.16), channel_id=1, source_target_pairs={{0,1},{1,2},{2,3},{3,0},{4,5},{5,6},{6,7},{7,4},{8,9},{9,10},{10,1... | collective-permute-start | bytes 608264 | tf_op jit(solution)/shard_map/ppermute | solution.py:270
  72.8 11.9 %collective-permute-start.9 = (bf16[6,66,256]{2,1,0:T(8,128)(2,1)S(1)}, bf16[6,66,256]{2,1,0:T(8,128)(2,1)S(1)}, u32[]{:S(2)}, u32[]{:S(2)}) collective-permute-start(bf16[6,66,256]{2,1,0:T(8,128)(2,1)S(1)} %fusion.16), channel_id=1, source_target_pairs={{0,2},{1,3},{2,0},{3,1},{4,6},{5,7},{6,4},{7,5},{8,10},{9,11},{10,... | collective-permute-start | bytes 608264 | tf_op jit(solution)/shard_map/ppermute | solution.py:270
  75.4 9.3 %collective-permute-start.10 = (bf16[6,66,256]{2,1,0:T(8,128)(2,1)S(1)}, bf16[6,66,256]{2,1,0:T(8,128)(2,1)S(1)}, u32[]{:S(2)}, u32[]{:S(2)}) collective-permute-start(bf16[6,66,256]{2,1,0:T(8,128)(2,1)S(1)} %fusion.16), channel_id=1, source_target_pairs={{0,3},{1,0},{2,1},{3,2},{4,7},{5,4},{6,5},{7,6},{8,11},{9,8},{10,9... | collective-permute-start | bytes 608264 | tf_op jit(solution)/shard_map/ppermute | solution.py:270
  76.5 13.0 %collective-permute-start.6 = (f32[1152,128]{1,0:T(8,128)S(1)}, f32[1152,128]{1,0:T(8,128)S(1)}, u32[]{:S(2)}, u32[]{:S(2)}) collective-permute-start(f32[1152,128]{1,0:T(8,128)S(1)} %constant_dynamic-update-slice_fusion.8), channel_id=1, source_target_pairs={{0,8},{4,60},{8,0},{12,20},{16,24},{20,12},{24,16},{28,36},{32,40}... | collective-permute-start | bytes 1769480 | tf_op jit(solution)/shard_map/ppermute | solution.py:62
  84.8 1.7 copy-start.23
  86.4 1.9 %copy-start.6 = (bf16[24,64,256]{2,1,0:T(8,128)(2,1)}, bf16[24,64,256]{2,1,0:T(8,128)(2,1)S(1)}, u32[]{:S(2)}) copy-start(bf16[24,64,256]{2,1,0:T(8,128)(2,1)S(1)} %get-tuple-element.64) | copy-start | bytes 2359300
  86.4 2.2 %copy-start.4 = (bf16[24,64,256]{2,1,0:T(8,128)(2,1)}, bf16[24,64,256]{2,1,0:T(8,128)(2,1)S(1)}, u32[]{:S(2)}) copy-start(bf16[24,64,256]{2,1,0:T(8,128)(2,1)S(1)} %get-tuple-element.68) | copy-start | bytes 2359300
  89.5 2.4 %copy-start.26 = (f32[128]{0:T(128)S(1)}, f32[128]{0:T(128)}, u32[]{:S(2)}) copy-start(f32[128]{0:T(128)} %param.19) | copy-start | bytes 1540
  89.6 4.4 %collective-permute-start.7 = (f32[2304,128]{1,0:T(8,128)S(1)}, f32[2304,128]{1,0:T(8,128)S(1)}, u32[]{:S(2)}, u32[]{:S(2)}) collective-permute-start(f32[2304,128]{1,0:T(8,128)S(1)} %constant_dynamic-update-slice_fusion.6), channel_id=1, source_target_pairs={{0,4},{4,0},{8,12},{12,8},{16,20},{20,16},{24,28},{28,24},{32,36},... | collective-permute-start | bytes 3538952 | tf_op jit(solution)/shard_map/ppermute | solution.py:62
  98.5 2.1 %copy-start.11 = (bf16[24,64,256]{2,1,0:T(8,128)(2,1)S(1)}, bf16[24,64,256]{2,1,0:T(8,128)(2,1)}, u32[]{:S(2)}) copy-start(bf16[24,64,256]{2,1,0:T(8,128)(2,1)} %copy-done.10) | copy-start | bytes 2359300
  98.5 3.2 %copy-start.9 = (bf16[24,64,256]{2,1,0:T(8,128)(2,1)S(1)}, bf16[24,64,256]{2,1,0:T(8,128)(2,1)}, u32[]{:S(2)}) copy-start(bf16[24,64,256]{2,1,0:T(8,128)(2,1)} %copy-done.8) | copy-start | bytes 2359300
  100.7 2.1 %copy-start.7 = (bf16[24,64,256]{2,1,0:T(8,128)(2,1)S(1)}, bf16[24,64,256]{2,1,0:T(8,128)(2,1)}, u32[]{:S(2)}) copy-start(bf16[24,64,256]{2,1,0:T(8,128)(2,1)} %copy-done.6) | copy-start | bytes 2359300
  102.8 2.1 %copy-start.5 = (bf16[24,64,256]{2,1,0:T(8,128)(2,1)S(1)}, bf16[24,64,256]{2,1,0:T(8,128)(2,1)}, u32[]{:S(2)}) copy-start(bf16[24,64,256]{2,1,0:T(8,128)(2,1)} %copy-done.4) | copy-start | bytes 2359300
  103.9 2.1 %copy-start.3 = (bf16[24,64,256]{2,1,0:T(8,128)(2,1)S(1)}, bf16[24,64,256]{2,1,0:T(8,128)(2,1)}, u32[]{:S(2)}) copy-start(bf16[24,64,256]{2,1,0:T(8,128)(2,1)} %copy-done.2) | copy-start | bytes 2359300
  176.3 4.0 %copy-start.21 = (f32[2048,128]{1,0:T(8,128)S(1)}, f32[2048,128]{1,0:T(8,128)}, u32[]{:S(2)}) copy-start(f32[2048,128]{1,0:T(8,128)} %get-tuple-element.49) | copy-start | bytes 3145732
  (14 other events, 16.6 us)

commit v9 on v8

--- a/solution.py
+++ b/solution.py
@@ -194,17 +194,21 @@
 
 def convolve(padded, weight, row_count, col_count):
     channels = padded.shape[-1]
+    width = -(-padded.shape[1] // 16) * 16
+    padded = jnp.pad(padded, ((0, 0), (0, width - padded.shape[1]), (0, 0)))
     running = None
-    for shift_row in range(3):
-        for shift_col in range(3):
-            window = padded[
-                shift_row : shift_row + row_count, shift_col : shift_col + col_count
-            ].reshape(row_count * col_count, channels)
+    for shift_col in range(3):
+        column_sum = None
+        for shift_row in range(3):
+            band = padded[shift_row : shift_row + row_count].reshape(row_count * width, channels)
             partial_term = jnp.dot(
-                window, weight[shift_row, shift_col], preferred_element_type=jnp.float32
+                band, weight[shift_row, shift_col], preferred_element_type=jnp.float32
             )
-            running = partial_term if running is None else running + partial_term
-    return running.reshape(row_count, col_count, weight.shape[-1])
+            column_sum = partial_term if column_sum is None else column_sum + partial_term
+        column_sum = column_sum.reshape(row_count, width, weight.shape[-1])
+        shifted = column_sum[:, shift_col : shift_col + col_count]
+        running = shifted if running is None else running + shifted
+    return running
 
 
 def pool_pairs(hidden):

time: 183 us -> 166 us (0.907)
  local copies, waits for them, and re-layouts: 39.4 us -> 22 us
  waiting for transfers between devices: 12.6 us -> 8.36 us
  starting transfers between devices: 30.8 us -> 34.6 us
    reshape x10 -> x1, local copies, waits for them, and re-layouts: 14.6 us -> 0.96 us  [pool_pairs(): hidden.reshape(row_count // 2, 2, col_count // 2, 2, channels)]
    ppermute x6, starting transfers between devices: 20.3 us -> 24.1 us  [tree_gather(): other = lax.ppermute(held, axis, pairs)]
    ppermute x3, waiting for transfers between devices: 4.85 us -> 1.11 us  [body(): lax.ppermute(pooled, 'chan', [(i, (i + shift) % chan_count) for i in rang...]
    unnamed x54 -> x24, local copies, waits for them, and re-layouts: 5.17 us -> 2.2 us
    mul x0 -> x2, other arithmetic: none -> 1.86 us  [the longest x1 1.19 us: swish_slope(): return sigma * (1.0 + value * (1.0 - sigma))]
    slice x2 -> x3, local copies, waits for them, and re-layouts: 4.1 us -> 3.1 us  [the longest x1 2.69 us: body(): padded_deep[shift_row:shift_row + half_rows, shift_col:shift_col + half_c...]
  transfers between devices with their start and end apart: 11 -> 11, of which waited for: 5 -> 4; matrix products, arithmetic and copies ran while one was open for 19% -> 12% of each run, Pallas kernels for 0% -> 0%
where the time goes in v9:
time: 166 us; the launch traced here: 165 us
  Pallas kernels  65.4 us (39%)
  starting transfers between devices  34.6 us (21%)
  matrix products  22.8 us (14%)
  local copies, waits for them, and re-layouts  22 us (13%)
  other arithmetic  10.3 us (6%)
  waiting for transfers between devices  8.36 us (5%)
    pallas_call x1, Pallas kernels, tree_sum(): pl.pallas_call(functools.partial(tree_kernel, count, chunk, width, dists,...  65.4 us
    ppermute x6, starting transfers between devices, tree_gather(): other = lax.ppermute(held, axis, pairs)  24.1 us
    dot_general x9, matrix products, body(): lax.dot_general(window, deep_grad, (((0,), (0,)), ((), ())), preferred_el...  10.7 us
    dot_general x18, matrix products, convolve(): jnp.dot(band, weight[shift_row, shift_col], preferred_element_type=jnp.fl...  7.34 us
    ppermute x6, waiting for transfers between devices, tree_gather(): other = lax.ppermute(held, axis, pairs)  6.08 us
    ppermute x3, starting transfers between devices, body(): lax.ppermute(pooled, 'chan', [(i, (i + shift) % chan_count) for i in rang...  5.05 us
    another operation x3, other arithmetic  3.97 us
    ppermute x1, starting transfers between devices, with_halo(): lax.ppermute(tail, axis, [(i, (i + 1) % count) for i in range(ends)])  3.49 us
  transfers between devices with their start and end apart: 11, of which 4 were waited for; matrix products, arithmetic and copies ran while one was open for 12% of the time, Pallas kernels for 0%

profile of v9, /device:TPU:1, one launch (start us, length us, event | category | flops | bytes accessed | tf_op | source)
XLA Modules:
  0.0 164.9 jit_solution(5285264610185493517)
XLA Ops:
  2.2 1.3 and_reduce_fusion
  3.6 2.7 %broadcast_select_fusion = f32[1,32]{1,0:T(1,128)S(1)} fusion(pred[]{:T(512)} %and_reduce_fusion, s32[]{:T(128)} %bitcast.2, s32[]{:T(128)} %bitcast.3, f32[1,32]{1,0:T(1,128)S(1)} %bitcast.190, s32[32]{0:T(128)} %param.21), kind=kLoop, calls=%fused_computation.150 | loop fusion | flops 64 | bytes 393 | tf_op jit(solution)/shard_map/select.4
  6.2 1.6 scatter.11
  8.7 7.7 %collective-permute-start.2 = (f32[72,128]{1,0:T(8,128)S(1)}, f32[72,128]{1,0:T(8,128)S(1)}, u32[]{:S(2)}, u32[]{:S(2)}) collective-permute-start(f32[72,128]{1,0:T(8,128)S(1)} %get-tuple-element.70), channel_id=1, source_target_pairs={{0,32},{4,36},{8,40},{12,44},{16,48},{20,52},{24,56},{28,60},{32,0... | collective-permute-start | bytes 110600 | tf_op jit(solution)/shard_map/ppermute | solution.py:62
  17.4 3.5 %collective-permute-start = (bf16[14,3,256]{2,1,0:T(4,128)(2,1)S(1)}, bf16[14,3,256]{2,1,0:T(4,128)(2,1)S(1)}, u32[]{:S(2)}, u32[]{:S(2)}) collective-permute-start(bf16[14,3,256]{2,1,0:T(4,128)(2,1)S(1)} %get-tuple-element.53), channel_id=1, source_target_pairs={{0,4},{4,8},{8,12},{12,16},{16,20},{20,24},{24,28},{28,32},{32,36}... | collective-permute-start | bytes 64520 | tf_op jit(solution)/shard_map/ppermute | solution.py:20
  20.9 1.9 %collective-permute-start.1 = (bf16[14,3,256]{2,1,0:T(4,128)(2,1)S(1)}, bf16[14,3,256]{2,1,0:T(4,128)(2,1)S(1)}, u32[]{:S(2)}, u32[]{:S(2)}) collective-permute-start(bf16[14,3,256]{2,1,0:T(4,128)(2,1)S(1)} %get-tuple-element.54), channel_id=1, source_target_pairs={{4,0},{8,4},{12,8},{16,12},{20,16},{24,20},{28,24},{32,28},{36,32}... | collective-permute-start | bytes 64520 | tf_op jit(solution)/shard_map/ppermute | solution.py:22
  26.1 1.6 pad_maximum_fusion
  27.7 2.8 %collective-permute-start.3 = (f32[144,128]{1,0:T(8,128)S(1)}, f32[144,128]{1,0:T(8,128)S(1)}, u32[]{:S(2)}, u32[]{:S(2)}) collective-permute-start(f32[144,128]{1,0:T(8,128)S(1)} %constant_dynamic-update-slice_fusion.14), channel_id=1, source_target_pairs={{0,128},{4,132},{8,136},{12,140},{16,144},{20,148},{24,152},{28,15... | collective-permute-start | bytes 221192 | tf_op jit(solution)/shard_map/ppermute | solution.py:62
  30.6 1.9 %collective-permute-done.3 = f32[144,128]{1,0:T(8,128)S(1)} collective-permute-done((f32[144,128]{1,0:T(8,128)S(1)}, f32[144,128]{1,0:T(8,128)S(1)}, u32[]{:S(2)}, u32[]{:S(2)}) %collective-permute-start.3) | collective-permute-done | bytes 73760 | tf_op jit(solution)/shard_map/ppermute | solution.py:62
  35.0 2.0 %collective-permute-start.4 = (f32[288,128]{1,0:T(8,128)S(1)}, f32[288,128]{1,0:T(8,128)}, u32[]{:S(2)}, u32[]{:S(2)}) collective-permute-start(f32[288,128]{1,0:T(8,128)S(1)} %constant_dynamic-update-slice_fusion.12), channel_id=1, source_target_pairs={{0,16},{4,20},{8,24},{12,60},{16,0},{20,4},{24,8},{28,44},{32,48},... | collective-permute-start | bytes 442376 | tf_op jit(solution)/shard_map/ppermute | solution.py:62
  43.5 2.5 %collective-permute-start.5 = (f32[576,128]{1,0:T(8,128)S(1)}, f32[576,128]{1,0:T(8,128)S(1)}, u32[]{:S(2)}, u32[]{:S(2)}) collective-permute-start(f32[576,128]{1,0:T(8,128)S(1)} %constant_dynamic-update-slice_fusion.10), channel_id=1, source_target_pairs={{0,64},{4,196},{8,72},{12,204},{16,80},{20,212},{24,88},{28,220},{... | collective-permute-start | bytes 884744 | tf_op jit(solution)/shard_map/ppermute | solution.py:62
  46.2 4.1 %collective-permute-done.5 = f32[576,128]{1,0:T(8,128)S(1)} collective-permute-done((f32[576,128]{1,0:T(8,128)S(1)}, f32[576,128]{1,0:T(8,128)S(1)}, u32[]{:S(2)}, u32[]{:S(2)}) %collective-permute-start.5) | collective-permute-done | bytes 294944 | tf_op jit(solution)/shard_map/ppermute | solution.py:62
  50.4 1.4 collective-permute-start.8
  51.7 2.6 %collective-permute-start.9 = (bf16[6,66,256]{2,1,0:T(8,128)(2,1)S(1)}, bf16[6,66,256]{2,1,0:T(8,128)(2,1)S(1)}, u32[]{:S(2)}, u32[]{:S(2)}) collective-permute-start(bf16[6,66,256]{2,1,0:T(8,128)(2,1)S(1)} %fusion.17), channel_id=1, source_target_pairs={{0,2},{1,3},{2,0},{3,1},{4,6},{5,7},{6,4},{7,5},{8,10},{9,11},{10,... | collective-permute-start | bytes 608264 | tf_op jit(solution)/shard_map/ppermute | solution.py:274
  55.4 5.2 %collective-permute-start.6 = (f32[1152,128]{1,0:T(8,128)S(1)}, f32[1152,128]{1,0:T(8,128)S(1)}, u32[]{:S(2)}, u32[]{:S(2)}) collective-permute-start(f32[1152,128]{1,0:T(8,128)S(1)} %constant_dynamic-update-slice_fusion.8), channel_id=1, source_target_pairs={{0,8},{4,60},{8,0},{12,20},{16,24},{20,12},{24,16},{28,36},{32,40}... | collective-permute-start | bytes 1769480 | tf_op jit(solution)/shard_map/ppermute | solution.py:62
  67.0 2.7 %pad_slice_fusion.6 = (bf16[24,64,256]{2,1,0:T(8,128)(2,1)S(1)}, bf16[24,64,256]{2,1,0:T(8,128)(2,1)}, bf16[24,64,256]{2,1,0:T(8,128)(2,1)}, bf16[24,64,256]{2,1...) fusion(bf16[24,66,256]{2,1,0:T(8,128)(2,1)S(1)} %constant_dynam, ...), kind=kLoop, calls=%fused_computation.155 | loop fusion | bytes 10321920 | tf_op jit(solution)/shard_map/slice | solution.py:300
  69.8 3.8 %collective-permute-start.7 = (f32[2304,128]{1,0:T(8,128)S(1)}, f32[2304,128]{1,0:T(8,128)S(1)}, u32[]{:S(2)}, u32[]{:S(2)}) collective-permute-start(f32[2304,128]{1,0:T(8,128)S(1)} %constant_dynamic-update-slice_fusion.6), channel_id=1, source_target_pairs={{0,4},{4,0},{8,12},{12,8},{16,20},{20,16},{24,28},{28,24},{32,36},... | collective-permute-start | bytes 3538952 | tf_op jit(solution)/shard_map/ppermute | solution.py:62
  74.7 1.2 fusion.9
  76.5 1.6 slice.261
  78.5 2.2 %gather_fusion.1 = f32[32,128]{1,0:T(8,128)S(1)} fusion(f32[4096,128]{1,0:T(8,128)} %bitcast.186, s32[1024]{0:T(1024)S(1)} %pad_clamp_fusion), kind=kCustom, calls=%fused_computation.1 | custom fusion | bytes 32896 | tf_op jit(solution)/shard_map/gather | solution.py:288
  80.7 2.1 %convert_reduce_fusion = (f32[128]{0:T(128)S(1)}, bf16[1536,128]{1,0:T(8,128)(2,1)S(1)}) fusion(f32[1536,128]{1,0:T(8,128)} %fusion.9, f32[32,128]{1,0:T(8,128)S(1)} %gather_fusion.1, f32[32]{0:T(128)S(1)} %fusion.3, s32[1536]{0:T(1024)S(1)} %eq.102), kind=kOutput, calls=%fused_computation.55 | convolution fusion | flops 76337024 | bytes 1202816 | tf_op jit(solution)/shard_map/dot_general | solution.py:289
  82.8 2.3 %convolution_dynamic-update-slice_fusion.8 = f32[2560,128]{1,0:T(8,128)} fusion(bf16[1536,256]{1,0:T(8,128)(2,1)} %bitcast.185, bf16[1536,128]{1,0:T(8,128)(2,1)S(1)} %get-tuple-element.75), kind=kOutput, calls=%fused_computation.31 | convolution fusion | flops 100663296 | bytes 1310720 | tf_op jit(solution)/shard_map/dot_general | solution.py:304
  94.3 65.4 %shard_map.112 = (f32[2560,128]{1,0:T(8,128)}, f32[2048,128]{1,0:T(8,128)}) custom-call(f32[2560,128]{1,0:T(8,128)} %pad_dynamic-update-slice_fusion.grads_ref, f32[32,128]{1,0:T(8,128)} %fusion.18.sums_ref), custom_call_target="tpu_custom_call" | custom-call | tf_op jit(solution)/shard_map/pallas_call | solution.py:169
  159.7 2.4 %slice.251 = f32[2304,128]{1,0:T(8,128)} slice(f32[2560,128]{1,0:T(8,128)} %get-tuple-element.50), slice={[0:2304], [0:128]} | slice | bytes 2359296 | tf_op jit(solution)/shard_map/slice | solution.py:320
  (115 shorter events, 36.7 us)
Async XLA Ops:
  7.8 15.0 %copy-start.1 = (bf16[48,128,256]{2,1,0:T(8,128)(2,1)S(1)}, bf16[48,128,256]{2,1,0:T(8,128)(2,1)}, u32[]{:S(2)}) copy-start(bf16[48,128,256]{2,1,0:T(8,128)(2,1)} %param.15) | copy-start | bytes 9437188
  8.7 18.9 %collective-permute-start.2 = (f32[72,128]{1,0:T(8,128)S(1)}, f32[72,128]{1,0:T(8,128)S(1)}, u32[]{:S(2)}, u32[]{:S(2)}) collective-permute-start(f32[72,128]{1,0:T(8,128)S(1)} %get-tuple-element.70), channel_id=1, source_target_pairs={{0,32},{4,36},{8,40},{12,44},{16,48},{20,52},{24,56},{28,60},{32,0... | collective-permute-start | bytes 110600 | tf_op jit(solution)/shard_map/ppermute | solution.py:62
  17.4 7.5 %collective-permute-start = (bf16[14,3,256]{2,1,0:T(4,128)(2,1)S(1)}, bf16[14,3,256]{2,1,0:T(4,128)(2,1)S(1)}, u32[]{:S(2)}, u32[]{:S(2)}) collective-permute-start(bf16[14,3,256]{2,1,0:T(4,128)(2,1)S(1)} %get-tuple-element.53), channel_id=1, source_target_pairs={{0,4},{4,8},{8,12},{12,16},{16,20},{20,24},{24,28},{28,32},{32,36}... | collective-permute-start | bytes 64520 | tf_op jit(solution)/shard_map/ppermute | solution.py:20
  20.8 3.0 %copy-start.10 = (s32[32]{0:T(128)S(1)}, s32[32]{0:T(128)}, u32[]{:S(2)}) copy-start(s32[32]{0:T(128)} %param.21) | copy-start | bytes 388
  20.9 3.0 %copy-start = (s32[64]{0:T(128)S(1)}, s32[64]{0:T(128)}, u32[]{:S(2)}) copy-start(s32[64]{0:T(128)} %constant.344.clone) | copy-start | bytes 772
  20.9 5.2 %collective-permute-start.1 = (bf16[14,3,256]{2,1,0:T(4,128)(2,1)S(1)}, bf16[14,3,256]{2,1,0:T(4,128)(2,1)S(1)}, u32[]{:S(2)}, u32[]{:S(2)}) collective-permute-start(bf16[14,3,256]{2,1,0:T(4,128)(2,1)S(1)} %get-tuple-element.54), channel_id=1, source_target_pairs={{4,0},{8,4},{12,8},{16,12},{20,16},{24,20},{28,24},{32,28},{36,32}... | collective-permute-start | bytes 64520 | tf_op jit(solution)/shard_map/ppermute | solution.py:22
  27.7 4.8 %collective-permute-start.3 = (f32[144,128]{1,0:T(8,128)S(1)}, f32[144,128]{1,0:T(8,128)S(1)}, u32[]{:S(2)}, u32[]{:S(2)}) collective-permute-start(f32[144,128]{1,0:T(8,128)S(1)} %constant_dynamic-update-slice_fusion.14), channel_id=1, source_target_pairs={{0,128},{4,132},{8,136},{12,140},{16,144},{20,148},{24,152},{28,15... | collective-permute-start | bytes 221192 | tf_op jit(solution)/shard_map/ppermute | solution.py:62
  32.5 1.3 copy-start.6
  35.0 7.6 %collective-permute-start.4 = (f32[288,128]{1,0:T(8,128)S(1)}, f32[288,128]{1,0:T(8,128)}, u32[]{:S(2)}, u32[]{:S(2)}) collective-permute-start(f32[288,128]{1,0:T(8,128)S(1)} %constant_dynamic-update-slice_fusion.12), channel_id=1, source_target_pairs={{0,16},{4,20},{8,24},{12,60},{16,0},{20,4},{24,8},{28,44},{32,48},... | collective-permute-start | bytes 442376 | tf_op jit(solution)/shard_map/ppermute | solution.py:62
  39.0 0.7 copy-start.9
  43.5 6.9 %collective-permute-start.5 = (f32[576,128]{1,0:T(8,128)S(1)}, f32[576,128]{1,0:T(8,128)S(1)}, u32[]{:S(2)}, u32[]{:S(2)}) collective-permute-start(f32[576,128]{1,0:T(8,128)S(1)} %constant_dynamic-update-slice_fusion.10), channel_id=1, source_target_pairs={{0,64},{4,196},{8,72},{12,204},{16,80},{20,212},{24,88},{28,220},{... | collective-permute-start | bytes 884744 | tf_op jit(solution)/shard_map/ppermute | solution.py:62
  50.4 10.5 %collective-permute-start.8 = (bf16[6,66,256]{2,1,0:T(8,128)(2,1)S(1)}, bf16[6,66,256]{2,1,0:T(8,128)(2,1)S(1)}, u32[]{:S(2)}, u32[]{:S(2)}) collective-permute-start(bf16[6,66,256]{2,1,0:T(8,128)(2,1)S(1)} %fusion.17), channel_id=1, source_target_pairs={{0,1},{1,2},{2,3},{3,0},{4,5},{5,6},{6,7},{7,4},{8,9},{9,10},{10,1... | collective-permute-start | bytes 608264 | tf_op jit(solution)/shard_map/ppermute | solution.py:274
  51.7 10.3 %collective-permute-start.9 = (bf16[6,66,256]{2,1,0:T(8,128)(2,1)S(1)}, bf16[6,66,256]{2,1,0:T(8,128)(2,1)S(1)}, u32[]{:S(2)}, u32[]{:S(2)}) collective-permute-start(bf16[6,66,256]{2,1,0:T(8,128)(2,1)S(1)} %fusion.17), channel_id=1, source_target_pairs={{0,2},{1,3},{2,0},{3,1},{4,6},{5,7},{6,4},{7,5},{8,10},{9,11},{10,... | collective-permute-start | bytes 608264 | tf_op jit(solution)/shard_map/ppermute | solution.py:274
  54.4 7.7 %collective-permute-start.10 = (bf16[6,66,256]{2,1,0:T(8,128)(2,1)S(1)}, bf16[6,66,256]{2,1,0:T(8,128)(2,1)S(1)}, u32[]{:S(2)}, u32[]{:S(2)}) collective-permute-start(bf16[6,66,256]{2,1,0:T(8,128)(2,1)S(1)} %fusion.17), channel_id=1, source_target_pairs={{0,3},{1,0},{2,1},{3,2},{4,7},{5,4},{6,5},{7,6},{8,11},{9,8},{10,9... | collective-permute-start | bytes 608264 | tf_op jit(solution)/shard_map/ppermute | solution.py:274
  55.4 14.3 %collective-permute-start.6 = (f32[1152,128]{1,0:T(8,128)S(1)}, f32[1152,128]{1,0:T(8,128)S(1)}, u32[]{:S(2)}, u32[]{:S(2)}) collective-permute-start(f32[1152,128]{1,0:T(8,128)S(1)} %constant_dynamic-update-slice_fusion.8), channel_id=1, source_target_pairs={{0,8},{4,60},{8,0},{12,20},{16,24},{20,12},{24,16},{28,36},{32,40}... | collective-permute-start | bytes 1769480 | tf_op jit(solution)/shard_map/ppermute | solution.py:62
  62.2 1.1 copy-start.8
  67.0 6.5 %copy-start.11 = (f32[128]{0:T(128)S(1)}, f32[128]{0:T(128)}, u32[]{:S(2)}) copy-start(f32[128]{0:T(128)} %param.19) | copy-start | bytes 1540
  69.8 6.4 %collective-permute-start.7 = (f32[2304,128]{1,0:T(8,128)S(1)}, f32[2304,128]{1,0:T(8,128)S(1)}, u32[]{:S(2)}, u32[]{:S(2)}) collective-permute-start(f32[2304,128]{1,0:T(8,128)S(1)} %constant_dynamic-update-slice_fusion.6), channel_id=1, source_target_pairs={{0,4},{4,0},{8,12},{12,8},{16,20},{20,16},{24,28},{28,24},{32,36},... | collective-permute-start | bytes 3538952 | tf_op jit(solution)/shard_map/ppermute | solution.py:62
  80.7 4.4 %copy-start.5 = (bf16[24,64,256]{2,1,0:T(8,128)(2,1)S(1)}, bf16[24,64,256]{2,1,0:T(8,128)(2,1)}, u32[]{:S(2)}) copy-start(bf16[24,64,256]{2,1,0:T(8,128)(2,1)} %get-tuple-element.63) | copy-start | bytes 2359300
  80.7 5.4 %copy-start.4 = (bf16[24,64,256]{2,1,0:T(8,128)(2,1)S(1)}, bf16[24,64,256]{2,1,0:T(8,128)(2,1)}, u32[]{:S(2)}) copy-start(bf16[24,64,256]{2,1,0:T(8,128)(2,1)} %get-tuple-element.64) | copy-start | bytes 2359300
  82.8 4.4 %copy-start.3 = (bf16[24,64,256]{2,1,0:T(8,128)(2,1)S(1)}, bf16[24,64,256]{2,1,0:T(8,128)(2,1)}, u32[]{:S(2)}) copy-start(bf16[24,64,256]{2,1,0:T(8,128)(2,1)} %get-tuple-element.69) | copy-start | bytes 2359300
  85.1 3.2 %copy-start.2 = (bf16[24,64,256]{2,1,0:T(8,128)(2,1)S(1)}, bf16[24,64,256]{2,1,0:T(8,128)(2,1)}, u32[]{:S(2)}) copy-start(bf16[24,64,256]{2,1,0:T(8,128)(2,1)} %get-tuple-element.68) | copy-start | bytes 2359300
  159.7 4.0 %copy-start.7 = (f32[2048,128]{1,0:T(8,128)S(1)}, f32[2048,128]{1,0:T(8,128)}, u32[]{:S(2)}) copy-start(f32[2048,128]{1,0:T(8,128)} %get-tuple-element.49) | copy-start | bytes 3145732

commit v10 on v9

--- a/solution.py
+++ b/solution.py
@@ -294,15 +294,25 @@
         preferred_element_type=jnp.float32,
     )
     deep_grad = (pixel_grad * swish_slope(deep_pre.reshape(-1, width_deep))).astype(jnp.bfloat16)
+    deep_width = -(-padded_deep.shape[1] // 16) * 16
+    wide_deep = jnp.pad(padded_deep, ((0, 0), (0, deep_width - padded_deep.shape[1]), (0, 0)))
+    grid_grad = deep_grad.reshape(half_rows, half_cols, width_deep)
+    placed_grads = [
+        jnp.pad(
+            grid_grad, ((0, 0), (shift_col, deep_width - half_cols - shift_col), (0, 0))
+        ).reshape(-1, width_deep)
+        for shift_col in range(3)
+    ]
     pieces = []
     for shift_row in range(3):
+        band = wide_deep[shift_row : shift_row + half_rows].reshape(-1, channels)
         for shift_col in range(3):
-            window = padded_deep[
-                shift_row : shift_row + half_rows, shift_col : shift_col + half_cols
-            ].reshape(-1, channels)
             pieces.append(
                 lax.dot_general(
-                    window, deep_grad, (((0,), (0,)), ((), ())), preferred_element_type=jnp.float32
+                    band,
+                    placed_grads[shift_col],
+                    (((0,), (0,)), ((), ())),
+                    preferred_element_type=jnp.float32,
                 )
             )
     local_bias = jnp.sum(deep_grad.astype(jnp.float32), axis=0)

time: 166 us -> 154 us (0.928)
  matrix products: 22.8 us -> 15.1 us
  local copies, waits for them, and re-layouts: 22 us -> 18.8 us
  waiting for transfers between devices: 8.36 us -> 11 us
  other arithmetic: 10.3 us -> 8.01 us
    dot_general x9, matrix products: 10.7 us -> 4.34 us  [body(): lax.dot_general(band, placed_grads[shift_col], (((0,), (0,)), ((), ())),...]
    slice x1 -> x0, local copies, waits for them, and re-layouts: 2.69 us -> none  [body(): padded_deep[shift_row:shift_row + half_rows, shift_col:shift_col + half_c...]
  transfers between devices with their start and end apart: 11 -> 11, of which waited for: 4 -> 6; matrix products, arithmetic and copies ran while one was open for 12% -> 9% of each run, Pallas kernels for 0% -> 0%
where the time goes in v10:
time: 154 us
  Pallas kernels  65.7 us (43%)
  starting transfers between devices  33.4 us (22%)
  local copies, waits for them, and re-layouts  18.8 us (12%)
  matrix products  15.1 us (10%)
  waiting for transfers between devices  11 us (7%)
  other arithmetic  8.01 us (5%)
  between operations  1.61 us (1%)
    pallas_call x1, Pallas kernels, tree_sum(): pl.pallas_call(functools.partial(tree_kernel, count, chunk, width, dists,...  65.7 us
    ppermute x6, starting transfers between devices, tree_gather(): other = lax.ppermute(held, axis, pairs)  23 us
    ppermute x6, waiting for transfers between devices, tree_gather(): other = lax.ppermute(held, axis, pairs)  7.37 us
    dot_general x18, matrix products, convolve(): jnp.dot(band, weight[shift_row, shift_col], preferred_element_type=jnp.fl...  7.3 us
    ppermute x3, starting transfers between devices, body(): lax.ppermute(pooled, 'chan', [(i, (i + shift) % chan_count) for i in rang...  5.07 us
    dot_general x9, matrix products, body(): lax.dot_general(band, placed_grads[shift_col], (((0,), (0,)), ((), ())),...  4.34 us
    another operation x3, other arithmetic  3.97 us
    ppermute x1, starting transfers between devices, with_halo(): lax.ppermute(tail, axis, [(i, (i + 1) % count) for i in range(ends)])  3.49 us
  transfers between devices with their start and end apart: 11, of which 6 were waited for; matrix products, arithmetic and copies ran while one was open for 9% of the time, Pallas kernels for 0%

profile of v10, /device:TPU:1, one launch (start us, length us, event | category | flops | bytes accessed | tf_op | source)
XLA Modules:
  0.0 153.7 jit_solution(1797637801526967913)
XLA Ops:
  2.2 1.3 and_reduce_fusion
  3.6 2.7 %broadcast_select_fusion = f32[1,32]{1,0:T(1,128)S(1)} fusion(pred[]{:T(512)} %and_reduce_fusion, s32[]{:T(128)} %bitcast.2, s32[]{:T(128)} %bitcast.3, f32[1,32]{1,0:T(1,128)S(1)} %bitcast.200, s32[32]{0:T(128)} %param.21), kind=kLoop, calls=%fused_computation.177 | loop fusion | flops 64 | bytes 393 | tf_op jit(solution)/shard_map/select.4
  6.2 1.6 %scatter.11 = f32[8,128]{1,0:T(8,128)S(1)} dynamic-update-slice(f32[8,128]{1,0:T(8,128)S(1)} %scatter.10, f32[1,32]{1,0:T(1,128)S(1)} %broadcast_select_fusion, s32[]{:T(128)} %bitcast.2, s32[]{:T(128)} %bitcast.3) | dynamic-update-slice | bytes 260 | tf_op jit(solution)/shard_map/scatter | solution.py:242
  8.6 7.7 %collective-permute-start.2 = (f32[72,128]{1,0:T(8,128)S(1)}, f32[72,128]{1,0:T(8,128)S(1)}, u32[]{:S(2)}, u32[]{:S(2)}) collective-permute-start(f32[72,128]{1,0:T(8,128)S(1)} %get-tuple-element.61), channel_id=1, source_target_pairs={{0,32},{4,36},{8,40},{12,44},{16,48},{20,52},{24,56},{28,60},{32,0... | collective-permute-start | bytes 110600 | tf_op jit(solution)/shard_map/ppermute | solution.py:62
  17.3 3.5 %collective-permute-start = (bf16[14,3,256]{2,1,0:T(4,128)(2,1)S(1)}, bf16[14,3,256]{2,1,0:T(4,128)(2,1)S(1)}, u32[]{:S(2)}, u32[]{:S(2)}) collective-permute-start(bf16[14,3,256]{2,1,0:T(4,128)(2,1)S(1)} %get-tuple-element.53), channel_id=1, source_target_pairs={{0,4},{4,8},{8,12},{12,16},{16,20},{20,24},{24,28},{28,32},{32,36}... | collective-permute-start | bytes 64520 | tf_op jit(solution)/shard_map/ppermute | solution.py:20
  20.9 1.9 %collective-permute-start.1 = (bf16[14,3,256]{2,1,0:T(4,128)(2,1)S(1)}, bf16[14,3,256]{2,1,0:T(4,128)(2,1)S(1)}, u32[]{:S(2)}, u32[]{:S(2)}) collective-permute-start(bf16[14,3,256]{2,1,0:T(4,128)(2,1)S(1)} %get-tuple-element.54), channel_id=1, source_target_pairs={{4,0},{8,4},{12,8},{16,12},{20,16},{24,20},{28,24},{32,28},{36,32}... | collective-permute-start | bytes 64520 | tf_op jit(solution)/shard_map/ppermute | solution.py:22
  24.0 2.1 %collective-permute-done.1 = bf16[14,3,256]{2,1,0:T(4,128)(2,1)S(1)} collective-permute-done((bf16[14,3,256]{2,1,0:T(4,128)(2,1)S(1)}, bf16[14,3,256]{2,1,0:T(4,128)(2,1)S(1)}, u32[]{:S(2)}, u32[]{:S(2)}) %collective-permute-start.1) | collective-permute-done | bytes 21536 | tf_op jit(solution)/shard_map/ppermute | solution.py:22
  26.5 2.8 %collective-permute-start.3 = (f32[144,128]{1,0:T(8,128)S(1)}, f32[144,128]{1,0:T(8,128)S(1)}, u32[]{:S(2)}, u32[]{:S(2)}) collective-permute-start(f32[144,128]{1,0:T(8,128)S(1)} %constant_dynamic-update-slice_fusion.14), channel_id=1, source_target_pairs={{0,128},{4,132},{8,136},{12,140},{16,144},{20,148},{24,152},{28,15... | collective-permute-start | bytes 221192 | tf_op jit(solution)/shard_map/ppermute | solution.py:62
  29.4 1.9 %collective-permute-done.3 = f32[144,128]{1,0:T(8,128)S(1)} collective-permute-done((f32[144,128]{1,0:T(8,128)S(1)}, f32[144,128]{1,0:T(8,128)S(1)}, u32[]{:S(2)}, u32[]{:S(2)}) %collective-permute-start.3) | collective-permute-done | bytes 73760 | tf_op jit(solution)/shard_map/ppermute | solution.py:62
  33.8 2.1 %collective-permute-start.4 = (f32[288,128]{1,0:T(8,128)S(1)}, f32[288,128]{1,0:T(8,128)}, u32[]{:S(2)}, u32[]{:S(2)}) collective-permute-start(f32[288,128]{1,0:T(8,128)S(1)} %constant_dynamic-update-slice_fusion.12), channel_id=1, source_target_pairs={{0,16},{4,20},{8,24},{12,60},{16,0},{20,4},{24,8},{28,44},{32,48},... | collective-permute-start | bytes 442376 | tf_op jit(solution)/shard_map/ppermute | solution.py:62
  40.2 1.1 reduce_sum.28
  42.3 2.6 %collective-permute-start.5 = (f32[576,128]{1,0:T(8,128)S(1)}, f32[576,128]{1,0:T(8,128)S(1)}, u32[]{:S(2)}, u32[]{:S(2)}) collective-permute-start(f32[576,128]{1,0:T(8,128)S(1)} %constant_dynamic-update-slice_fusion.10), channel_id=1, source_target_pairs={{0,64},{4,196},{8,72},{12,204},{16,80},{20,212},{24,88},{28,220},{... | collective-permute-start | bytes 884744 | tf_op jit(solution)/shard_map/ppermute | solution.py:62
  45.0 4.1 %collective-permute-done.5 = f32[576,128]{1,0:T(8,128)S(1)} collective-permute-done((f32[576,128]{1,0:T(8,128)S(1)}, f32[576,128]{1,0:T(8,128)S(1)}, u32[]{:S(2)}, u32[]{:S(2)}) %collective-permute-start.5) | collective-permute-done | bytes 294944 | tf_op jit(solution)/shard_map/ppermute | solution.py:62
  49.2 1.4 collective-permute-start.8
  50.6 2.6 %collective-permute-start.9 = (bf16[6,66,256]{2,1,0:T(8,128)(2,1)S(1)}, bf16[6,66,256]{2,1,0:T(8,128)(2,1)S(1)}, u32[]{:S(2)}, u32[]{:S(2)}) collective-permute-start(bf16[6,66,256]{2,1,0:T(8,128)(2,1)S(1)} %fusion.44), channel_id=1, source_target_pairs={{0,2},{1,3},{2,0},{3,1},{4,6},{5,7},{6,4},{7,5},{8,10},{9,11},{10,... | collective-permute-start | bytes 608264 | tf_op jit(solution)/shard_map/ppermute | solution.py:274
  54.3 5.1 %collective-permute-start.6 = (f32[1152,128]{1,0:T(8,128)S(1)}, f32[1152,128]{1,0:T(8,128)S(1)}, u32[]{:S(2)}, u32[]{:S(2)}) collective-permute-start(f32[1152,128]{1,0:T(8,128)S(1)} %constant_dynamic-update-slice_fusion.8), channel_id=1, source_target_pairs={{0,8},{4,60},{8,0},{12,20},{16,24},{20,12},{24,16},{28,36},{32,40}... | collective-permute-start | bytes 1769480 | tf_op jit(solution)/shard_map/ppermute | solution.py:62
  59.6 1.6 %collective-permute-done.9 = bf16[6,66,256]{2,1,0:T(8,128)(2,1)S(1)} collective-permute-done((bf16[6,66,256]{2,1,0:T(8,128)(2,1)S(1)}, bf16[6,66,256]{2,1,0:T(8,128)(2,1)S(1)}, u32[]{:S(2)}, u32[]{:S(2)}) %collective-permute-start.9) | collective-permute-done | bytes 202784 | tf_op jit(solution)/shard_map/ppermute | solution.py:274
  66.7 2.7 %collective-permute-start.7 = (f32[2304,128]{1,0:T(8,128)S(1)}, f32[2304,128]{1,0:T(8,128)S(1)}, u32[]{:S(2)}, u32[]{:S(2)}) collective-permute-start(f32[2304,128]{1,0:T(8,128)S(1)} %constant_dynamic-update-slice_fusion.6), channel_id=1, source_target_pairs={{0,4},{4,0},{8,12},{12,8},{16,20},{20,16},{24,28},{28,24},{32,36},... | collective-permute-start | bytes 3538952 | tf_op jit(solution)/shard_map/ppermute | solution.py:62
  72.2 1.6 %slice.225 = f32[64,64,128]{2,1,0:T(8,128)} slice(f32[64,72,128]{2,1,0:T(8,128)S(1)} %bitcast.180), slice={[0:64], [0:64], [0:128]} | slice | bytes 4194304 | tf_op jit(solution)/shard_map/slice | solution.py:266
  74.2 2.2 %gather_fusion.1 = f32[32,128]{1,0:T(8,128)S(1)} fusion(f32[4096,128]{1,0:T(8,128)} %bitcast.187, s32[1024]{0:T(1024)S(1)} %pad_clamp_fusion), kind=kCustom, calls=%fused_computation.1 | custom fusion | bytes 32896 | tf_op jit(solution)/shard_map/gather | solution.py:288
  82.8 65.7 %shard_map.112 = (f32[2560,128]{1,0:T(8,128)}, f32[2048,128]{1,0:T(8,128)}) custom-call(f32[2560,128]{1,0:T(8,128)} %copy-done.2, f32[32,128]{1,0:T(8,128)} %fusion.45.sums_ref), custom_call_target="tpu_custom_call" | custom-call | tf_op jit(solution)/shard_map/pallas_call | solution.py:169
  148.5 2.4 %slice.215 = f32[2304,128]{1,0:T(8,128)} slice(f32[2560,128]{1,0:T(8,128)} %get-tuple-element.50), slice={[0:2304], [0:128]} | slice | bytes 2359296 | tf_op jit(solution)/shard_map/slice | solution.py:330
  150.9 1.2 slice_bitcast_fusion
  152.5 1.2 convolution_divide_fusion
  (107 shorter events, 29.0 us)
Async XLA Ops:
  8.6 17.9 %collective-permute-start.2 = (f32[72,128]{1,0:T(8,128)S(1)}, f32[72,128]{1,0:T(8,128)S(1)}, u32[]{:S(2)}, u32[]{:S(2)}) collective-permute-start(f32[72,128]{1,0:T(8,128)S(1)} %get-tuple-element.61), channel_id=1, source_target_pairs={{0,32},{4,36},{8,40},{12,44},{16,48},{20,52},{24,56},{28,60},{32,0... | collective-permute-start | bytes 110600 | tf_op jit(solution)/shard_map/ppermute | solution.py:62
  16.3 6.5 %copy-start.1 = (bf16[48,128,256]{2,1,0:T(8,128)(2,1)S(1)}, bf16[48,128,256]{2,1,0:T(8,128)(2,1)}, u32[]{:S(2)}) copy-start(bf16[48,128,256]{2,1,0:T(8,128)(2,1)} %param.15) | copy-start | bytes 9437188
  17.3 6.6 %collective-permute-start = (bf16[14,3,256]{2,1,0:T(4,128)(2,1)S(1)}, bf16[14,3,256]{2,1,0:T(4,128)(2,1)S(1)}, u32[]{:S(2)}, u32[]{:S(2)}) collective-permute-start(bf16[14,3,256]{2,1,0:T(4,128)(2,1)S(1)} %get-tuple-element.53), channel_id=1, source_target_pairs={{0,4},{4,8},{8,12},{12,16},{16,20},{20,24},{24,28},{28,32},{32,36}... | collective-permute-start | bytes 64520 | tf_op jit(solution)/shard_map/ppermute | solution.py:20
  20.8 2.1 %copy-start.7 = (s32[32]{0:T(128)S(1)}, s32[32]{0:T(128)}, u32[]{:S(2)}) copy-start(s32[32]{0:T(128)} %param.21) | copy-start | bytes 388
  20.8 2.1 %copy-start = (s32[64]{0:T(128)S(1)}, s32[64]{0:T(128)}, u32[]{:S(2)}) copy-start(s32[64]{0:T(128)} %constant.344.clone) | copy-start | bytes 772
  20.9 5.2 %collective-permute-start.1 = (bf16[14,3,256]{2,1,0:T(4,128)(2,1)S(1)}, bf16[14,3,256]{2,1,0:T(4,128)(2,1)S(1)}, u32[]{:S(2)}, u32[]{:S(2)}) collective-permute-start(bf16[14,3,256]{2,1,0:T(4,128)(2,1)S(1)} %get-tuple-element.54), channel_id=1, source_target_pairs={{4,0},{8,4},{12,8},{16,12},{20,16},{24,20},{28,24},{32,28},{36,32}... | collective-permute-start | bytes 64520 | tf_op jit(solution)/shard_map/ppermute | solution.py:22
  26.5 4.8 %collective-permute-start.3 = (f32[144,128]{1,0:T(8,128)S(1)}, f32[144,128]{1,0:T(8,128)S(1)}, u32[]{:S(2)}, u32[]{:S(2)}) collective-permute-start(f32[144,128]{1,0:T(8,128)S(1)} %constant_dynamic-update-slice_fusion.14), channel_id=1, source_target_pairs={{0,128},{4,132},{8,136},{12,140},{16,144},{20,148},{24,152},{28,15... | collective-permute-start | bytes 221192 | tf_op jit(solution)/shard_map/ppermute | solution.py:62
  31.3 1.3 copy-start.3
  33.8 7.6 %collective-permute-start.4 = (f32[288,128]{1,0:T(8,128)S(1)}, f32[288,128]{1,0:T(8,128)}, u32[]{:S(2)}, u32[]{:S(2)}) collective-permute-start(f32[288,128]{1,0:T(8,128)S(1)} %constant_dynamic-update-slice_fusion.12), channel_id=1, source_target_pairs={{0,16},{4,20},{8,24},{12,60},{16,0},{20,4},{24,8},{28,44},{32,48},... | collective-permute-start | bytes 442376 | tf_op jit(solution)/shard_map/ppermute | solution.py:62
  37.9 0.7 copy-start.6
  42.3 6.9 %collective-permute-start.5 = (f32[576,128]{1,0:T(8,128)S(1)}, f32[576,128]{1,0:T(8,128)S(1)}, u32[]{:S(2)}, u32[]{:S(2)}) collective-permute-start(f32[576,128]{1,0:T(8,128)S(1)} %constant_dynamic-update-slice_fusion.10), channel_id=1, source_target_pairs={{0,64},{4,196},{8,72},{12,204},{16,80},{20,212},{24,88},{28,220},{... | collective-permute-start | bytes 884744 | tf_op jit(solution)/shard_map/ppermute | solution.py:62
  49.2 10.4 %collective-permute-start.8 = (bf16[6,66,256]{2,1,0:T(8,128)(2,1)S(1)}, bf16[6,66,256]{2,1,0:T(8,128)(2,1)S(1)}, u32[]{:S(2)}, u32[]{:S(2)}) collective-permute-start(bf16[6,66,256]{2,1,0:T(8,128)(2,1)S(1)} %fusion.44), channel_id=1, source_target_pairs={{0,1},{1,2},{2,3},{3,0},{4,5},{5,6},{6,7},{7,4},{8,9},{9,10},{10,1... | collective-permute-start | bytes 608264 | tf_op jit(solution)/shard_map/ppermute | solution.py:274
  50.6 10.6 %collective-permute-start.9 = (bf16[6,66,256]{2,1,0:T(8,128)(2,1)S(1)}, bf16[6,66,256]{2,1,0:T(8,128)(2,1)S(1)}, u32[]{:S(2)}, u32[]{:S(2)}) collective-permute-start(bf16[6,66,256]{2,1,0:T(8,128)(2,1)S(1)} %fusion.44), channel_id=1, source_target_pairs={{0,2},{1,3},{2,0},{3,1},{4,6},{5,7},{6,4},{7,5},{8,10},{9,11},{10,... | collective-permute-start | bytes 608264 | tf_op jit(solution)/shard_map/ppermute | solution.py:274
  53.2 8.0 %collective-permute-start.10 = (bf16[6,66,256]{2,1,0:T(8,128)(2,1)S(1)}, bf16[6,66,256]{2,1,0:T(8,128)(2,1)S(1)}, u32[]{:S(2)}, u32[]{:S(2)}) collective-permute-start(bf16[6,66,256]{2,1,0:T(8,128)(2,1)S(1)} %fusion.44), channel_id=1, source_target_pairs={{0,3},{1,0},{2,1},{3,2},{4,7},{5,4},{6,5},{7,6},{8,11},{9,8},{10,9... | collective-permute-start | bytes 608264 | tf_op jit(solution)/shard_map/ppermute | solution.py:274
  54.3 12.4 %collective-permute-start.6 = (f32[1152,128]{1,0:T(8,128)S(1)}, f32[1152,128]{1,0:T(8,128)S(1)}, u32[]{:S(2)}, u32[]{:S(2)}) collective-permute-start(f32[1152,128]{1,0:T(8,128)S(1)} %constant_dynamic-update-slice_fusion.8), channel_id=1, source_target_pairs={{0,8},{4,60},{8,0},{12,20},{16,24},{20,12},{24,16},{28,36},{32,40}... | collective-permute-start | bytes 1769480 | tf_op jit(solution)/shard_map/ppermute | solution.py:62
  61.3 1.1 copy-start.5
  65.7 3.7 %copy-start.8 = (f32[128]{0:T(128)S(1)}, f32[128]{0:T(128)}, u32[]{:S(2)}) copy-start(f32[128]{0:T(128)} %param.19) | copy-start | bytes 1540
  66.7 5.1 %collective-permute-start.7 = (f32[2304,128]{1,0:T(8,128)S(1)}, f32[2304,128]{1,0:T(8,128)S(1)}, u32[]{:S(2)}, u32[]{:S(2)}) collective-permute-start(f32[2304,128]{1,0:T(8,128)S(1)} %constant_dynamic-update-slice_fusion.6), channel_id=1, source_target_pairs={{0,4},{4,0},{8,12},{12,8},{16,20},{20,16},{24,28},{28,24},{32,36},... | collective-permute-start | bytes 3538952 | tf_op jit(solution)/shard_map/ppermute | solution.py:62
  81.7 1.1 copy-start.2
  148.4 4.0 %copy-start.4 = (f32[2048,128]{1,0:T(8,128)S(1)}, f32[2048,128]{1,0:T(8,128)}, u32[]{:S(2)}) copy-start(f32[2048,128]{1,0:T(8,128)} %get-tuple-element.49) | copy-start | bytes 3145732

commit v11 on v10

--- a/solution.py
+++ b/solution.py
@@ -237,9 +237,9 @@
     flat_labels = labels.reshape(-1)
     member = flat_labels[None, :] == jnp.arange(list_len, dtype=jnp.int32)[:, None]
     part_counts = jnp.sum(member.astype(jnp.float32), axis=1)
-    meta = jnp.zeros((8, lanes), jnp.float32)
-    meta = meta.at[0, :list_len].set(part_counts)
-    meta = meta.at[0, list_len : 2 * list_len].set(slot_ids.astype(jnp.float32))
+    meta = jnp.concatenate(
+        [part_counts, slot_ids.astype(jnp.float32), jnp.zeros((8 * lanes - 2 * list_len,), jnp.float32)]
+    ).reshape(8, lanes)
     packed = jnp.concatenate([embed_grad, meta], axis=0)
     halving = [1 << k for k in range(strip_count.bit_length() - 1)]
     if len(halving) == 6:
@@ -252,8 +252,6 @@
     padded_rows = jnp.pad(section_input, ((1, 1), (0, 0), (0, 0)))
     own_rows = lax.dynamic_slice_in_dim(padded_rows, chan_pos * row_part, row_part + 2, 0)
     extended = with_halo(own_rows, (("strip", 1),), 3)
-    extended, early = lax.optimization_barrier((extended, early))
-    early = tree_gather(early, "strip", order[2:4], shifted)
     hidden = swish(convolve(extended, conv_weight, row_part, col_local + 4) + conv_bias)
     pooled = pool_pairs(hidden)
     column = jnp.arange(half_cols + 2)
@@ -262,10 +260,7 @@
     )
     pooled = jnp.where(outside[None, :, None], jnp.zeros_like(pooled), pooled)
     pooled, early = lax.optimization_barrier((pooled, early))
-    every = tree_gather(early, "strip", order[4:], shifted).reshape(strip_count, owned + 8, lanes)
-    every_grad = every[:, :owned].reshape(strip_count * owned, lanes)
-    every_counts = every[:, owned, :list_len].reshape(-1)
-    every_slots = jnp.round(every[:, owned, list_len : 2 * list_len]).astype(jnp.int32).reshape(-1)
+    early = tree_gather(early, "strip", order[2:4], shifted)
     part_rows = pooled.shape[0]
     gathered = jnp.zeros((chan_count * part_rows,) + pooled.shape[1:], pooled.dtype)
     for shift in range(chan_count):
@@ -276,6 +271,11 @@
             )
         source = (chan_pos + chan_count - shift) % chan_count
         gathered = lax.dynamic_update_slice_in_dim(gathered, block, source * part_rows, 0)
+    gathered, early = lax.optimization_barrier((gathered, early))
+    every = tree_gather(early, "strip", order[4:], shifted).reshape(strip_count, owned + 8, lanes)
+    every_grad = every[:, :owned].reshape(strip_count * owned, lanes)
+    every_counts = every[:, owned, :list_len].reshape(-1)
+    every_slots = jnp.round(every[:, owned, list_len : 2 * list_len]).astype(jnp.int32).reshape(-1)
     padded_deep = jnp.pad(gathered, ((1, 1), (0, 0), (0, 0)))
     half_rows = gathered.shape[0]
     deep_pre = convolve(padded_deep, deep_weight, half_rows, half_cols) + deep_bias

time: 154 us -> 156 us (1.013)
  waiting for transfers between devices: 11 us -> 17.7 us
  other arithmetic: 8.01 us -> 5.55 us
  local copies, waits for them, and re-layouts: 18.8 us -> 16.4 us
    ppermute x6, waiting for transfers between devices: 7.37 us -> 14.8 us  [tree_gather(): other = lax.ppermute(held, axis, pairs)]
    another operation x3 -> x0, other arithmetic: 3.97 us -> none
    scatter x2 -> x0, local copies, waits for them, and re-layouts: 1.58 us -> none  [the longest x1 1.57 us: body(): meta = meta.at[0, list_len:2 * list_len].set(slot_ids.astype(jnp.float32))]
    ppermute x3, waiting for transfers between devices: 1.58 us -> 0.01 us  [body(): lax.ppermute(pooled, 'chan', [(i, (i + shift) % chan_count) for i in rang...]
    unnamed x18 -> x16, local copies, waits for them, and re-layouts: 3.27 us -> 3.27 us
  transfers between devices with their start and end apart: 11 -> 11, of which waited for: 6 -> 6; matrix products, arithmetic and copies ran while one was open for 9% -> 8% of each run, Pallas kernels for 0% -> 0%
where the time goes in v11:
time: 156 us
  Pallas kernels  66.2 us (42%)
  starting transfers between devices  33.5 us (21%)
  waiting for transfers between devices  17.7 us (11%)
  local copies, waits for them, and re-layouts  16.4 us (11%)
  matrix products  15.1 us (10%)
  other arithmetic  5.55 us (4%)
    pallas_call x1, Pallas kernels, tree_sum(): pl.pallas_call(functools.partial(tree_kernel, count, chunk, width, dists,...  66.2 us
    ppermute x6, starting transfers between devices, tree_gather(): other = lax.ppermute(held, axis, pairs)  23 us
    ppermute x6, waiting for transfers between devices, tree_gather(): other = lax.ppermute(held, axis, pairs)  14.8 us
    dot_general x18, matrix products, convolve(): jnp.dot(band, weight[shift_row, shift_col], preferred_element_type=jnp.fl...  7.3 us
    ppermute x3, starting transfers between devices, body(): lax.ppermute(pooled, 'chan', [(i, (i + shift) % chan_count) for i in rang...  5.08 us
    dot_general x9, matrix products, body(): lax.dot_general(band, placed_grads[shift_col], (((0,), (0,)), ((), ())),...  4.33 us
    ppermute x1, starting transfers between devices, with_halo(): lax.ppermute(tail, axis, [(i, (i + 1) % count) for i in range(ends)])  3.49 us
    unnamed x16, local copies, waits for them, and re-layouts  3.27 us
  transfers between devices with their start and end apart: 11, of which 6 were waited for; matrix products, arithmetic and copies ran while one was open for 8% of the time, Pallas kernels for 0%

profile of v11, /device:TPU:1, one launch (start us, length us, event | category | flops | bytes accessed | tf_op | source)
XLA Modules:
  0.0 155.9 jit_solution(1028357085276170526)
XLA Ops:
  2.3 1.4 gather_fusion
  5.3 7.7 %collective-permute-start.2 = (f32[72,128]{1,0:T(8,128)S(1)}, f32[72,128]{1,0:T(8,128)S(1)}, u32[]{:S(2)}, u32[]{:S(2)}) collective-permute-start(f32[72,128]{1,0:T(8,128)S(1)} %get-tuple-element.37), channel_id=1, source_target_pairs={{0,32},{4,36},{8,40},{12,44},{16,48},{20,52},{24,56},{28,60},{32,0... | collective-permute-start | bytes 110600 | tf_op jit(solution)/shard_map/ppermute | solution.py:62
  14.0 3.5 %collective-permute-start = (bf16[14,3,256]{2,1,0:T(4,128)(2,1)S(1)}, bf16[14,3,256]{2,1,0:T(4,128)(2,1)S(1)}, u32[]{:S(2)}, u32[]{:S(2)}) collective-permute-start(bf16[14,3,256]{2,1,0:T(4,128)(2,1)S(1)} %get-tuple-element.29), channel_id=1, source_target_pairs={{0,4},{4,8},{8,12},{12,16},{16,20},{20,24},{24,28},{28,32},{32,36}... | collective-permute-start | bytes 64520 | tf_op jit(solution)/shard_map/ppermute | solution.py:20
  17.5 1.9 %collective-permute-start.1 = (bf16[14,3,256]{2,1,0:T(4,128)(2,1)S(1)}, bf16[14,3,256]{2,1,0:T(4,128)(2,1)S(1)}, u32[]{:S(2)}, u32[]{:S(2)}) collective-permute-start(bf16[14,3,256]{2,1,0:T(4,128)(2,1)S(1)} %get-tuple-element.30), channel_id=1, source_target_pairs={{4,0},{8,4},{12,8},{16,12},{20,16},{24,20},{28,24},{32,28},{36,32}... | collective-permute-start | bytes 64520 | tf_op jit(solution)/shard_map/ppermute | solution.py:22
  19.9 2.8 %collective-permute-done.1 = bf16[14,3,256]{2,1,0:T(4,128)(2,1)S(1)} collective-permute-done((bf16[14,3,256]{2,1,0:T(4,128)(2,1)S(1)}, bf16[14,3,256]{2,1,0:T(4,128)(2,1)S(1)}, u32[]{:S(2)}, u32[]{:S(2)}) %collective-permute-start.1) | collective-permute-done | bytes 21536 | tf_op jit(solution)/shard_map/ppermute | solution.py:22
  30.0 1.1 reduce_sum.27
  31.3 2.8 %collective-permute-start.3 = (f32[144,128]{1,0:T(8,128)S(1)}, f32[144,128]{1,0:T(8,128)S(1)}, u32[]{:S(2)}, u32[]{:S(2)}) collective-permute-start(f32[144,128]{1,0:T(8,128)S(1)} %constant_dynamic-update-slice_fusion.14), channel_id=1, source_target_pairs={{0,128},{4,132},{8,136},{12,140},{16,144},{20,148},{24,152},{28,15... | collective-permute-start | bytes 221192 | tf_op jit(solution)/shard_map/ppermute | solution.py:62
  34.1 1.9 %collective-permute-done.3 = f32[144,128]{1,0:T(8,128)S(1)} collective-permute-done((f32[144,128]{1,0:T(8,128)S(1)}, f32[144,128]{1,0:T(8,128)S(1)}, u32[]{:S(2)}, u32[]{:S(2)}) %collective-permute-start.3) | collective-permute-done | bytes 73760 | tf_op jit(solution)/shard_map/ppermute | solution.py:62
  36.1 1.4 collective-permute-start.4
  37.5 2.6 %collective-permute-start.5 = (bf16[6,66,256]{2,1,0:T(8,128)(2,1)S(1)}, bf16[6,66,256]{2,1,0:T(8,128)(2,1)S(1)}, u32[]{:S(2)}, u32[]{:S(2)}) collective-permute-start(bf16[6,66,256]{2,1,0:T(8,128)(2,1)S(1)} %fusion.49), channel_id=1, source_target_pairs={{0,2},{1,3},{2,0},{3,1},{4,6},{5,7},{6,4},{7,5},{8,10},{9,11},{10,... | collective-permute-start | bytes 608264 | tf_op jit(solution)/shard_map/ppermute | solution.py:269
  40.1 1.1 collective-permute-start.6
  41.2 2.0 %collective-permute-start.7 = (f32[288,128]{1,0:T(8,128)S(1)}, f32[288,128]{1,0:T(8,128)S(1)}, u32[]{:S(2)}, u32[]{:S(2)}) collective-permute-start(f32[288,128]{1,0:T(8,128)S(1)} %constant_dynamic-update-slice_fusion.12), channel_id=1, source_target_pairs={{0,16},{4,20},{8,24},{12,60},{16,0},{20,4},{24,8},{28,44},{32,48},... | collective-permute-start | bytes 442376 | tf_op jit(solution)/shard_map/ppermute | solution.py:62
  43.3 3.1 %collective-permute-done.7 = f32[288,128]{1,0:T(8,128)S(1)} collective-permute-done((f32[288,128]{1,0:T(8,128)S(1)}, f32[288,128]{1,0:T(8,128)S(1)}, u32[]{:S(2)}, u32[]{:S(2)}) %collective-permute-start.7) | collective-permute-done | bytes 147488 | tf_op jit(solution)/shard_map/ppermute | solution.py:62
  46.4 2.7 %collective-permute-start.8 = (f32[576,128]{1,0:T(8,128)S(1)}, f32[576,128]{1,0:T(8,128)S(1)}, u32[]{:S(2)}, u32[]{:S(2)}) collective-permute-start(f32[576,128]{1,0:T(8,128)S(1)} %constant_dynamic-update-slice_fusion.6), channel_id=1, source_target_pairs={{0,64},{4,196},{8,72},{12,204},{16,80},{20,212},{24,88},{28,220},{... | collective-permute-start | bytes 884744 | tf_op jit(solution)/shard_map/ppermute | solution.py:62
  49.3 4.1 %collective-permute-done.8 = f32[576,128]{1,0:T(8,128)S(1)} collective-permute-done((f32[576,128]{1,0:T(8,128)S(1)}, f32[576,128]{1,0:T(8,128)S(1)}, u32[]{:S(2)}, u32[]{:S(2)}) %collective-permute-start.8) | collective-permute-done | bytes 294944 | tf_op jit(solution)/shard_map/ppermute | solution.py:62
  55.7 7.5 %collective-permute-start.9 = (f32[1152,128]{1,0:T(8,128)S(1)}, f32[1152,128]{1,0:T(8,128)S(1)}, u32[]{:S(2)}, u32[]{:S(2)}) collective-permute-start(f32[1152,128]{1,0:T(8,128)S(1)} %constant_dynamic-update-slice_fusion.4), channel_id=1, source_target_pairs={{0,8},{4,60},{8,0},{12,20},{16,24},{20,12},{24,16},{28,36},{32,40}... | collective-permute-start | bytes 1769480 | tf_op jit(solution)/shard_map/ppermute | solution.py:62
  65.9 4.6 %collective-permute-done.9 = f32[1152,128]{1,0:T(8,128)S(1)} collective-permute-done((f32[1152,128]{1,0:T(8,128)S(1)}, f32[1152,128]{1,0:T(8,128)S(1)}, u32[]{:S(2)}, u32[]{:S(2)}) %collective-permute-start.9) | collective-permute-done | bytes 589856 | tf_op jit(solution)/shard_map/ppermute | solution.py:62
  73.9 1.6 %slice.188 = f32[64,64,128]{2,1,0:T(8,128)} slice(f32[64,72,128]{2,1,0:T(8,128)S(1)} %bitcast.177), slice={[0:64], [0:64], [0:128]} | slice | bytes 4194304 | tf_op jit(solution)/shard_map/slice | solution.py:276
  75.9 2.2 %gather_fusion.1 = f32[32,128]{1,0:T(8,128)S(1)} fusion(f32[4096,128]{1,0:T(8,128)} %bitcast.184, s32[1024]{0:T(1024)S(1)} %pad_clamp_fusion), kind=kCustom, calls=%fused_computation.1 | custom fusion | bytes 32896 | tf_op jit(solution)/shard_map/gather | solution.py:288
  83.4 1.1 copy-done.1
  84.5 66.2 %shard_map.112 = (f32[2560,128]{1,0:T(8,128)}, f32[2048,128]{1,0:T(8,128)}) custom-call(f32[2560,128]{1,0:T(8,128)} %copy-done.1, f32[32,128]{1,0:T(8,128)} %fusion.50.sums_ref), custom_call_target="tpu_custom_call" | custom-call | tf_op jit(solution)/shard_map/pallas_call | solution.py:169
  150.7 2.4 %slice.175 = f32[2304,128]{1,0:T(8,128)} slice(f32[2560,128]{1,0:T(8,128)} %get-tuple-element.26), slice={[0:2304], [0:128]} | slice | bytes 2359296 | tf_op jit(solution)/shard_map/slice | solution.py:330
  153.2 1.2 slice_bitcast_fusion
  154.8 1.2 convolution_divide_fusion
  (101 shorter events, 26.1 us)
Async XLA Ops:
  5.3 26.0 %collective-permute-start.2 = (f32[72,128]{1,0:T(8,128)S(1)}, f32[72,128]{1,0:T(8,128)S(1)}, u32[]{:S(2)}, u32[]{:S(2)}) collective-permute-start(f32[72,128]{1,0:T(8,128)S(1)} %get-tuple-element.37), channel_id=1, source_target_pairs={{0,32},{4,36},{8,40},{12,44},{16,48},{20,52},{24,56},{28,60},{32,0... | collective-permute-start | bytes 110600 | tf_op jit(solution)/shard_map/ppermute | solution.py:62
  13.0 6.4 %copy-start = (bf16[48,128,256]{2,1,0:T(8,128)(2,1)S(1)}, bf16[48,128,256]{2,1,0:T(8,128)(2,1)}, u32[]{:S(2)}) copy-start(bf16[48,128,256]{2,1,0:T(8,128)(2,1)} %param.11) | copy-start | bytes 9437188
  14.0 5.8 %collective-permute-start = (bf16[14,3,256]{2,1,0:T(4,128)(2,1)S(1)}, bf16[14,3,256]{2,1,0:T(4,128)(2,1)S(1)}, u32[]{:S(2)}, u32[]{:S(2)}) collective-permute-start(bf16[14,3,256]{2,1,0:T(4,128)(2,1)S(1)} %get-tuple-element.29), channel_id=1, source_target_pairs={{0,4},{4,8},{8,12},{12,16},{16,20},{20,24},{24,28},{28,32},{32,36}... | collective-permute-start | bytes 64520 | tf_op jit(solution)/shard_map/ppermute | solution.py:20
  17.5 5.2 %collective-permute-start.1 = (bf16[14,3,256]{2,1,0:T(4,128)(2,1)S(1)}, bf16[14,3,256]{2,1,0:T(4,128)(2,1)S(1)}, u32[]{:S(2)}, u32[]{:S(2)}) collective-permute-start(bf16[14,3,256]{2,1,0:T(4,128)(2,1)S(1)} %get-tuple-element.30), channel_id=1, source_target_pairs={{4,0},{8,4},{12,8},{16,12},{20,16},{24,20},{28,24},{32,28},{36,32}... | collective-permute-start | bytes 64520 | tf_op jit(solution)/shard_map/ppermute | solution.py:22
  23.2 1.3 copy-start.2
  27.7 0.7 copy-start.5
  31.3 4.8 %collective-permute-start.3 = (f32[144,128]{1,0:T(8,128)S(1)}, f32[144,128]{1,0:T(8,128)S(1)}, u32[]{:S(2)}, u32[]{:S(2)}) collective-permute-start(f32[144,128]{1,0:T(8,128)S(1)} %constant_dynamic-update-slice_fusion.14), channel_id=1, source_target_pairs={{0,128},{4,132},{8,136},{12,140},{16,144},{20,148},{24,152},{28,15... | collective-permute-start | bytes 221192 | tf_op jit(solution)/shard_map/ppermute | solution.py:62
  36.1 13.1 %collective-permute-start.4 = (bf16[6,66,256]{2,1,0:T(8,128)(2,1)S(1)}, bf16[6,66,256]{2,1,0:T(8,128)(2,1)S(1)}, u32[]{:S(2)}, u32[]{:S(2)}) collective-permute-start(bf16[6,66,256]{2,1,0:T(8,128)(2,1)S(1)} %fusion.49), channel_id=1, source_target_pairs={{0,1},{1,2},{2,3},{3,0},{4,5},{5,6},{6,7},{7,4},{8,9},{9,10},{10,1... | collective-permute-start | bytes 608264 | tf_op jit(solution)/shard_map/ppermute | solution.py:269
  37.5 11.7 %collective-permute-start.5 = (bf16[6,66,256]{2,1,0:T(8,128)(2,1)S(1)}, bf16[6,66,256]{2,1,0:T(8,128)(2,1)S(1)}, u32[]{:S(2)}, u32[]{:S(2)}) collective-permute-start(bf16[6,66,256]{2,1,0:T(8,128)(2,1)S(1)} %fusion.49), channel_id=1, source_target_pairs={{0,2},{1,3},{2,0},{3,1},{4,6},{5,7},{6,4},{7,5},{8,10},{9,11},{10,... | collective-permute-start | bytes 608264 | tf_op jit(solution)/shard_map/ppermute | solution.py:269
  40.1 9.2 %collective-permute-start.6 = (bf16[6,66,256]{2,1,0:T(8,128)(2,1)S(1)}, bf16[6,66,256]{2,1,0:T(8,128)(2,1)S(1)}, u32[]{:S(2)}, u32[]{:S(2)}) collective-permute-start(bf16[6,66,256]{2,1,0:T(8,128)(2,1)S(1)} %fusion.49), channel_id=1, source_target_pairs={{0,3},{1,0},{2,1},{3,2},{4,7},{5,4},{6,5},{7,6},{8,11},{9,8},{10,9... | collective-permute-start | bytes 608264 | tf_op jit(solution)/shard_map/ppermute | solution.py:269
  41.2 5.2 %collective-permute-start.7 = (f32[288,128]{1,0:T(8,128)S(1)}, f32[288,128]{1,0:T(8,128)S(1)}, u32[]{:S(2)}, u32[]{:S(2)}) collective-permute-start(f32[288,128]{1,0:T(8,128)S(1)} %constant_dynamic-update-slice_fusion.12), channel_id=1, source_target_pairs={{0,16},{4,20},{8,24},{12,60},{16,0},{20,4},{24,8},{28,44},{32,48},... | collective-permute-start | bytes 442376 | tf_op jit(solution)/shard_map/ppermute | solution.py:62
  46.4 7.1 %collective-permute-start.8 = (f32[576,128]{1,0:T(8,128)S(1)}, f32[576,128]{1,0:T(8,128)S(1)}, u32[]{:S(2)}, u32[]{:S(2)}) collective-permute-start(f32[576,128]{1,0:T(8,128)S(1)} %constant_dynamic-update-slice_fusion.6), channel_id=1, source_target_pairs={{0,64},{4,196},{8,72},{12,204},{16,80},{20,212},{24,88},{28,220},{... | collective-permute-start | bytes 884744 | tf_op jit(solution)/shard_map/ppermute | solution.py:62
  53.4 1.1 copy-start.4
  55.7 14.8 %collective-permute-start.9 = (f32[1152,128]{1,0:T(8,128)S(1)}, f32[1152,128]{1,0:T(8,128)S(1)}, u32[]{:S(2)}, u32[]{:S(2)}) collective-permute-start(f32[1152,128]{1,0:T(8,128)S(1)} %constant_dynamic-update-slice_fusion.4), channel_id=1, source_target_pairs={{0,8},{4,60},{8,0},{12,20},{16,24},{20,12},{24,16},{28,36},{32,40}... | collective-permute-start | bytes 1769480 | tf_op jit(solution)/shard_map/ppermute | solution.py:62
  65.5 5.3 %copy-start.7 = (f32[128]{0:T(128)S(1)}, f32[128]{0:T(128)}, u32[]{:S(2)}) copy-start(f32[128]{0:T(128)} %param.15) | copy-start | bytes 1540
  70.6 2.9 %collective-permute-start.10 = (f32[2304,128]{1,0:T(8,128)S(1)}, f32[2304,128]{1,0:T(8,128)S(1)}, u32[]{:S(2)}, u32[]{:S(2)}) collective-permute-start(f32[2304,128]{1,0:T(8,128)S(1)} %constant_dynamic-update-slice_fusion.2), channel_id=1, source_target_pairs={{0,4},{4,0},{8,12},{12,8},{16,20},{20,16},{24,28},{28,24},{32,36},... | collective-permute-start | bytes 3538952 | tf_op jit(solution)/shard_map/ppermute | solution.py:62
  73.9 1.8 %copy-start.6 = (s32[32]{0:T(128)S(1)}, s32[32]{0:T(128)}, u32[]{:S(2)}) copy-start(s32[32]{0:T(128)} %param.17) | copy-start | bytes 388
  83.4 1.1 copy-start.1
  150.7 4.0 %copy-start.3 = (f32[2048,128]{1,0:T(8,128)S(1)}, f32[2048,128]{1,0:T(8,128)}, u32[]{:S(2)}) copy-start(f32[2048,128]{1,0:T(8,128)} %get-tuple-element.25) | copy-start | bytes 3145732

commit v12 on v10

--- a/solution.py
+++ b/solution.py
@@ -237,9 +237,9 @@
     flat_labels = labels.reshape(-1)
     member = flat_labels[None, :] == jnp.arange(list_len, dtype=jnp.int32)[:, None]
     part_counts = jnp.sum(member.astype(jnp.float32), axis=1)
-    meta = jnp.zeros((8, lanes), jnp.float32)
-    meta = meta.at[0, :list_len].set(part_counts)
-    meta = meta.at[0, list_len : 2 * list_len].set(slot_ids.astype(jnp.float32))
+    meta = jnp.concatenate(
+        [part_counts, slot_ids.astype(jnp.float32), jnp.zeros((8 * lanes - 2 * list_len,), jnp.float32)]
+    ).reshape(8, lanes)
     packed = jnp.concatenate([embed_grad, meta], axis=0)
     halving = [1 << k for k in range(strip_count.bit_length() - 1)]
     if len(halving) == 6:

time: 154 us -> 151 us (0.981)
  other arithmetic: 8.01 us -> 5.5 us
    another operation x3 -> x0, other arithmetic: 3.97 us -> none
    scatter x2 -> x0, local copies, waits for them, and re-layouts: 1.58 us -> none  [the longest x1 1.57 us: body(): meta = meta.at[0, list_len:2 * list_len].set(slot_ids.astype(jnp.float32))]
    unnamed x18 -> x16, local copies, waits for them, and re-layouts: 3.27 us -> 3.26 us
where the time goes in v12:
time: 151 us; the launch traced here: 150 us
  Pallas kernels  65.6 us (43%)
  starting transfers between devices  33.5 us (22%)
  local copies, waits for them, and re-layouts  17.3 us (11%)
  matrix products  15.1 us (10%)
  waiting for transfers between devices  11.8 us (8%)
  other arithmetic  5.5 us (4%)
  between operations  1.55 us (1%)
    pallas_call x1, Pallas kernels, tree_sum(): pl.pallas_call(functools.partial(tree_kernel, count, chunk, width, dists,...  65.6 us
    ppermute x6, starting transfers between devices, tree_gather(): other = lax.ppermute(held, axis, pairs)  23 us
    ppermute x6, waiting for transfers between devices, tree_gather(): other = lax.ppermute(held, axis, pairs)  7.37 us
    dot_general x18, matrix products, convolve(): jnp.dot(band, weight[shift_row, shift_col], preferred_element_type=jnp.fl...  7.29 us
    ppermute x3, starting transfers between devices, body(): lax.ppermute(pooled, 'chan', [(i, (i + shift) % chan_count) for i in rang...  5.1 us
    dot_general x9, matrix products, body(): lax.dot_general(band, placed_grads[shift_col], (((0,), (0,)), ((), ())),...  4.34 us
    ppermute x1, starting transfers between devices, with_halo(): lax.ppermute(tail, axis, [(i, (i + 1) % count) for i in range(ends)])  3.49 us
    unnamed x16, local copies, waits for them, and re-layouts  3.26 us
  transfers between devices with their start and end apart: 11, of which 6 were waited for; matrix products, arithmetic and copies ran while one was open for 9% of the time, Pallas kernels for 0%

profile of v12, /device:TPU:1, one launch (start us, length us, event | category | flops | bytes accessed | tf_op | source)
XLA Modules:
  0.0 150.3 jit_solution(16459854945290227260)
XLA Ops:
  2.3 1.4 gather_fusion
  5.3 7.7 %collective-permute-start.2 = (f32[72,128]{1,0:T(8,128)S(1)}, f32[72,128]{1,0:T(8,128)S(1)}, u32[]{:S(2)}, u32[]{:S(2)}) collective-permute-start(f32[72,128]{1,0:T(8,128)S(1)} %get-tuple-element.37), channel_id=1, source_target_pairs={{0,32},{4,36},{8,40},{12,44},{16,48},{20,52},{24,56},{28,60},{32,0... | collective-permute-start | bytes 110600 | tf_op jit(solution)/shard_map/ppermute | solution.py:62
  14.0 3.5 %collective-permute-start = (bf16[14,3,256]{2,1,0:T(4,128)(2,1)S(1)}, bf16[14,3,256]{2,1,0:T(4,128)(2,1)S(1)}, u32[]{:S(2)}, u32[]{:S(2)}) collective-permute-start(bf16[14,3,256]{2,1,0:T(4,128)(2,1)S(1)} %get-tuple-element.29), channel_id=1, source_target_pairs={{0,4},{4,8},{8,12},{12,16},{16,20},{20,24},{24,28},{28,32},{32,36}... | collective-permute-start | bytes 64520 | tf_op jit(solution)/shard_map/ppermute | solution.py:20
  17.5 1.9 %collective-permute-start.1 = (bf16[14,3,256]{2,1,0:T(4,128)(2,1)S(1)}, bf16[14,3,256]{2,1,0:T(4,128)(2,1)S(1)}, u32[]{:S(2)}, u32[]{:S(2)}) collective-permute-start(bf16[14,3,256]{2,1,0:T(4,128)(2,1)S(1)} %get-tuple-element.30), channel_id=1, source_target_pairs={{4,0},{8,4},{12,8},{16,12},{20,16},{24,20},{28,24},{32,28},{36,32}... | collective-permute-start | bytes 64520 | tf_op jit(solution)/shard_map/ppermute | solution.py:22
  19.9 2.8 %collective-permute-done.1 = bf16[14,3,256]{2,1,0:T(4,128)(2,1)S(1)} collective-permute-done((bf16[14,3,256]{2,1,0:T(4,128)(2,1)S(1)}, bf16[14,3,256]{2,1,0:T(4,128)(2,1)S(1)}, u32[]{:S(2)}, u32[]{:S(2)}) %collective-permute-start.1) | collective-permute-done | bytes 21536 | tf_op jit(solution)/shard_map/ppermute | solution.py:22
  23.2 2.8 %collective-permute-start.3 = (f32[144,128]{1,0:T(8,128)S(1)}, f32[144,128]{1,0:T(8,128)S(1)}, u32[]{:S(2)}, u32[]{:S(2)}) collective-permute-start(f32[144,128]{1,0:T(8,128)S(1)} %constant_dynamic-update-slice_fusion.14), channel_id=1, source_target_pairs={{0,128},{4,132},{8,136},{12,140},{16,144},{20,148},{24,152},{28,15... | collective-permute-start | bytes 221192 | tf_op jit(solution)/shard_map/ppermute | solution.py:62
  26.0 1.9 %collective-permute-done.3 = f32[144,128]{1,0:T(8,128)S(1)} collective-permute-done((f32[144,128]{1,0:T(8,128)S(1)}, f32[144,128]{1,0:T(8,128)S(1)}, u32[]{:S(2)}, u32[]{:S(2)}) %collective-permute-start.3) | collective-permute-done | bytes 73760 | tf_op jit(solution)/shard_map/ppermute | solution.py:62
  30.4 2.0 %collective-permute-start.4 = (f32[288,128]{1,0:T(8,128)S(1)}, f32[288,128]{1,0:T(8,128)}, u32[]{:S(2)}, u32[]{:S(2)}) collective-permute-start(f32[288,128]{1,0:T(8,128)S(1)} %constant_dynamic-update-slice_fusion.12), channel_id=1, source_target_pairs={{0,16},{4,20},{8,24},{12,60},{16,0},{20,4},{24,8},{28,44},{32,48},... | collective-permute-start | bytes 442376 | tf_op jit(solution)/shard_map/ppermute | solution.py:62
  36.8 1.1 reduce_sum.28
  38.9 2.6 %collective-permute-start.5 = (f32[576,128]{1,0:T(8,128)S(1)}, f32[576,128]{1,0:T(8,128)S(1)}, u32[]{:S(2)}, u32[]{:S(2)}) collective-permute-start(f32[576,128]{1,0:T(8,128)S(1)} %constant_dynamic-update-slice_fusion.10), channel_id=1, source_target_pairs={{0,64},{4,196},{8,72},{12,204},{16,80},{20,212},{24,88},{28,220},{... | collective-permute-start | bytes 884744 | tf_op jit(solution)/shard_map/ppermute | solution.py:62
  41.7 4.1 %collective-permute-done.5 = f32[576,128]{1,0:T(8,128)S(1)} collective-permute-done((f32[576,128]{1,0:T(8,128)S(1)}, f32[576,128]{1,0:T(8,128)S(1)}, u32[]{:S(2)}, u32[]{:S(2)}) %collective-permute-start.5) | collective-permute-done | bytes 294944 | tf_op jit(solution)/shard_map/ppermute | solution.py:62
  45.8 1.4 collective-permute-start.8
  47.2 2.6 %collective-permute-start.9 = (bf16[6,66,256]{2,1,0:T(8,128)(2,1)S(1)}, bf16[6,66,256]{2,1,0:T(8,128)(2,1)S(1)}, u32[]{:S(2)}, u32[]{:S(2)}) collective-permute-start(bf16[6,66,256]{2,1,0:T(8,128)(2,1)S(1)} %fusion.44), channel_id=1, source_target_pairs={{0,2},{1,3},{2,0},{3,1},{4,6},{5,7},{6,4},{7,5},{8,10},{9,11},{10,... | collective-permute-start | bytes 608264 | tf_op jit(solution)/shard_map/ppermute | solution.py:274
  49.9 1.1 collective-permute-start.10
  50.9 5.1 %collective-permute-start.6 = (f32[1152,128]{1,0:T(8,128)S(1)}, f32[1152,128]{1,0:T(8,128)S(1)}, u32[]{:S(2)}, u32[]{:S(2)}) collective-permute-start(f32[1152,128]{1,0:T(8,128)S(1)} %constant_dynamic-update-slice_fusion.8), channel_id=1, source_target_pairs={{0,8},{4,60},{8,0},{12,20},{16,24},{20,12},{24,16},{28,36},{32,40}... | collective-permute-start | bytes 1769480 | tf_op jit(solution)/shard_map/ppermute | solution.py:62
  56.3 1.6 %collective-permute-done.9 = bf16[6,66,256]{2,1,0:T(8,128)(2,1)S(1)} collective-permute-done((bf16[6,66,256]{2,1,0:T(8,128)(2,1)S(1)}, bf16[6,66,256]{2,1,0:T(8,128)(2,1)S(1)}, u32[]{:S(2)}, u32[]{:S(2)}) %collective-permute-start.9) | collective-permute-done | bytes 202784 | tf_op jit(solution)/shard_map/ppermute | solution.py:274
  63.4 2.7 %collective-permute-start.7 = (f32[2304,128]{1,0:T(8,128)S(1)}, f32[2304,128]{1,0:T(8,128)S(1)}, u32[]{:S(2)}, u32[]{:S(2)}) collective-permute-start(f32[2304,128]{1,0:T(8,128)S(1)} %constant_dynamic-update-slice_fusion.6), channel_id=1, source_target_pairs={{0,4},{4,0},{8,12},{12,8},{16,20},{20,16},{24,28},{28,24},{32,36},... | collective-permute-start | bytes 3538952 | tf_op jit(solution)/shard_map/ppermute | solution.py:62
  68.9 1.6 %slice.185 = f32[64,64,128]{2,1,0:T(8,128)} slice(f32[64,72,128]{2,1,0:T(8,128)S(1)} %bitcast.177), slice={[0:64], [0:64], [0:128]} | slice | bytes 4194304 | tf_op jit(solution)/shard_map/slice | solution.py:266
  70.9 2.2 %gather_fusion.1 = f32[32,128]{1,0:T(8,128)S(1)} fusion(f32[4096,128]{1,0:T(8,128)} %bitcast.184, s32[1024]{0:T(1024)S(1)} %pad_clamp_fusion), kind=kCustom, calls=%fused_computation.1 | custom fusion | bytes 32896 | tf_op jit(solution)/shard_map/gather | solution.py:288
  78.4 1.1 copy-done.1
  79.5 65.6 %shard_map.112 = (f32[2560,128]{1,0:T(8,128)}, f32[2048,128]{1,0:T(8,128)}) custom-call(f32[2560,128]{1,0:T(8,128)} %copy-done.1, f32[32,128]{1,0:T(8,128)} %fusion.45.sums_ref), custom_call_target="tpu_custom_call" | custom-call | tf_op jit(solution)/shard_map/pallas_call | solution.py:169
  145.1 2.4 %slice.175 = f32[2304,128]{1,0:T(8,128)} slice(f32[2560,128]{1,0:T(8,128)} %get-tuple-element.26), slice={[0:2304], [0:128]} | slice | bytes 2359296 | tf_op jit(solution)/shard_map/slice | solution.py:330
  147.5 1.2 slice_bitcast_fusion
  149.1 1.2 convolution_divide_fusion
  (101 shorter events, 27.0 us)
Async XLA Ops:
  5.3 17.9 %collective-permute-start.2 = (f32[72,128]{1,0:T(8,128)S(1)}, f32[72,128]{1,0:T(8,128)S(1)}, u32[]{:S(2)}, u32[]{:S(2)}) collective-permute-start(f32[72,128]{1,0:T(8,128)S(1)} %get-tuple-element.37), channel_id=1, source_target_pairs={{0,32},{4,36},{8,40},{12,44},{16,48},{20,52},{24,56},{28,60},{32,0... | collective-permute-start | bytes 110600 | tf_op jit(solution)/shard_map/ppermute | solution.py:62
  13.0 6.4 %copy-start = (bf16[48,128,256]{2,1,0:T(8,128)(2,1)S(1)}, bf16[48,128,256]{2,1,0:T(8,128)(2,1)}, u32[]{:S(2)}) copy-start(bf16[48,128,256]{2,1,0:T(8,128)(2,1)} %param.11) | copy-start | bytes 9437188
  14.0 5.8 %collective-permute-start = (bf16[14,3,256]{2,1,0:T(4,128)(2,1)S(1)}, bf16[14,3,256]{2,1,0:T(4,128)(2,1)S(1)}, u32[]{:S(2)}, u32[]{:S(2)}) collective-permute-start(bf16[14,3,256]{2,1,0:T(4,128)(2,1)S(1)} %get-tuple-element.29), channel_id=1, source_target_pairs={{0,4},{4,8},{8,12},{12,16},{16,20},{20,24},{24,28},{28,32},{32,36}... | collective-permute-start | bytes 64520 | tf_op jit(solution)/shard_map/ppermute | solution.py:20
  17.5 5.2 %collective-permute-start.1 = (bf16[14,3,256]{2,1,0:T(4,128)(2,1)S(1)}, bf16[14,3,256]{2,1,0:T(4,128)(2,1)S(1)}, u32[]{:S(2)}, u32[]{:S(2)}) collective-permute-start(bf16[14,3,256]{2,1,0:T(4,128)(2,1)S(1)} %get-tuple-element.30), channel_id=1, source_target_pairs={{4,0},{8,4},{12,8},{16,12},{20,16},{24,20},{28,24},{32,28},{36,32}... | collective-permute-start | bytes 64520 | tf_op jit(solution)/shard_map/ppermute | solution.py:22
  23.2 4.8 %collective-permute-start.3 = (f32[144,128]{1,0:T(8,128)S(1)}, f32[144,128]{1,0:T(8,128)S(1)}, u32[]{:S(2)}, u32[]{:S(2)}) collective-permute-start(f32[144,128]{1,0:T(8,128)S(1)} %constant_dynamic-update-slice_fusion.14), channel_id=1, source_target_pairs={{0,128},{4,132},{8,136},{12,140},{16,144},{20,148},{24,152},{28,15... | collective-permute-start | bytes 221192 | tf_op jit(solution)/shard_map/ppermute | solution.py:62
  28.0 1.3 copy-start.2
  30.4 7.6 %collective-permute-start.4 = (f32[288,128]{1,0:T(8,128)S(1)}, f32[288,128]{1,0:T(8,128)}, u32[]{:S(2)}, u32[]{:S(2)}) collective-permute-start(f32[288,128]{1,0:T(8,128)S(1)} %constant_dynamic-update-slice_fusion.12), channel_id=1, source_target_pairs={{0,16},{4,20},{8,24},{12,60},{16,0},{20,4},{24,8},{28,44},{32,48},... | collective-permute-start | bytes 442376 | tf_op jit(solution)/shard_map/ppermute | solution.py:62
  34.5 0.7 copy-start.5
  38.9 6.9 %collective-permute-start.5 = (f32[576,128]{1,0:T(8,128)S(1)}, f32[576,128]{1,0:T(8,128)S(1)}, u32[]{:S(2)}, u32[]{:S(2)}) collective-permute-start(f32[576,128]{1,0:T(8,128)S(1)} %constant_dynamic-update-slice_fusion.10), channel_id=1, source_target_pairs={{0,64},{4,196},{8,72},{12,204},{16,80},{20,212},{24,88},{28,220},{... | collective-permute-start | bytes 884744 | tf_op jit(solution)/shard_map/ppermute | solution.py:62
  45.8 10.5 %collective-permute-start.8 = (bf16[6,66,256]{2,1,0:T(8,128)(2,1)S(1)}, bf16[6,66,256]{2,1,0:T(8,128)(2,1)S(1)}, u32[]{:S(2)}, u32[]{:S(2)}) collective-permute-start(bf16[6,66,256]{2,1,0:T(8,128)(2,1)S(1)} %fusion.44), channel_id=1, source_target_pairs={{0,1},{1,2},{2,3},{3,0},{4,5},{5,6},{6,7},{7,4},{8,9},{9,10},{10,1... | collective-permute-start | bytes 608264 | tf_op jit(solution)/shard_map/ppermute | solution.py:274
  47.2 10.7 %collective-permute-start.9 = (bf16[6,66,256]{2,1,0:T(8,128)(2,1)S(1)}, bf16[6,66,256]{2,1,0:T(8,128)(2,1)S(1)}, u32[]{:S(2)}, u32[]{:S(2)}) collective-permute-start(bf16[6,66,256]{2,1,0:T(8,128)(2,1)S(1)} %fusion.44), channel_id=1, source_target_pairs={{0,2},{1,3},{2,0},{3,1},{4,6},{5,7},{6,4},{7,5},{8,10},{9,11},{10,... | collective-permute-start | bytes 608264 | tf_op jit(solution)/shard_map/ppermute | solution.py:274
  49.9 8.1 %collective-permute-start.10 = (bf16[6,66,256]{2,1,0:T(8,128)(2,1)S(1)}, bf16[6,66,256]{2,1,0:T(8,128)(2,1)S(1)}, u32[]{:S(2)}, u32[]{:S(2)}) collective-permute-start(bf16[6,66,256]{2,1,0:T(8,128)(2,1)S(1)} %fusion.44), channel_id=1, source_target_pairs={{0,3},{1,0},{2,1},{3,2},{4,7},{5,4},{6,5},{7,6},{8,11},{9,8},{10,9... | collective-permute-start | bytes 608264 | tf_op jit(solution)/shard_map/ppermute | solution.py:274
  50.9 12.4 %collective-permute-start.6 = (f32[1152,128]{1,0:T(8,128)S(1)}, f32[1152,128]{1,0:T(8,128)S(1)}, u32[]{:S(2)}, u32[]{:S(2)}) collective-permute-start(f32[1152,128]{1,0:T(8,128)S(1)} %constant_dynamic-update-slice_fusion.8), channel_id=1, source_target_pairs={{0,8},{4,60},{8,0},{12,20},{16,24},{20,12},{24,16},{28,36},{32,40}... | collective-permute-start | bytes 1769480 | tf_op jit(solution)/shard_map/ppermute | solution.py:62
  58.0 1.1 copy-start.4
  62.4 3.7 %copy-start.7 = (f32[128]{0:T(128)S(1)}, f32[128]{0:T(128)}, u32[]{:S(2)}) copy-start(f32[128]{0:T(128)} %param.15) | copy-start | bytes 1540
  63.4 5.1 %collective-permute-start.7 = (f32[2304,128]{1,0:T(8,128)S(1)}, f32[2304,128]{1,0:T(8,128)S(1)}, u32[]{:S(2)}, u32[]{:S(2)}) collective-permute-start(f32[2304,128]{1,0:T(8,128)S(1)} %constant_dynamic-update-slice_fusion.6), channel_id=1, source_target_pairs={{0,4},{4,0},{8,12},{12,8},{16,20},{20,16},{24,28},{28,24},{32,36},... | collective-permute-start | bytes 3538952 | tf_op jit(solution)/shard_map/ppermute | solution.py:62
  68.9 1.8 %copy-start.6 = (s32[32]{0:T(128)S(1)}, s32[32]{0:T(128)}, u32[]{:S(2)}) copy-start(s32[32]{0:T(128)} %param.17) | copy-start | bytes 388
  78.4 1.1 copy-start.1
  145.1 4.0 %copy-start.3 = (f32[2048,128]{1,0:T(8,128)S(1)}, f32[2048,128]{1,0:T(8,128)}, u32[]{:S(2)}) copy-start(f32[2048,128]{1,0:T(8,128)} %get-tuple-element.25) | copy-start | bytes 3145732

commit v13 on v12

--- a/solution.py
+++ b/solution.py
@@ -263,7 +263,6 @@
     pooled = jnp.where(outside[None, :, None], jnp.zeros_like(pooled), pooled)
     pooled, early = lax.optimization_barrier((pooled, early))
     every = tree_gather(early, "strip", order[4:], shifted).reshape(strip_count, owned + 8, lanes)
-    every_grad = every[:, :owned].reshape(strip_count * owned, lanes)
     every_counts = every[:, owned, :list_len].reshape(-1)
     every_slots = jnp.round(every[:, owned, list_len : 2 * list_len]).astype(jnp.int32).reshape(-1)
     part_rows = pooled.shape[0]
@@ -284,8 +283,7 @@
 
     same_slot = (slot_ids[:, None] == every_slots[None, :]).astype(jnp.float32)
     entry_counts = jnp.dot(same_slot, every_counts, precision=lax.Precision.HIGHEST)
-    grad_row = position[slot_ids // owned] * owned + slot_ids % owned
-    entry_grad = every_grad[grad_row] / jnp.maximum(entry_counts, 1.0)[:, None]
+    entry_grad = every[position[slot_ids // owned], slot_ids % owned] / jnp.maximum(entry_counts, 1.0)[:, None]
     pixel_grad = lax.dot_general(
         member.astype(jnp.float32),
         entry_grad,

time: 151 us -> 148 us (0.980)
  local copies, waits for them, and re-layouts: 17.3 us -> 15.4 us
    slice x1 -> x0, local copies, waits for them, and re-layouts: 1.61 us -> none  [body(): every_grad = every[:, :owned].reshape(strip_count * owned, lanes)]
    gather x2, local copies, waits for them, and re-layouts: 3.58 us -> 2.04 us  [the longest x1 1.34 us: body(): every[position[slot_ids // owned], slot_ids % owned]]
    unnamed x16 -> x20, local copies, waits for them, and re-layouts: 3.26 us -> 4.52 us
where the time goes in v13:
time: 148 us; the launch traced here: 147 us
  Pallas kernels  65.7 us (44%)
  starting transfers between devices  33.5 us (23%)
  local copies, waits for them, and re-layouts  15.4 us (10%)
  matrix products  15.1 us (10%)
  waiting for transfers between devices  11 us (7%)
  other arithmetic  4.84 us (3%)
  between operations  1.57 us (1%)
    pallas_call x1, Pallas kernels, tree_sum(): pl.pallas_call(functools.partial(tree_kernel, count, chunk, width, dists,...  65.7 us
    ppermute x6, starting transfers between devices, tree_gather(): other = lax.ppermute(held, axis, pairs)  23 us
    ppermute x6, waiting for transfers between devices, tree_gather(): other = lax.ppermute(held, axis, pairs)  7.36 us
    dot_general x18, matrix products, convolve(): jnp.dot(band, weight[shift_row, shift_col], preferred_element_type=jnp.fl...  7.29 us
    ppermute x3, starting transfers between devices, body(): lax.ppermute(pooled, 'chan', [(i, (i + shift) % chan_count) for i in rang...  5.05 us
    unnamed x20, local copies, waits for them, and re-layouts  4.52 us
    dot_general x9, matrix products, body(): lax.dot_general(band, placed_grads[shift_col], (((0,), (0,)), ((), ())),...  4.34 us
    ppermute x1, starting transfers between devices, with_halo(): lax.ppermute(tail, axis, [(i, (i + 1) % count) for i in range(ends)])  3.49 us
  transfers between devices with their start and end apart: 11, of which 6 were waited for; matrix products, arithmetic and copies ran while one was open for 9% of the time, Pallas kernels for 0%

profile of v13, /device:TPU:1, one launch (start us, length us, event | category | flops | bytes accessed | tf_op | source)
XLA Modules:
  0.0 147.2 jit_solution(9853758923477543798)
XLA Ops:
  3.2 7.7 %collective-permute-start.2 = (f32[72,128]{1,0:T(8,128)S(1)}, f32[72,128]{1,0:T(8,128)S(1)}, u32[]{:S(2)}, u32[]{:S(2)}) collective-permute-start(f32[72,128]{1,0:T(8,128)S(1)} %get-tuple-element.37), channel_id=1, source_target_pairs={{0,32},{4,36},{8,40},{12,44},{16,48},{20,52},{24,56},{28,60},{32,0... | collective-permute-start | bytes 110600 | tf_op jit(solution)/shard_map/ppermute | solution.py:62
  12.0 3.5 %collective-permute-start = (bf16[14,3,256]{2,1,0:T(4,128)(2,1)S(1)}, bf16[14,3,256]{2,1,0:T(4,128)(2,1)S(1)}, u32[]{:S(2)}, u32[]{:S(2)}) collective-permute-start(bf16[14,3,256]{2,1,0:T(4,128)(2,1)S(1)} %get-tuple-element.29), channel_id=1, source_target_pairs={{0,4},{4,8},{8,12},{12,16},{16,20},{20,24},{24,28},{28,32},{32,36}... | collective-permute-start | bytes 64520 | tf_op jit(solution)/shard_map/ppermute | solution.py:20
  15.5 1.9 %collective-permute-start.1 = (bf16[14,3,256]{2,1,0:T(4,128)(2,1)S(1)}, bf16[14,3,256]{2,1,0:T(4,128)(2,1)S(1)}, u32[]{:S(2)}, u32[]{:S(2)}) collective-permute-start(bf16[14,3,256]{2,1,0:T(4,128)(2,1)S(1)} %get-tuple-element.30), channel_id=1, source_target_pairs={{4,0},{8,4},{12,8},{16,12},{20,16},{24,20},{28,24},{32,28},{36,32}... | collective-permute-start | bytes 64520 | tf_op jit(solution)/shard_map/ppermute | solution.py:22
  18.6 2.1 %collective-permute-done.1 = bf16[14,3,256]{2,1,0:T(4,128)(2,1)S(1)} collective-permute-done((bf16[14,3,256]{2,1,0:T(4,128)(2,1)S(1)}, bf16[14,3,256]{2,1,0:T(4,128)(2,1)S(1)}, u32[]{:S(2)}, u32[]{:S(2)}) %collective-permute-start.1) | collective-permute-done | bytes 21536 | tf_op jit(solution)/shard_map/ppermute | solution.py:22
  21.2 2.8 %collective-permute-start.3 = (f32[144,128]{1,0:T(8,128)S(1)}, f32[144,128]{1,0:T(8,128)S(1)}, u32[]{:S(2)}, u32[]{:S(2)}) collective-permute-start(f32[144,128]{1,0:T(8,128)S(1)} %constant_dynamic-update-slice_fusion.14), channel_id=1, source_target_pairs={{0,128},{4,132},{8,136},{12,140},{16,144},{20,148},{24,152},{28,15... | collective-permute-start | bytes 221192 | tf_op jit(solution)/shard_map/ppermute | solution.py:62
  24.0 1.9 %collective-permute-done.3 = f32[144,128]{1,0:T(8,128)S(1)} collective-permute-done((f32[144,128]{1,0:T(8,128)S(1)}, f32[144,128]{1,0:T(8,128)S(1)}, u32[]{:S(2)}, u32[]{:S(2)}) %collective-permute-start.3) | collective-permute-done | bytes 73760 | tf_op jit(solution)/shard_map/ppermute | solution.py:62
  26.2 1.1 copy-done.4
  28.4 2.1 %collective-permute-start.4 = (f32[288,128]{1,0:T(8,128)S(1)}, f32[288,128]{1,0:T(8,128)}, u32[]{:S(2)}, u32[]{:S(2)}) collective-permute-start(f32[288,128]{1,0:T(8,128)S(1)} %constant_dynamic-update-slice_fusion.12), channel_id=1, source_target_pairs={{0,16},{4,20},{8,24},{12,60},{16,0},{20,4},{24,8},{28,44},{32,48},... | collective-permute-start | bytes 442376 | tf_op jit(solution)/shard_map/ppermute | solution.py:62
  34.8 1.1 reduce_sum.28
  37.0 2.6 %collective-permute-start.5 = (f32[576,128]{1,0:T(8,128)S(1)}, f32[576,128]{1,0:T(8,128)S(1)}, u32[]{:S(2)}, u32[]{:S(2)}) collective-permute-start(f32[576,128]{1,0:T(8,128)S(1)} %constant_dynamic-update-slice_fusion.10), channel_id=1, source_target_pairs={{0,64},{4,196},{8,72},{12,204},{16,80},{20,212},{24,88},{28,220},{... | collective-permute-start | bytes 884744 | tf_op jit(solution)/shard_map/ppermute | solution.py:62
  39.7 4.1 %collective-permute-done.5 = f32[576,128]{1,0:T(8,128)S(1)} collective-permute-done((f32[576,128]{1,0:T(8,128)S(1)}, f32[576,128]{1,0:T(8,128)S(1)}, u32[]{:S(2)}, u32[]{:S(2)}) %collective-permute-start.5) | collective-permute-done | bytes 294944 | tf_op jit(solution)/shard_map/ppermute | solution.py:62
  43.9 1.4 collective-permute-start.8
  45.2 2.6 %collective-permute-start.9 = (bf16[6,66,256]{2,1,0:T(8,128)(2,1)S(1)}, bf16[6,66,256]{2,1,0:T(8,128)(2,1)S(1)}, u32[]{:S(2)}, u32[]{:S(2)}) collective-permute-start(bf16[6,66,256]{2,1,0:T(8,128)(2,1)S(1)} %fusion.44), channel_id=1, source_target_pairs={{0,2},{1,3},{2,0},{3,1},{4,6},{5,7},{6,4},{7,5},{8,10},{9,11},{10,... | collective-permute-start | bytes 608264 | tf_op jit(solution)/shard_map/ppermute | solution.py:273
  47.9 1.0 collective-permute-start.10
  48.9 5.1 %collective-permute-start.6 = (f32[1152,128]{1,0:T(8,128)S(1)}, f32[1152,128]{1,0:T(8,128)S(1)}, u32[]{:S(2)}, u32[]{:S(2)}) collective-permute-start(f32[1152,128]{1,0:T(8,128)S(1)} %constant_dynamic-update-slice_fusion.8), channel_id=1, source_target_pairs={{0,8},{4,60},{8,0},{12,20},{16,24},{20,12},{24,16},{28,36},{32,40}... | collective-permute-start | bytes 1769480 | tf_op jit(solution)/shard_map/ppermute | solution.py:62
  54.3 1.6 %collective-permute-done.9 = bf16[6,66,256]{2,1,0:T(8,128)(2,1)S(1)} collective-permute-done((bf16[6,66,256]{2,1,0:T(8,128)(2,1)S(1)}, bf16[6,66,256]{2,1,0:T(8,128)(2,1)S(1)}, u32[]{:S(2)}, u32[]{:S(2)}) %collective-permute-start.9) | collective-permute-done | bytes 202784 | tf_op jit(solution)/shard_map/ppermute | solution.py:273
  61.4 2.7 %collective-permute-start.7 = (f32[2304,128]{1,0:T(8,128)S(1)}, f32[2304,128]{1,0:T(8,128)S(1)}, u32[]{:S(2)}, u32[]{:S(2)}) collective-permute-start(f32[2304,128]{1,0:T(8,128)S(1)} %constant_dynamic-update-slice_fusion.6), channel_id=1, source_target_pairs={{0,4},{4,0},{8,12},{12,8},{16,20},{20,16},{24,28},{28,24},{32,36},... | collective-permute-start | bytes 3538952 | tf_op jit(solution)/shard_map/ppermute | solution.py:62
  66.8 1.3 copy-done.2
  68.3 1.3 gather_fusion.1
  75.2 1.1 copy-done.3
  76.2 65.7 %shard_map.112 = (f32[2560,128]{1,0:T(8,128)}, f32[2048,128]{1,0:T(8,128)}) custom-call(f32[2560,128]{1,0:T(8,128)} %copy-done.3, f32[32,128]{1,0:T(8,128)} %fusion.45.sums_ref), custom_call_target="tpu_custom_call" | custom-call | tf_op jit(solution)/shard_map/pallas_call | solution.py:169
  142.0 2.4 %slice.171 = f32[2304,128]{1,0:T(8,128)} slice(f32[2560,128]{1,0:T(8,128)} %get-tuple-element.26), slice={[0:2304], [0:128]} | slice | bytes 2359296 | tf_op jit(solution)/shard_map/slice | solution.py:328
  144.4 1.2 slice_bitcast_fusion
  146.0 1.2 convolution_divide_fusion
  (103 shorter events, 26.1 us)
Async XLA Ops:
  3.2 17.9 %collective-permute-start.2 = (f32[72,128]{1,0:T(8,128)S(1)}, f32[72,128]{1,0:T(8,128)S(1)}, u32[]{:S(2)}, u32[]{:S(2)}) collective-permute-start(f32[72,128]{1,0:T(8,128)S(1)} %get-tuple-element.37), channel_id=1, source_target_pairs={{0,32},{4,36},{8,40},{12,44},{16,48},{20,52},{24,56},{28,60},{32,0... | collective-permute-start | bytes 110600 | tf_op jit(solution)/shard_map/ppermute | solution.py:62
  11.0 6.5 %copy-start.1 = (bf16[48,128,256]{2,1,0:T(8,128)(2,1)S(1)}, bf16[48,128,256]{2,1,0:T(8,128)(2,1)}, u32[]{:S(2)}) copy-start(bf16[48,128,256]{2,1,0:T(8,128)(2,1)} %param.11) | copy-start | bytes 9437188
  12.0 6.6 %collective-permute-start = (bf16[14,3,256]{2,1,0:T(4,128)(2,1)S(1)}, bf16[14,3,256]{2,1,0:T(4,128)(2,1)S(1)}, u32[]{:S(2)}, u32[]{:S(2)}) collective-permute-start(bf16[14,3,256]{2,1,0:T(4,128)(2,1)S(1)} %get-tuple-element.29), channel_id=1, source_target_pairs={{0,4},{4,8},{8,12},{12,16},{16,20},{20,24},{24,28},{28,32},{32,36}... | collective-permute-start | bytes 64520 | tf_op jit(solution)/shard_map/ppermute | solution.py:20
  15.5 2.1 %copy-start = (s32[64]{0:T(128)S(1)}, s32[64]{0:T(128)}, u32[]{:S(2)}) copy-start(s32[64]{0:T(128)} %constant.295.clone) | copy-start | bytes 772
  15.5 2.8 %copy-start.9 = (s32[32]{0:T(128)S(1)}, s32[32]{0:T(128)}, u32[]{:S(2)}) copy-start(s32[32]{0:T(128)} %param.17) | copy-start | bytes 388
  15.5 5.2 %collective-permute-start.1 = (bf16[14,3,256]{2,1,0:T(4,128)(2,1)S(1)}, bf16[14,3,256]{2,1,0:T(4,128)(2,1)S(1)}, u32[]{:S(2)}, u32[]{:S(2)}) collective-permute-start(bf16[14,3,256]{2,1,0:T(4,128)(2,1)S(1)} %get-tuple-element.30), channel_id=1, source_target_pairs={{4,0},{8,4},{12,8},{16,12},{20,16},{24,20},{28,24},{32,28},{36,32}... | collective-permute-start | bytes 64520 | tf_op jit(solution)/shard_map/ppermute | solution.py:22
  21.2 4.8 %collective-permute-start.3 = (f32[144,128]{1,0:T(8,128)S(1)}, f32[144,128]{1,0:T(8,128)S(1)}, u32[]{:S(2)}, u32[]{:S(2)}) collective-permute-start(f32[144,128]{1,0:T(8,128)S(1)} %constant_dynamic-update-slice_fusion.14), channel_id=1, source_target_pairs={{0,128},{4,132},{8,136},{12,140},{16,144},{20,148},{24,152},{28,15... | collective-permute-start | bytes 221192 | tf_op jit(solution)/shard_map/ppermute | solution.py:62
  26.0 1.3 copy-start.4
  28.4 7.6 %collective-permute-start.4 = (f32[288,128]{1,0:T(8,128)S(1)}, f32[288,128]{1,0:T(8,128)}, u32[]{:S(2)}, u32[]{:S(2)}) collective-permute-start(f32[288,128]{1,0:T(8,128)S(1)} %constant_dynamic-update-slice_fusion.12), channel_id=1, source_target_pairs={{0,16},{4,20},{8,24},{12,60},{16,0},{20,4},{24,8},{28,44},{32,48},... | collective-permute-start | bytes 442376 | tf_op jit(solution)/shard_map/ppermute | solution.py:62
  32.5 0.7 copy-start.7
  37.0 6.9 %collective-permute-start.5 = (f32[576,128]{1,0:T(8,128)S(1)}, f32[576,128]{1,0:T(8,128)S(1)}, u32[]{:S(2)}, u32[]{:S(2)}) collective-permute-start(f32[576,128]{1,0:T(8,128)S(1)} %constant_dynamic-update-slice_fusion.10), channel_id=1, source_target_pairs={{0,64},{4,196},{8,72},{12,204},{16,80},{20,212},{24,88},{28,220},{... | collective-permute-start | bytes 884744 | tf_op jit(solution)/shard_map/ppermute | solution.py:62
  43.9 10.4 %collective-permute-start.8 = (bf16[6,66,256]{2,1,0:T(8,128)(2,1)S(1)}, bf16[6,66,256]{2,1,0:T(8,128)(2,1)S(1)}, u32[]{:S(2)}, u32[]{:S(2)}) collective-permute-start(bf16[6,66,256]{2,1,0:T(8,128)(2,1)S(1)} %fusion.44), channel_id=1, source_target_pairs={{0,1},{1,2},{2,3},{3,0},{4,5},{5,6},{6,7},{7,4},{8,9},{9,10},{10,1... | collective-permute-start | bytes 608264 | tf_op jit(solution)/shard_map/ppermute | solution.py:273
  45.2 10.7 %collective-permute-start.9 = (bf16[6,66,256]{2,1,0:T(8,128)(2,1)S(1)}, bf16[6,66,256]{2,1,0:T(8,128)(2,1)S(1)}, u32[]{:S(2)}, u32[]{:S(2)}) collective-permute-start(bf16[6,66,256]{2,1,0:T(8,128)(2,1)S(1)} %fusion.44), channel_id=1, source_target_pairs={{0,2},{1,3},{2,0},{3,1},{4,6},{5,7},{6,4},{7,5},{8,10},{9,11},{10,... | collective-permute-start | bytes 608264 | tf_op jit(solution)/shard_map/ppermute | solution.py:273
  47.9 8.1 %collective-permute-start.10 = (bf16[6,66,256]{2,1,0:T(8,128)(2,1)S(1)}, bf16[6,66,256]{2,1,0:T(8,128)(2,1)S(1)}, u32[]{:S(2)}, u32[]{:S(2)}) collective-permute-start(bf16[6,66,256]{2,1,0:T(8,128)(2,1)S(1)} %fusion.44), channel_id=1, source_target_pairs={{0,3},{1,0},{2,1},{3,2},{4,7},{5,4},{6,5},{7,6},{8,11},{9,8},{10,9... | collective-permute-start | bytes 608264 | tf_op jit(solution)/shard_map/ppermute | solution.py:273
  48.9 12.4 %collective-permute-start.6 = (f32[1152,128]{1,0:T(8,128)S(1)}, f32[1152,128]{1,0:T(8,128)S(1)}, u32[]{:S(2)}, u32[]{:S(2)}) collective-permute-start(f32[1152,128]{1,0:T(8,128)S(1)} %constant_dynamic-update-slice_fusion.8), channel_id=1, source_target_pairs={{0,8},{4,60},{8,0},{12,20},{16,24},{20,12},{24,16},{28,36},{32,40}... | collective-permute-start | bytes 1769480 | tf_op jit(solution)/shard_map/ppermute | solution.py:62
  56.0 1.1 copy-start.6
  60.4 3.6 %copy-start.8 = (f32[128]{0:T(128)S(1)}, f32[128]{0:T(128)}, u32[]{:S(2)}) copy-start(f32[128]{0:T(128)} %param.15) | copy-start | bytes 1540
  61.4 5.1 %collective-permute-start.7 = (f32[2304,128]{1,0:T(8,128)S(1)}, f32[2304,128]{1,0:T(8,128)S(1)}, u32[]{:S(2)}, u32[]{:S(2)}) collective-permute-start(f32[2304,128]{1,0:T(8,128)S(1)} %constant_dynamic-update-slice_fusion.6), channel_id=1, source_target_pairs={{0,4},{4,0},{8,12},{12,8},{16,20},{20,16},{24,28},{28,24},{32,36},... | collective-permute-start | bytes 3538952 | tf_op jit(solution)/shard_map/ppermute | solution.py:62
  66.6 1.4 copy-start.2
  75.2 1.1 copy-start.3
  141.9 4.0 %copy-start.5 = (f32[2048,128]{1,0:T(8,128)S(1)}, f32[2048,128]{1,0:T(8,128)}, u32[]{:S(2)}) copy-start(f32[2048,128]{1,0:T(8,128)} %get-tuple-element.25) | copy-start | bytes 3145732

commit v14 on v13

--- a/solution.py
+++ b/solution.py
@@ -252,7 +252,6 @@
     padded_rows = jnp.pad(section_input, ((1, 1), (0, 0), (0, 0)))
     own_rows = lax.dynamic_slice_in_dim(padded_rows, chan_pos * row_part, row_part + 2, 0)
     extended = with_halo(own_rows, (("strip", 1),), 3)
-    extended, early = lax.optimization_barrier((extended, early))
     early = tree_gather(early, "strip", order[2:4], shifted)
     hidden = swish(convolve(extended, conv_weight, row_part, col_local + 4) + conv_bias)
     pooled = pool_pairs(hidden)

time: 148 us -> 150 us (1.014)
  Pallas kernels: 65.7 us -> 67.2 us
    ppermute x6, waiting for transfers between devices: 7.36 us -> 8.96 us  [tree_gather(): other = lax.ppermute(held, axis, pairs)]
    ppermute x3, waiting for transfers between devices: 1.58 us -> 0.01 us  [body(): lax.ppermute(pooled, 'chan', [(i, (i + shift) % chan_count) for i in rang...]
    pallas_call x1, Pallas kernels: 65.7 us -> 67.2 us  [tree_sum(): pl.pallas_call(functools.partial(tree_kernel, count, chunk, width, dists,...]
  transfers between devices with their start and end apart: 11 -> 11, of which waited for: 6 -> 6; matrix products, arithmetic and copies ran while one was open for 9% -> 10% of each run, Pallas kernels for 0% -> 0%
where the time goes in v14:
time: 150 us
  Pallas kernels  67.2 us (45%)
  starting transfers between devices  34.6 us (23%)
  local copies, waits for them, and re-layouts  15.2 us (10%)
  matrix products  15.2 us (10%)
  waiting for transfers between devices  11.1 us (7%)
  other arithmetic  4.89 us (3%)
  between operations  1.57 us (1%)
    pallas_call x1, Pallas kernels, tree_sum(): pl.pallas_call(functools.partial(tree_kernel, count, chunk, width, dists,...  67.2 us
    ppermute x6, starting transfers between devices, tree_gather(): other = lax.ppermute(held, axis, pairs)  24.2 us
    ppermute x6, waiting for transfers between devices, tree_gather(): other = lax.ppermute(held, axis, pairs)  8.96 us
    dot_general x18, matrix products, convolve(): jnp.dot(band, weight[shift_row, shift_col], preferred_element_type=jnp.fl...  7.33 us
    ppermute x3, starting transfers between devices, body(): lax.ppermute(pooled, 'chan', [(i, (i + shift) % chan_count) for i in rang...  5.04 us
    dot_general x9, matrix products, body(): lax.dot_general(band, placed_grads[shift_col], (((0,), (0,)), ((), ())),...  4.33 us
    unnamed x20, local copies, waits for them, and re-layouts  4.28 us
    ppermute x1, starting transfers between devices, with_halo(): lax.ppermute(tail, axis, [(i, (i + 1) % count) for i in range(ends)])  3.49 us
  transfers between devices with their start and end apart: 11, of which 6 were waited for; matrix products, arithmetic and copies ran while one was open for 10% of the time, Pallas kernels for 0%

profile of v14, /device:TPU:1, one launch (start us, length us, event | category | flops | bytes accessed | tf_op | source)
XLA Modules:
  0.0 149.7 jit_solution(4864854858459115569)
XLA Ops:
  3.2 7.7 %collective-permute-start.2 = (f32[72,128]{1,0:T(8,128)S(1)}, f32[72,128]{1,0:T(8,128)S(1)}, u32[]{:S(2)}, u32[]{:S(2)}) collective-permute-start(f32[72,128]{1,0:T(8,128)S(1)} %get-tuple-element.33), channel_id=1, source_target_pairs={{0,32},{4,36},{8,40},{12,44},{16,48},{20,52},{24,56},{28,60},{32,0... | collective-permute-start | bytes 110600 | tf_op jit(solution)/shard_map/ppermute | solution.py:62
  12.0 3.5 %collective-permute-start = (bf16[14,3,256]{2,1,0:T(4,128)(2,1)S(1)}, bf16[14,3,256]{2,1,0:T(4,128)(2,1)S(1)}, u32[]{:S(2)}, u32[]{:S(2)}) collective-permute-start(bf16[14,3,256]{2,1,0:T(4,128)(2,1)S(1)} %get-tuple-element.25), channel_id=1, source_target_pairs={{0,4},{4,8},{8,12},{12,16},{16,20},{20,24},{24,28},{28,32},{32,36}... | collective-permute-start | bytes 64520 | tf_op jit(solution)/shard_map/ppermute | solution.py:20
  15.5 1.9 %collective-permute-start.1 = (bf16[14,3,256]{2,1,0:T(4,128)(2,1)S(1)}, bf16[14,3,256]{2,1,0:T(4,128)(2,1)S(1)}, u32[]{:S(2)}, u32[]{:S(2)}) collective-permute-start(bf16[14,3,256]{2,1,0:T(4,128)(2,1)S(1)} %get-tuple-element.26), channel_id=1, source_target_pairs={{4,0},{8,4},{12,8},{16,12},{20,16},{24,20},{28,24},{32,28},{36,32}... | collective-permute-start | bytes 64520 | tf_op jit(solution)/shard_map/ppermute | solution.py:22
  18.6 2.1 %collective-permute-done.1 = bf16[14,3,256]{2,1,0:T(4,128)(2,1)S(1)} collective-permute-done((bf16[14,3,256]{2,1,0:T(4,128)(2,1)S(1)}, bf16[14,3,256]{2,1,0:T(4,128)(2,1)S(1)}, u32[]{:S(2)}, u32[]{:S(2)}) %collective-permute-start.1) | collective-permute-done | bytes 21536 | tf_op jit(solution)/shard_map/ppermute | solution.py:22
  21.4 1.1 copy-done.4
  26.2 2.8 %collective-permute-start.3 = (f32[144,128]{1,0:T(8,128)S(1)}, f32[144,128]{1,0:T(8,128)S(1)}, u32[]{:S(2)}, u32[]{:S(2)}) collective-permute-start(f32[144,128]{1,0:T(8,128)S(1)} %constant_dynamic-update-slice_fusion.14), channel_id=1, source_target_pairs={{0,128},{4,132},{8,136},{12,140},{16,144},{20,148},{24,152},{28,15... | collective-permute-start | bytes 221192 | tf_op jit(solution)/shard_map/ppermute | solution.py:62
  29.0 1.9 %collective-permute-done.3 = f32[144,128]{1,0:T(8,128)S(1)} collective-permute-done((f32[144,128]{1,0:T(8,128)S(1)}, f32[144,128]{1,0:T(8,128)S(1)}, u32[]{:S(2)}, u32[]{:S(2)}) %collective-permute-start.3) | collective-permute-done | bytes 73760 | tf_op jit(solution)/shard_map/ppermute | solution.py:62
  31.0 2.0 %collective-permute-start.4 = (f32[288,128]{1,0:T(8,128)S(1)}, f32[288,128]{1,0:T(8,128)}, u32[]{:S(2)}, u32[]{:S(2)}) collective-permute-start(f32[288,128]{1,0:T(8,128)S(1)} %constant_dynamic-update-slice_fusion.12), channel_id=1, source_target_pairs={{0,16},{4,20},{8,24},{12,60},{16,0},{20,4},{24,8},{28,44},{32,48},... | collective-permute-start | bytes 442376 | tf_op jit(solution)/shard_map/ppermute | solution.py:62
  34.7 1.1 reduce_sum.27
  37.0 3.8 %collective-permute-start.5 = (f32[576,128]{1,0:T(8,128)S(1)}, f32[576,128]{1,0:T(8,128)S(1)}, u32[]{:S(2)}, u32[]{:S(2)}) collective-permute-start(f32[576,128]{1,0:T(8,128)S(1)} %constant_dynamic-update-slice_fusion.10), channel_id=1, source_target_pairs={{0,64},{4,196},{8,72},{12,204},{16,80},{20,212},{24,88},{28,220},{... | collective-permute-start | bytes 884744 | tf_op jit(solution)/shard_map/ppermute | solution.py:62
  41.0 3.9 %collective-permute-done.5 = f32[576,128]{1,0:T(8,128)S(1)} collective-permute-done((f32[576,128]{1,0:T(8,128)S(1)}, f32[576,128]{1,0:T(8,128)S(1)}, u32[]{:S(2)}, u32[]{:S(2)}) %collective-permute-start.5) | collective-permute-done | bytes 294944 | tf_op jit(solution)/shard_map/ppermute | solution.py:62
  45.0 1.4 collective-permute-start.8
  46.3 2.5 %collective-permute-start.9 = (bf16[6,66,256]{2,1,0:T(8,128)(2,1)S(1)}, bf16[6,66,256]{2,1,0:T(8,128)(2,1)S(1)}, u32[]{:S(2)}, u32[]{:S(2)}) collective-permute-start(bf16[6,66,256]{2,1,0:T(8,128)(2,1)S(1)} %fusion.49), channel_id=1, source_target_pairs={{0,2},{1,3},{2,0},{3,1},{4,6},{5,7},{6,4},{7,5},{8,10},{9,11},{10,... | collective-permute-start | bytes 608264 | tf_op jit(solution)/shard_map/ppermute | solution.py:272
  48.8 1.2 collective-permute-start.10
  50.0 6.5 %collective-permute-start.6 = (f32[1152,128]{1,0:T(8,128)S(1)}, f32[1152,128]{1,0:T(8,128)S(1)}, u32[]{:S(2)}, u32[]{:S(2)}) collective-permute-start(f32[1152,128]{1,0:T(8,128)S(1)} %constant_dynamic-update-slice_fusion.8), channel_id=1, source_target_pairs={{0,8},{4,60},{8,0},{12,20},{16,24},{20,12},{24,16},{28,36},{32,40}... | collective-permute-start | bytes 1769480 | tf_op jit(solution)/shard_map/ppermute | solution.py:62
  61.7 2.1 %collective-permute-done.6 = f32[1152,128]{1,0:T(8,128)S(1)} collective-permute-done((f32[1152,128]{1,0:T(8,128)S(1)}, f32[1152,128]{1,0:T(8,128)S(1)}, u32[]{:S(2)}, u32[]{:S(2)}) %collective-permute-start.6) | collective-permute-done | bytes 589856 | tf_op jit(solution)/shard_map/ppermute | solution.py:62
  63.9 1.2 collective-permute-start.7
  67.7 1.3 copy-done.2
  69.2 1.4 gather_fusion.1
  76.2 1.1 copy-done.3
  77.2 67.2 %shard_map.112 = (f32[2560,128]{1,0:T(8,128)}, f32[2048,128]{1,0:T(8,128)}) custom-call(f32[2560,128]{1,0:T(8,128)} %copy-done.3, f32[32,128]{1,0:T(8,128)} %fusion.50.sums_ref), custom_call_target="tpu_custom_call" | custom-call | tf_op jit(solution)/shard_map/pallas_call | solution.py:169
  144.5 2.4 %slice.171 = f32[2304,128]{1,0:T(8,128)} slice(f32[2560,128]{1,0:T(8,128)} %get-tuple-element.22), slice={[0:2304], [0:128]} | slice | bytes 2359296 | tf_op jit(solution)/shard_map/slice | solution.py:327
  146.9 1.2 slice_bitcast_fusion
  148.5 1.2 convolution_divide_fusion
  (103 shorter events, 25.6 us)
Async XLA Ops:
  3.2 22.9 %collective-permute-start.2 = (f32[72,128]{1,0:T(8,128)S(1)}, f32[72,128]{1,0:T(8,128)S(1)}, u32[]{:S(2)}, u32[]{:S(2)}) collective-permute-start(f32[72,128]{1,0:T(8,128)S(1)} %get-tuple-element.33), channel_id=1, source_target_pairs={{0,32},{4,36},{8,40},{12,44},{16,48},{20,52},{24,56},{28,60},{32,0... | collective-permute-start | bytes 110600 | tf_op jit(solution)/shard_map/ppermute | solution.py:62
  11.0 6.5 %copy-start.1 = (bf16[48,128,256]{2,1,0:T(8,128)(2,1)S(1)}, bf16[48,128,256]{2,1,0:T(8,128)(2,1)}, u32[]{:S(2)}) copy-start(bf16[48,128,256]{2,1,0:T(8,128)(2,1)} %param.11) | copy-start | bytes 9437188
  12.0 6.6 %collective-permute-start = (bf16[14,3,256]{2,1,0:T(4,128)(2,1)S(1)}, bf16[14,3,256]{2,1,0:T(4,128)(2,1)S(1)}, u32[]{:S(2)}, u32[]{:S(2)}) collective-permute-start(bf16[14,3,256]{2,1,0:T(4,128)(2,1)S(1)} %get-tuple-element.25), channel_id=1, source_target_pairs={{0,4},{4,8},{8,12},{12,16},{16,20},{20,24},{24,28},{28,32},{32,36}... | collective-permute-start | bytes 64520 | tf_op jit(solution)/shard_map/ppermute | solution.py:20
  15.5 2.1 %copy-start = (s32[64]{0:T(128)S(1)}, s32[64]{0:T(128)}, u32[]{:S(2)}) copy-start(s32[64]{0:T(128)} %constant.295.clone) | copy-start | bytes 772
  15.5 2.8 %copy-start.9 = (s32[32]{0:T(128)S(1)}, s32[32]{0:T(128)}, u32[]{:S(2)}) copy-start(s32[32]{0:T(128)} %param.17) | copy-start | bytes 388
  15.5 5.2 %collective-permute-start.1 = (bf16[14,3,256]{2,1,0:T(4,128)(2,1)S(1)}, bf16[14,3,256]{2,1,0:T(4,128)(2,1)S(1)}, u32[]{:S(2)}, u32[]{:S(2)}) collective-permute-start(bf16[14,3,256]{2,1,0:T(4,128)(2,1)S(1)} %get-tuple-element.26), channel_id=1, source_target_pairs={{4,0},{8,4},{12,8},{16,12},{20,16},{24,20},{28,24},{32,28},{36,32}... | collective-permute-start | bytes 64520 | tf_op jit(solution)/shard_map/ppermute | solution.py:22
  21.2 1.3 copy-start.4
  25.7 7.3 %copy-start.7 = (f32[256]{0:T(256)S(1)}, f32[256]{0:T(256)}, u32[]{:S(2)}) copy-start(f32[256]{0:T(256)} %param.13) | copy-start | bytes 3076
  26.2 4.8 %collective-permute-start.3 = (f32[144,128]{1,0:T(8,128)S(1)}, f32[144,128]{1,0:T(8,128)S(1)}, u32[]{:S(2)}, u32[]{:S(2)}) collective-permute-start(f32[144,128]{1,0:T(8,128)S(1)} %constant_dynamic-update-slice_fusion.14), channel_id=1, source_target_pairs={{0,128},{4,132},{8,136},{12,140},{16,144},{20,148},{24,152},{28,15... | collective-permute-start | bytes 221192 | tf_op jit(solution)/shard_map/ppermute | solution.py:62
  31.0 5.1 %collective-permute-start.4 = (f32[288,128]{1,0:T(8,128)S(1)}, f32[288,128]{1,0:T(8,128)}, u32[]{:S(2)}, u32[]{:S(2)}) collective-permute-start(f32[288,128]{1,0:T(8,128)S(1)} %constant_dynamic-update-slice_fusion.12), channel_id=1, source_target_pairs={{0,16},{4,20},{8,24},{12,60},{16,0},{20,4},{24,8},{28,44},{32,48},... | collective-permute-start | bytes 442376 | tf_op jit(solution)/shard_map/ppermute | solution.py:62
  37.0 8.0 %collective-permute-start.5 = (f32[576,128]{1,0:T(8,128)S(1)}, f32[576,128]{1,0:T(8,128)S(1)}, u32[]{:S(2)}, u32[]{:S(2)}) collective-permute-start(f32[576,128]{1,0:T(8,128)S(1)} %constant_dynamic-update-slice_fusion.10), channel_id=1, source_target_pairs={{0,64},{4,196},{8,72},{12,204},{16,80},{20,212},{24,88},{28,220},{... | collective-permute-start | bytes 884744 | tf_op jit(solution)/shard_map/ppermute | solution.py:62
  45.0 11.8 %collective-permute-start.8 = (bf16[6,66,256]{2,1,0:T(8,128)(2,1)S(1)}, bf16[6,66,256]{2,1,0:T(8,128)(2,1)S(1)}, u32[]{:S(2)}, u32[]{:S(2)}) collective-permute-start(bf16[6,66,256]{2,1,0:T(8,128)(2,1)S(1)} %fusion.49), channel_id=1, source_target_pairs={{0,1},{1,2},{2,3},{3,0},{4,5},{5,6},{6,7},{7,4},{8,9},{9,10},{10,1... | collective-permute-start | bytes 608264 | tf_op jit(solution)/shard_map/ppermute | solution.py:272
  46.3 10.5 %collective-permute-start.9 = (bf16[6,66,256]{2,1,0:T(8,128)(2,1)S(1)}, bf16[6,66,256]{2,1,0:T(8,128)(2,1)S(1)}, u32[]{:S(2)}, u32[]{:S(2)}) collective-permute-start(bf16[6,66,256]{2,1,0:T(8,128)(2,1)S(1)} %fusion.49), channel_id=1, source_target_pairs={{0,2},{1,3},{2,0},{3,1},{4,6},{5,7},{6,4},{7,5},{8,10},{9,11},{10,... | collective-permute-start | bytes 608264 | tf_op jit(solution)/shard_map/ppermute | solution.py:272
  48.8 8.0 %collective-permute-start.10 = (bf16[6,66,256]{2,1,0:T(8,128)(2,1)S(1)}, bf16[6,66,256]{2,1,0:T(8,128)(2,1)S(1)}, u32[]{:S(2)}, u32[]{:S(2)}) collective-permute-start(bf16[6,66,256]{2,1,0:T(8,128)(2,1)S(1)} %fusion.49), channel_id=1, source_target_pairs={{0,3},{1,0},{2,1},{3,2},{4,7},{5,4},{6,5},{7,6},{8,11},{9,8},{10,9... | collective-permute-start | bytes 608264 | tf_op jit(solution)/shard_map/ppermute | solution.py:272
  50.0 13.8 %collective-permute-start.6 = (f32[1152,128]{1,0:T(8,128)S(1)}, f32[1152,128]{1,0:T(8,128)S(1)}, u32[]{:S(2)}, u32[]{:S(2)}) collective-permute-start(f32[1152,128]{1,0:T(8,128)S(1)} %constant_dynamic-update-slice_fusion.8), channel_id=1, source_target_pairs={{0,8},{4,60},{8,0},{12,20},{16,24},{20,12},{24,16},{28,36},{32,40}... | collective-permute-start | bytes 1769480 | tf_op jit(solution)/shard_map/ppermute | solution.py:62
  56.9 1.1 copy-start.6
  61.3 3.7 %copy-start.8 = (f32[128]{0:T(128)S(1)}, f32[128]{0:T(128)}, u32[]{:S(2)}) copy-start(f32[128]{0:T(128)} %param.15) | copy-start | bytes 1540
  63.9 3.6 %collective-permute-start.7 = (f32[2304,128]{1,0:T(8,128)S(1)}, f32[2304,128]{1,0:T(8,128)S(1)}, u32[]{:S(2)}, u32[]{:S(2)}) collective-permute-start(f32[2304,128]{1,0:T(8,128)S(1)} %constant_dynamic-update-slice_fusion.6), channel_id=1, source_target_pairs={{0,4},{4,0},{8,12},{12,8},{16,20},{20,16},{24,28},{28,24},{32,36},... | collective-permute-start | bytes 3538952 | tf_op jit(solution)/shard_map/ppermute | solution.py:62
  67.6 1.4 copy-start.2
  76.2 1.1 copy-start.3
  144.5 4.0 %copy-start.5 = (f32[2048,128]{1,0:T(8,128)S(1)}, f32[2048,128]{1,0:T(8,128)}, u32[]{:S(2)}) copy-start(f32[2048,128]{1,0:T(8,128)} %get-tuple-element.21) | copy-start | bytes 3145732

commit v15 on v13

--- a/solution.py
+++ b/solution.py
@@ -75,7 +75,9 @@
     )
 
 
-def tree_kernel(count, chunk, width, dists, shifted, grads_ref, sums_ref, out_ref, every_ref, landing, sems, free):
+def tree_kernel(
+    count, chunk, width, dists, shifted, grads_ref, sums_ref, out_ref, every_ref, landing, sems, free, load
+):
     me = lax.axis_index("strip")
     chan = lax.axis_index("chan")
     mesh_id = pl.DeviceIdType.MESH
@@ -83,12 +85,14 @@
     def partner(dist):
         return strip_partner(me, dist, shifted)
 
+    staging = pltpu.make_async_copy(grads_ref, out_ref, load.at[0])
+    staging.start()
     barrier = pltpu.get_barrier_semaphore()
     for dist in dists:
         pl.semaphore_signal(barrier, inc=1, device_id=(partner(dist), chan), device_id_type=mesh_id)
     pl.semaphore_wait(barrier, len(dists))
 
-    out_ref[...] = grads_ref[...]
+    staging.wait()
     place = 0
     for k, dist in enumerate(dists):
         place = place + (strip_bit(me, dist, shifted)) * (count >> (k + 1))
@@ -172,12 +176,13 @@
             jax.ShapeDtypeStruct((rows, lanes), jnp.float32),
             jax.ShapeDtypeStruct((count * width, lanes), jnp.float32),
         ),
-        in_specs=[pl.BlockSpec(memory_space=pltpu.VMEM)] * 2,
+        in_specs=[pl.BlockSpec(memory_space=pl.ANY), pl.BlockSpec(memory_space=pltpu.VMEM)],
         out_specs=(pl.BlockSpec(memory_space=pltpu.VMEM),) * 2,
         scratch_shapes=[
             pltpu.VMEM((rows, lanes), jnp.float32),
             pltpu.SemaphoreType.DMA((6, steps)),
             pltpu.SemaphoreType.REGULAR((steps,)),
+            pltpu.SemaphoreType.DMA((1,)),
         ],
         compiler_params=pltpu.CompilerParams(collective_id=0, has_side_effects=True),
     )(grads, sums)

time: 148 us -> 147 us (level)
  no operation moved by 1% of the time
where the time goes in v15:
time: 147 us; the launch traced here: 146 us
  Pallas kernels  65 us (44%)
  starting transfers between devices  33.5 us (23%)
  local copies, waits for them, and re-layouts  15.4 us (10%)
  matrix products  15.1 us (10%)
  waiting for transfers between devices  11 us (7%)
  other arithmetic  4.84 us (3%)
  between operations  1.57 us (1%)
    pallas_call x1, Pallas kernels, tree_sum(): pl.pallas_call(functools.partial(tree_kernel, count, chunk, width, dists,...  65 us
    ppermute x6, starting transfers between devices, tree_gather(): other = lax.ppermute(held, axis, pairs)  23 us
    ppermute x6, waiting for transfers between devices, tree_gather(): other = lax.ppermute(held, axis, pairs)  7.36 us
    dot_general x18, matrix products, convolve(): jnp.dot(band, weight[shift_row, shift_col], preferred_element_type=jnp.fl...  7.29 us
    ppermute x3, starting transfers between devices, body(): lax.ppermute(pooled, 'chan', [(i, (i + shift) % chan_count) for i in rang...  5.05 us
    unnamed x20, local copies, waits for them, and re-layouts  4.52 us
    dot_general x9, matrix products, body(): lax.dot_general(band, placed_grads[shift_col], (((0,), (0,)), ((), ())),...  4.33 us
    ppermute x1, starting transfers between devices, with_halo(): lax.ppermute(tail, axis, [(i, (i + 1) % count) for i in range(ends)])  3.49 us
  transfers between devices with their start and end apart: 11, of which 6 were waited for; matrix products, arithmetic and copies ran while one was open for 9% of the time, Pallas kernels for 0%

profile of v15, /device:TPU:1, one launch (start us, length us, event | category | flops | bytes accessed | tf_op | source)
XLA Modules:
  0.0 146.5 jit_solution(7244374674287179114)
XLA Ops:
  3.2 7.7 %collective-permute-start.2 = (f32[72,128]{1,0:T(8,128)S(1)}, f32[72,128]{1,0:T(8,128)S(1)}, u32[]{:S(2)}, u32[]{:S(2)}) collective-permute-start(f32[72,128]{1,0:T(8,128)S(1)} %get-tuple-element.37), channel_id=1, source_target_pairs={{0,32},{4,36},{8,40},{12,44},{16,48},{20,52},{24,56},{28,60},{32,0... | collective-permute-start | bytes 110600 | tf_op jit(solution)/shard_map/ppermute | solution.py:62
  12.0 3.5 %collective-permute-start = (bf16[14,3,256]{2,1,0:T(4,128)(2,1)S(1)}, bf16[14,3,256]{2,1,0:T(4,128)(2,1)S(1)}, u32[]{:S(2)}, u32[]{:S(2)}) collective-permute-start(bf16[14,3,256]{2,1,0:T(4,128)(2,1)S(1)} %get-tuple-element.29), channel_id=1, source_target_pairs={{0,4},{4,8},{8,12},{12,16},{16,20},{20,24},{24,28},{28,32},{32,36}... | collective-permute-start | bytes 64520 | tf_op jit(solution)/shard_map/ppermute | solution.py:20
  15.5 1.9 %collective-permute-start.1 = (bf16[14,3,256]{2,1,0:T(4,128)(2,1)S(1)}, bf16[14,3,256]{2,1,0:T(4,128)(2,1)S(1)}, u32[]{:S(2)}, u32[]{:S(2)}) collective-permute-start(bf16[14,3,256]{2,1,0:T(4,128)(2,1)S(1)} %get-tuple-element.30), channel_id=1, source_target_pairs={{4,0},{8,4},{12,8},{16,12},{20,16},{24,20},{28,24},{32,28},{36,32}... | collective-permute-start | bytes 64520 | tf_op jit(solution)/shard_map/ppermute | solution.py:22
  18.6 2.1 %collective-permute-done.1 = bf16[14,3,256]{2,1,0:T(4,128)(2,1)S(1)} collective-permute-done((bf16[14,3,256]{2,1,0:T(4,128)(2,1)S(1)}, bf16[14,3,256]{2,1,0:T(4,128)(2,1)S(1)}, u32[]{:S(2)}, u32[]{:S(2)}) %collective-permute-start.1) | collective-permute-done | bytes 21536 | tf_op jit(solution)/shard_map/ppermute | solution.py:22
  21.2 2.8 %collective-permute-start.3 = (f32[144,128]{1,0:T(8,128)S(1)}, f32[144,128]{1,0:T(8,128)S(1)}, u32[]{:S(2)}, u32[]{:S(2)}) collective-permute-start(f32[144,128]{1,0:T(8,128)S(1)} %constant_dynamic-update-slice_fusion.14), channel_id=1, source_target_pairs={{0,128},{4,132},{8,136},{12,140},{16,144},{20,148},{24,152},{28,15... | collective-permute-start | bytes 221192 | tf_op jit(solution)/shard_map/ppermute | solution.py:62
  24.0 1.9 %collective-permute-done.3 = f32[144,128]{1,0:T(8,128)S(1)} collective-permute-done((f32[144,128]{1,0:T(8,128)S(1)}, f32[144,128]{1,0:T(8,128)S(1)}, u32[]{:S(2)}, u32[]{:S(2)}) %collective-permute-start.3) | collective-permute-done | bytes 73760 | tf_op jit(solution)/shard_map/ppermute | solution.py:62
  26.2 1.1 copy-done.4
  28.4 2.1 %collective-permute-start.4 = (f32[288,128]{1,0:T(8,128)S(1)}, f32[288,128]{1,0:T(8,128)}, u32[]{:S(2)}, u32[]{:S(2)}) collective-permute-start(f32[288,128]{1,0:T(8,128)S(1)} %constant_dynamic-update-slice_fusion.12), channel_id=1, source_target_pairs={{0,16},{4,20},{8,24},{12,60},{16,0},{20,4},{24,8},{28,44},{32,48},... | collective-permute-start | bytes 442376 | tf_op jit(solution)/shard_map/ppermute | solution.py:62
  34.8 1.1 reduce_sum.28
  37.0 2.6 %collective-permute-start.5 = (f32[576,128]{1,0:T(8,128)S(1)}, f32[576,128]{1,0:T(8,128)S(1)}, u32[]{:S(2)}, u32[]{:S(2)}) collective-permute-start(f32[576,128]{1,0:T(8,128)S(1)} %constant_dynamic-update-slice_fusion.10), channel_id=1, source_target_pairs={{0,64},{4,196},{8,72},{12,204},{16,80},{20,212},{24,88},{28,220},{... | collective-permute-start | bytes 884744 | tf_op jit(solution)/shard_map/ppermute | solution.py:62
  39.7 4.1 %collective-permute-done.5 = f32[576,128]{1,0:T(8,128)S(1)} collective-permute-done((f32[576,128]{1,0:T(8,128)S(1)}, f32[576,128]{1,0:T(8,128)S(1)}, u32[]{:S(2)}, u32[]{:S(2)}) %collective-permute-start.5) | collective-permute-done | bytes 294944 | tf_op jit(solution)/shard_map/ppermute | solution.py:62
  43.9 1.4 collective-permute-start.8
  45.2 2.6 %collective-permute-start.9 = (bf16[6,66,256]{2,1,0:T(8,128)(2,1)S(1)}, bf16[6,66,256]{2,1,0:T(8,128)(2,1)S(1)}, u32[]{:S(2)}, u32[]{:S(2)}) collective-permute-start(bf16[6,66,256]{2,1,0:T(8,128)(2,1)S(1)} %fusion.44), channel_id=1, source_target_pairs={{0,2},{1,3},{2,0},{3,1},{4,6},{5,7},{6,4},{7,5},{8,10},{9,11},{10,... | collective-permute-start | bytes 608264 | tf_op jit(solution)/shard_map/ppermute | solution.py:278
  47.9 1.0 collective-permute-start.10
  48.9 5.1 %collective-permute-start.6 = (f32[1152,128]{1,0:T(8,128)S(1)}, f32[1152,128]{1,0:T(8,128)S(1)}, u32[]{:S(2)}, u32[]{:S(2)}) collective-permute-start(f32[1152,128]{1,0:T(8,128)S(1)} %constant_dynamic-update-slice_fusion.8), channel_id=1, source_target_pairs={{0,8},{4,60},{8,0},{12,20},{16,24},{20,12},{24,16},{28,36},{32,40}... | collective-permute-start | bytes 1769480 | tf_op jit(solution)/shard_map/ppermute | solution.py:62
  54.3 1.6 %collective-permute-done.9 = bf16[6,66,256]{2,1,0:T(8,128)(2,1)S(1)} collective-permute-done((bf16[6,66,256]{2,1,0:T(8,128)(2,1)S(1)}, bf16[6,66,256]{2,1,0:T(8,128)(2,1)S(1)}, u32[]{:S(2)}, u32[]{:S(2)}) %collective-permute-start.9) | collective-permute-done | bytes 202784 | tf_op jit(solution)/shard_map/ppermute | solution.py:278
  61.4 2.7 %collective-permute-start.7 = (f32[2304,128]{1,0:T(8,128)S(1)}, f32[2304,128]{1,0:T(8,128)S(1)}, u32[]{:S(2)}, u32[]{:S(2)}) collective-permute-start(f32[2304,128]{1,0:T(8,128)S(1)} %constant_dynamic-update-slice_fusion.6), channel_id=1, source_target_pairs={{0,4},{4,0},{8,12},{12,8},{16,20},{20,16},{24,28},{28,24},{32,36},... | collective-permute-start | bytes 3538952 | tf_op jit(solution)/shard_map/ppermute | solution.py:62
  66.8 1.3 copy-done.2
  68.3 1.4 gather_fusion.1
  75.2 1.1 copy-done.3
  76.3 65.0 %shard_map.112 = (f32[2560,128]{1,0:T(8,128)}, f32[2048,128]{1,0:T(8,128)}) custom-call(f32[2560,128]{1,0:T(8,128)} %copy-done.3, f32[32,128]{1,0:T(8,128)} %fusion.45.sums_ref), custom_call_target="tpu_custom_call" | custom-call | tf_op jit(solution)/shard_map/pallas_call | solution.py:173
  141.3 2.4 %slice.171 = f32[2304,128]{1,0:T(8,128)} slice(f32[2560,128]{1,0:T(8,128)} %get-tuple-element.26), slice={[0:2304], [0:128]} | slice | bytes 2359296 | tf_op jit(solution)/shard_map/slice | solution.py:333
  143.7 1.2 slice_bitcast_fusion
  145.3 1.2 convolution_divide_fusion
  (103 shorter events, 26.1 us)
Async XLA Ops:
  3.2 17.9 %collective-permute-start.2 = (f32[72,128]{1,0:T(8,128)S(1)}, f32[72,128]{1,0:T(8,128)S(1)}, u32[]{:S(2)}, u32[]{:S(2)}) collective-permute-start(f32[72,128]{1,0:T(8,128)S(1)} %get-tuple-element.37), channel_id=1, source_target_pairs={{0,32},{4,36},{8,40},{12,44},{16,48},{20,52},{24,56},{28,60},{32,0... | collective-permute-start | bytes 110600 | tf_op jit(solution)/shard_map/ppermute | solution.py:62
  11.0 6.5 %copy-start.1 = (bf16[48,128,256]{2,1,0:T(8,128)(2,1)S(1)}, bf16[48,128,256]{2,1,0:T(8,128)(2,1)}, u32[]{:S(2)}) copy-start(bf16[48,128,256]{2,1,0:T(8,128)(2,1)} %param.11) | copy-start | bytes 9437188
  12.0 6.6 %collective-permute-start = (bf16[14,3,256]{2,1,0:T(4,128)(2,1)S(1)}, bf16[14,3,256]{2,1,0:T(4,128)(2,1)S(1)}, u32[]{:S(2)}, u32[]{:S(2)}) collective-permute-start(bf16[14,3,256]{2,1,0:T(4,128)(2,1)S(1)} %get-tuple-element.29), channel_id=1, source_target_pairs={{0,4},{4,8},{8,12},{12,16},{16,20},{20,24},{24,28},{28,32},{32,36}... | collective-permute-start | bytes 64520 | tf_op jit(solution)/shard_map/ppermute | solution.py:20
  15.5 2.1 %copy-start = (s32[64]{0:T(128)S(1)}, s32[64]{0:T(128)}, u32[]{:S(2)}) copy-start(s32[64]{0:T(128)} %constant.295.clone) | copy-start | bytes 772
  15.5 2.8 %copy-start.9 = (s32[32]{0:T(128)S(1)}, s32[32]{0:T(128)}, u32[]{:S(2)}) copy-start(s32[32]{0:T(128)} %param.17) | copy-start | bytes 388
  15.5 5.2 %collective-permute-start.1 = (bf16[14,3,256]{2,1,0:T(4,128)(2,1)S(1)}, bf16[14,3,256]{2,1,0:T(4,128)(2,1)S(1)}, u32[]{:S(2)}, u32[]{:S(2)}) collective-permute-start(bf16[14,3,256]{2,1,0:T(4,128)(2,1)S(1)} %get-tuple-element.30), channel_id=1, source_target_pairs={{4,0},{8,4},{12,8},{16,12},{20,16},{24,20},{28,24},{32,28},{36,32}... | collective-permute-start | bytes 64520 | tf_op jit(solution)/shard_map/ppermute | solution.py:22
  21.2 4.8 %collective-permute-start.3 = (f32[144,128]{1,0:T(8,128)S(1)}, f32[144,128]{1,0:T(8,128)S(1)}, u32[]{:S(2)}, u32[]{:S(2)}) collective-permute-start(f32[144,128]{1,0:T(8,128)S(1)} %constant_dynamic-update-slice_fusion.14), channel_id=1, source_target_pairs={{0,128},{4,132},{8,136},{12,140},{16,144},{20,148},{24,152},{28,15... | collective-permute-start | bytes 221192 | tf_op jit(solution)/shard_map/ppermute | solution.py:62
  26.0 1.3 copy-start.4
  28.4 7.6 %collective-permute-start.4 = (f32[288,128]{1,0:T(8,128)S(1)}, f32[288,128]{1,0:T(8,128)}, u32[]{:S(2)}, u32[]{:S(2)}) collective-permute-start(f32[288,128]{1,0:T(8,128)S(1)} %constant_dynamic-update-slice_fusion.12), channel_id=1, source_target_pairs={{0,16},{4,20},{8,24},{12,60},{16,0},{20,4},{24,8},{28,44},{32,48},... | collective-permute-start | bytes 442376 | tf_op jit(solution)/shard_map/ppermute | solution.py:62
  32.5 0.7 copy-start.7
  37.0 6.9 %collective-permute-start.5 = (f32[576,128]{1,0:T(8,128)S(1)}, f32[576,128]{1,0:T(8,128)S(1)}, u32[]{:S(2)}, u32[]{:S(2)}) collective-permute-start(f32[576,128]{1,0:T(8,128)S(1)} %constant_dynamic-update-slice_fusion.10), channel_id=1, source_target_pairs={{0,64},{4,196},{8,72},{12,204},{16,80},{20,212},{24,88},{28,220},{... | collective-permute-start | bytes 884744 | tf_op jit(solution)/shard_map/ppermute | solution.py:62
  43.9 10.4 %collective-permute-start.8 = (bf16[6,66,256]{2,1,0:T(8,128)(2,1)S(1)}, bf16[6,66,256]{2,1,0:T(8,128)(2,1)S(1)}, u32[]{:S(2)}, u32[]{:S(2)}) collective-permute-start(bf16[6,66,256]{2,1,0:T(8,128)(2,1)S(1)} %fusion.44), channel_id=1, source_target_pairs={{0,1},{1,2},{2,3},{3,0},{4,5},{5,6},{6,7},{7,4},{8,9},{9,10},{10,1... | collective-permute-start | bytes 608264 | tf_op jit(solution)/shard_map/ppermute | solution.py:278
  45.2 10.7 %collective-permute-start.9 = (bf16[6,66,256]{2,1,0:T(8,128)(2,1)S(1)}, bf16[6,66,256]{2,1,0:T(8,128)(2,1)S(1)}, u32[]{:S(2)}, u32[]{:S(2)}) collective-permute-start(bf16[6,66,256]{2,1,0:T(8,128)(2,1)S(1)} %fusion.44), channel_id=1, source_target_pairs={{0,2},{1,3},{2,0},{3,1},{4,6},{5,7},{6,4},{7,5},{8,10},{9,11},{10,... | collective-permute-start | bytes 608264 | tf_op jit(solution)/shard_map/ppermute | solution.py:278
  47.9 8.1 %collective-permute-start.10 = (bf16[6,66,256]{2,1,0:T(8,128)(2,1)S(1)}, bf16[6,66,256]{2,1,0:T(8,128)(2,1)S(1)}, u32[]{:S(2)}, u32[]{:S(2)}) collective-permute-start(bf16[6,66,256]{2,1,0:T(8,128)(2,1)S(1)} %fusion.44), channel_id=1, source_target_pairs={{0,3},{1,0},{2,1},{3,2},{4,7},{5,4},{6,5},{7,6},{8,11},{9,8},{10,9... | collective-permute-start | bytes 608264 | tf_op jit(solution)/shard_map/ppermute | solution.py:278
  48.9 12.4 %collective-permute-start.6 = (f32[1152,128]{1,0:T(8,128)S(1)}, f32[1152,128]{1,0:T(8,128)S(1)}, u32[]{:S(2)}, u32[]{:S(2)}) collective-permute-start(f32[1152,128]{1,0:T(8,128)S(1)} %constant_dynamic-update-slice_fusion.8), channel_id=1, source_target_pairs={{0,8},{4,60},{8,0},{12,20},{16,24},{20,12},{24,16},{28,36},{32,40}... | collective-permute-start | bytes 1769480 | tf_op jit(solution)/shard_map/ppermute | solution.py:62
  56.0 1.1 copy-start.6
  60.4 3.6 %copy-start.8 = (f32[128]{0:T(128)S(1)}, f32[128]{0:T(128)}, u32[]{:S(2)}) copy-start(f32[128]{0:T(128)} %param.15) | copy-start | bytes 1540
  61.4 5.1 %collective-permute-start.7 = (f32[2304,128]{1,0:T(8,128)S(1)}, f32[2304,128]{1,0:T(8,128)S(1)}, u32[]{:S(2)}, u32[]{:S(2)}) collective-permute-start(f32[2304,128]{1,0:T(8,128)S(1)} %constant_dynamic-update-slice_fusion.6), channel_id=1, source_target_pairs={{0,4},{4,0},{8,12},{12,8},{16,20},{20,16},{24,28},{28,24},{32,36},... | collective-permute-start | bytes 3538952 | tf_op jit(solution)/shard_map/ppermute | solution.py:62
  66.6 1.4 copy-start.2
  75.2 1.1 copy-start.3
  141.3 4.0 %copy-start.5 = (f32[2048,128]{1,0:T(8,128)S(1)}, f32[2048,128]{1,0:T(8,128)}, u32[]{:S(2)}) copy-start(f32[2048,128]{1,0:T(8,128)} %get-tuple-element.25) | copy-start | bytes 3145732

commit v16 on v13

--- a/solution.py
+++ b/solution.py
@@ -295,24 +295,23 @@
     deep_width = -(-padded_deep.shape[1] // 16) * 16
     wide_deep = jnp.pad(padded_deep, ((0, 0), (0, deep_width - padded_deep.shape[1]), (0, 0)))
     grid_grad = deep_grad.reshape(half_rows, half_cols, width_deep)
-    placed_grads = [
-        jnp.pad(
-            grid_grad, ((0, 0), (shift_col, deep_width - half_cols - shift_col), (0, 0))
-        ).reshape(-1, width_deep)
-        for shift_col in range(3)
-    ]
+    placed_grads = jnp.concatenate(
+        [
+            jnp.pad(
+                grid_grad, ((0, 0), (shift_col, deep_width - half_cols - shift_col), (0, 0))
+            ).reshape(-1, width_deep)
+            for shift_col in range(3)
+        ],
+        axis=1,
+    )
     pieces = []
     for shift_row in range(3):
         band = wide_deep[shift_row : shift_row + half_rows].reshape(-1, channels)
+        row_terms = lax.dot_general(
+            band, placed_grads, (((0,), (0,)), ((), ())), preferred_element_type=jnp.float32
+        )
         for shift_col in range(3):
-            pieces.append(
-                lax.dot_general(
-                    band,
-                    placed_grads[shift_col],
-                    (((0,), (0,)), ((), ())),
-                    preferred_element_type=jnp.float32,
-                )
-            )
+            pieces.append(row_terms[:, shift_col * width_deep : (shift_col + 1) * width_deep])
     local_bias = jnp.sum(deep_grad.astype(jnp.float32), axis=0)
     bias_rows = jnp.zeros((strip_count * 8 - 9 * channels % (strip_count * 8), width_deep), jnp.float32)
     bias_rows = bias_rows.at[0].set(local_bias)

time: 148 us -> 148 us (level)
  other arithmetic: 4.84 us -> 7.05 us
  waiting for transfers between devices: 11 us -> 9.37 us
    dot_general x9 -> x3, matrix products: 4.34 us -> 2.26 us  [body(): lax.dot_general(band, placed_grads, (((0,), (0,)), ((), ())), preferred_e...]
    unnamed x20 -> x29, local copies, waits for them, and re-layouts: 4.52 us -> 4.6 us
  transfers between devices with their start and end apart: 11 -> 11, of which waited for: 6 -> 5; matrix products, arithmetic and copies ran while one was open for 9% -> 11% of each run, Pallas kernels for 0% -> 0%
where the time goes in v16:
time: 148 us; the launch traced here: 147 us
  Pallas kernels  65.2 us (44%)
  starting transfers between devices  33.4 us (23%)
  local copies, waits for them, and re-layouts  16.6 us (11%)
  matrix products  14.2 us (10%)
  waiting for transfers between devices  9.37 us (6%)
  other arithmetic  7.05 us (5%)
  between operations  1.58 us (1%)
    pallas_call x1, Pallas kernels, tree_sum(): pl.pallas_call(functools.partial(tree_kernel, count, chunk, width, dists,...  65.2 us
    ppermute x6, starting transfers between devices, tree_gather(): other = lax.ppermute(held, axis, pairs)  23 us
    dot_general x18, matrix products, convolve(): jnp.dot(band, weight[shift_row, shift_col], preferred_element_type=jnp.fl...  7.33 us
    ppermute x6, waiting for transfers between devices, tree_gather(): other = lax.ppermute(held, axis, pairs)  6.99 us
    ppermute x3, starting transfers between devices, body(): lax.ppermute(pooled, 'chan', [(i, (i + shift) % chan_count) for i in rang...  5.07 us
    unnamed x29, local copies, waits for them, and re-layouts  4.6 us
    ppermute x1, starting transfers between devices, with_halo(): lax.ppermute(tail, axis, [(i, (i + 1) % count) for i in range(ends)])  3.49 us
  transfers between devices with their start and end apart: 11, of which 5 were waited for; matrix products, arithmetic and copies ran while one was open for 11% of the time, Pallas kernels for 0%

profile of v16, /device:TPU:1, one launch (start us, length us, event | category | flops | bytes accessed | tf_op | source)
XLA Modules:
  0.0 147.4 jit_solution(9466120801622227741)
XLA Ops:
  3.4 7.7 %collective-permute-start.2 = (f32[72,128]{1,0:T(8,128)S(1)}, f32[72,128]{1,0:T(8,128)S(1)}, u32[]{:S(2)}, u32[]{:S(2)}) collective-permute-start(f32[72,128]{1,0:T(8,128)S(1)} %get-tuple-element.40), channel_id=1, source_target_pairs={{0,32},{4,36},{8,40},{12,44},{16,48},{20,52},{24,56},{28,60},{32,0... | collective-permute-start | bytes 110600 | tf_op jit(solution)/shard_map/ppermute | solution.py:62
  12.0 3.5 %collective-permute-start = (bf16[14,3,256]{2,1,0:T(4,128)(2,1)S(1)}, bf16[14,3,256]{2,1,0:T(4,128)(2,1)S(1)}, u32[]{:S(2)}, u32[]{:S(2)}) collective-permute-start(bf16[14,3,256]{2,1,0:T(4,128)(2,1)S(1)} %get-tuple-element.29), channel_id=1, source_target_pairs={{0,4},{4,8},{8,12},{12,16},{16,20},{20,24},{24,28},{28,32},{32,36}... | collective-permute-start | bytes 64520 | tf_op jit(solution)/shard_map/ppermute | solution.py:20
  15.5 1.9 %collective-permute-start.1 = (bf16[14,3,256]{2,1,0:T(4,128)(2,1)S(1)}, bf16[14,3,256]{2,1,0:T(4,128)(2,1)S(1)}, u32[]{:S(2)}, u32[]{:S(2)}) collective-permute-start(bf16[14,3,256]{2,1,0:T(4,128)(2,1)S(1)} %get-tuple-element.30), channel_id=1, source_target_pairs={{4,0},{8,4},{12,8},{16,12},{20,16},{24,20},{28,24},{32,28},{36,32}... | collective-permute-start | bytes 64520 | tf_op jit(solution)/shard_map/ppermute | solution.py:22
  19.5 1.2 collective-permute-done.1
  20.7 1.6 %pad_maximum_fusion.1 = bf16[14,134,256]{2,1,0:T(8,128)(2,1)S(1)} fusion(bf16[14,3,256]{2,1,0:T(4,128)(2,1)S(1)} %collective-permute-done.1, bf16[14,128,256]{2,1,0:T(8,128)(2,1)} %pad_dynamic-slice_fusion.2, bf16[14,3,256]{2,1,0:T(4,128)(2,1)S(1)} %collective-permute-done), kind=kLoop, calls=%fused_computation.32 | loop fusion | flops 2881536 | bytes 1921024 | tf_op jit(solution)/shard_map/concatenate | solution.py:18
  22.4 2.8 %collective-permute-start.3 = (f32[144,128]{1,0:T(8,128)S(1)}, f32[144,128]{1,0:T(8,128)S(1)}, u32[]{:S(2)}, u32[]{:S(2)}) collective-permute-start(f32[144,128]{1,0:T(8,128)S(1)} %constant_dynamic-update-slice_fusion.14), channel_id=1, source_target_pairs={{0,128},{4,132},{8,136},{12,140},{16,144},{20,148},{24,152},{28,15... | collective-permute-start | bytes 221192 | tf_op jit(solution)/shard_map/ppermute | solution.py:62
  25.2 1.9 %collective-permute-done.3 = f32[144,128]{1,0:T(8,128)S(1)} collective-permute-done((f32[144,128]{1,0:T(8,128)S(1)}, f32[144,128]{1,0:T(8,128)S(1)}, u32[]{:S(2)}, u32[]{:S(2)}) %collective-permute-start.3) | collective-permute-done | bytes 73760 | tf_op jit(solution)/shard_map/ppermute | solution.py:62
  29.6 2.1 %collective-permute-start.4 = (f32[288,128]{1,0:T(8,128)S(1)}, f32[288,128]{1,0:T(8,128)}, u32[]{:S(2)}, u32[]{:S(2)}) collective-permute-start(f32[288,128]{1,0:T(8,128)S(1)} %constant_dynamic-update-slice_fusion.12), channel_id=1, source_target_pairs={{0,16},{4,20},{8,24},{12,60},{16,0},{20,4},{24,8},{28,44},{32,48},... | collective-permute-start | bytes 442376 | tf_op jit(solution)/shard_map/ppermute | solution.py:62
  36.1 1.1 reduce_sum.28
  38.2 2.5 %collective-permute-start.5 = (f32[576,128]{1,0:T(8,128)S(1)}, f32[576,128]{1,0:T(8,128)S(1)}, u32[]{:S(2)}, u32[]{:S(2)}) collective-permute-start(f32[576,128]{1,0:T(8,128)S(1)} %constant_dynamic-update-slice_fusion.10), channel_id=1, source_target_pairs={{0,64},{4,196},{8,72},{12,204},{16,80},{20,212},{24,88},{28,220},{... | collective-permute-start | bytes 884744 | tf_op jit(solution)/shard_map/ppermute | solution.py:62
  40.9 4.1 %collective-permute-done.5 = f32[576,128]{1,0:T(8,128)S(1)} collective-permute-done((f32[576,128]{1,0:T(8,128)S(1)}, f32[576,128]{1,0:T(8,128)S(1)}, u32[]{:S(2)}, u32[]{:S(2)}) %collective-permute-start.5) | collective-permute-done | bytes 294944 | tf_op jit(solution)/shard_map/ppermute | solution.py:62
  45.1 1.4 collective-permute-start.8
  46.5 2.6 %collective-permute-start.9 = (bf16[6,66,256]{2,1,0:T(8,128)(2,1)S(1)}, bf16[6,66,256]{2,1,0:T(8,128)(2,1)S(1)}, u32[]{:S(2)}, u32[]{:S(2)}) collective-permute-start(bf16[6,66,256]{2,1,0:T(8,128)(2,1)S(1)} %fusion.17), channel_id=1, source_target_pairs={{0,2},{1,3},{2,0},{3,1},{4,6},{5,7},{6,4},{7,5},{8,10},{9,11},{10,... | collective-permute-start | bytes 608264 | tf_op jit(solution)/shard_map/ppermute | solution.py:273
  50.1 5.2 %collective-permute-start.6 = (f32[1152,128]{1,0:T(8,128)S(1)}, f32[1152,128]{1,0:T(8,128)S(1)}, u32[]{:S(2)}, u32[]{:S(2)}) collective-permute-start(f32[1152,128]{1,0:T(8,128)S(1)} %constant_dynamic-update-slice_fusion.8), channel_id=1, source_target_pairs={{0,8},{4,60},{8,0},{12,20},{16,24},{20,12},{24,16},{28,36},{32,40}... | collective-permute-start | bytes 1769480 | tf_op jit(solution)/shard_map/ppermute | solution.py:62
  55.6 1.2 collective-permute-done.9
  62.6 2.6 %collective-permute-start.7 = (f32[2304,128]{1,0:T(8,128)S(1)}, f32[2304,128]{1,0:T(8,128)S(1)}, u32[]{:S(2)}, u32[]{:S(2)}) collective-permute-start(f32[2304,128]{1,0:T(8,128)S(1)} %constant_dynamic-update-slice_fusion.6), channel_id=1, source_target_pairs={{0,4},{4,0},{8,12},{12,8},{16,20},{20,16},{24,28},{28,24},{32,36},... | collective-permute-start | bytes 3538952 | tf_op jit(solution)/shard_map/ppermute | solution.py:62
  66.4 1.1 fusion.9
  68.0 1.3 copy-done.2
  69.5 1.4 gather_fusion.1
  71.1 2.0 %convert_reduce_fusion = (f32[128]{0:T(128)S(1)}, bf16[1536,128]{1,0:T(8,128)(2,1)S(1)}) fusion(f32[1536,128]{1,0:T(8,128)} %fusion.9, f32[32,128]{1,0:T(8,128)S(1)} %gather_fusion.1, f32[32]{0:T(128)S(1)} %fusion.3, s32[1536]{0:T(1024)S(1)} %eq.102), kind=kOutput, calls=%fused_computation.47 | convolution fusion | flops 76337024 | bytes 1202816 | tf_op jit(solution)/shard_map/dot_general | solution.py:287
  77.0 65.2 %shard_map.112 = (f32[2560,128]{1,0:T(8,128)}, f32[2048,128]{1,0:T(8,128)}) custom-call(f32[2560,128]{1,0:T(8,128)} %copy-done.3, f32[32,128]{1,0:T(8,128)} %fusion.18.sums_ref), custom_call_target="tpu_custom_call" | custom-call | tf_op jit(solution)/shard_map/pallas_call | solution.py:169
  142.2 2.4 %slice.207 = f32[2304,128]{1,0:T(8,128)} slice(f32[2560,128]{1,0:T(8,128)} %get-tuple-element.26), slice={[0:2304], [0:128]} | slice | bytes 2359296 | tf_op jit(solution)/shard_map/slice | solution.py:327
  144.7 1.2 slice_bitcast_fusion
  146.2 1.2 convolution_divide_fusion
  (107 shorter events, 26.5 us)
Async XLA Ops:
  2.5 15.0 %copy-start.1 = (bf16[48,128,256]{2,1,0:T(8,128)(2,1)S(1)}, bf16[48,128,256]{2,1,0:T(8,128)(2,1)}, u32[]{:S(2)}) copy-start(bf16[48,128,256]{2,1,0:T(8,128)(2,1)} %param.11) | copy-start | bytes 9437188
  3.4 18.9 %collective-permute-start.2 = (f32[72,128]{1,0:T(8,128)S(1)}, f32[72,128]{1,0:T(8,128)S(1)}, u32[]{:S(2)}, u32[]{:S(2)}) collective-permute-start(f32[72,128]{1,0:T(8,128)S(1)} %get-tuple-element.40), channel_id=1, source_target_pairs={{0,32},{4,36},{8,40},{12,44},{16,48},{20,52},{24,56},{28,60},{32,0... | collective-permute-start | bytes 110600 | tf_op jit(solution)/shard_map/ppermute | solution.py:62
  12.0 7.5 %collective-permute-start = (bf16[14,3,256]{2,1,0:T(4,128)(2,1)S(1)}, bf16[14,3,256]{2,1,0:T(4,128)(2,1)S(1)}, u32[]{:S(2)}, u32[]{:S(2)}) collective-permute-start(bf16[14,3,256]{2,1,0:T(4,128)(2,1)S(1)} %get-tuple-element.29), channel_id=1, source_target_pairs={{0,4},{4,8},{8,12},{12,16},{16,20},{20,24},{24,28},{28,32},{32,36}... | collective-permute-start | bytes 64520 | tf_op jit(solution)/shard_map/ppermute | solution.py:20
  15.5 3.0 %copy-start = (s32[64]{0:T(128)S(1)}, s32[64]{0:T(128)}, u32[]{:S(2)}) copy-start(s32[64]{0:T(128)} %constant.295.clone) | copy-start | bytes 772
  15.5 3.7 %copy-start.9 = (s32[32]{0:T(128)S(1)}, s32[32]{0:T(128)}, u32[]{:S(2)}) copy-start(s32[32]{0:T(128)} %param.17) | copy-start | bytes 388
  15.5 5.2 %collective-permute-start.1 = (bf16[14,3,256]{2,1,0:T(4,128)(2,1)S(1)}, bf16[14,3,256]{2,1,0:T(4,128)(2,1)S(1)}, u32[]{:S(2)}, u32[]{:S(2)}) collective-permute-start(bf16[14,3,256]{2,1,0:T(4,128)(2,1)S(1)} %get-tuple-element.30), channel_id=1, source_target_pairs={{4,0},{8,4},{12,8},{16,12},{20,16},{24,20},{28,24},{32,28},{36,32}... | collective-permute-start | bytes 64520 | tf_op jit(solution)/shard_map/ppermute | solution.py:22
  22.4 4.8 %collective-permute-start.3 = (f32[144,128]{1,0:T(8,128)S(1)}, f32[144,128]{1,0:T(8,128)S(1)}, u32[]{:S(2)}, u32[]{:S(2)}) collective-permute-start(f32[144,128]{1,0:T(8,128)S(1)} %constant_dynamic-update-slice_fusion.14), channel_id=1, source_target_pairs={{0,128},{4,132},{8,136},{12,140},{16,144},{20,148},{24,152},{28,15... | collective-permute-start | bytes 221192 | tf_op jit(solution)/shard_map/ppermute | solution.py:62
  27.2 1.3 copy-start.4
  29.6 7.6 %collective-permute-start.4 = (f32[288,128]{1,0:T(8,128)S(1)}, f32[288,128]{1,0:T(8,128)}, u32[]{:S(2)}, u32[]{:S(2)}) collective-permute-start(f32[288,128]{1,0:T(8,128)S(1)} %constant_dynamic-update-slice_fusion.12), channel_id=1, source_target_pairs={{0,16},{4,20},{8,24},{12,60},{16,0},{20,4},{24,8},{28,44},{32,48},... | collective-permute-start | bytes 442376 | tf_op jit(solution)/shard_map/ppermute | solution.py:62
  33.7 0.7 copy-start.7
  38.2 6.9 %collective-permute-start.5 = (f32[576,128]{1,0:T(8,128)S(1)}, f32[576,128]{1,0:T(8,128)S(1)}, u32[]{:S(2)}, u32[]{:S(2)}) collective-permute-start(f32[576,128]{1,0:T(8,128)S(1)} %constant_dynamic-update-slice_fusion.10), channel_id=1, source_target_pairs={{0,64},{4,196},{8,72},{12,204},{16,80},{20,212},{24,88},{28,220},{... | collective-permute-start | bytes 884744 | tf_op jit(solution)/shard_map/ppermute | solution.py:62
  45.1 10.5 %collective-permute-start.8 = (bf16[6,66,256]{2,1,0:T(8,128)(2,1)S(1)}, bf16[6,66,256]{2,1,0:T(8,128)(2,1)S(1)}, u32[]{:S(2)}, u32[]{:S(2)}) collective-permute-start(bf16[6,66,256]{2,1,0:T(8,128)(2,1)S(1)} %fusion.17), channel_id=1, source_target_pairs={{0,1},{1,2},{2,3},{3,0},{4,5},{5,6},{6,7},{7,4},{8,9},{9,10},{10,1... | collective-permute-start | bytes 608264 | tf_op jit(solution)/shard_map/ppermute | solution.py:273
  46.5 10.3 %collective-permute-start.9 = (bf16[6,66,256]{2,1,0:T(8,128)(2,1)S(1)}, bf16[6,66,256]{2,1,0:T(8,128)(2,1)S(1)}, u32[]{:S(2)}, u32[]{:S(2)}) collective-permute-start(bf16[6,66,256]{2,1,0:T(8,128)(2,1)S(1)} %fusion.17), channel_id=1, source_target_pairs={{0,2},{1,3},{2,0},{3,1},{4,6},{5,7},{6,4},{7,5},{8,10},{9,11},{10,... | collective-permute-start | bytes 608264 | tf_op jit(solution)/shard_map/ppermute | solution.py:273
  49.0 7.7 %collective-permute-start.10 = (bf16[6,66,256]{2,1,0:T(8,128)(2,1)S(1)}, bf16[6,66,256]{2,1,0:T(8,128)(2,1)S(1)}, u32[]{:S(2)}, u32[]{:S(2)}) collective-permute-start(bf16[6,66,256]{2,1,0:T(8,128)(2,1)S(1)} %fusion.17), channel_id=1, source_target_pairs={{0,3},{1,0},{2,1},{3,2},{4,7},{5,4},{6,5},{7,6},{8,11},{9,8},{10,9... | collective-permute-start | bytes 608264 | tf_op jit(solution)/shard_map/ppermute | solution.py:273
  50.1 12.4 %collective-permute-start.6 = (f32[1152,128]{1,0:T(8,128)S(1)}, f32[1152,128]{1,0:T(8,128)S(1)}, u32[]{:S(2)}, u32[]{:S(2)}) collective-permute-start(f32[1152,128]{1,0:T(8,128)S(1)} %constant_dynamic-update-slice_fusion.8), channel_id=1, source_target_pairs={{0,8},{4,60},{8,0},{12,20},{16,24},{20,12},{24,16},{28,36},{32,40}... | collective-permute-start | bytes 1769480 | tf_op jit(solution)/shard_map/ppermute | solution.py:62
  56.8 1.1 copy-start.6
  61.2 4.0 %copy-start.8 = (f32[128]{0:T(128)S(1)}, f32[128]{0:T(128)}, u32[]{:S(2)}) copy-start(f32[128]{0:T(128)} %param.15) | copy-start | bytes 1540
  62.6 5.2 %collective-permute-start.7 = (f32[2304,128]{1,0:T(8,128)S(1)}, f32[2304,128]{1,0:T(8,128)S(1)}, u32[]{:S(2)}, u32[]{:S(2)}) collective-permute-start(f32[2304,128]{1,0:T(8,128)S(1)} %constant_dynamic-update-slice_fusion.6), channel_id=1, source_target_pairs={{0,4},{4,0},{8,12},{12,8},{16,20},{20,16},{24,28},{28,24},{32,36},... | collective-permute-start | bytes 3538952 | tf_op jit(solution)/shard_map/ppermute | solution.py:62
  67.9 1.4 copy-start.2
  75.9 1.1 copy-start.3
  142.2 4.0 %copy-start.5 = (f32[2048,128]{1,0:T(8,128)S(1)}, f32[2048,128]{1,0:T(8,128)}, u32[]{:S(2)}) copy-start(f32[2048,128]{1,0:T(8,128)} %get-tuple-element.25) | copy-start | bytes 3145732

commit v17 on v13

--- a/solution.py
+++ b/solution.py
@@ -243,7 +243,7 @@
     packed = jnp.concatenate([embed_grad, meta], axis=0)
     halving = [1 << k for k in range(strip_count.bit_length() - 1)]
     if len(halving) == 6:
-        halving = [1, 2, 16, 4, 32, 8]
+        halving = [1, 2, 16, 4, 8, 32]
     order = halving[::-1]
     shifted = strip_count == 64
     position = jnp.asarray(gather_position(order, strip_count, shifted))

time: 148 us -> 151 us (1.020)
  waiting for transfers between devices: 11 us -> 14.8 us
  starting transfers between devices: 33.5 us -> 31.4 us
    ppermute x6, starting transfers between devices: 23 us -> 20.1 us  [tree_gather(): other = lax.ppermute(held, axis, pairs)]
    ppermute x3, waiting for transfers between devices: 1.58 us -> 3.97 us  [body(): lax.ppermute(pooled, 'chan', [(i, (i + shift) % chan_count) for i in rang...]
where the time goes in v17:
time: 151 us; the launch traced here: 150 us
  Pallas kernels  66.5 us (44%)
  starting transfers between devices  31.4 us (21%)
  local copies, waits for them, and re-layouts  15.4 us (10%)
  matrix products  15.1 us (10%)
  waiting for transfers between devices  14.8 us (10%)
  other arithmetic  4.84 us (3%)
  between operations  1.57 us (1%)
    pallas_call x1, Pallas kernels, tree_sum(): pl.pallas_call(functools.partial(tree_kernel, count, chunk, width, dists,...  66.5 us
    ppermute x6, starting transfers between devices, tree_gather(): other = lax.ppermute(held, axis, pairs)  20.1 us
    ppermute x6, waiting for transfers between devices, tree_gather(): other = lax.ppermute(held, axis, pairs)  8.72 us
    dot_general x18, matrix products, convolve(): jnp.dot(band, weight[shift_row, shift_col], preferred_element_type=jnp.fl...  7.28 us
    ppermute x3, starting transfers between devices, body(): lax.ppermute(pooled, 'chan', [(i, (i + shift) % chan_count) for i in rang...  5.03 us
    unnamed x20, local copies, waits for them, and re-layouts  4.52 us
    ppermute x1, starting transfers between devices, with_halo(): lax.ppermute(tail, axis, [(i, (i + 1) % count) for i in range(ends)])  4.39 us
    dot_general x9, matrix products, body(): lax.dot_general(band, placed_grads[shift_col], (((0,), (0,)), ((), ())),...  4.34 us
  transfers between devices with their start and end apart: 11, of which 6 were waited for; matrix products, arithmetic and copies ran while one was open for 9% of the time, Pallas kernels for 0%

profile of v17, /device:TPU:1, one launch (start us, length us, event | category | flops | bytes accessed | tf_op | source)
XLA Modules:
  0.0 149.7 jit_solution(8194390562415770108)
XLA Ops:
  3.2 3.6 %collective-permute-start.2 = (f32[72,128]{1,0:T(8,128)S(1)}, f32[72,128]{1,0:T(8,128)S(1)}, u32[]{:S(2)}, u32[]{:S(2)}) collective-permute-start(f32[72,128]{1,0:T(8,128)S(1)} %get-tuple-element.37), channel_id=1, source_target_pairs={{0,128},{4,132},{8,136},{12,140},{16,144},{20,148},{24,152},{28,15... | collective-permute-start | bytes 110600 | tf_op jit(solution)/shard_map/ppermute | solution.py:62
  6.8 1.0 pad_dynamic-slice_fusion.1
  7.8 4.4 %collective-permute-start = (bf16[14,3,256]{2,1,0:T(4,128)(2,1)S(1)}, bf16[14,3,256]{2,1,0:T(4,128)(2,1)S(1)}, u32[]{:S(2)}, u32[]{:S(2)}) collective-permute-start(bf16[14,3,256]{2,1,0:T(4,128)(2,1)S(1)} %get-tuple-element.29), channel_id=1, source_target_pairs={{0,4},{4,8},{8,12},{12,16},{16,20},{20,24},{24,28},{28,32},{32,36}... | collective-permute-start | bytes 64520 | tf_op jit(solution)/shard_map/ppermute | solution.py:20
  12.3 1.9 %collective-permute-start.1 = (bf16[14,3,256]{2,1,0:T(4,128)(2,1)S(1)}, bf16[14,3,256]{2,1,0:T(4,128)(2,1)S(1)}, u32[]{:S(2)}, u32[]{:S(2)}) collective-permute-start(bf16[14,3,256]{2,1,0:T(4,128)(2,1)S(1)} %get-tuple-element.30), channel_id=1, source_target_pairs={{4,0},{8,4},{12,8},{16,12},{20,16},{24,20},{28,24},{32,28},{36,32}... | collective-permute-start | bytes 64520 | tf_op jit(solution)/shard_map/ppermute | solution.py:22
  15.3 2.1 %collective-permute-done.1 = bf16[14,3,256]{2,1,0:T(4,128)(2,1)S(1)} collective-permute-done((bf16[14,3,256]{2,1,0:T(4,128)(2,1)S(1)}, bf16[14,3,256]{2,1,0:T(4,128)(2,1)S(1)}, u32[]{:S(2)}, u32[]{:S(2)}) %collective-permute-start.1) | collective-permute-done | bytes 21536 | tf_op jit(solution)/shard_map/ppermute | solution.py:22
  17.9 6.1 %collective-permute-start.3 = (f32[144,128]{1,0:T(8,128)S(1)}, f32[144,128]{1,0:T(8,128)S(1)}, u32[]{:S(2)}, u32[]{:S(2)}) collective-permute-start(f32[144,128]{1,0:T(8,128)S(1)} %constant_dynamic-update-slice_fusion.14), channel_id=1, source_target_pairs={{0,32},{4,36},{8,40},{12,44},{16,48},{20,52},{24,56},{28,60},{32,0... | collective-permute-start | bytes 221192 | tf_op jit(solution)/shard_map/ppermute | solution.py:62
  24.0 2.0 %collective-permute-done.3 = f32[144,128]{1,0:T(8,128)S(1)} collective-permute-done((f32[144,128]{1,0:T(8,128)S(1)}, f32[144,128]{1,0:T(8,128)S(1)}, u32[]{:S(2)}, u32[]{:S(2)}) %collective-permute-start.3) | collective-permute-done | bytes 73760 | tf_op jit(solution)/shard_map/ppermute | solution.py:62
  26.3 1.1 copy-done.4
  28.5 3.5 %collective-permute-start.4 = (f32[288,128]{1,0:T(8,128)S(1)}, f32[288,128]{1,0:T(8,128)}, u32[]{:S(2)}, u32[]{:S(2)}) collective-permute-start(f32[288,128]{1,0:T(8,128)S(1)} %constant_dynamic-update-slice_fusion.12), channel_id=1, source_target_pairs={{0,16},{4,20},{8,24},{12,60},{16,0},{20,4},{24,8},{28,44},{32,48},... | collective-permute-start | bytes 442376 | tf_op jit(solution)/shard_map/ppermute | solution.py:62
  36.4 1.1 reduce_sum.28
  39.8 5.7 %collective-permute-done.5 = f32[576,128]{1,0:T(8,128)S(1)} collective-permute-done((f32[576,128]{1,0:T(8,128)S(1)}, f32[576,128]{1,0:T(8,128)S(1)}, u32[]{:S(2)}, u32[]{:S(2)}) %collective-permute-start.5) | collective-permute-done | bytes 294944 | tf_op jit(solution)/shard_map/ppermute | solution.py:62
  45.6 1.3 collective-permute-start.8
  46.9 2.7 %collective-permute-start.9 = (bf16[6,66,256]{2,1,0:T(8,128)(2,1)S(1)}, bf16[6,66,256]{2,1,0:T(8,128)(2,1)S(1)}, u32[]{:S(2)}, u32[]{:S(2)}) collective-permute-start(bf16[6,66,256]{2,1,0:T(8,128)(2,1)S(1)} %fusion.44), channel_id=1, source_target_pairs={{0,2},{1,3},{2,0},{3,1},{4,6},{5,7},{6,4},{7,5},{8,10},{9,11},{10,... | collective-permute-start | bytes 608264 | tf_op jit(solution)/shard_map/ppermute | solution.py:273
  49.6 1.0 collective-permute-start.10
  50.6 4.1 %collective-permute-start.6 = (f32[1152,128]{1,0:T(8,128)S(1)}, f32[1152,128]{1,0:T(8,128)S(1)}, u32[]{:S(2)}, u32[]{:S(2)}) collective-permute-start(f32[1152,128]{1,0:T(8,128)S(1)} %constant_dynamic-update-slice_fusion.8), channel_id=1, source_target_pairs={{0,8},{4,60},{8,0},{12,20},{16,24},{20,12},{24,16},{28,36},{32,40}... | collective-permute-start | bytes 1769480 | tf_op jit(solution)/shard_map/ppermute | solution.py:62
  55.0 4.0 %collective-permute-done.9 = bf16[6,66,256]{2,1,0:T(8,128)(2,1)S(1)} collective-permute-done((bf16[6,66,256]{2,1,0:T(8,128)(2,1)S(1)}, bf16[6,66,256]{2,1,0:T(8,128)(2,1)S(1)}, u32[]{:S(2)}, u32[]{:S(2)}) %collective-permute-start.9) | collective-permute-done | bytes 202784 | tf_op jit(solution)/shard_map/ppermute | solution.py:273
  63.9 1.8 %collective-permute-start.7 = (f32[2304,128]{1,0:T(8,128)S(1)}, f32[2304,128]{1,0:T(8,128)S(1)}, u32[]{:S(2)}, u32[]{:S(2)}) collective-permute-start(f32[2304,128]{1,0:T(8,128)S(1)} %constant_dynamic-update-slice_fusion.6), channel_id=1, source_target_pairs={{0,4},{4,0},{8,12},{12,8},{16,20},{20,16},{24,28},{28,24},{32,36},... | collective-permute-start | bytes 3538952 | tf_op jit(solution)/shard_map/ppermute | solution.py:62
  68.5 1.3 copy-done.2
  70.0 1.4 gather_fusion.1
  76.9 1.1 copy-done.3
  78.0 66.5 %shard_map.112 = (f32[2560,128]{1,0:T(8,128)}, f32[2048,128]{1,0:T(8,128)}) custom-call(f32[2560,128]{1,0:T(8,128)} %copy-done.3, f32[32,128]{1,0:T(8,128)} %fusion.45.sums_ref), custom_call_target="tpu_custom_call" | custom-call | tf_op jit(solution)/shard_map/pallas_call | solution.py:169
  144.5 2.4 %slice.171 = f32[2304,128]{1,0:T(8,128)} slice(f32[2560,128]{1,0:T(8,128)} %get-tuple-element.26), slice={[0:2304], [0:128]} | slice | bytes 2359296 | tf_op jit(solution)/shard_map/slice | solution.py:328
  146.9 1.2 slice_bitcast_fusion
  148.5 1.2 convolution_divide_fusion
  (103 shorter events, 25.6 us)
Async XLA Ops:
  3.2 14.6 %collective-permute-start.2 = (f32[72,128]{1,0:T(8,128)S(1)}, f32[72,128]{1,0:T(8,128)S(1)}, u32[]{:S(2)}, u32[]{:S(2)}) collective-permute-start(f32[72,128]{1,0:T(8,128)S(1)} %get-tuple-element.37), channel_id=1, source_target_pairs={{0,128},{4,132},{8,136},{12,140},{16,144},{20,148},{24,152},{28,15... | collective-permute-start | bytes 110600 | tf_op jit(solution)/shard_map/ppermute | solution.py:62
  6.8 7.4 %copy-start.1 = (bf16[48,128,256]{2,1,0:T(8,128)(2,1)S(1)}, bf16[48,128,256]{2,1,0:T(8,128)(2,1)}, u32[]{:S(2)}) copy-start(bf16[48,128,256]{2,1,0:T(8,128)(2,1)} %param.11) | copy-start | bytes 9437188
  7.8 7.5 %collective-permute-start = (bf16[14,3,256]{2,1,0:T(4,128)(2,1)S(1)}, bf16[14,3,256]{2,1,0:T(4,128)(2,1)S(1)}, u32[]{:S(2)}, u32[]{:S(2)}) collective-permute-start(bf16[14,3,256]{2,1,0:T(4,128)(2,1)S(1)} %get-tuple-element.29), channel_id=1, source_target_pairs={{0,4},{4,8},{8,12},{12,16},{16,20},{20,24},{24,28},{28,32},{32,36}... | collective-permute-start | bytes 64520 | tf_op jit(solution)/shard_map/ppermute | solution.py:20
  12.2 2.1 %copy-start = (s32[64]{0:T(128)S(1)}, s32[64]{0:T(128)}, u32[]{:S(2)}) copy-start(s32[64]{0:T(128)} %constant.295.clone) | copy-start | bytes 772
  12.2 2.8 %copy-start.9 = (s32[32]{0:T(128)S(1)}, s32[32]{0:T(128)}, u32[]{:S(2)}) copy-start(s32[32]{0:T(128)} %param.17) | copy-start | bytes 388
  12.3 5.2 %collective-permute-start.1 = (bf16[14,3,256]{2,1,0:T(4,128)(2,1)S(1)}, bf16[14,3,256]{2,1,0:T(4,128)(2,1)S(1)}, u32[]{:S(2)}, u32[]{:S(2)}) collective-permute-start(bf16[14,3,256]{2,1,0:T(4,128)(2,1)S(1)} %get-tuple-element.30), channel_id=1, source_target_pairs={{4,0},{8,4},{12,8},{16,12},{20,16},{24,20},{28,24},{32,28},{36,32}... | collective-permute-start | bytes 64520 | tf_op jit(solution)/shard_map/ppermute | solution.py:22
  17.9 8.2 %collective-permute-start.3 = (f32[144,128]{1,0:T(8,128)S(1)}, f32[144,128]{1,0:T(8,128)S(1)}, u32[]{:S(2)}, u32[]{:S(2)}) collective-permute-start(f32[144,128]{1,0:T(8,128)S(1)} %constant_dynamic-update-slice_fusion.14), channel_id=1, source_target_pairs={{0,32},{4,36},{8,40},{12,44},{16,48},{20,52},{24,56},{28,60},{32,0... | collective-permute-start | bytes 221192 | tf_op jit(solution)/shard_map/ppermute | solution.py:62
  26.1 1.3 copy-start.4
  28.5 9.2 %collective-permute-start.4 = (f32[288,128]{1,0:T(8,128)S(1)}, f32[288,128]{1,0:T(8,128)}, u32[]{:S(2)}, u32[]{:S(2)}) collective-permute-start(f32[288,128]{1,0:T(8,128)S(1)} %constant_dynamic-update-slice_fusion.12), channel_id=1, source_target_pairs={{0,16},{4,20},{8,24},{12,60},{16,0},{20,4},{24,8},{28,44},{32,48},... | collective-permute-start | bytes 442376 | tf_op jit(solution)/shard_map/ppermute | solution.py:62
  34.1 0.7 copy-start.7
  38.7 6.9 %collective-permute-start.5 = (f32[576,128]{1,0:T(8,128)S(1)}, f32[576,128]{1,0:T(8,128)S(1)}, u32[]{:S(2)}, u32[]{:S(2)}) collective-permute-start(f32[576,128]{1,0:T(8,128)S(1)} %constant_dynamic-update-slice_fusion.10), channel_id=1, source_target_pairs={{0,64},{4,196},{8,72},{12,204},{16,80},{20,212},{24,88},{28,220},{... | collective-permute-start | bytes 884744 | tf_op jit(solution)/shard_map/ppermute | solution.py:62
  45.6 9.4 %collective-permute-start.8 = (bf16[6,66,256]{2,1,0:T(8,128)(2,1)S(1)}, bf16[6,66,256]{2,1,0:T(8,128)(2,1)S(1)}, u32[]{:S(2)}, u32[]{:S(2)}) collective-permute-start(bf16[6,66,256]{2,1,0:T(8,128)(2,1)S(1)} %fusion.44), channel_id=1, source_target_pairs={{0,1},{1,2},{2,3},{3,0},{4,5},{5,6},{6,7},{7,4},{8,9},{9,10},{10,1... | collective-permute-start | bytes 608264 | tf_op jit(solution)/shard_map/ppermute | solution.py:273
  46.9 12.0 %collective-permute-start.9 = (bf16[6,66,256]{2,1,0:T(8,128)(2,1)S(1)}, bf16[6,66,256]{2,1,0:T(8,128)(2,1)S(1)}, u32[]{:S(2)}, u32[]{:S(2)}) collective-permute-start(bf16[6,66,256]{2,1,0:T(8,128)(2,1)S(1)} %fusion.44), channel_id=1, source_target_pairs={{0,2},{1,3},{2,0},{3,1},{4,6},{5,7},{6,4},{7,5},{8,10},{9,11},{10,... | collective-permute-start | bytes 608264 | tf_op jit(solution)/shard_map/ppermute | solution.py:273
  49.6 9.4 %collective-permute-start.10 = (bf16[6,66,256]{2,1,0:T(8,128)(2,1)S(1)}, bf16[6,66,256]{2,1,0:T(8,128)(2,1)S(1)}, u32[]{:S(2)}, u32[]{:S(2)}) collective-permute-start(bf16[6,66,256]{2,1,0:T(8,128)(2,1)S(1)} %fusion.44), channel_id=1, source_target_pairs={{0,3},{1,0},{2,1},{3,2},{4,7},{5,4},{6,5},{7,6},{8,11},{9,8},{10,9... | collective-permute-start | bytes 608264 | tf_op jit(solution)/shard_map/ppermute | solution.py:273
  50.6 13.3 %collective-permute-start.6 = (f32[1152,128]{1,0:T(8,128)S(1)}, f32[1152,128]{1,0:T(8,128)S(1)}, u32[]{:S(2)}, u32[]{:S(2)}) collective-permute-start(f32[1152,128]{1,0:T(8,128)S(1)} %constant_dynamic-update-slice_fusion.8), channel_id=1, source_target_pairs={{0,8},{4,60},{8,0},{12,20},{16,24},{20,12},{24,16},{28,36},{32,40}... | collective-permute-start | bytes 1769480 | tf_op jit(solution)/shard_map/ppermute | solution.py:62
  59.0 1.1 copy-start.6
  63.4 2.3 %copy-start.8 = (f32[128]{0:T(128)S(1)}, f32[128]{0:T(128)}, u32[]{:S(2)}) copy-start(f32[128]{0:T(128)} %param.15) | copy-start | bytes 1540
  63.9 4.3 %collective-permute-start.7 = (f32[2304,128]{1,0:T(8,128)S(1)}, f32[2304,128]{1,0:T(8,128)S(1)}, u32[]{:S(2)}, u32[]{:S(2)}) collective-permute-start(f32[2304,128]{1,0:T(8,128)S(1)} %constant_dynamic-update-slice_fusion.6), channel_id=1, source_target_pairs={{0,4},{4,0},{8,12},{12,8},{16,20},{20,16},{24,28},{28,24},{32,36},... | collective-permute-start | bytes 3538952 | tf_op jit(solution)/shard_map/ppermute | solution.py:62
  68.3 1.4 copy-start.2
  76.9 1.1 copy-start.3
  144.5 4.0 %copy-start.5 = (f32[2048,128]{1,0:T(8,128)S(1)}, f32[2048,128]{1,0:T(8,128)}, u32[]{:S(2)}) copy-start(f32[2048,128]{1,0:T(8,128)} %get-tuple-element.25) | copy-start | bytes 3145732

commit v18 on v13

--- a/solution.py
+++ b/solution.py
@@ -321,7 +321,7 @@
     total_grads, every_sums = tree_sum(local_grads, part_sums, "strip", halving, shifted)
     mine = strip_pos * owned + jnp.arange(owned, dtype=jnp.int32)
     pick = (mine[:, None] == every_slots[None, :]).astype(jnp.float32)
-    slot_sums = jnp.dot(pick, every_sums, precision=lax.Precision.HIGHEST)
+    slot_sums = jnp.dot(pick, every_sums, precision=lax.Precision.HIGH)
     slot_counts = jnp.dot(pick, every_counts, precision=lax.Precision.HIGHEST)
     embeddings = slot_sums / jnp.maximum(slot_counts, 1.0)[:, None]
 

time: 148 us -> 148 us (level)
  no operation moved by 1% of the time
where the time goes in v18:
time: 148 us; the launch traced here: 147 us
  Pallas kernels  65.7 us (44%)
  starting transfers between devices  33.5 us (23%)
  local copies, waits for them, and re-layouts  15.4 us (10%)
  matrix products  15 us (10%)
  waiting for transfers between devices  11 us (7%)
  other arithmetic  4.84 us (3%)
  between operations  1.57 us (1%)
    pallas_call x1, Pallas kernels, tree_sum(): pl.pallas_call(functools.partial(tree_kernel, count, chunk, width, dists,...  65.7 us
    ppermute x6, starting transfers between devices, tree_gather(): other = lax.ppermute(held, axis, pairs)  23 us
    ppermute x6, waiting for transfers between devices, tree_gather(): other = lax.ppermute(held, axis, pairs)  7.36 us
    dot_general x18, matrix products, convolve(): jnp.dot(band, weight[shift_row, shift_col], preferred_element_type=jnp.fl...  7.29 us
    ppermute x3, starting transfers between devices, body(): lax.ppermute(pooled, 'chan', [(i, (i + shift) % chan_count) for i in rang...  5.05 us
    unnamed x20, local copies, waits for them, and re-layouts  4.52 us
    dot_general x9, matrix products, body(): lax.dot_general(band, placed_grads[shift_col], (((0,), (0,)), ((), ())),...  4.33 us
    ppermute x1, starting transfers between devices, with_halo(): lax.ppermute(tail, axis, [(i, (i + 1) % count) for i in range(ends)])  3.49 us
  transfers between devices with their start and end apart: 11, of which 6 were waited for; matrix products, arithmetic and copies ran while one was open for 9% of the time, Pallas kernels for 0%

profile of v18, /device:TPU:1, one launch (start us, length us, event | category | flops | bytes accessed | tf_op | source)
XLA Modules:
  0.0 147.0 jit_solution(16371819587193666021)
XLA Ops:
  3.2 7.7 %collective-permute-start.2 = (f32[72,128]{1,0:T(8,128)S(1)}, f32[72,128]{1,0:T(8,128)S(1)}, u32[]{:S(2)}, u32[]{:S(2)}) collective-permute-start(f32[72,128]{1,0:T(8,128)S(1)} %get-tuple-element.37), channel_id=1, source_target_pairs={{0,32},{4,36},{8,40},{12,44},{16,48},{20,52},{24,56},{28,60},{32,0... | collective-permute-start | bytes 110600 | tf_op jit(solution)/shard_map/ppermute | solution.py:62
  12.0 3.5 %collective-permute-start = (bf16[14,3,256]{2,1,0:T(4,128)(2,1)S(1)}, bf16[14,3,256]{2,1,0:T(4,128)(2,1)S(1)}, u32[]{:S(2)}, u32[]{:S(2)}) collective-permute-start(bf16[14,3,256]{2,1,0:T(4,128)(2,1)S(1)} %get-tuple-element.29), channel_id=1, source_target_pairs={{0,4},{4,8},{8,12},{12,16},{16,20},{20,24},{24,28},{28,32},{32,36}... | collective-permute-start | bytes 64520 | tf_op jit(solution)/shard_map/ppermute | solution.py:20
  15.5 1.9 %collective-permute-start.1 = (bf16[14,3,256]{2,1,0:T(4,128)(2,1)S(1)}, bf16[14,3,256]{2,1,0:T(4,128)(2,1)S(1)}, u32[]{:S(2)}, u32[]{:S(2)}) collective-permute-start(bf16[14,3,256]{2,1,0:T(4,128)(2,1)S(1)} %get-tuple-element.30), channel_id=1, source_target_pairs={{4,0},{8,4},{12,8},{16,12},{20,16},{24,20},{28,24},{32,28},{36,32}... | collective-permute-start | bytes 64520 | tf_op jit(solution)/shard_map/ppermute | solution.py:22
  18.6 2.1 %collective-permute-done.1 = bf16[14,3,256]{2,1,0:T(4,128)(2,1)S(1)} collective-permute-done((bf16[14,3,256]{2,1,0:T(4,128)(2,1)S(1)}, bf16[14,3,256]{2,1,0:T(4,128)(2,1)S(1)}, u32[]{:S(2)}, u32[]{:S(2)}) %collective-permute-start.1) | collective-permute-done | bytes 21536 | tf_op jit(solution)/shard_map/ppermute | solution.py:22
  21.2 2.8 %collective-permute-start.3 = (f32[144,128]{1,0:T(8,128)S(1)}, f32[144,128]{1,0:T(8,128)S(1)}, u32[]{:S(2)}, u32[]{:S(2)}) collective-permute-start(f32[144,128]{1,0:T(8,128)S(1)} %constant_dynamic-update-slice_fusion.14), channel_id=1, source_target_pairs={{0,128},{4,132},{8,136},{12,140},{16,144},{20,148},{24,152},{28,15... | collective-permute-start | bytes 221192 | tf_op jit(solution)/shard_map/ppermute | solution.py:62
  24.0 1.9 %collective-permute-done.3 = f32[144,128]{1,0:T(8,128)S(1)} collective-permute-done((f32[144,128]{1,0:T(8,128)S(1)}, f32[144,128]{1,0:T(8,128)S(1)}, u32[]{:S(2)}, u32[]{:S(2)}) %collective-permute-start.3) | collective-permute-done | bytes 73760 | tf_op jit(solution)/shard_map/ppermute | solution.py:62
  26.2 1.1 copy-done.4
  28.4 2.1 %collective-permute-start.4 = (f32[288,128]{1,0:T(8,128)S(1)}, f32[288,128]{1,0:T(8,128)}, u32[]{:S(2)}, u32[]{:S(2)}) collective-permute-start(f32[288,128]{1,0:T(8,128)S(1)} %constant_dynamic-update-slice_fusion.12), channel_id=1, source_target_pairs={{0,16},{4,20},{8,24},{12,60},{16,0},{20,4},{24,8},{28,44},{32,48},... | collective-permute-start | bytes 442376 | tf_op jit(solution)/shard_map/ppermute | solution.py:62
  34.8 1.1 reduce_sum.28
  37.0 2.6 %collective-permute-start.5 = (f32[576,128]{1,0:T(8,128)S(1)}, f32[576,128]{1,0:T(8,128)S(1)}, u32[]{:S(2)}, u32[]{:S(2)}) collective-permute-start(f32[576,128]{1,0:T(8,128)S(1)} %constant_dynamic-update-slice_fusion.10), channel_id=1, source_target_pairs={{0,64},{4,196},{8,72},{12,204},{16,80},{20,212},{24,88},{28,220},{... | collective-permute-start | bytes 884744 | tf_op jit(solution)/shard_map/ppermute | solution.py:62
  39.7 4.1 %collective-permute-done.5 = f32[576,128]{1,0:T(8,128)S(1)} collective-permute-done((f32[576,128]{1,0:T(8,128)S(1)}, f32[576,128]{1,0:T(8,128)S(1)}, u32[]{:S(2)}, u32[]{:S(2)}) %collective-permute-start.5) | collective-permute-done | bytes 294944 | tf_op jit(solution)/shard_map/ppermute | solution.py:62
  43.9 1.4 collective-permute-start.8
  45.2 2.6 %collective-permute-start.9 = (bf16[6,66,256]{2,1,0:T(8,128)(2,1)S(1)}, bf16[6,66,256]{2,1,0:T(8,128)(2,1)S(1)}, u32[]{:S(2)}, u32[]{:S(2)}) collective-permute-start(bf16[6,66,256]{2,1,0:T(8,128)(2,1)S(1)} %fusion.44), channel_id=1, source_target_pairs={{0,2},{1,3},{2,0},{3,1},{4,6},{5,7},{6,4},{7,5},{8,10},{9,11},{10,... | collective-permute-start | bytes 608264 | tf_op jit(solution)/shard_map/ppermute | solution.py:273
  47.9 1.0 collective-permute-start.10
  48.9 5.1 %collective-permute-start.6 = (f32[1152,128]{1,0:T(8,128)S(1)}, f32[1152,128]{1,0:T(8,128)S(1)}, u32[]{:S(2)}, u32[]{:S(2)}) collective-permute-start(f32[1152,128]{1,0:T(8,128)S(1)} %constant_dynamic-update-slice_fusion.8), channel_id=1, source_target_pairs={{0,8},{4,60},{8,0},{12,20},{16,24},{20,12},{24,16},{28,36},{32,40}... | collective-permute-start | bytes 1769480 | tf_op jit(solution)/shard_map/ppermute | solution.py:62
  54.3 1.6 %collective-permute-done.9 = bf16[6,66,256]{2,1,0:T(8,128)(2,1)S(1)} collective-permute-done((bf16[6,66,256]{2,1,0:T(8,128)(2,1)S(1)}, bf16[6,66,256]{2,1,0:T(8,128)(2,1)S(1)}, u32[]{:S(2)}, u32[]{:S(2)}) %collective-permute-start.9) | collective-permute-done | bytes 202784 | tf_op jit(solution)/shard_map/ppermute | solution.py:273
  61.4 2.7 %collective-permute-start.7 = (f32[2304,128]{1,0:T(8,128)S(1)}, f32[2304,128]{1,0:T(8,128)S(1)}, u32[]{:S(2)}, u32[]{:S(2)}) collective-permute-start(f32[2304,128]{1,0:T(8,128)S(1)} %constant_dynamic-update-slice_fusion.6), channel_id=1, source_target_pairs={{0,4},{4,0},{8,12},{12,8},{16,20},{20,16},{24,28},{28,24},{32,36},... | collective-permute-start | bytes 3538952 | tf_op jit(solution)/shard_map/ppermute | solution.py:62
  66.8 1.3 copy-done.2
  68.3 1.4 gather_fusion.1
  75.2 1.1 copy-done.3
  76.3 65.7 %shard_map.112 = (f32[2560,128]{1,0:T(8,128)}, f32[2048,128]{1,0:T(8,128)}) custom-call(f32[2560,128]{1,0:T(8,128)} %copy-done.3, f32[32,128]{1,0:T(8,128)} %fusion.45.sums_ref), custom_call_target="tpu_custom_call" | custom-call | tf_op jit(solution)/shard_map/pallas_call | solution.py:169
  142.0 2.4 %slice.171 = f32[2304,128]{1,0:T(8,128)} slice(f32[2560,128]{1,0:T(8,128)} %get-tuple-element.26), slice={[0:2304], [0:128]} | slice | bytes 2359296 | tf_op jit(solution)/shard_map/slice | solution.py:328
  144.4 1.2 slice_bitcast_fusion
  146.0 1.0 convolution_divide_fusion
  (103 shorter events, 26.1 us)
Async XLA Ops:
  3.2 17.9 %collective-permute-start.2 = (f32[72,128]{1,0:T(8,128)S(1)}, f32[72,128]{1,0:T(8,128)S(1)}, u32[]{:S(2)}, u32[]{:S(2)}) collective-permute-start(f32[72,128]{1,0:T(8,128)S(1)} %get-tuple-element.37), channel_id=1, source_target_pairs={{0,32},{4,36},{8,40},{12,44},{16,48},{20,52},{24,56},{28,60},{32,0... | collective-permute-start | bytes 110600 | tf_op jit(solution)/shard_map/ppermute | solution.py:62
  11.0 6.5 %copy-start.1 = (bf16[48,128,256]{2,1,0:T(8,128)(2,1)S(1)}, bf16[48,128,256]{2,1,0:T(8,128)(2,1)}, u32[]{:S(2)}) copy-start(bf16[48,128,256]{2,1,0:T(8,128)(2,1)} %param.11) | copy-start | bytes 9437188
  12.0 6.6 %collective-permute-start = (bf16[14,3,256]{2,1,0:T(4,128)(2,1)S(1)}, bf16[14,3,256]{2,1,0:T(4,128)(2,1)S(1)}, u32[]{:S(2)}, u32[]{:S(2)}) collective-permute-start(bf16[14,3,256]{2,1,0:T(4,128)(2,1)S(1)} %get-tuple-element.29), channel_id=1, source_target_pairs={{0,4},{4,8},{8,12},{12,16},{16,20},{20,24},{24,28},{28,32},{32,36}... | collective-permute-start | bytes 64520 | tf_op jit(solution)/shard_map/ppermute | solution.py:20
  15.5 2.1 %copy-start = (s32[64]{0:T(128)S(1)}, s32[64]{0:T(128)}, u32[]{:S(2)}) copy-start(s32[64]{0:T(128)} %constant.295.clone) | copy-start | bytes 772
  15.5 2.8 %copy-start.9 = (s32[32]{0:T(128)S(1)}, s32[32]{0:T(128)}, u32[]{:S(2)}) copy-start(s32[32]{0:T(128)} %param.17) | copy-start | bytes 388
  15.5 5.2 %collective-permute-start.1 = (bf16[14,3,256]{2,1,0:T(4,128)(2,1)S(1)}, bf16[14,3,256]{2,1,0:T(4,128)(2,1)S(1)}, u32[]{:S(2)}, u32[]{:S(2)}) collective-permute-start(bf16[14,3,256]{2,1,0:T(4,128)(2,1)S(1)} %get-tuple-element.30), channel_id=1, source_target_pairs={{4,0},{8,4},{12,8},{16,12},{20,16},{24,20},{28,24},{32,28},{36,32}... | collective-permute-start | bytes 64520 | tf_op jit(solution)/shard_map/ppermute | solution.py:22
  21.2 4.8 %collective-permute-start.3 = (f32[144,128]{1,0:T(8,128)S(1)}, f32[144,128]{1,0:T(8,128)S(1)}, u32[]{:S(2)}, u32[]{:S(2)}) collective-permute-start(f32[144,128]{1,0:T(8,128)S(1)} %constant_dynamic-update-slice_fusion.14), channel_id=1, source_target_pairs={{0,128},{4,132},{8,136},{12,140},{16,144},{20,148},{24,152},{28,15... | collective-permute-start | bytes 221192 | tf_op jit(solution)/shard_map/ppermute | solution.py:62
  26.0 1.3 copy-start.4
  28.4 7.6 %collective-permute-start.4 = (f32[288,128]{1,0:T(8,128)S(1)}, f32[288,128]{1,0:T(8,128)}, u32[]{:S(2)}, u32[]{:S(2)}) collective-permute-start(f32[288,128]{1,0:T(8,128)S(1)} %constant_dynamic-update-slice_fusion.12), channel_id=1, source_target_pairs={{0,16},{4,20},{8,24},{12,60},{16,0},{20,4},{24,8},{28,44},{32,48},... | collective-permute-start | bytes 442376 | tf_op jit(solution)/shard_map/ppermute | solution.py:62
  32.5 0.7 copy-start.7
  37.0 6.9 %collective-permute-start.5 = (f32[576,128]{1,0:T(8,128)S(1)}, f32[576,128]{1,0:T(8,128)S(1)}, u32[]{:S(2)}, u32[]{:S(2)}) collective-permute-start(f32[576,128]{1,0:T(8,128)S(1)} %constant_dynamic-update-slice_fusion.10), channel_id=1, source_target_pairs={{0,64},{4,196},{8,72},{12,204},{16,80},{20,212},{24,88},{28,220},{... | collective-permute-start | bytes 884744 | tf_op jit(solution)/shard_map/ppermute | solution.py:62
  43.9 10.4 %collective-permute-start.8 = (bf16[6,66,256]{2,1,0:T(8,128)(2,1)S(1)}, bf16[6,66,256]{2,1,0:T(8,128)(2,1)S(1)}, u32[]{:S(2)}, u32[]{:S(2)}) collective-permute-start(bf16[6,66,256]{2,1,0:T(8,128)(2,1)S(1)} %fusion.44), channel_id=1, source_target_pairs={{0,1},{1,2},{2,3},{3,0},{4,5},{5,6},{6,7},{7,4},{8,9},{9,10},{10,1... | collective-permute-start | bytes 608264 | tf_op jit(solution)/shard_map/ppermute | solution.py:273
  45.2 10.7 %collective-permute-start.9 = (bf16[6,66,256]{2,1,0:T(8,128)(2,1)S(1)}, bf16[6,66,256]{2,1,0:T(8,128)(2,1)S(1)}, u32[]{:S(2)}, u32[]{:S(2)}) collective-permute-start(bf16[6,66,256]{2,1,0:T(8,128)(2,1)S(1)} %fusion.44), channel_id=1, source_target_pairs={{0,2},{1,3},{2,0},{3,1},{4,6},{5,7},{6,4},{7,5},{8,10},{9,11},{10,... | collective-permute-start | bytes 608264 | tf_op jit(solution)/shard_map/ppermute | solution.py:273
  47.9 8.1 %collective-permute-start.10 = (bf16[6,66,256]{2,1,0:T(8,128)(2,1)S(1)}, bf16[6,66,256]{2,1,0:T(8,128)(2,1)S(1)}, u32[]{:S(2)}, u32[]{:S(2)}) collective-permute-start(bf16[6,66,256]{2,1,0:T(8,128)(2,1)S(1)} %fusion.44), channel_id=1, source_target_pairs={{0,3},{1,0},{2,1},{3,2},{4,7},{5,4},{6,5},{7,6},{8,11},{9,8},{10,9... | collective-permute-start | bytes 608264 | tf_op jit(solution)/shard_map/ppermute | solution.py:273
  48.9 12.4 %collective-permute-start.6 = (f32[1152,128]{1,0:T(8,128)S(1)}, f32[1152,128]{1,0:T(8,128)S(1)}, u32[]{:S(2)}, u32[]{:S(2)}) collective-permute-start(f32[1152,128]{1,0:T(8,128)S(1)} %constant_dynamic-update-slice_fusion.8), channel_id=1, source_target_pairs={{0,8},{4,60},{8,0},{12,20},{16,24},{20,12},{24,16},{28,36},{32,40}... | collective-permute-start | bytes 1769480 | tf_op jit(solution)/shard_map/ppermute | solution.py:62
  56.0 1.1 copy-start.6
  60.4 3.6 %copy-start.8 = (f32[128]{0:T(128)S(1)}, f32[128]{0:T(128)}, u32[]{:S(2)}) copy-start(f32[128]{0:T(128)} %param.15) | copy-start | bytes 1540
  61.4 5.1 %collective-permute-start.7 = (f32[2304,128]{1,0:T(8,128)S(1)}, f32[2304,128]{1,0:T(8,128)S(1)}, u32[]{:S(2)}, u32[]{:S(2)}) collective-permute-start(f32[2304,128]{1,0:T(8,128)S(1)} %constant_dynamic-update-slice_fusion.6), channel_id=1, source_target_pairs={{0,4},{4,0},{8,12},{12,8},{16,20},{20,16},{24,28},{28,24},{32,36},... | collective-permute-start | bytes 3538952 | tf_op jit(solution)/shard_map/ppermute | solution.py:62
  66.6 1.4 copy-start.2
  75.2 1.1 copy-start.3
  142.0 4.0 %copy-start.5 = (f32[2048,128]{1,0:T(8,128)S(1)}, f32[2048,128]{1,0:T(8,128)}, u32[]{:S(2)}) copy-start(f32[2048,128]{1,0:T(8,128)} %get-tuple-element.25) | copy-start | bytes 3145732
